TPU v7x, 128 devices: a whole 4x4x4 slice. The times are simulated.
128 devices in a mesh: lat: 8 (over y_hi, x), lon: 16 (over z, y_lo, core).
Axes of the slice: x: 4, y: 4 (y_hi: 2, y_lo: 2; y = y_hi * 2 + y_lo), z: 4, core: 2. Of those that a mesh axis runs over, the one named last changes fastest.
Arguments:
- state: bfloat16 [64, 512, 128], P('lat', 'lon'), may hold values from -6 to 6
- kernel_in: bfloat16 [3, 3, 3, 32, 32], replicated, may hold values from -0.21875 to 0.21875
- kernel_mid: bfloat16 [3, 3, 3, 32, 64], replicated, may hold values from -0.21875 to 0.21875
- kernel_out: bfloat16 [3, 3, 3, 32, 32], replicated, may hold values from -0.21875 to 0.21875
- lift: bfloat16 [64, 32], replicated, may hold values from -0.75 to 0.75
- obs_cells: int32 [8, 256, 256, 4], P('lat', 'lon'), may hold values from 0 to 255, as said below
- obs_chan: int32 [8, 256, 256], P('lat', 'lon'), may hold values from 0 to 127
- obs_weights: float32 [8, 256, 256, 4], P('lat', 'lon'), may hold values from 0 to 1
- obs_value: float32 [8, 256, 256], P('lat', 'lon'), may hold values from -6 to 6
- obs_count: int32 [8, 256], P('lat', 'lon'), may hold values from 0 to 256, as said below
Outputs:
- gradient: float32 [64, 512, 128], P('lat', 'lon')
- innovation: float32 [8, 256, 256], P('lat', 'lon')
Inputs may be any that keep to these rules, and one draw needn't show every extreme that they name: `obs_cells`: each slot's four cells are a base cell, the next column, the next row and the cell diagonal to it, all inside one tile. `obs_count`: in every latitude tile row some destination tile receives 256 live slots from every owner.
All inputs are finite; a program needn't handle non-finite values.
Results may differ from a plain program's by a relative error of at most 0.0075.
Values may be sent and summed in bfloat16 or wider, within the bound.
A program may use at most 64 MiB of HBM per device.

v0:
```python
import jax
import jax.numpy as jnp
from jax import lax
from jax.sharding import PartitionSpec as P

C = 32
C2 = 64
LEV = 4


def with_halo(block, sides, width, periodic):
    for axis, dim in sides:
        count = lax.axis_size(axis)
        forward = [(i, i + 1) for i in range(count - 1)]
        if periodic:
            forward.append((count - 1, 0))
        backward = [(target, source) for source, target in forward]
        low = lax.ppermute(
            lax.slice_in_dim(block, block.shape[dim] - width, None, axis=dim), axis, forward
        )
        high = lax.ppermute(lax.slice_in_dim(block, 0, width, axis=dim), axis, backward)
        block = jnp.concatenate([low, block, high], axis=dim)
    return block


def banded(kernel, levels):
    lin = jnp.arange(levels, dtype=jnp.int32)
    taps = jnp.arange(3, dtype=jnp.int32)
    select = (lin[:, None, None] - lin[None, :, None] + 1 == taps[None, None, :]).astype(
        jnp.float32
    )
    full = jnp.einsum("pqt,abtcg->abpcqg", select, kernel.astype(jnp.float32))
    cin = kernel.shape[3]
    cout = kernel.shape[4]
    return full.reshape(9, levels * cin, levels * cout).astype(jnp.bfloat16)


def gelu_slope(value):
    inner = 0.7978845608 * (value + 0.044715 * value**3)
    tval = jnp.tanh(inner)
    return 0.5 * (1.0 + tval) + 0.5 * value * (1.0 - tval * tval) * 0.7978845608 * (
        1.0 + 0.134145 * value * value
    )


def extend(field):
    wide = with_halo(field, (("lon", 1),), 1, True)
    return with_halo(wide, (("lat", 0),), 1, False)


def conv_valid(padded, matrices, rows, cols):
    total = jnp.zeros((rows, cols, matrices.shape[2]), jnp.float32)
    for row_off in range(3):
        for col_off in range(3):
            piece = padded[row_off : row_off + rows, col_off : col_off + cols]
            total = total + jnp.einsum(
                "ijf,fg->ijg",
                piece,
                matrices[row_off * 3 + col_off],
                preferred_element_type=jnp.float32,
            )
    return total


def adjoint_valid(padded, matrices, rows, cols):
    total = jnp.zeros((rows, cols, matrices.shape[1]), jnp.float32)
    for row_off in range(3):
        for col_off in range(3):
            piece = padded[2 - row_off : 2 - row_off + rows, 2 - col_off : 2 - col_off + cols]
            total = total + jnp.einsum(
                "ijg,fg->ijf",
                piece,
                matrices[row_off * 3 + col_off],
                preferred_element_type=jnp.float32,
            )
    return total


def convolve(field, matrices):
    return conv_valid(extend(field), matrices, field.shape[0], field.shape[1])


def convolve_adjoint(grads, matrices):
    return adjoint_valid(extend(grads), matrices, grads.shape[0], grads.shape[1])


def widen(coarse):
    rows, cols, feats = coarse.shape
    return jnp.broadcast_to(coarse[:, None, :, None, :], (rows, 2, cols, 2, feats)).reshape(
        rows * 2, cols * 2, feats
    )


def block_sum(fine):
    rows, cols, feats = fine.shape
    return fine.reshape(rows // 2, 2, cols // 2, 2, feats).sum(axis=(1, 3))


def shards(
    state,
    kernel_in,
    kernel_mid,
    kernel_out,
    lift,
    obs_cells,
    obs_chan,
    obs_weights,
    obs_value,
    obs_count,
):
    feats = LEV * C
    rows, cols = (state.shape[0], state.shape[1])
    mat_in = banded(kernel_in, LEV)
    mat_mid = banded(kernel_mid, LEV)
    mat_out = banded(kernel_out, LEV)
    lift_full = (
        jnp.einsum("pq,cg->pcqg", jnp.eye(LEV, dtype=jnp.float32), lift.astype(jnp.float32))
        .reshape(LEV * C2, feats)
        .astype(jnp.bfloat16)
    )
    pre_first = convolve(state, mat_in)
    act_first = jax.nn.gelu(pre_first, approximate=True).astype(jnp.bfloat16)
    pooled = (block_sum(act_first.astype(jnp.float32)) * 0.25).astype(jnp.bfloat16)
    pre_mid = convolve(pooled, mat_mid)
    act_mid = jax.nn.gelu(pre_mid, approximate=True).astype(jnp.bfloat16)
    lifted = jnp.einsum("ijg,gf->ijf", act_mid, lift_full, preferred_element_type=jnp.float32)
    merged = (act_first.astype(jnp.float32) + widen(lifted)).astype(jnp.bfloat16)
    pre_last = convolve(merged, mat_out)
    slope_first = gelu_slope(pre_first)
    slope_mid = gelu_slope(pre_mid)
    output = state.astype(jnp.float32) + jax.nn.gelu(pre_last, approximate=True)
    flat_out = output.reshape(-1)
    slots = lax.broadcasted_iota(jnp.int32, obs_chan.shape, 2)
    live = (slots < obs_count[:, :, None]).astype(jnp.float32)
    weights = obs_weights * live[..., None]
    values = obs_value * live
    position = (obs_cells * feats + obs_chan[..., None]).astype(jnp.float32)
    found = jnp.take(
        flat_out,
        lax.all_to_all(position, "lon", split_axis=1, concat_axis=1, tiled=True).astype(jnp.int32),
    )
    samples = lax.all_to_all(
        found.astype(jnp.bfloat16), "lon", split_axis=1, concat_axis=1, tiled=True
    ).astype(found.dtype)
    innovation = jnp.sum(weights * samples, axis=-1) - values
    where_got, terms = (
        lax.all_to_all(position, "lon", split_axis=1, concat_axis=1, tiled=True),
        lax.all_to_all(
            weights * innovation[..., None], "lon", split_axis=1, concat_axis=1, tiled=True
        ),
    )
    grad_out = (
        jnp.zeros((rows * cols * feats,), jnp.float32)
        .at[where_got.astype(jnp.int32).reshape(-1)]
        .add(terms.reshape(-1))
        .reshape(rows, cols, feats)
    )
    grad_pre_last = (grad_out * gelu_slope(pre_last)).astype(jnp.bfloat16)
    grad_merged = convolve_adjoint(grad_pre_last, mat_out)
    grad_coarse = block_sum(grad_merged).astype(jnp.bfloat16)
    back_mid = jnp.einsum("ijf,gf->ijg", grad_coarse, lift_full, preferred_element_type=jnp.float32)
    grad_mid = (back_mid * slope_mid).astype(jnp.bfloat16)
    grad_pooled = convolve_adjoint(grad_mid, mat_mid)
    grad_first = ((grad_merged + widen(grad_pooled) * 0.25) * slope_first).astype(jnp.bfloat16)
    gradient = grad_out + convolve_adjoint(grad_first, mat_in)
    return (gradient, innovation)


def solution(mesh):
    placed = (
        P("lat", "lon", None),
        P(),
        P(),
        P(),
        P(),
        P("lat", "lon", None, None),
        P("lat", "lon", None),
        P("lat", "lon", None, None),
        P("lat", "lon", None),
        P("lat", "lon"),
    )
    return jax.shard_map(
        shards,
        mesh=mesh,
        in_specs=placed,
        out_specs=(P("lat", "lon", None), P("lat", "lon", None)),
        check_vma=False,
    )
```

profile of v0, /device:TPU:16, one launch (start us, length us, event | category | flops | bytes accessed | tf_op | source)
XLA Modules:
  0.0 343.6 jit_solution(10368958294693932492)
XLA Ops:
  0.6 0.7 fusion.204
  1.5 4.3 %collective-permute-start.1 = (bf16[8,1,128]{2,1,0:T(2,128)(2,1)S(1)}, bf16[8,1,128]{2,1,0:T(2,128)(2,1)S(1)}, u32[]{:S(2)}, u32[]{:S(2)}) collective-permute-start(bf16[8,1,128]{2,1,0:T(2,128)(2,1)S(1)} %get-tuple-element.25), channel_id=1, source_target_pairs={{1,0},{2,1},{3,2},{4,3},{5,4},{6,5},{7,6},{8,7},{9,8},{10,9},{11,1... | collective-permute-start | bytes 6152 | tf_op jit(solution)/shard_map/ppermute | solution.py:21
  5.7 1.5 fusion.137
  7.2 3.8 %all-to-all-start = ((f32[1,16,256,4]{2,3,0,1:T(4,128)}), f32[1,16,256,4]{2,3,0,1:T(4,128)S(1)}, u32[]{:S(2)}, u32[]{:S(2)}) async-start(f32[1,16,256,4]{2,3,0,1:T(4,128)} %fusion.137), calls=%async_computation | async-start | bytes 131072 | tf_op jit(solution)/shard_map/all_to_all | solution.py:147
  11.0 1.5 fusion
  12.5 0.5 copy.49
  13.1 0.6 convert_element_type.105
  13.7 0.2 copy-done.6
  13.9 0.8 convolution_bitcast_fusion
  14.7 0.6 fusion.1
  15.3 0.6 fusion.2
  16.0 0.7 fusion.179
  16.7 0.5 copy.51
  17.2 0.7 convert_element_type.111
  18.0 0.8 convert_element_type.115
  18.8 0.7 copy.54
  19.5 0.6 convert_element_type.119
  20.2 3.5 %collective-permute-start.2 = (bf16[1,34,128]{2,1,0:T(8,128)(2,1)S(1)}, bf16[1,34,128]{2,1,0:T(8,128)(2,1)S(1)}, u32[]{:S(2)}, u32[]{:S(2)}) collective-permute-start(bf16[1,34,128]{2,1,0:T(8,128)(2,1)S(1)} %get-tuple-element.16), channel_id=1, source_target_pairs={{0,16},{16,32},{32,48},{48,64},{64,80},{80,96},{96,112},{1,17},{17... | collective-permute-start | bytes 26120 | tf_op jit(solution)/shard_map/ppermute | solution.py:18
  23.7 6.1 %collective-permute-start.3 = (bf16[1,34,128]{2,1,0:T(8,128)(2,1)S(1)}, bf16[1,34,128]{2,1,0:T(8,128)(2,1)S(1)}, u32[]{:S(2)}, u32[]{:S(2)}) collective-permute-start(bf16[1,34,128]{2,1,0:T(8,128)(2,1)S(1)} %get-tuple-element.17), channel_id=1, source_target_pairs={{16,0},{32,16},{48,32},{64,48},{80,64},{96,80},{112,96},{17,1},{33... | collective-permute-start | bytes 26120 | tf_op jit(solution)/shard_map/ppermute | solution.py:21
  30.1 1.1 collective-permute-done.3
  32.4 3.8 %collective-permute-start.5 = (bf16[4,1,128]{2,1,0:T(2,128)(2,1)S(1)}, bf16[4,1,128]{2,1,0:T(2,128)(2,1)S(1)}, u32[]{:S(2)}, u32[]{:S(2)}) collective-permute-start(bf16[4,1,128]{2,1,0:T(2,128)(2,1)S(1)} %get-tuple-element.37), channel_id=1, source_target_pairs={{1,0},{2,1},{3,2},{4,3},{5,4},{6,5},{7,6},{8,7},{9,8},{10,9},{11,1... | collective-permute-start | bytes 3080 | tf_op jit(solution)/shard_map/ppermute | solution.py:21
  36.4 1.1 collective-permute-done.4
  37.6 1.9 collective-permute-start.6
  39.5 7.8 %collective-permute-start.7 = (bf16[1,18,128]{2,1,0:T(8,128)(2,1)S(1)}, bf16[1,18,128]{2,1,0:T(8,128)(2,1)S(1)}, u32[]{:S(2)}, u32[]{:S(2)}) collective-permute-start(bf16[1,18,128]{2,1,0:T(8,128)(2,1)S(1)} %get-tuple-element.35), channel_id=1, source_target_pairs={{16,0},{32,16},{48,32},{64,48},{80,64},{96,80},{112,96},{17,1},{33... | collective-permute-start | bytes 13832 | tf_op jit(solution)/shard_map/ppermute | solution.py:21
  47.5 1.2 collective-permute-done.7
  50.1 0.2 copy-done.19
  50.4 3.6 %collective-permute-start.9 = (bf16[8,1,128]{2,1,0:T(2,128)(2,1)S(1)}, bf16[8,1,128]{2,1,0:T(2,128)(2,1)S(1)}, u32[]{:S(2)}, u32[]{:S(2)}) collective-permute-start(bf16[8,1,128]{2,1,0:T(2,128)(2,1)S(1)} %get-tuple-element.23), channel_id=1, source_target_pairs={{1,0},{2,1},{3,2},{4,3},{5,4},{6,5},{7,6},{8,7},{9,8},{10,9},{11,1... | collective-permute-start | bytes 6152 | tf_op jit(solution)/shard_map/ppermute | solution.py:21
  54.1 1.1 collective-permute-done.8
  55.3 1.9 collective-permute-start.10
  57.2 8.0 %collective-permute-start.11 = (bf16[1,34,128]{2,1,0:T(8,128)(2,1)S(1)}, bf16[1,34,128]{2,1,0:T(8,128)(2,1)S(1)}, u32[]{:S(2)}, u32[]{:S(2)}) collective-permute-start(bf16[1,34,128]{2,1,0:T(8,128)(2,1)S(1)} %get-tuple-element.13), channel_id=1, source_target_pairs={{16,0},{32,16},{48,32},{64,48},{80,64},{96,80},{112,96},{17,1},{33... | collective-permute-start | bytes 26120 | tf_op jit(solution)/shard_map/ppermute | solution.py:21
  65.4 1.0 collective-permute-done.11
  67.4 0.9 multiply_add_fusion
  68.3 0.6 copy.55
  68.9 1.6 reshape.171
  70.6 100.9 %gather_fusion = bf16[16384]{0:T(1024)(128)(2,1)S(1)} fusion(bf16[32768]{0:T(1024)(128)(2,1)S(1)} %bitcast.210, s32[16384]{0:T(1024)S(1)} %broadcast_clamp_fusion), kind=kCustom, calls=%fused_computation | custom fusion | bytes 131072 | tf_op jit(solution)/shard_map/jit(_take)/gather | solution.py:138
  171.5 2.2 reshape.170
  173.8 0.4 copy.56
  174.2 0.6 copy.57
  174.8 4.9 %all-to-all-start.1 = ((bf16[1,16,256,4]{2,3,0,1:T(4,128)(2,1)}), bf16[1,16,256,4]{2,3,0,1:T(4,128)(2,1)S(1)}, u32[]{:S(2)}, u32[]{:S(2)}) async-start(bf16[1,16,256,4]{2,3,0,1:T(4,128)(2,1)} %copy.57), calls=%async_computation.1 | async-start | bytes 65536 | tf_op jit(solution)/shard_map/all_to_all | solution.py:142
  179.8 0.6 copy.46
  180.5 1.7 reshape.162
  182.3 3.6 %all-to-all-done.1 = bf16[1,16,256,4]{2,3,0,1:T(4,128)(2,1)S(1)} async-done(((bf16[1,16,256,4]{2,3,0,1:T(4,128)(2,1)}), bf16[1,16,256,4]{2,3,0,1:T(4,128)(2,1)S(1)}, u32[]{:S(2)}, u32[]{:S(2)}) %all-to-all-start.1) | async-done | bytes 32800 | tf_op jit(solution)/shard_map/all_to_all | solution.py:142
  186.0 0.7 fusion.140
  186.7 3.5 %all-to-all-start.2 = ((f32[1,16,256,4]{2,3,0,1:T(4,128)}), f32[1,16,256,4]{2,3,0,1:T(4,128)S(1)}, u32[]{:S(2)}, u32[]{:S(2)}) async-start(f32[1,16,256,4]{2,3,0,1:T(4,128)} %fusion.140), calls=%async_computation.2 | async-start | bytes 131072 | tf_op jit(solution)/shard_map/all_to_all | solution.py:148
  190.3 6.0 %all-to-all-done.2 = f32[1,16,256,4]{2,3,0,1:T(4,128)S(1)} async-done(((f32[1,16,256,4]{2,3,0,1:T(4,128)}), f32[1,16,256,4]{2,3,0,1:T(4,128)S(1)}, u32[]{:S(2)}, u32[]{:S(2)}) %all-to-all-start.2) | async-done | bytes 65568 | tf_op jit(solution)/shard_map/all_to_all | solution.py:148
  196.3 0.6 copy.58
  197.0 1.7 reshape.181
  198.6 85.9 %scatter_custom_fusion = f32[32768]{0:T(1024)S(1)} fusion(s32[16384]{0:T(1024)S(1)} %bitcast.218, f32[16384]{0:T(1024)S(1)} %reshape.181, f32[]{:T(128)} %constant.13.clone.1), kind=kCustom, calls=%fused_computation.202 | custom fusion | flops 16384 | bytes 131076 | tf_op jit(solution)/shard_map/scatter-add | solution.py:155
  284.8 3.8 %collective-permute-start.13 = (bf16[8,1,128]{2,1,0:T(2,128)(2,1)S(1)}, bf16[8,1,128]{2,1,0:T(2,128)(2,1)S(1)}, u32[]{:S(2)}, u32[]{:S(2)}) collective-permute-start(bf16[8,1,128]{2,1,0:T(2,128)(2,1)S(1)} %get-tuple-element.21), channel_id=1, source_target_pairs={{1,0},{2,1},{3,2},{4,3},{5,4},{6,5},{7,6},{8,7},{9,8},{10,9},{11,1... | collective-permute-start | bytes 6152 | tf_op jit(solution)/shard_map/ppermute | solution.py:21
  288.7 1.1 collective-permute-done.12
  289.9 6.9 %collective-permute-start.14 = (bf16[1,34,128]{2,1,0:T(8,128)(2,1)S(1)}, bf16[1,34,128]{2,1,0:T(8,128)(2,1)S(1)}, u32[]{:S(2)}, u32[]{:S(2)}) collective-permute-start(bf16[1,34,128]{2,1,0:T(8,128)(2,1)S(1)} %get-tuple-element.8), channel_id=1, source_target_pairs={{16,0},{32,16},{48,32},{64,48},{80,64},{96,80},{112,96},{17,1},{33... | collective-permute-start | bytes 26120 | tf_op jit(solution)/shard_map/ppermute | solution.py:21
  296.8 2.1 collective-permute-start.15
  299.1 6.9 %collective-permute-done.15 = bf16[1,34,128]{2,1,0:T(8,128)(2,1)S(1)} collective-permute-done((bf16[1,34,128]{2,1,0:T(8,128)(2,1)S(1)}, bf16[1,34,128]{2,1,0:T(8,128)(2,1)S(1)}, u32[]{:S(2)}, u32[]{:S(2)}) %collective-permute-start.15) | collective-permute-done | bytes 8736 | tf_op jit(solution)/shard_map/ppermute | solution.py:18
  307.6 3.8 %collective-permute-start.17 = (bf16[4,1,256]{2,1,0:T(2,128)(2,1)S(1)}, bf16[4,1,256]{2,1,0:T(2,128)(2,1)S(1)}, u32[]{:S(2)}, u32[]{:S(2)}) collective-permute-start(bf16[4,1,256]{2,1,0:T(2,128)(2,1)S(1)} %get-tuple-element.31), channel_id=1, source_target_pairs={{1,0},{2,1},{3,2},{4,3},{5,4},{6,5},{7,6},{8,7},{9,8},{10,9},{11,1... | collective-permute-start | bytes 6152 | tf_op jit(solution)/shard_map/ppermute | solution.py:21
  311.6 1.2 collective-permute-done.16
  312.8 1.9 collective-permute-start.18
  314.8 3.9 %collective-permute-start.19 = (bf16[1,18,256]{2,1,0:T(8,128)(2,1)S(1)}, bf16[1,18,256]{2,1,0:T(8,128)(2,1)S(1)}, u32[]{:S(2)}, u32[]{:S(2)}) collective-permute-start(bf16[1,18,256]{2,1,0:T(8,128)(2,1)S(1)} %get-tuple-element.29), channel_id=1, source_target_pairs={{0,16},{16,32},{32,48},{48,64},{64,80},{80,96},{96,112},{1,17},{17... | collective-permute-start | bytes 27656 | tf_op jit(solution)/shard_map/ppermute | solution.py:18
  318.8 5.1 %collective-permute-done.19 = bf16[1,18,256]{2,1,0:T(8,128)(2,1)S(1)} collective-permute-done((bf16[1,18,256]{2,1,0:T(8,128)(2,1)S(1)}, bf16[1,18,256]{2,1,0:T(8,128)(2,1)S(1)}, u32[]{:S(2)}, u32[]{:S(2)}) %collective-permute-start.19) | collective-permute-done | bytes 9248 | tf_op jit(solution)/shard_map/ppermute | solution.py:18
  325.4 3.8 %collective-permute-start.21 = (bf16[8,1,128]{2,1,0:T(2,128)(2,1)S(1)}, bf16[8,1,128]{2,1,0:T(2,128)(2,1)S(1)}, u32[]{:S(2)}, u32[]{:S(2)}) collective-permute-start(bf16[8,1,128]{2,1,0:T(2,128)(2,1)S(1)} %get-tuple-element.19), channel_id=1, source_target_pairs={{1,0},{2,1},{3,2},{4,3},{5,4},{6,5},{7,6},{8,7},{9,8},{10,9},{11,1... | collective-permute-start | bytes 6152 | tf_op jit(solution)/shard_map/ppermute | solution.py:21
  329.4 1.1 collective-permute-done.20
  330.6 1.9 collective-permute-start.22
  332.5 3.9 %collective-permute-start.23 = (bf16[1,34,128]{2,1,0:T(8,128)(2,1)S(1)}, bf16[1,34,128]{2,1,0:T(8,128)(2,1)S(1)}, u32[]{:S(2)}, u32[]{:S(2)}) collective-permute-start(bf16[1,34,128]{2,1,0:T(8,128)(2,1)S(1)} %get-tuple-element.5), channel_id=1, source_target_pairs={{0,16},{16,32},{32,48},{48,64},{64,80},{80,96},{96,112},{1,17},{17... | collective-permute-start | bytes 26120 | tf_op jit(solution)/shard_map/ppermute | solution.py:18
  336.6 5.1 %collective-permute-done.23 = bf16[1,34,128]{2,1,0:T(8,128)(2,1)S(1)} collective-permute-done((bf16[1,34,128]{2,1,0:T(8,128)(2,1)S(1)}, bf16[1,34,128]{2,1,0:T(8,128)(2,1)S(1)}, u32[]{:S(2)}, u32[]{:S(2)}) %collective-permute-start.23) | collective-permute-done | bytes 8736 | tf_op jit(solution)/shard_map/ppermute | solution.py:18
  342.7 0.8 fusion.6
  (159 shorter events, 10.2 us)
Async XLA Ops:
  1.4 18.8 %collective-permute-start = (bf16[8,1,128]{2,1,0:T(2,128)(2,1)S(1)}, bf16[8,1,128]{2,1,0:T(2,128)(2,1)S(1)}, u32[]{:S(2)}, u32[]{:S(2)}) collective-permute-start(bf16[8,1,128]{2,1,0:T(2,128)(2,1)S(1)} %get-tuple-element.24), channel_id=1, source_target_pairs={{0,1},{1,2},{2,3},{3,4},{4,5},{5,6},{6,7},{7,8},{8,9},{9,10},{10,1... | collective-permute-start | bytes 6152 | tf_op jit(solution)/shard_map/ppermute | solution.py:18
  1.5 18.7 %collective-permute-start.1 = (bf16[8,1,128]{2,1,0:T(2,128)(2,1)S(1)}, bf16[8,1,128]{2,1,0:T(2,128)(2,1)S(1)}, u32[]{:S(2)}, u32[]{:S(2)}) collective-permute-start(bf16[8,1,128]{2,1,0:T(2,128)(2,1)S(1)} %get-tuple-element.25), channel_id=1, source_target_pairs={{1,0},{2,1},{3,2},{4,3},{5,4},{6,5},{7,6},{8,7},{9,8},{10,9},{11,1... | collective-permute-start | bytes 6152 | tf_op jit(solution)/shard_map/ppermute | solution.py:21
  7.2 61.0 %all-to-all-start = ((f32[1,16,256,4]{2,3,0,1:T(4,128)}), f32[1,16,256,4]{2,3,0,1:T(4,128)S(1)}, u32[]{:S(2)}, u32[]{:S(2)}) async-start(f32[1,16,256,4]{2,3,0,1:T(4,128)} %fusion.137), calls=%async_computation | async-start | bytes 131072 | tf_op jit(solution)/shard_map/all_to_all | solution.py:147
  13.1 0.8 copy-start.6
  13.1 1.7 copy-start.13
  13.9 18.1 %copy-start.2 = (bf16[9,128,128]{2,1,0:T(8,128)(2,1)}, bf16[9,128,128]{2,1,0:T(8,128)(2,1)S(1)}, u32[]{:S(2)}) copy-start(bf16[9,128,128]{2,1,0:T(8,128)(2,1)S(1)} %convert_element_type.105) | copy-start | bytes 884740
  13.9 1.4 copy-start.23
  13.9 1.4 copy-start.14
  15.3 0.7 copy-start.24
  18.0 31.6 %copy-start = (bf16[9,128,256]{2,1,0:T(8,128)(2,1)}, bf16[9,128,256]{2,1,0:T(8,128)(2,1)S(1)}, u32[]{:S(2)}) copy-start(bf16[9,128,256]{2,1,0:T(8,128)(2,1)S(1)} %convert_element_type.111) | copy-start | bytes 1769476
  20.1 47.2 %copy-start.4 = (bf16[9,128,128]{2,1,0:T(8,128)(2,1)}, bf16[9,128,128]{2,1,0:T(8,128)(2,1)S(1)}, u32[]{:S(2)}) copy-start(bf16[9,128,128]{2,1,0:T(8,128)(2,1)S(1)} %convert_element_type.119) | copy-start | bytes 884740
  20.1 11.8 %copy-start.12 = (f32[8,32,128]{2,1,0:T(8,128)S(1)}, f32[8,32,128]{2,1,0:T(8,128)}, u32[]{:S(2)}) copy-start(f32[8,32,128]{2,1,0:T(8,128)} %convolution_bitcast_fusion) | copy-start | bytes 393220
  20.2 9.9 %collective-permute-start.2 = (bf16[1,34,128]{2,1,0:T(8,128)(2,1)S(1)}, bf16[1,34,128]{2,1,0:T(8,128)(2,1)S(1)}, u32[]{:S(2)}, u32[]{:S(2)}) collective-permute-start(bf16[1,34,128]{2,1,0:T(8,128)(2,1)S(1)} %get-tuple-element.16), channel_id=1, source_target_pairs={{0,16},{16,32},{32,48},{48,64},{64,80},{80,96},{96,112},{1,17},{17... | collective-permute-start | bytes 26120 | tf_op jit(solution)/shard_map/ppermute | solution.py:18
  23.7 7.4 %collective-permute-start.3 = (bf16[1,34,128]{2,1,0:T(8,128)(2,1)S(1)}, bf16[1,34,128]{2,1,0:T(8,128)(2,1)S(1)}, u32[]{:S(2)}, u32[]{:S(2)}) collective-permute-start(bf16[1,34,128]{2,1,0:T(8,128)(2,1)S(1)} %get-tuple-element.17), channel_id=1, source_target_pairs={{16,0},{32,16},{48,32},{64,48},{80,64},{96,80},{112,96},{17,1},{33... | collective-permute-start | bytes 26120 | tf_op jit(solution)/shard_map/ppermute | solution.py:21
  32.2 17.7 %copy-start.7 = (f32[8,32,128]{2,1,0:T(8,128)}, f32[8,32,128]{2,1,0:T(8,128)S(1)}, u32[]{:S(2)}) copy-start(f32[8,32,128]{2,1,0:T(8,128)S(1)} %get-tuple-element.39) | copy-start | bytes 393220
  32.2 17.5 %copy-start.17 = (bf16[256,128]{0,1:T(8,128)(2,1)S(1)}, bf16[256,128]{0,1:T(8,128)(2,1)}, u32[]{:S(2)}) copy-start(bf16[256,128]{0,1:T(8,128)(2,1)} %convert_element_type.115) | copy-start | bytes 196612
  32.4 5.2 %collective-permute-start.4 = (bf16[4,1,128]{2,1,0:T(2,128)(2,1)S(1)}, bf16[4,1,128]{2,1,0:T(2,128)(2,1)S(1)}, u32[]{:S(2)}, u32[]{:S(2)}) collective-permute-start(bf16[4,1,128]{2,1,0:T(2,128)(2,1)S(1)} %get-tuple-element.36), channel_id=1, source_target_pairs={{0,1},{1,2},{2,3},{3,4},{4,5},{5,6},{6,7},{7,8},{8,9},{9,10},{10,1... | collective-permute-start | bytes 3080 | tf_op jit(solution)/shard_map/ppermute | solution.py:18
  32.4 5.2 %collective-permute-start.5 = (bf16[4,1,128]{2,1,0:T(2,128)(2,1)S(1)}, bf16[4,1,128]{2,1,0:T(2,128)(2,1)S(1)}, u32[]{:S(2)}, u32[]{:S(2)}) collective-permute-start(bf16[4,1,128]{2,1,0:T(2,128)(2,1)S(1)} %get-tuple-element.37), channel_id=1, source_target_pairs={{1,0},{2,1},{3,2},{4,3},{5,4},{6,5},{7,6},{8,7},{9,8},{10,9},{11,1... | collective-permute-start | bytes 3080 | tf_op jit(solution)/shard_map/ppermute | solution.py:21
  37.6 9.9 %collective-permute-start.6 = (bf16[1,18,128]{2,1,0:T(8,128)(2,1)S(1)}, bf16[1,18,128]{2,1,0:T(8,128)(2,1)S(1)}, u32[]{:S(2)}, u32[]{:S(2)}) collective-permute-start(bf16[1,18,128]{2,1,0:T(8,128)(2,1)S(1)} %get-tuple-element.34), channel_id=1, source_target_pairs={{0,16},{16,32},{32,48},{48,64},{64,80},{80,96},{96,112},{1,17},{17... | collective-permute-start | bytes 13832 | tf_op jit(solution)/shard_map/ppermute | solution.py:18
  39.5 9.1 %collective-permute-start.7 = (bf16[1,18,128]{2,1,0:T(8,128)(2,1)S(1)}, bf16[1,18,128]{2,1,0:T(8,128)(2,1)S(1)}, u32[]{:S(2)}, u32[]{:S(2)}) collective-permute-start(bf16[1,18,128]{2,1,0:T(8,128)(2,1)S(1)} %get-tuple-element.35), channel_id=1, source_target_pairs={{16,0},{32,16},{48,32},{64,48},{80,64},{96,80},{112,96},{17,1},{33... | collective-permute-start | bytes 13832 | tf_op jit(solution)/shard_map/ppermute | solution.py:21
  49.7 0.6 copy-start.19
  50.0 5.2 %collective-permute-start.8 = (bf16[8,1,128]{2,1,0:T(2,128)(2,1)S(1)}, bf16[8,1,128]{2,1,0:T(2,128)(2,1)S(1)}, u32[]{:S(2)}, u32[]{:S(2)}) collective-permute-start(bf16[8,1,128]{2,1,0:T(2,128)(2,1)S(1)} %get-tuple-element.22), channel_id=1, source_target_pairs={{0,1},{1,2},{2,3},{3,4},{4,5},{5,6},{6,7},{7,8},{8,9},{9,10},{10,1... | collective-permute-start | bytes 6152 | tf_op jit(solution)/shard_map/ppermute | solution.py:18
  50.4 4.9 %collective-permute-start.9 = (bf16[8,1,128]{2,1,0:T(2,128)(2,1)S(1)}, bf16[8,1,128]{2,1,0:T(2,128)(2,1)S(1)}, u32[]{:S(2)}, u32[]{:S(2)}) collective-permute-start(bf16[8,1,128]{2,1,0:T(2,128)(2,1)S(1)} %get-tuple-element.23), channel_id=1, source_target_pairs={{1,0},{2,1},{3,2},{4,3},{5,4},{6,5},{7,6},{8,7},{9,8},{10,9},{11,1... | collective-permute-start | bytes 6152 | tf_op jit(solution)/shard_map/ppermute | solution.py:21
  55.3 10.1 %collective-permute-start.10 = (bf16[1,34,128]{2,1,0:T(8,128)(2,1)S(1)}, bf16[1,34,128]{2,1,0:T(8,128)(2,1)S(1)}, u32[]{:S(2)}, u32[]{:S(2)}) collective-permute-start(bf16[1,34,128]{2,1,0:T(8,128)(2,1)S(1)} %get-tuple-element.12), channel_id=1, source_target_pairs={{0,16},{16,32},{32,48},{48,64},{64,80},{80,96},{96,112},{1,17},{17... | collective-permute-start | bytes 26120 | tf_op jit(solution)/shard_map/ppermute | solution.py:18
  57.2 9.2 %collective-permute-start.11 = (bf16[1,34,128]{2,1,0:T(8,128)(2,1)S(1)}, bf16[1,34,128]{2,1,0:T(8,128)(2,1)S(1)}, u32[]{:S(2)}, u32[]{:S(2)}) collective-permute-start(bf16[1,34,128]{2,1,0:T(8,128)(2,1)S(1)} %get-tuple-element.13), channel_id=1, source_target_pairs={{16,0},{32,16},{48,32},{64,48},{80,64},{96,80},{112,96},{17,1},{33... | collective-permute-start | bytes 26120 | tf_op jit(solution)/shard_map/ppermute | solution.py:21
  68.2 2.3 copy-start.9
  171.5 2.6 copy-start.10
  174.8 11.0 %all-to-all-start.1 = ((bf16[1,16,256,4]{2,3,0,1:T(4,128)(2,1)}), bf16[1,16,256,4]{2,3,0,1:T(4,128)(2,1)S(1)}, u32[]{:S(2)}, u32[]{:S(2)}) async-start(bf16[1,16,256,4]{2,3,0,1:T(4,128)(2,1)} %copy.57), calls=%async_computation.1 | async-start | bytes 65536 | tf_op jit(solution)/shard_map/all_to_all | solution.py:142
  180.5 5.4 %copy-start.15 = (f32[1,16,256,4]{2,3,1,0:T(4,128)S(1)}, f32[1,16,256,4]{2,3,1,0:T(4,128)}, u32[]{:S(2)}) copy-start(f32[1,16,256,4]{2,3,1,0:T(4,128)} %param.17) | copy-start | bytes 196612
  180.5 5.4 %copy-start.16 = (f32[16,256]{1,0:T(8,128)S(1)}, f32[16,256]{1,0:T(8,128)}, u32[]{:S(2)}) copy-start(f32[16,256]{1,0:T(8,128)} %fusion.179) | copy-start | bytes 49156
  180.5 5.5 %copy-start.22 = (f32[1,16,256]{2,1,0:T(8,128)S(1)}, f32[1,16,256]{2,1,0:T(8,128)}, u32[]{:S(2)}) copy-start(f32[1,16,256]{2,1,0:T(8,128)} %param.18) | copy-start | bytes 49156
  180.5 5.5 %copy-start.25 = (s32[1,16]{1,0:T(1,128)S(1)}, s32[1,16]{1,0:T(1,128)}, u32[]{:S(2)}) copy-start(s32[1,16]{1,0:T(1,128)} %param.19) | copy-start | bytes 196
  186.0 10.9 %copy-start.21 = (f32[1,16,256]{2,1,0:T(8,128)}, f32[1,16,256]{2,1,0:T(8,128)S(1)}, u32[]{:S(2)}) copy-start(f32[1,16,256]{2,1,0:T(8,128)S(1)} %bitcast_subtract_fusion) | copy-start | bytes 49156
  186.7 9.6 %all-to-all-start.2 = ((f32[1,16,256,4]{2,3,0,1:T(4,128)}), f32[1,16,256,4]{2,3,0,1:T(4,128)S(1)}, u32[]{:S(2)}, u32[]{:S(2)}) async-start(f32[1,16,256,4]{2,3,0,1:T(4,128)} %fusion.140), calls=%async_computation.2 | async-start | bytes 131072 | tf_op jit(solution)/shard_map/all_to_all | solution.py:148
  196.9 87.5 %copy-start.11 = (f32[8,32,128]{2,1,0:T(8,128)S(1)}, f32[8,32,128]{2,1,0:T(8,128)}, u32[]{:S(2)}) copy-start(f32[8,32,128]{2,1,0:T(8,128)} %get-tuple-element.41) | copy-start | bytes 393220
  197.0 91.6 %copy-start.5 = (bf16[9,128,128]{2,1,0:T(8,128)(2,1)S(1)}, bf16[9,128,128]{2,1,0:T(8,128)(2,1)}, u32[]{:S(2)}) copy-start(bf16[9,128,128]{2,1,0:T(8,128)(2,1)} %copy-done.4) | copy-start | bytes 884740
  284.6 5.2 %collective-permute-start.12 = (bf16[8,1,128]{2,1,0:T(2,128)(2,1)S(1)}, bf16[8,1,128]{2,1,0:T(2,128)(2,1)S(1)}, u32[]{:S(2)}, u32[]{:S(2)}) collective-permute-start(bf16[8,1,128]{2,1,0:T(2,128)(2,1)S(1)} %get-tuple-element.20), channel_id=1, source_target_pairs={{0,1},{1,2},{2,3},{3,4},{4,5},{5,6},{6,7},{7,8},{8,9},{9,10},{10,1... | collective-permute-start | bytes 6152 | tf_op jit(solution)/shard_map/ppermute | solution.py:18
  284.8 5.1 %collective-permute-start.13 = (bf16[8,1,128]{2,1,0:T(2,128)(2,1)S(1)}, bf16[8,1,128]{2,1,0:T(2,128)(2,1)S(1)}, u32[]{:S(2)}, u32[]{:S(2)}) collective-permute-start(bf16[8,1,128]{2,1,0:T(2,128)(2,1)S(1)} %get-tuple-element.21), channel_id=1, source_target_pairs={{1,0},{2,1},{3,2},{4,3},{5,4},{6,5},{7,6},{8,7},{9,8},{10,9},{11,1... | collective-permute-start | bytes 6152 | tf_op jit(solution)/shard_map/ppermute | solution.py:21
  289.9 9.2 %collective-permute-start.14 = (bf16[1,34,128]{2,1,0:T(8,128)(2,1)S(1)}, bf16[1,34,128]{2,1,0:T(8,128)(2,1)S(1)}, u32[]{:S(2)}, u32[]{:S(2)}) collective-permute-start(bf16[1,34,128]{2,1,0:T(8,128)(2,1)S(1)} %get-tuple-element.8), channel_id=1, source_target_pairs={{16,0},{32,16},{48,32},{64,48},{80,64},{96,80},{112,96},{17,1},{33... | collective-permute-start | bytes 26120 | tf_op jit(solution)/shard_map/ppermute | solution.py:21
  296.8 9.2 %collective-permute-start.15 = (bf16[1,34,128]{2,1,0:T(8,128)(2,1)S(1)}, bf16[1,34,128]{2,1,0:T(8,128)(2,1)S(1)}, u32[]{:S(2)}, u32[]{:S(2)}) collective-permute-start(bf16[1,34,128]{2,1,0:T(8,128)(2,1)S(1)} %get-tuple-element.9), channel_id=1, source_target_pairs={{0,16},{16,32},{32,48},{48,64},{64,80},{80,96},{96,112},{1,17},{17... | collective-permute-start | bytes 26120 | tf_op jit(solution)/shard_map/ppermute | solution.py:18
  306.4 1.0 copy-start.18
  306.4 1.0 copy-start.20
  306.7 4.7 %copy-start.1 = (bf16[9,128,256]{2,1,0:T(8,128)(2,1)S(1)}, bf16[9,128,256]{2,1,0:T(8,128)(2,1)}, u32[]{:S(2)}) copy-start(bf16[9,128,256]{2,1,0:T(8,128)(2,1)} %copy-done) | copy-start | bytes 1769476
  307.4 17.8 %copy-start.8 = (f32[8,32,128]{2,1,0:T(8,128)S(1)}, f32[8,32,128]{2,1,0:T(8,128)}, u32[]{:S(2)}) copy-start(f32[8,32,128]{2,1,0:T(8,128)} %copy-done.7) | copy-start | bytes 393220
  307.6 5.2 %collective-permute-start.16 = (bf16[4,1,256]{2,1,0:T(2,128)(2,1)S(1)}, bf16[4,1,256]{2,1,0:T(2,128)(2,1)S(1)}, u32[]{:S(2)}, u32[]{:S(2)}) collective-permute-start(bf16[4,1,256]{2,1,0:T(2,128)(2,1)S(1)} %get-tuple-element.30), channel_id=1, source_target_pairs={{0,1},{1,2},{2,3},{3,4},{4,5},{5,6},{6,7},{7,8},{8,9},{9,10},{10,1... | collective-permute-start | bytes 6152 | tf_op jit(solution)/shard_map/ppermute | solution.py:18
  307.6 21.6 %copy-start.3 = (bf16[9,128,128]{2,1,0:T(8,128)(2,1)S(1)}, bf16[9,128,128]{2,1,0:T(8,128)(2,1)}, u32[]{:S(2)}) copy-start(bf16[9,128,128]{2,1,0:T(8,128)(2,1)} %copy-done.2) | copy-start | bytes 884740
  307.6 5.2 %collective-permute-start.17 = (bf16[4,1,256]{2,1,0:T(2,128)(2,1)S(1)}, bf16[4,1,256]{2,1,0:T(2,128)(2,1)S(1)}, u32[]{:S(2)}, u32[]{:S(2)}) collective-permute-start(bf16[4,1,256]{2,1,0:T(2,128)(2,1)S(1)} %get-tuple-element.31), channel_id=1, source_target_pairs={{1,0},{2,1},{3,2},{4,3},{5,4},{6,5},{7,6},{8,7},{9,8},{10,9},{11,1... | collective-permute-start | bytes 6152 | tf_op jit(solution)/shard_map/ppermute | solution.py:21
  312.8 6.0 %collective-permute-start.18 = (bf16[1,18,256]{2,1,0:T(8,128)(2,1)S(1)}, bf16[1,18,256]{2,1,0:T(8,128)(2,1)S(1)}, u32[]{:S(2)}, u32[]{:S(2)}) collective-permute-start(bf16[1,18,256]{2,1,0:T(8,128)(2,1)S(1)} %get-tuple-element.28), channel_id=1, source_target_pairs={{16,0},{32,16},{48,32},{64,48},{80,64},{96,80},{112,96},{17,1},{33... | collective-permute-start | bytes 27656 | tf_op jit(solution)/shard_map/ppermute | solution.py:21
  314.8 9.2 %collective-permute-start.19 = (bf16[1,18,256]{2,1,0:T(8,128)(2,1)S(1)}, bf16[1,18,256]{2,1,0:T(8,128)(2,1)S(1)}, u32[]{:S(2)}, u32[]{:S(2)}) collective-permute-start(bf16[1,18,256]{2,1,0:T(8,128)(2,1)S(1)} %get-tuple-element.29), channel_id=1, source_target_pairs={{0,16},{16,32},{32,48},{48,64},{64,80},{80,96},{96,112},{1,17},{17... | collective-permute-start | bytes 27656 | tf_op jit(solution)/shard_map/ppermute | solution.py:18
  325.3 5.2 %collective-permute-start.20 = (bf16[8,1,128]{2,1,0:T(2,128)(2,1)S(1)}, bf16[8,1,128]{2,1,0:T(2,128)(2,1)S(1)}, u32[]{:S(2)}, u32[]{:S(2)}) collective-permute-start(bf16[8,1,128]{2,1,0:T(2,128)(2,1)S(1)} %get-tuple-element.18), channel_id=1, source_target_pairs={{0,1},{1,2},{2,3},{3,4},{4,5},{5,6},{6,7},{7,8},{8,9},{9,10},{10,1... | collective-permute-start | bytes 6152 | tf_op jit(solution)/shard_map/ppermute | solution.py:18
  325.4 5.2 %collective-permute-start.21 = (bf16[8,1,128]{2,1,0:T(2,128)(2,1)S(1)}, bf16[8,1,128]{2,1,0:T(2,128)(2,1)S(1)}, u32[]{:S(2)}, u32[]{:S(2)}) collective-permute-start(bf16[8,1,128]{2,1,0:T(2,128)(2,1)S(1)} %get-tuple-element.19), channel_id=1, source_target_pairs={{1,0},{2,1},{3,2},{4,3},{5,4},{6,5},{7,6},{8,7},{9,8},{10,9},{11,1... | collective-permute-start | bytes 6152 | tf_op jit(solution)/shard_map/ppermute | solution.py:21
  330.6 6.0 %collective-permute-start.22 = (bf16[1,34,128]{2,1,0:T(8,128)(2,1)S(1)}, bf16[1,34,128]{2,1,0:T(8,128)(2,1)S(1)}, u32[]{:S(2)}, u32[]{:S(2)}) collective-permute-start(bf16[1,34,128]{2,1,0:T(8,128)(2,1)S(1)} %get-tuple-element.4), channel_id=1, source_target_pairs={{16,0},{32,16},{48,32},{64,48},{80,64},{96,80},{112,96},{17,1},{33... | collective-permute-start | bytes 26120 | tf_op jit(solution)/shard_map/ppermute | solution.py:21
  332.5 9.2 %collective-permute-start.23 = (bf16[1,34,128]{2,1,0:T(8,128)(2,1)S(1)}, bf16[1,34,128]{2,1,0:T(8,128)(2,1)S(1)}, u32[]{:S(2)}, u32[]{:S(2)}) collective-permute-start(bf16[1,34,128]{2,1,0:T(8,128)(2,1)S(1)} %get-tuple-element.5), channel_id=1, source_target_pairs={{0,16},{16,32},{32,48},{48,64},{64,80},{80,96},{96,112},{1,17},{17... | collective-permute-start | bytes 26120 | tf_op jit(solution)/shard_map/ppermute | solution.py:18
where the time goes:
time: 344 us
  local copies, waits for them, and re-layouts  117 us (34%)
  other arithmetic  89.9 us (26%)
  starting transfers between devices  85.9 us (25%)
  waiting for transfers between devices  35.9 us (10%)
  matrix products  13.1 us (4%)
    gather x3, local copies, waits for them, and re-layouts, shards(): jnp.take(flat_out, lax.all_to_all(position, 'lon', split_axis=1, concat_a...  104 us
    scatter-add x1, other arithmetic, shards(): grad_out = jnp.zeros((rows * cols * feats,), jnp.float32).at[where_got.as...  85.9 us
    ppermute x12, starting transfers between devices, with_halo(): lax.ppermute(lax.slice_in_dim(block, 0, width, axis=dim), axis, backward)  55.8 us
    ppermute x12, waiting for transfers between devices, with_halo(): lax.ppermute(lax.slice_in_dim(block, block.shape[dim] - width, None, axis...  22.7 us
    ppermute x12, starting transfers between devices, with_halo(): lax.ppermute(lax.slice_in_dim(block, block.shape[dim] - width, None, axis...  17.9 us
  transfers between devices with their start and end apart: 27, of which 13 were waited for; matrix products, arithmetic and copies ran while one was open for 5% of the time, Pallas kernels for 0%

commit v1 on v0

--- a/solution.py
+++ b/solution.py
@@ -94,6 +94,62 @@
 def block_sum(fine):
     rows, cols, feats = fine.shape
     return fine.reshape(rows // 2, 2, cols // 2, 2, feats).sum(axis=(1, 3))
+
+
+def split_bf16(value):
+    high = value.astype(jnp.bfloat16)
+    low = (value - high.astype(jnp.float32)).astype(jnp.bfloat16)
+    return high, low
+
+
+def observe(output, obs_cells, obs_chan, obs_weights, obs_value, obs_count):
+    rows, cols, feats = output.shape
+    ncell = rows * cols
+    slots = lax.broadcasted_iota(jnp.int32, obs_chan.shape, 2)
+    live = (slots < obs_count[:, :, None]).astype(jnp.float32)
+    weights = obs_weights * live[..., None]
+    values = obs_value * live
+    packed = jnp.concatenate(
+        [
+            obs_cells.astype(jnp.float32),
+            obs_chan[..., None].astype(jnp.float32),
+            weights,
+            values[..., None],
+        ],
+        axis=-1,
+    )
+    got = lax.all_to_all(packed, "lon", split_axis=1, concat_axis=1, tiled=True)
+    got = got.reshape(-1, packed.shape[-1])
+    cells = got[:, 0:4].astype(jnp.int32)
+    chan = got[:, 4:5].astype(jnp.int32)
+    wts = got[:, 5:9]
+    vals = got[:, 9]
+    count = got.shape[0]
+    cell_ids = lax.broadcasted_iota(jnp.int32, (count, ncell), 1)
+    table = jnp.zeros((count, ncell), jnp.float32)
+    for j in range(4):
+        table = table + jnp.where(cell_ids == cells[:, j : j + 1], wts[:, j : j + 1], 0.0)
+    t_hi, t_lo = split_bf16(table)
+    o_hi, o_lo = split_bf16(output.reshape(ncell, feats))
+    both = jnp.dot(t_hi, jnp.concatenate([o_hi, o_lo], axis=1), preferred_element_type=jnp.float32)
+    picked = both[:, :feats] + both[:, feats:] + jnp.dot(
+        t_lo, o_hi, preferred_element_type=jnp.float32
+    )
+    pick = lax.broadcasted_iota(jnp.int32, (count, feats), 1) == chan
+    innov = jnp.sum(jnp.where(pick, picked, 0.0), axis=1) - vals
+    spread = jnp.where(pick, innov[:, None], 0.0)
+    s_hi, s_lo = split_bf16(spread)
+    dims = (((0,), (0,)), ((), ()))
+    back = lax.dot_general(
+        t_hi, jnp.concatenate([s_hi, s_lo], axis=1), dims, preferred_element_type=jnp.float32
+    )
+    grad = back[:, :feats] + back[:, feats:] + lax.dot_general(
+        t_lo, s_hi, dims, preferred_element_type=jnp.float32
+    )
+    innovation = lax.all_to_all(
+        innov.reshape(obs_value.shape), "lon", split_axis=1, concat_axis=1, tiled=True
+    )
+    return grad.reshape(rows, cols, feats), innovation
 
 
 def shards(
@@ -129,31 +185,8 @@
     slope_first = gelu_slope(pre_first)
     slope_mid = gelu_slope(pre_mid)
     output = state.astype(jnp.float32) + jax.nn.gelu(pre_last, approximate=True)
-    flat_out = output.reshape(-1)
-    slots = lax.broadcasted_iota(jnp.int32, obs_chan.shape, 2)
-    live = (slots < obs_count[:, :, None]).astype(jnp.float32)
-    weights = obs_weights * live[..., None]
-    values = obs_value * live
-    position = (obs_cells * feats + obs_chan[..., None]).astype(jnp.float32)
-    found = jnp.take(
-        flat_out,
-        lax.all_to_all(position, "lon", split_axis=1, concat_axis=1, tiled=True).astype(jnp.int32),
-    )
-    samples = lax.all_to_all(
-        found.astype(jnp.bfloat16), "lon", split_axis=1, concat_axis=1, tiled=True
-    ).astype(found.dtype)
-    innovation = jnp.sum(weights * samples, axis=-1) - values
-    where_got, terms = (
-        lax.all_to_all(position, "lon", split_axis=1, concat_axis=1, tiled=True),
-        lax.all_to_all(
-            weights * innovation[..., None], "lon", split_axis=1, concat_axis=1, tiled=True
-        ),
-    )
-    grad_out = (
-        jnp.zeros((rows * cols * feats,), jnp.float32)
-        .at[where_got.astype(jnp.int32).reshape(-1)]
-        .add(terms.reshape(-1))
-        .reshape(rows, cols, feats)
+    grad_out, innovation = observe(
+        output, obs_cells, obs_chan, obs_weights, obs_value, obs_count
     )
     grad_pre_last = (grad_out * gelu_slope(pre_last)).astype(jnp.bfloat16)
     grad_merged = convolve_adjoint(grad_pre_last, mat_out)

time: 344 us -> 166 us (0.48)
  local copies, waits for them, and re-layouts: 117 us -> 11.6 us
  other arithmetic: 89.9 us -> 7.58 us
  matrix products: 13.1 us -> 37.2 us
  waiting for transfers between devices: 35.9 us -> 24.5 us
  starting transfers between devices: 85.9 us -> 82.3 us
    gather x3 -> x0, local copies, waits for them, and re-layouts: 104 us -> none  [shards(): jnp.take(flat_out, lax.all_to_all(position, 'lon', split_axis=1, concat_a...]
    scatter-add x1 -> x0, other arithmetic: 85.9 us -> none  [shards(): grad_out = jnp.zeros((rows * cols * feats,), jnp.float32).at[where_got.as...]
    dot_general x0 -> x4, matrix products: none -> 24.5 us  [the longest x1 8.81 us: observe(): jnp.dot(t_lo, o_hi, preferred_element_type=jnp.float32)]
    all_to_all x3 -> x2, waiting for transfers between devices: 9.64 us -> 0.01 us  [the longest x1 0.01 us: observe(): got = lax.all_to_all(packed, 'lon', split_axis=1, concat_axis=1, tiled=True)]
    convert_element_type x6, local copies, waits for them, and re-layouts: 3.62 us -> 8.64 us  [banded(): return full.reshape(9, levels * cin, levels * cout).astype(jnp.bfloat16)]
    all_to_all x3 -> x2, starting transfers between devices: 12.2 us -> 7.69 us  [the longest x1 4.2 us: observe(): got = lax.all_to_all(packed, 'lon', split_axis=1, concat_axis=1, tiled=True)]
  transfers between devices with their start and end apart: 27 -> 26, of which waited for: 13 -> 10; matrix products, arithmetic and copies ran while one was open for 5% -> 16% of each run, Pallas kernels for 0% -> 0%
where the time goes in v1:
time: 166 us; the launch traced here: 165 us
  starting transfers between devices  82.3 us (50%)
  matrix products  37.2 us (22%)
  waiting for transfers between devices  24.5 us (15%)
  local copies, waits for them, and re-layouts  11.6 us (7%)
  other arithmetic  7.58 us (5%)
    ppermute x12, starting transfers between devices, with_halo(): lax.ppermute(lax.slice_in_dim(block, 0, width, axis=dim), axis, backward)  57 us
    ppermute x12, waiting for transfers between devices, with_halo(): lax.ppermute(lax.slice_in_dim(block, block.shape[dim] - width, None, axis...  21 us
    ppermute x12, starting transfers between devices, with_halo(): lax.ppermute(lax.slice_in_dim(block, block.shape[dim] - width, None, axis...  17.7 us
    dot_general x1, matrix products, observe(): jnp.dot(t_lo, o_hi, preferred_element_type=jnp.float32)  8.81 us
    convert_element_type x6, local copies, waits for them, and re-layouts, banded(): return full.reshape(9, levels * cin, levels * cout).astype(jnp.bfloat16)  8.64 us
    dot_general x1, matrix products, observe(): lax.dot_general(t_hi, jnp.concatenate([s_hi, s_lo], axis=1), dims, prefer...  5.5 us
    dot_general x1, matrix products, observe(): lax.dot_general(t_lo, s_hi, dims, preferred_element_type=jnp.float32)  5.49 us
    dot_general x27, matrix products, adjoint_valid(): jnp.einsum('ijg,fg->ijf', piece, matrices[row_off * 3 + col_off], preferr...  4.92 us
  transfers between devices with their start and end apart: 26, of which 10 were waited for; matrix products, arithmetic and copies ran while one was open for 16% of the time, Pallas kernels for 0%

profile of v1, /device:TPU:16, one launch (start us, length us, event | category | flops | bytes accessed | tf_op | source)
XLA Modules:
  0.0 164.7 jit_solution(6744589853599436764)
XLA Ops:
  0.6 0.8 fusion.220
  1.5 4.3 %collective-permute-start.1 = (bf16[8,1,128]{2,1,0:T(2,128)(2,1)S(1)}, bf16[8,1,128]{2,1,0:T(2,128)(2,1)S(1)}, u32[]{:S(2)}, u32[]{:S(2)}) collective-permute-start(bf16[8,1,128]{2,1,0:T(2,128)(2,1)S(1)} %get-tuple-element.40), channel_id=1, source_target_pairs={{1,0},{2,1},{3,2},{4,3},{5,4},{6,5},{7,6},{8,7},{9,8},{10,9},{11,1... | collective-permute-start | bytes 6152 | tf_op jit(solution)/shard_map/ppermute | solution.py:21
  5.8 0.7 convert_element_type.171
  6.5 0.7 fusion.188
  7.2 0.9 bitcast_convert_fusion.1
  8.1 0.8 fusion.178
  8.9 0.9 bitcast_multiply_fusion
  9.8 0.8 pad_maximum_fusion
  10.5 4.2 %all-to-all-start = ((f32[1,16,256,10]{2,3,0,1:T(8,128)}), f32[1,16,256,10]{2,3,0,1:T(8,128)}, u32[]{:S(2)}, u32[]{:S(2)}) async-start(f32[1,16,256,10]{2,3,0,1:T(8,128)} %pad_maximum_fusion), calls=%async_computation | async-start | bytes 524288 | tf_op jit(solution)/shard_map/all_to_all | solution.py:121
  14.8 0.7 convert.7
  15.5 1.5 fusion.8
  17.0 1.5 fusion.9
  18.5 0.6 fusion.7
  19.1 1.5 copy.35
  20.6 2.0 %convert_element_type.144 = bf16[9,128,128]{2,1,0:T(8,128)(2,1)S(1)} reshape(bf16[3,3,4,32,4,32]{5,4,3,2,1,0:T(4,128)(2,1)} %copy.35) | data formatting | bytes 589824 | tf_op jit(solution)/shard_map/convert_element_type | solution.py:35
  23.1 1.5 copy.37
  24.6 2.2 %convert_element_type.150 = bf16[9,128,256]{2,1,0:T(8,128)(2,1)S(1)} reshape(bf16[3,3,4,32,4,64]{5,4,3,2,1,0:T(4,128)(2,1)} %copy.37) | data formatting | bytes 1179648 | tf_op jit(solution)/shard_map/convert_element_type | solution.py:35
  26.8 0.7 copy.40
  27.6 0.6 convert_element_type.158
  28.2 3.4 %collective-permute-start.2 = (bf16[1,34,128]{2,1,0:T(8,128)(2,1)S(1)}, bf16[1,34,128]{2,1,0:T(8,128)(2,1)S(1)}, u32[]{:S(2)}, u32[]{:S(2)}) collective-permute-start(bf16[1,34,128]{2,1,0:T(8,128)(2,1)S(1)} %get-tuple-element.27), channel_id=1, source_target_pairs={{0,16},{16,32},{32,48},{48,64},{64,80},{80,96},{96,112},{1,17},{17... | collective-permute-start | bytes 26120 | tf_op jit(solution)/shard_map/ppermute | solution.py:18
  31.6 6.1 %collective-permute-start.3 = (bf16[1,34,128]{2,1,0:T(8,128)(2,1)S(1)}, bf16[1,34,128]{2,1,0:T(8,128)(2,1)S(1)}, u32[]{:S(2)}, u32[]{:S(2)}) collective-permute-start(bf16[1,34,128]{2,1,0:T(8,128)(2,1)S(1)} %get-tuple-element.28), channel_id=1, source_target_pairs={{16,0},{32,16},{48,32},{64,48},{80,64},{96,80},{112,96},{17,1},{33... | collective-permute-start | bytes 26120 | tf_op jit(solution)/shard_map/ppermute | solution.py:21
  38.0 1.1 collective-permute-done.3
  39.9 0.2 fusion.88
  40.3 3.8 %collective-permute-start.5 = (bf16[4,1,128]{2,1,0:T(2,128)(2,1)S(1)}, bf16[4,1,128]{2,1,0:T(2,128)(2,1)S(1)}, u32[]{:S(2)}, u32[]{:S(2)}) collective-permute-start(bf16[4,1,128]{2,1,0:T(2,128)(2,1)S(1)} %get-tuple-element.52), channel_id=1, source_target_pairs={{1,0},{2,1},{3,2},{4,3},{5,4},{6,5},{7,6},{8,7},{9,8},{10,9},{11,1... | collective-permute-start | bytes 3080 | tf_op jit(solution)/shard_map/ppermute | solution.py:21
  44.3 1.1 collective-permute-done.4
  45.5 1.9 %collective-permute-start.6 = (bf16[1,18,128]{2,1,0:T(8,128)(2,1)S(1)}, bf16[1,18,128]{2,1,0:T(8,128)(2,1)S(1)}, u32[]{:S(2)}, u32[]{:S(2)}) collective-permute-start(bf16[1,18,128]{2,1,0:T(8,128)(2,1)S(1)} %get-tuple-element.49), channel_id=1, source_target_pairs={{0,16},{16,32},{32,48},{48,64},{64,80},{80,96},{96,112},{1,17},{17... | collective-permute-start | bytes 13832 | tf_op jit(solution)/shard_map/ppermute | solution.py:18
  47.4 7.8 %collective-permute-start.7 = (bf16[1,18,128]{2,1,0:T(8,128)(2,1)S(1)}, bf16[1,18,128]{2,1,0:T(8,128)(2,1)S(1)}, u32[]{:S(2)}, u32[]{:S(2)}) collective-permute-start(bf16[1,18,128]{2,1,0:T(8,128)(2,1)S(1)} %get-tuple-element.50), channel_id=1, source_target_pairs={{16,0},{32,16},{48,32},{64,48},{80,64},{96,80},{112,96},{17,1},{33... | collective-permute-start | bytes 13832 | tf_op jit(solution)/shard_map/ppermute | solution.py:21
  55.3 1.2 collective-permute-done.7
  57.9 3.8 %collective-permute-start.9 = (bf16[8,1,128]{2,1,0:T(2,128)(2,1)S(1)}, bf16[8,1,128]{2,1,0:T(2,128)(2,1)S(1)}, u32[]{:S(2)}, u32[]{:S(2)}) collective-permute-start(bf16[8,1,128]{2,1,0:T(2,128)(2,1)S(1)} %get-tuple-element.38), channel_id=1, source_target_pairs={{1,0},{2,1},{3,2},{4,3},{5,4},{6,5},{7,6},{8,7},{9,8},{10,9},{11,1... | collective-permute-start | bytes 6152 | tf_op jit(solution)/shard_map/ppermute | solution.py:21
  61.9 1.1 collective-permute-done.8
  63.1 1.9 %collective-permute-start.10 = (bf16[1,34,128]{2,1,0:T(8,128)(2,1)S(1)}, bf16[1,34,128]{2,1,0:T(8,128)(2,1)S(1)}, u32[]{:S(2)}, u32[]{:S(2)}) collective-permute-start(bf16[1,34,128]{2,1,0:T(8,128)(2,1)S(1)} %get-tuple-element.23), channel_id=1, source_target_pairs={{0,16},{16,32},{32,48},{48,64},{64,80},{80,96},{96,112},{1,17},{17... | collective-permute-start | bytes 26120 | tf_op jit(solution)/shard_map/ppermute | solution.py:18
  65.0 8.0 %collective-permute-start.11 = (bf16[1,34,128]{2,1,0:T(8,128)(2,1)S(1)}, bf16[1,34,128]{2,1,0:T(8,128)(2,1)S(1)}, u32[]{:S(2)}, u32[]{:S(2)}) collective-permute-start(bf16[1,34,128]{2,1,0:T(8,128)(2,1)S(1)} %get-tuple-element.24), channel_id=1, source_target_pairs={{16,0},{32,16},{48,32},{64,48},{80,64},{96,80},{112,96},{17,1},{33... | collective-permute-start | bytes 26120 | tf_op jit(solution)/shard_map/ppermute | solution.py:21
  73.2 1.0 collective-permute-done.11
  75.2 0.2 multiply_add_fusion
  75.4 1.1 copy.66
  76.8 4.7 %fusion.76 = f32[4096,256]{0,1:T(8,128)S(1)} fusion(bf16[256,128]{1,0:T(8,128)(2,1)S(1)} %get-tuple-element.4, bf16[256,128]{1,0:T(8,128)(2,1)S(1)} %get-tuple-element.5, f32[4096]{0:T(1024)S(1)} %bitcast.243, s32[4096]{0:T(1024)S(1)} %bitcast.263, f32[4096]{0:T(1024)S(1)} %bitcast.247, s32[4096]{0:T(1024)S(1)} %bitcast.267, f32[4096]{0:T(1024)S(1)} %bitcast.251, ...), kind=kOutput, calls=%fused_computation.112 | convolution fusion | flops 549715968 | bytes 4456448 | tf_op jit(solution)/shard_map/dot_general | solution.py:134
  81.5 8.8 %fusion.10 = f32[4096]{0:T(1024)S(1)} fusion(bf16[256,128]{1,0:T(8,128)(2,1)S(1)} %get-tuple-element.5, f32[4096,256]{0,1:T(8,128)S(1)} %fusion.76, s32[4096]{0:T(1024)S(1)} %bitcast.233, f32[4096]{0:T(1024)S(1)} %bitcast.244, s32[4096]{0:T(1024)S(1)} %bitcast.264, f32[4096]{0:T(1024)S(1)} %bitcast.248, s32[4096]{0:T(1024)S(1)} %bitcast.268, ...), kind=kOutput, calls=%fused_computation.24 | convolution fusion | flops 286781440 | bytes 4423680 | tf_op jit(solution)/shard_map/dot_general | solution.py:135
  90.3 0.3 fusion.2
  90.6 0.2 select_convert_fusion
  90.8 5.5 %fusion.3 = f32[256,256]{1,0:T(8,128)S(1)} fusion(bf16[4096,128]{0,1:T(8,128)(2,1)S(1)} %fusion.2, bf16[4096,128]{0,1:T(8,128)(2,1)S(1)} %select_convert_fusion, f32[4096]{0:T(1024)S(1)} %bitcast.245, s32[4096]{0:T(1024)S(1)} %bitcast.265, f32[4096]{0:T(1024)S(1)} %bitcast.249, s32[4096]{0:T(1024)S(1)} %bitcast.269, f32[4096]{0:T(1024)S(1)} %bitcast.253, ...), kind=kOutput, calls=%fused_computation.13 | convolution fusion | flops 553648128 | bytes 2490368 | tf_op jit(solution)/shard_map/dot_general | solution.py:143
  96.3 5.5 %convolution_add_fusion.1 = f32[256,128]{1,0:T(8,128)S(1)} fusion(f32[4096]{0:T(1024)S(1)} %bitcast.239, s32[4096]{0:T(1024)S(1)} %bitcast.236, f32[256,256]{1,0:T(8,128)S(1)} %fusion.3, f32[4096]{0:T(1024)S(1)} %bitcast.246, s32[4096]{0:T(1024)S(1)} %bitcast.266, f32[4096]{0:T(1024)S(1)} %bitcast.250, s32[4096]{0:T(1024)S(1)} %bitcast.270, ...), kind=kOutput, calls=%fused_computation.25 | convolution fusion | flops 285278208 | bytes 557056 | tf_op jit(solution)/shard_map/dot_general | solution.py:146
  102.0 3.8 %collective-permute-start.13 = (bf16[8,1,128]{2,1,0:T(2,128)(2,1)S(1)}, bf16[8,1,128]{2,1,0:T(2,128)(2,1)S(1)}, u32[]{:S(2)}, u32[]{:S(2)}) collective-permute-start(bf16[8,1,128]{2,1,0:T(2,128)(2,1)S(1)} %get-tuple-element.32), channel_id=1, source_target_pairs={{1,0},{2,1},{3,2},{4,3},{5,4},{6,5},{7,6},{8,7},{9,8},{10,9},{11,1... | collective-permute-start | bytes 6152 | tf_op jit(solution)/shard_map/ppermute | solution.py:21
  106.0 0.6 sub.85
  106.7 3.5 %all-to-all-start.1 = ((f32[1,16,256]{2,0,1:T(1,128)}), f32[1,16,256]{2,0,1:T(1,128)S(1)}, u32[]{:S(2)}, u32[]{:S(2)}) async-start(f32[1,16,256]{2,0,1:T(1,128)} %sub.85), calls=%async_computation.1 | async-start | bytes 32768 | tf_op jit(solution)/shard_map/all_to_all | solution.py:149
  110.2 7.8 %collective-permute-start.14 = (bf16[1,34,128]{2,1,0:T(8,128)(2,1)S(1)}, bf16[1,34,128]{2,1,0:T(8,128)(2,1)S(1)}, u32[]{:S(2)}, u32[]{:S(2)}) collective-permute-start(bf16[1,34,128]{2,1,0:T(8,128)(2,1)S(1)} %get-tuple-element.19), channel_id=1, source_target_pairs={{16,0},{32,16},{48,32},{64,48},{80,64},{96,80},{112,96},{17,1},{33... | collective-permute-start | bytes 26120 | tf_op jit(solution)/shard_map/ppermute | solution.py:21
  118.0 2.1 %collective-permute-start.15 = (bf16[1,34,128]{2,1,0:T(8,128)(2,1)S(1)}, bf16[1,34,128]{2,1,0:T(8,128)(2,1)S(1)}, u32[]{:S(2)}, u32[]{:S(2)}) collective-permute-start(bf16[1,34,128]{2,1,0:T(8,128)(2,1)S(1)} %get-tuple-element.20), channel_id=1, source_target_pairs={{0,16},{16,32},{32,48},{48,64},{64,80},{80,96},{96,112},{1,17},{17... | collective-permute-start | bytes 26120 | tf_op jit(solution)/shard_map/ppermute | solution.py:18
  120.3 6.9 %collective-permute-done.15 = bf16[1,34,128]{2,1,0:T(8,128)(2,1)S(1)} collective-permute-done((bf16[1,34,128]{2,1,0:T(8,128)(2,1)S(1)}, bf16[1,34,128]{2,1,0:T(8,128)(2,1)S(1)}, u32[]{:S(2)}, u32[]{:S(2)}) %collective-permute-start.15) | collective-permute-done | bytes 8736 | tf_op jit(solution)/shard_map/ppermute | solution.py:18
  127.8 0.2 fusion.105
  128.1 0.2 fusion.23
  128.3 0.2 fusion.20
  128.8 3.8 %collective-permute-start.17 = (bf16[4,1,256]{2,1,0:T(2,128)(2,1)S(1)}, bf16[4,1,256]{2,1,0:T(2,128)(2,1)S(1)}, u32[]{:S(2)}, u32[]{:S(2)}) collective-permute-start(bf16[4,1,256]{2,1,0:T(2,128)(2,1)S(1)} %get-tuple-element.46), channel_id=1, source_target_pairs={{1,0},{2,1},{3,2},{4,3},{5,4},{6,5},{7,6},{8,7},{9,8},{10,9},{11,1... | collective-permute-start | bytes 6152 | tf_op jit(solution)/shard_map/ppermute | solution.py:21
  132.8 1.2 collective-permute-done.16
  134.0 1.9 %collective-permute-start.18 = (bf16[1,18,256]{2,1,0:T(8,128)(2,1)S(1)}, bf16[1,18,256]{2,1,0:T(8,128)(2,1)S(1)}, u32[]{:S(2)}, u32[]{:S(2)}) collective-permute-start(bf16[1,18,256]{2,1,0:T(8,128)(2,1)S(1)} %get-tuple-element.43), channel_id=1, source_target_pairs={{16,0},{32,16},{48,32},{64,48},{80,64},{96,80},{112,96},{17,1},{33... | collective-permute-start | bytes 27656 | tf_op jit(solution)/shard_map/ppermute | solution.py:21
  135.9 3.9 %collective-permute-start.19 = (bf16[1,18,256]{2,1,0:T(8,128)(2,1)S(1)}, bf16[1,18,256]{2,1,0:T(8,128)(2,1)S(1)}, u32[]{:S(2)}, u32[]{:S(2)}) collective-permute-start(bf16[1,18,256]{2,1,0:T(8,128)(2,1)S(1)} %get-tuple-element.44), channel_id=1, source_target_pairs={{0,16},{16,32},{32,48},{48,64},{64,80},{80,96},{96,112},{1,17},{17... | collective-permute-start | bytes 27656 | tf_op jit(solution)/shard_map/ppermute | solution.py:18
  140.0 0.6 copy.43
  140.6 4.5 %collective-permute-done.19 = bf16[1,18,256]{2,1,0:T(8,128)(2,1)S(1)} collective-permute-done((bf16[1,18,256]{2,1,0:T(8,128)(2,1)S(1)}, bf16[1,18,256]{2,1,0:T(8,128)(2,1)S(1)}, u32[]{:S(2)}, u32[]{:S(2)}) %collective-permute-start.19) | collective-permute-done | bytes 9248 | tf_op jit(solution)/shard_map/ppermute | solution.py:18
  145.9 0.2 fusion.50
  146.5 3.8 %collective-permute-start.21 = (bf16[8,1,128]{2,1,0:T(2,128)(2,1)S(1)}, bf16[8,1,128]{2,1,0:T(2,128)(2,1)S(1)}, u32[]{:S(2)}, u32[]{:S(2)}) collective-permute-start(bf16[8,1,128]{2,1,0:T(2,128)(2,1)S(1)} %get-tuple-element.30), channel_id=1, source_target_pairs={{1,0},{2,1},{3,2},{4,3},{5,4},{6,5},{7,6},{8,7},{9,8},{10,9},{11,1... | collective-permute-start | bytes 6152 | tf_op jit(solution)/shard_map/ppermute | solution.py:21
  150.5 1.1 collective-permute-done.20
  151.7 1.9 %collective-permute-start.22 = (bf16[1,34,128]{2,1,0:T(8,128)(2,1)S(1)}, bf16[1,34,128]{2,1,0:T(8,128)(2,1)S(1)}, u32[]{:S(2)}, u32[]{:S(2)}) collective-permute-start(bf16[1,34,128]{2,1,0:T(8,128)(2,1)S(1)} %get-tuple-element.15), channel_id=1, source_target_pairs={{16,0},{32,16},{48,32},{64,48},{80,64},{96,80},{112,96},{17,1},{33... | collective-permute-start | bytes 26120 | tf_op jit(solution)/shard_map/ppermute | solution.py:21
  153.6 3.9 %collective-permute-start.23 = (bf16[1,34,128]{2,1,0:T(8,128)(2,1)S(1)}, bf16[1,34,128]{2,1,0:T(8,128)(2,1)S(1)}, u32[]{:S(2)}, u32[]{:S(2)}) collective-permute-start(bf16[1,34,128]{2,1,0:T(8,128)(2,1)S(1)} %get-tuple-element.16), channel_id=1, source_target_pairs={{0,16},{16,32},{32,48},{48,64},{64,80},{80,96},{96,112},{1,17},{17... | collective-permute-start | bytes 26120 | tf_op jit(solution)/shard_map/ppermute | solution.py:18
  157.7 5.1 %collective-permute-done.23 = bf16[1,34,128]{2,1,0:T(8,128)(2,1)S(1)} collective-permute-done((bf16[1,34,128]{2,1,0:T(8,128)(2,1)S(1)}, bf16[1,34,128]{2,1,0:T(8,128)(2,1)S(1)}, u32[]{:S(2)}, u32[]{:S(2)}) %collective-permute-start.23) | collective-permute-done | bytes 8736 | tf_op jit(solution)/shard_map/ppermute | solution.py:18
  163.7 0.2 fusion.17
  163.9 0.9 fusion.14
  (110 shorter events, 9.2 us)
Async XLA Ops:
  0.6 17.9 %copy-start.1 = (bf16[3,3,3,32,32]{4,3,2,1,0:T(8,128)(2,1)S(1)}, bf16[3,3,3,32,32]{4,3,2,1,0:T(8,128)(2,1)}, u32[]{:S(2)}) copy-start(bf16[3,3,3,32,32]{4,3,2,1,0:T(8,128)(2,1)} %param.11) | copy-start | bytes 165892
  1.4 26.8 %collective-permute-start = (bf16[8,1,128]{2,1,0:T(2,128)(2,1)S(1)}, bf16[8,1,128]{2,1,0:T(2,128)(2,1)S(1)}, u32[]{:S(2)}, u32[]{:S(2)}) collective-permute-start(bf16[8,1,128]{2,1,0:T(2,128)(2,1)S(1)} %get-tuple-element.39), channel_id=1, source_target_pairs={{0,1},{1,2},{2,3},{3,4},{4,5},{5,6},{6,7},{7,8},{8,9},{9,10},{10,1... | collective-permute-start | bytes 6152 | tf_op jit(solution)/shard_map/ppermute | solution.py:18
  1.5 26.7 %collective-permute-start.1 = (bf16[8,1,128]{2,1,0:T(2,128)(2,1)S(1)}, bf16[8,1,128]{2,1,0:T(2,128)(2,1)S(1)}, u32[]{:S(2)}, u32[]{:S(2)}) collective-permute-start(bf16[8,1,128]{2,1,0:T(2,128)(2,1)S(1)} %get-tuple-element.40), channel_id=1, source_target_pairs={{1,0},{2,1},{3,2},{4,3},{5,4},{6,5},{7,6},{8,7},{9,8},{10,9},{11,1... | collective-permute-start | bytes 6152 | tf_op jit(solution)/shard_map/ppermute | solution.py:21
  10.5 64.9 %all-to-all-start = ((f32[1,16,256,10]{2,3,0,1:T(8,128)}), f32[1,16,256,10]{2,3,0,1:T(8,128)}, u32[]{:S(2)}, u32[]{:S(2)}) async-start(f32[1,16,256,10]{2,3,0,1:T(8,128)} %pad_maximum_fusion), calls=%async_computation | async-start | bytes 524288 | tf_op jit(solution)/shard_map/all_to_all | solution.py:121
  14.7 7.9 %copy-start = (bf16[8,32,128]{2,1,0:T(8,128)(2,1)S(1)}, bf16[8,32,128]{2,1,0:T(8,128)(2,1)}, u32[]{:S(2)}) copy-start(bf16[8,32,128]{2,1,0:T(8,128)(2,1)} %param.10) | copy-start | bytes 196612
  28.2 9.8 %collective-permute-start.2 = (bf16[1,34,128]{2,1,0:T(8,128)(2,1)S(1)}, bf16[1,34,128]{2,1,0:T(8,128)(2,1)S(1)}, u32[]{:S(2)}, u32[]{:S(2)}) collective-permute-start(bf16[1,34,128]{2,1,0:T(8,128)(2,1)S(1)} %get-tuple-element.27), channel_id=1, source_target_pairs={{0,16},{16,32},{32,48},{48,64},{64,80},{80,96},{96,112},{1,17},{17... | collective-permute-start | bytes 26120 | tf_op jit(solution)/shard_map/ppermute | solution.py:18
  31.6 7.4 %collective-permute-start.3 = (bf16[1,34,128]{2,1,0:T(8,128)(2,1)S(1)}, bf16[1,34,128]{2,1,0:T(8,128)(2,1)S(1)}, u32[]{:S(2)}, u32[]{:S(2)}) collective-permute-start(bf16[1,34,128]{2,1,0:T(8,128)(2,1)S(1)} %get-tuple-element.28), channel_id=1, source_target_pairs={{16,0},{32,16},{48,32},{64,48},{80,64},{96,80},{112,96},{17,1},{33... | collective-permute-start | bytes 26120 | tf_op jit(solution)/shard_map/ppermute | solution.py:21
  40.2 5.2 %collective-permute-start.4 = (bf16[4,1,128]{2,1,0:T(2,128)(2,1)S(1)}, bf16[4,1,128]{2,1,0:T(2,128)(2,1)S(1)}, u32[]{:S(2)}, u32[]{:S(2)}) collective-permute-start(bf16[4,1,128]{2,1,0:T(2,128)(2,1)S(1)} %get-tuple-element.51), channel_id=1, source_target_pairs={{0,1},{1,2},{2,3},{3,4},{4,5},{5,6},{6,7},{7,8},{8,9},{9,10},{10,1... | collective-permute-start | bytes 3080 | tf_op jit(solution)/shard_map/ppermute | solution.py:18
  40.3 5.2 %collective-permute-start.5 = (bf16[4,1,128]{2,1,0:T(2,128)(2,1)S(1)}, bf16[4,1,128]{2,1,0:T(2,128)(2,1)S(1)}, u32[]{:S(2)}, u32[]{:S(2)}) collective-permute-start(bf16[4,1,128]{2,1,0:T(2,128)(2,1)S(1)} %get-tuple-element.52), channel_id=1, source_target_pairs={{1,0},{2,1},{3,2},{4,3},{5,4},{6,5},{7,6},{8,7},{9,8},{10,9},{11,1... | collective-permute-start | bytes 3080 | tf_op jit(solution)/shard_map/ppermute | solution.py:21
  45.5 9.9 %collective-permute-start.6 = (bf16[1,18,128]{2,1,0:T(8,128)(2,1)S(1)}, bf16[1,18,128]{2,1,0:T(8,128)(2,1)S(1)}, u32[]{:S(2)}, u32[]{:S(2)}) collective-permute-start(bf16[1,18,128]{2,1,0:T(8,128)(2,1)S(1)} %get-tuple-element.49), channel_id=1, source_target_pairs={{0,16},{16,32},{32,48},{48,64},{64,80},{80,96},{96,112},{1,17},{17... | collective-permute-start | bytes 13832 | tf_op jit(solution)/shard_map/ppermute | solution.py:18
  47.4 9.1 %collective-permute-start.7 = (bf16[1,18,128]{2,1,0:T(8,128)(2,1)S(1)}, bf16[1,18,128]{2,1,0:T(8,128)(2,1)S(1)}, u32[]{:S(2)}, u32[]{:S(2)}) collective-permute-start(bf16[1,18,128]{2,1,0:T(8,128)(2,1)S(1)} %get-tuple-element.50), channel_id=1, source_target_pairs={{16,0},{32,16},{48,32},{64,48},{80,64},{96,80},{112,96},{17,1},{33... | collective-permute-start | bytes 13832 | tf_op jit(solution)/shard_map/ppermute | solution.py:21
  57.8 5.2 %collective-permute-start.8 = (bf16[8,1,128]{2,1,0:T(2,128)(2,1)S(1)}, bf16[8,1,128]{2,1,0:T(2,128)(2,1)S(1)}, u32[]{:S(2)}, u32[]{:S(2)}) collective-permute-start(bf16[8,1,128]{2,1,0:T(2,128)(2,1)S(1)} %get-tuple-element.37), channel_id=1, source_target_pairs={{0,1},{1,2},{2,3},{3,4},{4,5},{5,6},{6,7},{7,8},{8,9},{9,10},{10,1... | collective-permute-start | bytes 6152 | tf_op jit(solution)/shard_map/ppermute | solution.py:18
  57.9 5.2 %collective-permute-start.9 = (bf16[8,1,128]{2,1,0:T(2,128)(2,1)S(1)}, bf16[8,1,128]{2,1,0:T(2,128)(2,1)S(1)}, u32[]{:S(2)}, u32[]{:S(2)}) collective-permute-start(bf16[8,1,128]{2,1,0:T(2,128)(2,1)S(1)} %get-tuple-element.38), channel_id=1, source_target_pairs={{1,0},{2,1},{3,2},{4,3},{5,4},{6,5},{7,6},{8,7},{9,8},{10,9},{11,1... | collective-permute-start | bytes 6152 | tf_op jit(solution)/shard_map/ppermute | solution.py:21
  63.1 10.1 %collective-permute-start.10 = (bf16[1,34,128]{2,1,0:T(8,128)(2,1)S(1)}, bf16[1,34,128]{2,1,0:T(8,128)(2,1)S(1)}, u32[]{:S(2)}, u32[]{:S(2)}) collective-permute-start(bf16[1,34,128]{2,1,0:T(8,128)(2,1)S(1)} %get-tuple-element.23), channel_id=1, source_target_pairs={{0,16},{16,32},{32,48},{48,64},{64,80},{80,96},{96,112},{1,17},{17... | collective-permute-start | bytes 26120 | tf_op jit(solution)/shard_map/ppermute | solution.py:18
  65.0 9.2 %collective-permute-start.11 = (bf16[1,34,128]{2,1,0:T(8,128)(2,1)S(1)}, bf16[1,34,128]{2,1,0:T(8,128)(2,1)S(1)}, u32[]{:S(2)}, u32[]{:S(2)}) collective-permute-start(bf16[1,34,128]{2,1,0:T(8,128)(2,1)S(1)} %get-tuple-element.24), channel_id=1, source_target_pairs={{16,0},{32,16},{48,32},{64,48},{80,64},{96,80},{112,96},{17,1},{33... | collective-permute-start | bytes 26120 | tf_op jit(solution)/shard_map/ppermute | solution.py:21
  102.0 8.2 %collective-permute-start.12 = (bf16[8,1,128]{2,1,0:T(2,128)(2,1)S(1)}, bf16[8,1,128]{2,1,0:T(2,128)(2,1)S(1)}, u32[]{:S(2)}, u32[]{:S(2)}) collective-permute-start(bf16[8,1,128]{2,1,0:T(2,128)(2,1)S(1)} %get-tuple-element.31), channel_id=1, source_target_pairs={{0,1},{1,2},{2,3},{3,4},{4,5},{5,6},{6,7},{7,8},{8,9},{9,10},{10,1... | collective-permute-start | bytes 6152 | tf_op jit(solution)/shard_map/ppermute | solution.py:18
  102.0 8.1 %collective-permute-start.13 = (bf16[8,1,128]{2,1,0:T(2,128)(2,1)S(1)}, bf16[8,1,128]{2,1,0:T(2,128)(2,1)S(1)}, u32[]{:S(2)}, u32[]{:S(2)}) collective-permute-start(bf16[8,1,128]{2,1,0:T(2,128)(2,1)S(1)} %get-tuple-element.32), channel_id=1, source_target_pairs={{1,0},{2,1},{3,2},{4,3},{5,4},{6,5},{7,6},{8,7},{9,8},{10,9},{11,1... | collective-permute-start | bytes 6152 | tf_op jit(solution)/shard_map/ppermute | solution.py:21
  106.7 33.3 %all-to-all-start.1 = ((f32[1,16,256]{2,0,1:T(1,128)}), f32[1,16,256]{2,0,1:T(1,128)S(1)}, u32[]{:S(2)}, u32[]{:S(2)}) async-start(f32[1,16,256]{2,0,1:T(1,128)} %sub.85), calls=%async_computation.1 | async-start | bytes 32768 | tf_op jit(solution)/shard_map/all_to_all | solution.py:149
  110.2 10.1 %collective-permute-start.14 = (bf16[1,34,128]{2,1,0:T(8,128)(2,1)S(1)}, bf16[1,34,128]{2,1,0:T(8,128)(2,1)S(1)}, u32[]{:S(2)}, u32[]{:S(2)}) collective-permute-start(bf16[1,34,128]{2,1,0:T(8,128)(2,1)S(1)} %get-tuple-element.19), channel_id=1, source_target_pairs={{16,0},{32,16},{48,32},{64,48},{80,64},{96,80},{112,96},{17,1},{33... | collective-permute-start | bytes 26120 | tf_op jit(solution)/shard_map/ppermute | solution.py:21
  118.0 9.2 %collective-permute-start.15 = (bf16[1,34,128]{2,1,0:T(8,128)(2,1)S(1)}, bf16[1,34,128]{2,1,0:T(8,128)(2,1)S(1)}, u32[]{:S(2)}, u32[]{:S(2)}) collective-permute-start(bf16[1,34,128]{2,1,0:T(8,128)(2,1)S(1)} %get-tuple-element.20), channel_id=1, source_target_pairs={{0,16},{16,32},{32,48},{48,64},{64,80},{80,96},{96,112},{1,17},{17... | collective-permute-start | bytes 26120 | tf_op jit(solution)/shard_map/ppermute | solution.py:18
  128.7 5.2 %collective-permute-start.16 = (bf16[4,1,256]{2,1,0:T(2,128)(2,1)S(1)}, bf16[4,1,256]{2,1,0:T(2,128)(2,1)S(1)}, u32[]{:S(2)}, u32[]{:S(2)}) collective-permute-start(bf16[4,1,256]{2,1,0:T(2,128)(2,1)S(1)} %get-tuple-element.45), channel_id=1, source_target_pairs={{0,1},{1,2},{2,3},{3,4},{4,5},{5,6},{6,7},{7,8},{8,9},{9,10},{10,1... | collective-permute-start | bytes 6152 | tf_op jit(solution)/shard_map/ppermute | solution.py:18
  128.8 5.2 %collective-permute-start.17 = (bf16[4,1,256]{2,1,0:T(2,128)(2,1)S(1)}, bf16[4,1,256]{2,1,0:T(2,128)(2,1)S(1)}, u32[]{:S(2)}, u32[]{:S(2)}) collective-permute-start(bf16[4,1,256]{2,1,0:T(2,128)(2,1)S(1)} %get-tuple-element.46), channel_id=1, source_target_pairs={{1,0},{2,1},{3,2},{4,3},{5,4},{6,5},{7,6},{8,7},{9,8},{10,9},{11,1... | collective-permute-start | bytes 6152 | tf_op jit(solution)/shard_map/ppermute | solution.py:21
  134.0 6.6 %collective-permute-start.18 = (bf16[1,18,256]{2,1,0:T(8,128)(2,1)S(1)}, bf16[1,18,256]{2,1,0:T(8,128)(2,1)S(1)}, u32[]{:S(2)}, u32[]{:S(2)}) collective-permute-start(bf16[1,18,256]{2,1,0:T(8,128)(2,1)S(1)} %get-tuple-element.43), channel_id=1, source_target_pairs={{16,0},{32,16},{48,32},{64,48},{80,64},{96,80},{112,96},{17,1},{33... | collective-permute-start | bytes 27656 | tf_op jit(solution)/shard_map/ppermute | solution.py:21
  135.9 9.2 %collective-permute-start.19 = (bf16[1,18,256]{2,1,0:T(8,128)(2,1)S(1)}, bf16[1,18,256]{2,1,0:T(8,128)(2,1)S(1)}, u32[]{:S(2)}, u32[]{:S(2)}) collective-permute-start(bf16[1,18,256]{2,1,0:T(8,128)(2,1)S(1)} %get-tuple-element.44), channel_id=1, source_target_pairs={{0,16},{16,32},{32,48},{48,64},{64,80},{80,96},{96,112},{1,17},{17... | collective-permute-start | bytes 27656 | tf_op jit(solution)/shard_map/ppermute | solution.py:18
  146.4 5.2 %collective-permute-start.20 = (bf16[8,1,128]{2,1,0:T(2,128)(2,1)S(1)}, bf16[8,1,128]{2,1,0:T(2,128)(2,1)S(1)}, u32[]{:S(2)}, u32[]{:S(2)}) collective-permute-start(bf16[8,1,128]{2,1,0:T(2,128)(2,1)S(1)} %get-tuple-element.29), channel_id=1, source_target_pairs={{0,1},{1,2},{2,3},{3,4},{4,5},{5,6},{6,7},{7,8},{8,9},{9,10},{10,1... | collective-permute-start | bytes 6152 | tf_op jit(solution)/shard_map/ppermute | solution.py:18
  146.5 5.2 %collective-permute-start.21 = (bf16[8,1,128]{2,1,0:T(2,128)(2,1)S(1)}, bf16[8,1,128]{2,1,0:T(2,128)(2,1)S(1)}, u32[]{:S(2)}, u32[]{:S(2)}) collective-permute-start(bf16[8,1,128]{2,1,0:T(2,128)(2,1)S(1)} %get-tuple-element.30), channel_id=1, source_target_pairs={{1,0},{2,1},{3,2},{4,3},{5,4},{6,5},{7,6},{8,7},{9,8},{10,9},{11,1... | collective-permute-start | bytes 6152 | tf_op jit(solution)/shard_map/ppermute | solution.py:21
  151.7 6.0 %collective-permute-start.22 = (bf16[1,34,128]{2,1,0:T(8,128)(2,1)S(1)}, bf16[1,34,128]{2,1,0:T(8,128)(2,1)S(1)}, u32[]{:S(2)}, u32[]{:S(2)}) collective-permute-start(bf16[1,34,128]{2,1,0:T(8,128)(2,1)S(1)} %get-tuple-element.15), channel_id=1, source_target_pairs={{16,0},{32,16},{48,32},{64,48},{80,64},{96,80},{112,96},{17,1},{33... | collective-permute-start | bytes 26120 | tf_op jit(solution)/shard_map/ppermute | solution.py:21
  153.6 9.2 %collective-permute-start.23 = (bf16[1,34,128]{2,1,0:T(8,128)(2,1)S(1)}, bf16[1,34,128]{2,1,0:T(8,128)(2,1)S(1)}, u32[]{:S(2)}, u32[]{:S(2)}) collective-permute-start(bf16[1,34,128]{2,1,0:T(8,128)(2,1)S(1)} %get-tuple-element.16), channel_id=1, source_target_pairs={{0,16},{16,32},{32,48},{48,64},{64,80},{80,96},{96,112},{1,17},{17... | collective-permute-start | bytes 26120 | tf_op jit(solution)/shard_map/ppermute | solution.py:18

commit v2 on v1

--- a/solution.py
+++ b/solution.py
@@ -24,15 +24,22 @@
 
 
 def banded(kernel, levels):
-    lin = jnp.arange(levels, dtype=jnp.int32)
-    taps = jnp.arange(3, dtype=jnp.int32)
-    select = (lin[:, None, None] - lin[None, :, None] + 1 == taps[None, None, :]).astype(
-        jnp.float32
-    )
-    full = jnp.einsum("pqt,abtcg->abpcqg", select, kernel.astype(jnp.float32))
-    cin = kernel.shape[3]
-    cout = kernel.shape[4]
-    return full.reshape(9, levels * cin, levels * cout).astype(jnp.bfloat16)
+    zero = jnp.zeros(kernel.shape[:2] + kernel.shape[3:], kernel.dtype)
+    rows = []
+    for p in range(levels):
+        blocks = [kernel[:, :, p - q + 1] if 0 <= p - q + 1 < 3 else zero for q in range(levels)]
+        rows.append(jnp.concatenate(blocks, axis=-1))
+    full = jnp.concatenate(rows, axis=-2)
+    return full.reshape(9, full.shape[2], full.shape[3])
+
+
+def block_diagonal(matrix, levels):
+    zero = jnp.zeros_like(matrix)
+    rows = [
+        jnp.concatenate([matrix if p == q else zero for q in range(levels)], axis=1)
+        for p in range(levels)
+    ]
+    return jnp.concatenate(rows, axis=0)
 
 
 def gelu_slope(value):
@@ -97,9 +104,8 @@
 
 
 def split_bf16(value):
-    high = value.astype(jnp.bfloat16)
-    low = (value - high.astype(jnp.float32)).astype(jnp.bfloat16)
-    return high, low
+    high = lax.reduce_precision(value, exponent_bits=8, mantissa_bits=7)
+    return high.astype(jnp.bfloat16), (value - high).astype(jnp.bfloat16)
 
 
 def observe(output, obs_cells, obs_chan, obs_weights, obs_value, obs_count):
@@ -152,6 +158,23 @@
     return grad.reshape(rows, cols, feats), innovation
 
 
+def exchange(block, width):
+    wide = with_halo(block, (("lon", 1),), width, True)
+    return with_halo(wide, (("lat", 0),), width, False)
+
+
+def inside(field, tile_rows, halo):
+    rows = field.shape[0]
+    first = lax.axis_index("lat") * tile_rows - halo
+    where = first + lax.broadcasted_iota(jnp.int32, (rows, 1, 1), 0)
+    keep = (where >= 0) & (where < lax.axis_size("lat") * tile_rows)
+    return jnp.where(keep, field, jnp.zeros_like(field))
+
+
+def trim(field, width):
+    return field[width : field.shape[0] - width, width : field.shape[1] - width]
+
+
 def shards(
     state,
     kernel_in,
@@ -164,38 +187,41 @@
     obs_value,
     obs_count,
 ):
-    feats = LEV * C
     rows, cols = (state.shape[0], state.shape[1])
+    crows = rows // 2
     mat_in = banded(kernel_in, LEV)
     mat_mid = banded(kernel_mid, LEV)
     mat_out = banded(kernel_out, LEV)
-    lift_full = (
-        jnp.einsum("pq,cg->pcqg", jnp.eye(LEV, dtype=jnp.float32), lift.astype(jnp.float32))
-        .reshape(LEV * C2, feats)
-        .astype(jnp.bfloat16)
-    )
-    pre_first = convolve(state, mat_in)
+    lift_full = block_diagonal(lift, LEV)
+    padded = exchange(state, 7)
+    pre_first = conv_valid(padded, mat_in, rows + 12, cols + 12)
     act_first = jax.nn.gelu(pre_first, approximate=True).astype(jnp.bfloat16)
     pooled = (block_sum(act_first.astype(jnp.float32)) * 0.25).astype(jnp.bfloat16)
-    pre_mid = convolve(pooled, mat_mid)
-    act_mid = jax.nn.gelu(pre_mid, approximate=True).astype(jnp.bfloat16)
+    pooled = inside(pooled, crows, 3)
+    pre_mid = conv_valid(pooled, mat_mid, crows + 4, cols // 2 + 4)
+    act_mid = jax.nn.gelu(trim(pre_mid, 1), approximate=True).astype(jnp.bfloat16)
     lifted = jnp.einsum("ijg,gf->ijf", act_mid, lift_full, preferred_element_type=jnp.float32)
-    merged = (act_first.astype(jnp.float32) + widen(lifted)).astype(jnp.bfloat16)
-    pre_last = convolve(merged, mat_out)
-    slope_first = gelu_slope(pre_first)
+    merged = (trim(act_first, 5).astype(jnp.float32) + trim(widen(lifted), 1)).astype(jnp.bfloat16)
+    merged = inside(merged, rows, 1)
+    pre_last = conv_valid(merged, mat_out, rows, cols)
+    slope_first = gelu_slope(trim(pre_first, 5))
     slope_mid = gelu_slope(pre_mid)
     output = state.astype(jnp.float32) + jax.nn.gelu(pre_last, approximate=True)
     grad_out, innovation = observe(
         output, obs_cells, obs_chan, obs_weights, obs_value, obs_count
     )
     grad_pre_last = (grad_out * gelu_slope(pre_last)).astype(jnp.bfloat16)
-    grad_merged = convolve_adjoint(grad_pre_last, mat_out)
+    grads = exchange(grad_pre_last, 5)
+    grad_merged = adjoint_valid(grads, mat_out, rows + 8, cols + 8)
     grad_coarse = block_sum(grad_merged).astype(jnp.bfloat16)
     back_mid = jnp.einsum("ijf,gf->ijg", grad_coarse, lift_full, preferred_element_type=jnp.float32)
-    grad_mid = (back_mid * slope_mid).astype(jnp.bfloat16)
-    grad_pooled = convolve_adjoint(grad_mid, mat_mid)
-    grad_first = ((grad_merged + widen(grad_pooled) * 0.25) * slope_first).astype(jnp.bfloat16)
-    gradient = grad_out + convolve_adjoint(grad_first, mat_in)
+    grad_mid = inside((back_mid * slope_mid).astype(jnp.bfloat16), crows, 2)
+    grad_pooled = adjoint_valid(grad_mid, mat_mid, crows + 2, cols // 2 + 2)
+    grad_first = (
+        (trim(grad_merged, 3) + trim(widen(grad_pooled), 1) * 0.25) * slope_first
+    ).astype(jnp.bfloat16)
+    grad_first = inside(grad_first, rows, 1)
+    gradient = grad_out + adjoint_valid(grad_first, mat_in, rows, cols)
     return (gradient, innovation)
 
 

time: 166 us -> 93.9 us (0.57)
  the two profiles are of different devices: /device:TPU:16 before, /device:TPU:14 now
where the time goes in v2:
time: 93.9 us; the launch traced here: 93.2 us
  matrix products  36.2 us (39%)
  starting transfers between devices  29 us (31%)
  waiting for transfers between devices  13 us (14%)
  other arithmetic  8.14 us (9%)
  local copies, waits for them, and re-layouts  5.54 us (6%)
  between operations  1.3 us (1%)
    ppermute x4, waiting for transfers between devices, with_halo(): lax.ppermute(lax.slice_in_dim(block, 0, width, axis=dim), axis, backward)  12.8 us
    ppermute x4, starting transfers between devices, with_halo(): lax.ppermute(lax.slice_in_dim(block, 0, width, axis=dim), axis, backward)  9.53 us
    dot_general x1, matrix products, observe(): jnp.dot(t_lo, o_hi, preferred_element_type=jnp.float32)  8.99 us
    all_to_all x1, starting transfers between devices, observe(): got = lax.all_to_all(packed, 'lon', split_axis=1, concat_axis=1, tiled=True)  6.79 us
    ppermute x4, starting transfers between devices, with_halo(): lax.ppermute(lax.slice_in_dim(block, block.shape[dim] - width, None, axis...  6.36 us
    all_to_all x1, starting transfers between devices, observe(): lax.all_to_all(innov.reshape(obs_value.shape), 'lon', split_axis=1, conca...  6.31 us
    dot_general x27, matrix products, adjoint_valid(): jnp.einsum('ijg,fg->ijf', piece, matrices[row_off * 3 + col_off], preferr...  5.85 us
    dot_general x1, matrix products, observe(): lax.dot_general(t_hi, jnp.concatenate([s_hi, s_lo], axis=1), dims, prefer...  5.7 us
  transfers between devices with their start and end apart: 10, of which 3 were waited for; matrix products, arithmetic and copies ran while one was open for 18% of the time, Pallas kernels for 0%

profile of v2, /device:TPU:14, one launch (start us, length us, event | category | flops | bytes accessed | tf_op | source)
XLA Modules:
  0.0 93.2 jit_solution(16357354385362695461)
XLA Ops:
  0.6 0.8 fusion.200
  1.5 1.7 %collective-permute-start.1 = (bf16[8,7,128]{2,1,0:T(8,128)(2,1)S(1)}, bf16[8,7,128]{2,1,0:T(8,128)(2,1)S(1)}, u32[]{:S(2)}, u32[]{:S(2)}) collective-permute-start(bf16[8,7,128]{2,1,0:T(8,128)(2,1)S(1)} %get-tuple-element.29), channel_id=1, source_target_pairs={{1,0},{2,1},{3,2},{4,3},{5,4},{6,5},{7,6},{8,7},{9,8},{10,9},{11,1... | collective-permute-start | bytes 43016 | tf_op jit(solution)/shard_map/ppermute | solution.py:21
  3.2 0.7 convert_element_type.103
  4.0 0.7 fusion.177
  4.7 0.9 bitcast_convert_fusion
  5.5 0.8 fusion.176
  6.4 0.9 bitcast_multiply_fusion
  7.2 0.8 pad_maximum_fusion.9
  8.0 6.8 %all-to-all-start = ((f32[1,16,256,10]{2,3,0,1:T(8,128)}), f32[1,16,256,10]{2,3,0,1:T(8,128)S(1)}, u32[]{:S(2)}, u32[]{:S(2)}) async-start(f32[1,16,256,10]{2,3,0,1:T(8,128)} %pad_maximum_fusion.9), calls=%async_computation | async-start | bytes 524288 | tf_op jit(solution)/shard_map/all_to_all | solution.py:127
  14.8 1.0 %slice_bitcast_fusion.7 = (bf16[3,3,32,32]{3,2,1,0:T(8,128)(2,1)S(1)}, bf16[3,3,32,32]{3,2,1,0:T(8,128)(2,1)S(1)}, bf16[3,3,32,32]{3,2,1,0:T(8,128)(2,1)S(1)}) fusion(bf16[3,3,3,32,32]{4,3,2,1,0:T(8,128)(2,1)} %param.11), kind=kLoop, calls=%fused_computation.221 | loop fusion | bytes 110592 | tf_op jit(solution)/shard_map/squeeze | solution.py:30
  15.8 1.0 %slice_bitcast_fusion.4 = (bf16[3,3,32,64]{3,2,1,0:T(8,128)(2,1)S(1)}, bf16[3,3,32,64]{3,2,1,0:T(8,128)(2,1)S(1)}, bf16[3,3,32,64]{3,2,1,0:T(8,128)(2,1)S(1)}) fusion(bf16[3,3,3,32,64]{4,3,2,1,0:T(8,128)(2,1)} %param.12), kind=kLoop, calls=%fused_computation.218 | loop fusion | bytes 221184 | tf_op jit(solution)/shard_map/squeeze | solution.py:30
  16.8 1.0 %slice_bitcast_fusion.1 = (bf16[3,3,32,32]{3,2,1,0:T(8,128)(2,1)S(1)}, bf16[3,3,32,32]{3,2,1,0:T(8,128)(2,1)S(1)}, bf16[3,3,32,32]{3,2,1,0:T(8,128)(2,1)S(1)}) fusion(bf16[3,3,3,32,32]{4,3,2,1,0:T(8,128)(2,1)} %param.13), kind=kLoop, calls=%fused_computation.215 | loop fusion | bytes 110592 | tf_op jit(solution)/shard_map/squeeze | solution.py:30
  17.8 0.3 fusion.38
  18.1 0.3 fusion.41
  18.5 0.3 maximum_maximum_fusion
  19.0 4.3 %collective-permute-start.2 = (bf16[7,46,128]{2,1,0:T(8,128)(2,1)S(1)}, bf16[7,46,128]{2,1,0:T(8,128)(2,1)S(1)}, u32[]{:S(2)}, u32[]{:S(2)}) collective-permute-start(bf16[7,46,128]{2,1,0:T(8,128)(2,1)S(1)} %get-tuple-element.24), channel_id=1, source_target_pairs={{0,16},{16,32},{32,48},{48,64},{64,80},{80,96},{96,112},{1,17},{17... | collective-permute-start | bytes 247304 | tf_op jit(solution)/shard_map/ppermute | solution.py:18
  23.3 1.9 %collective-permute-start.3 = (bf16[7,46,128]{2,1,0:T(8,128)(2,1)S(1)}, bf16[7,46,128]{2,1,0:T(8,128)(2,1)S(1)}, u32[]{:S(2)}, u32[]{:S(2)}) collective-permute-start(bf16[7,46,128]{2,1,0:T(8,128)(2,1)S(1)} %get-tuple-element.25), channel_id=1, source_target_pairs={{16,0},{32,16},{48,32},{64,48},{80,64},{96,80},{112,96},{17,1},{33... | collective-permute-start | bytes 247304 | tf_op jit(solution)/shard_map/ppermute | solution.py:21
  25.3 0.2 collective-permute-done.2
  25.5 7.9 %collective-permute-done.3 = bf16[7,46,128]{2,1,0:T(8,128)(2,1)S(1)} collective-permute-done((bf16[7,46,128]{2,1,0:T(8,128)(2,1)S(1)}, bf16[7,46,128]{2,1,0:T(8,128)(2,1)S(1)}, u32[]{:S(2)}, u32[]{:S(2)}) %collective-permute-start.3) | collective-permute-done | bytes 82464 | tf_op jit(solution)/shard_map/ppermute | solution.py:21
  33.4 0.2 fusion.48
  33.6 0.2 fusion.50
  33.8 0.2 fusion.52
  34.0 0.2 fusion.54
  34.2 0.2 fusion.56
  34.4 0.2 fusion.58
  34.6 0.2 fusion.60
  34.9 0.2 fusion.62
  35.1 0.4 fusion.35
  35.5 0.3 reshape.174
  35.8 0.3 reduce_sum.31
  37.8 0.2 fusion.134
  39.5 0.2 multiply_add_fusion
  40.2 4.7 %fusion.25 = f32[4096,256]{0,1:T(8,128)S(1)} fusion(f32[4096]{0:T(1024)S(1)} %bitcast.287, s32[4096]{0:T(1024)S(1)} %bitcast.307, f32[4096]{0:T(1024)S(1)} %bitcast.291, s32[4096]{0:T(1024)S(1)} %bitcast.311, f32[4096]{0:T(1024)S(1)} %bitcast.295, s32[4096]{0:T(1024)S(1)} %bitcast.315, f32[4096]{0:T(1024)S(1)} %bitcast.299, s32[4096]{0:T(1024)S(1)} %bitcast.303, ...), kind=kOutput, calls=%fused_computation.73 | convolution fusion | flops 550764544 | bytes 4456448 | tf_op jit(solution)/shard_map/dot_general | solution.py:140
  44.9 9.0 %fusion.7 = f32[4096]{0:T(1024)S(1)} fusion(bf16[256,128]{1,0:T(8,128)(2,1)S(1)} %get-tuple-element.21, f32[4096,256]{0,1:T(8,128)S(1)} %fusion.25, s32[4096]{0:T(1024)S(1)} %bitcast.279, f32[4096]{0:T(1024)S(1)} %bitcast.288, s32[4096]{0:T(1024)S(1)} %bitcast.308, f32[4096]{0:T(1024)S(1)} %bitcast.292, s32[4096]{0:T(1024)S(1)} %bitcast.312, ...), kind=kOutput, calls=%fused_computation.19 | convolution fusion | flops 285732864 | bytes 4423680 | tf_op jit(solution)/shard_map/dot_general | solution.py:141
  53.9 0.4 reduce-precision_convert_fusion.1
  54.4 5.7 %fusion.3 = f32[256,256]{1,0:T(8,128)S(1)} fusion(bf16[4096,128]{0,1:T(8,128)(2,1)S(1)} %get-tuple-element.35, bf16[4096,128]{0,1:T(8,128)(2,1)S(1)} %get-tuple-element.34, f32[4096]{0:T(1024)S(1)} %bitcast.289, s32[4096]{0:T(1024)S(1)} %bitcast.309, f32[4096]{0:T(1024)S(1)} %bitcast.293, s32[4096]{0:T(1024)S(1)} %bitcast.313, f32[4096]{0:T(1024)S(1)} %bitcast.297, ...), kind=kOutput, calls=%fused_computation.14 | convolution fusion | flops 554696704 | bytes 2490368 | tf_op jit(solution)/shard_map/dot_general | solution.py:149
  60.1 5.5 %convolution_add_fusion.11 = f32[256,128]{1,0:T(8,128)S(1)} fusion(f32[4096]{0:T(1024)S(1)} %bitcast.290, s32[4096]{0:T(1024)S(1)} %bitcast.310, f32[4096]{0:T(1024)S(1)} %bitcast.294, s32[4096]{0:T(1024)S(1)} %bitcast.314, f32[4096]{0:T(1024)S(1)} %bitcast.298, s32[4096]{0:T(1024)S(1)} %bitcast.318, f32[4096]{0:T(1024)S(1)} %bitcast.302, ...), kind=kOutput, calls=%fused_computation.46 | convolution fusion | flops 285278208 | bytes 557056 | tf_op jit(solution)/shard_map/dot_general | solution.py:152
  65.8 1.7 %collective-permute-start.5 = (bf16[8,5,128]{2,1,0:T(8,128)(2,1)S(1)}, bf16[8,5,128]{2,1,0:T(8,128)(2,1)S(1)}, u32[]{:S(2)}, u32[]{:S(2)}) collective-permute-start(bf16[8,5,128]{2,1,0:T(8,128)(2,1)S(1)} %get-tuple-element.27), channel_id=1, source_target_pairs={{1,0},{2,1},{3,2},{4,3},{5,4},{6,5},{7,6},{8,7},{9,8},{10,9},{11,1... | collective-permute-start | bytes 30728 | tf_op jit(solution)/shard_map/ppermute | solution.py:21
  67.5 0.6 sub.51
  68.1 6.3 %all-to-all-start.1 = ((f32[1,16,256]{2,0,1:T(1,128)}), f32[1,16,256]{2,0,1:T(1,128)S(1)}, u32[]{:S(2)}, u32[]{:S(2)}) async-start(f32[1,16,256]{2,0,1:T(1,128)} %sub.51), calls=%async_computation.1 | async-start | bytes 32768 | tf_op jit(solution)/shard_map/all_to_all | solution.py:155
  74.5 1.9 %collective-permute-start.6 = (bf16[5,42,128]{2,1,0:T(8,128)(2,1)S(1)}, bf16[5,42,128]{2,1,0:T(8,128)(2,1)S(1)}, u32[]{:S(2)}, u32[]{:S(2)}) collective-permute-start(bf16[5,42,128]{2,1,0:T(8,128)(2,1)S(1)} %get-tuple-element.22), channel_id=1, source_target_pairs={{0,16},{16,32},{32,48},{48,64},{64,80},{80,96},{96,112},{1,17},{17... | collective-permute-start | bytes 161288 | tf_op jit(solution)/shard_map/ppermute | solution.py:18
  76.4 4.1 %collective-permute-start.7 = (bf16[5,42,128]{2,1,0:T(8,128)(2,1)S(1)}, bf16[5,42,128]{2,1,0:T(8,128)(2,1)S(1)}, u32[]{:S(2)}, u32[]{:S(2)}) collective-permute-start(bf16[5,42,128]{2,1,0:T(8,128)(2,1)S(1)} %get-tuple-element.23), channel_id=1, source_target_pairs={{16,0},{32,16},{48,32},{64,48},{80,64},{96,80},{112,96},{17,1},{33... | collective-permute-start | bytes 161288 | tf_op jit(solution)/shard_map/ppermute | solution.py:21
  80.6 0.6 copy.59
  81.2 4.9 %collective-permute-done.7 = bf16[5,42,128]{2,1,0:T(8,128)(2,1)S(1)} collective-permute-done((bf16[5,42,128]{2,1,0:T(8,128)(2,1)S(1)}, bf16[5,42,128]{2,1,0:T(8,128)(2,1)S(1)}, u32[]{:S(2)}, u32[]{:S(2)}) %collective-permute-start.7) | collective-permute-done | bytes 53792 | tf_op jit(solution)/shard_map/ppermute | solution.py:21
  86.2 0.2 fusion.83
  86.4 0.2 fusion.85
  86.7 0.2 fusion.87
  86.9 0.2 fusion.89
  87.2 0.2 fusion.91
  87.4 0.2 fusion.93
  87.7 0.2 fusion.95
  87.9 0.2 fusion.97
  88.2 0.3 fusion.21
  88.4 0.2 reduce_sum.34
  88.7 0.3 fusion.24
  89.2 0.2 convolution_add_fusion.35
  89.3 0.2 convolution_add_fusion.34
  89.5 0.2 convolution_add_fusion.33
  89.9 0.2 convolution_add_fusion.31
  90.1 0.2 convolution_add_fusion.30
  90.2 0.2 convolution_add_fusion.29
  90.4 0.2 convolution_add_fusion.28
  90.8 0.2 broadcast_select_fusion
  92.4 0.8 fusion.23
  (71 shorter events, 6.0 us)
Async XLA Ops:
  0.6 18.3 %copy-start = (bf16[8,32,128]{2,1,0:T(8,128)(2,1)S(1)}, bf16[8,32,128]{2,1,0:T(8,128)(2,1)}, u32[]{:S(2)}) copy-start(bf16[8,32,128]{2,1,0:T(8,128)(2,1)} %param.10) | copy-start | bytes 196612
  0.6 18.2 %copy-start.1 = (bf16[64,32]{0,1:T(8,128)(2,1)S(1)}, bf16[64,32]{0,1:T(8,128)(2,1)}, u32[]{:S(2)}) copy-start(bf16[64,32]{0,1:T(8,128)(2,1)} %param.14) | copy-start | bytes 12292
  1.4 17.5 %collective-permute-start = (bf16[8,7,128]{2,1,0:T(8,128)(2,1)S(1)}, bf16[8,7,128]{2,1,0:T(8,128)(2,1)S(1)}, u32[]{:S(2)}, u32[]{:S(2)}) collective-permute-start(bf16[8,7,128]{2,1,0:T(8,128)(2,1)S(1)} %get-tuple-element.28), channel_id=1, source_target_pairs={{0,1},{1,2},{2,3},{3,4},{4,5},{5,6},{6,7},{7,8},{8,9},{9,10},{10,1... | collective-permute-start | bytes 43016 | tf_op jit(solution)/shard_map/ppermute | solution.py:18
  1.5 17.4 %collective-permute-start.1 = (bf16[8,7,128]{2,1,0:T(8,128)(2,1)S(1)}, bf16[8,7,128]{2,1,0:T(8,128)(2,1)S(1)}, u32[]{:S(2)}, u32[]{:S(2)}) collective-permute-start(bf16[8,7,128]{2,1,0:T(8,128)(2,1)S(1)} %get-tuple-element.29), channel_id=1, source_target_pairs={{1,0},{2,1},{3,2},{4,3},{5,4},{6,5},{7,6},{8,7},{9,8},{10,9},{11,1... | collective-permute-start | bytes 43016 | tf_op jit(solution)/shard_map/ppermute | solution.py:21
  8.0 31.8 %all-to-all-start = ((f32[1,16,256,10]{2,3,0,1:T(8,128)}), f32[1,16,256,10]{2,3,0,1:T(8,128)S(1)}, u32[]{:S(2)}, u32[]{:S(2)}) async-start(f32[1,16,256,10]{2,3,0,1:T(8,128)} %pad_maximum_fusion.9), calls=%async_computation | async-start | bytes 524288 | tf_op jit(solution)/shard_map/all_to_all | solution.py:127
  19.0 6.4 %collective-permute-start.2 = (bf16[7,46,128]{2,1,0:T(8,128)(2,1)S(1)}, bf16[7,46,128]{2,1,0:T(8,128)(2,1)S(1)}, u32[]{:S(2)}, u32[]{:S(2)}) collective-permute-start(bf16[7,46,128]{2,1,0:T(8,128)(2,1)S(1)} %get-tuple-element.24), channel_id=1, source_target_pairs={{0,16},{16,32},{32,48},{48,64},{64,80},{80,96},{96,112},{1,17},{17... | collective-permute-start | bytes 247304 | tf_op jit(solution)/shard_map/ppermute | solution.py:18
  23.3 10.0 %collective-permute-start.3 = (bf16[7,46,128]{2,1,0:T(8,128)(2,1)S(1)}, bf16[7,46,128]{2,1,0:T(8,128)(2,1)S(1)}, u32[]{:S(2)}, u32[]{:S(2)}) collective-permute-start(bf16[7,46,128]{2,1,0:T(8,128)(2,1)S(1)} %get-tuple-element.25), channel_id=1, source_target_pairs={{16,0},{32,16},{48,32},{64,48},{80,64},{96,80},{112,96},{17,1},{33... | collective-permute-start | bytes 247304 | tf_op jit(solution)/shard_map/ppermute | solution.py:21
  65.7 8.8 %collective-permute-start.4 = (bf16[8,5,128]{2,1,0:T(8,128)(2,1)S(1)}, bf16[8,5,128]{2,1,0:T(8,128)(2,1)S(1)}, u32[]{:S(2)}, u32[]{:S(2)}) collective-permute-start(bf16[8,5,128]{2,1,0:T(8,128)(2,1)S(1)} %get-tuple-element.26), channel_id=1, source_target_pairs={{0,1},{1,2},{2,3},{3,4},{4,5},{5,6},{6,7},{7,8},{8,9},{9,10},{10,1... | collective-permute-start | bytes 30728 | tf_op jit(solution)/shard_map/ppermute | solution.py:18
  65.8 8.7 %collective-permute-start.5 = (bf16[8,5,128]{2,1,0:T(8,128)(2,1)S(1)}, bf16[8,5,128]{2,1,0:T(8,128)(2,1)S(1)}, u32[]{:S(2)}, u32[]{:S(2)}) collective-permute-start(bf16[8,5,128]{2,1,0:T(8,128)(2,1)S(1)} %get-tuple-element.27), channel_id=1, source_target_pairs={{1,0},{2,1},{3,2},{4,3},{5,4},{6,5},{7,6},{8,7},{9,8},{10,9},{11,1... | collective-permute-start | bytes 30728 | tf_op jit(solution)/shard_map/ppermute | solution.py:21
  68.1 12.5 %all-to-all-start.1 = ((f32[1,16,256]{2,0,1:T(1,128)}), f32[1,16,256]{2,0,1:T(1,128)S(1)}, u32[]{:S(2)}, u32[]{:S(2)}) async-start(f32[1,16,256]{2,0,1:T(1,128)} %sub.51), calls=%async_computation.1 | async-start | bytes 32768 | tf_op jit(solution)/shard_map/all_to_all | solution.py:155
  74.5 6.7 %collective-permute-start.6 = (bf16[5,42,128]{2,1,0:T(8,128)(2,1)S(1)}, bf16[5,42,128]{2,1,0:T(8,128)(2,1)S(1)}, u32[]{:S(2)}, u32[]{:S(2)}) collective-permute-start(bf16[5,42,128]{2,1,0:T(8,128)(2,1)S(1)} %get-tuple-element.22), channel_id=1, source_target_pairs={{0,16},{16,32},{32,48},{48,64},{64,80},{80,96},{96,112},{1,17},{17... | collective-permute-start | bytes 161288 | tf_op jit(solution)/shard_map/ppermute | solution.py:18
  76.4 9.7 %collective-permute-start.7 = (bf16[5,42,128]{2,1,0:T(8,128)(2,1)S(1)}, bf16[5,42,128]{2,1,0:T(8,128)(2,1)S(1)}, u32[]{:S(2)}, u32[]{:S(2)}) collective-permute-start(bf16[5,42,128]{2,1,0:T(8,128)(2,1)S(1)} %get-tuple-element.23), channel_id=1, source_target_pairs={{16,0},{32,16},{48,32},{64,48},{80,64},{96,80},{112,96},{17,1},{33... | collective-permute-start | bytes 161288 | tf_op jit(solution)/shard_map/ppermute | solution.py:21

commit v3 on v2

--- a/solution.py
+++ b/solution.py
@@ -159,8 +159,26 @@
 
 
 def exchange(block, width):
-    wide = with_halo(block, (("lon", 1),), width, True)
-    return with_halo(wide, (("lat", 0),), width, False)
+    nlat = lax.axis_size("lat")
+    nlon = lax.axis_size("lon")
+    rows, cols = block.shape[0], block.shape[1]
+    row_part = {-1: slice(rows - width, rows), 0: slice(0, rows), 1: slice(0, width)}
+    col_part = {-1: slice(cols - width, cols), 0: slice(0, cols), 1: slice(0, width)}
+    got = {}
+    for a in (-1, 0, 1):
+        for b in (-1, 0, 1):
+            if a == 0 and b == 0:
+                got[a, b] = block
+                continue
+            pairs = [
+                (i * nlon + j, (i - a) * nlon + (j - b) % nlon)
+                for i in range(nlat)
+                for j in range(nlon)
+                if 0 <= i - a < nlat
+            ]
+            got[a, b] = lax.ppermute(block[row_part[a], col_part[b]], ("lat", "lon"), pairs)
+    bands = [jnp.concatenate([got[a, b] for b in (-1, 0, 1)], axis=1) for a in (-1, 0, 1)]
+    return jnp.concatenate(bands, axis=0)
 
 
 def inside(field, tile_rows, halo):

time: 93.9 us -> 135 us (1.44)
  the two profiles are of different devices: /device:TPU:14 before, /device:TPU:6 now
where the time goes in v3:
time: 135 us; the launch traced here: 134 us
  starting transfers between devices  67 us (50%)
  matrix products  36.1 us (27%)
  waiting for transfers between devices  13.7 us (10%)
  other arithmetic  8.15 us (6%)
  local copies, waits for them, and re-layouts  7.24 us (5%)
  between operations  1.39 us (1%)
    ppermute x16, starting transfers between devices, exchange(): lax.ppermute(block[row_part[a], col_part[b]], ('lat', 'lon'), pairs)  58.8 us
    ppermute x16, waiting for transfers between devices, exchange(): lax.ppermute(block[row_part[a], col_part[b]], ('lat', 'lon'), pairs)  13.7 us
    dot_general x1, matrix products, observe(): jnp.dot(t_lo, o_hi, preferred_element_type=jnp.float32)  8.99 us
    dot_general x27, matrix products, adjoint_valid(): jnp.einsum('ijg,fg->ijf', piece, matrices[row_off * 3 + col_off], preferr...  5.87 us
    dot_general x1, matrix products, observe(): lax.dot_general(t_hi, jnp.concatenate([s_hi, s_lo], axis=1), dims, prefer...  5.69 us
    dot_general x1, matrix products, observe(): lax.dot_general(t_lo, s_hi, dims, preferred_element_type=jnp.float32)  5.46 us
    dot_general x27, matrix products, conv_valid(): jnp.einsum('ijf,fg->ijg', piece, matrices[row_off * 3 + col_off], preferr...  4.9 us
    all_to_all x1, starting transfers between devices, observe(): got = lax.all_to_all(packed, 'lon', split_axis=1, concat_axis=1, tiled=True)  4.79 us
  transfers between devices with their start and end apart: 18, of which 2 were waited for; matrix products, arithmetic and copies ran while one was open for 13% of the time, Pallas kernels for 0%

profile of v3, /device:TPU:6, one launch (start us, length us, event | category | flops | bytes accessed | tf_op | source)
XLA Modules:
  0.0 133.6 jit_solution(2993801916912560394)
XLA Ops:
  0.7 0.8 fusion.174
  1.5 4.6 %collective-permute-start.4 = (bf16[8,7,128]{2,1,0:T(8,128)(2,1)S(1)}, bf16[8,7,128]{2,1,0:T(8,128)(2,1)S(1)}, u32[]{:S(2)}, u32[]{:S(2)}) collective-permute-start(bf16[8,7,128]{2,1,0:T(8,128)(2,1)S(1)} %get-tuple-element.37), channel_id=1, source_target_pairs={{0,15},{1,0},{2,1},{3,2},{4,3},{5,4},{6,5},{7,6},{8,7},{9,8},{10,9... | collective-permute-start | bytes 43016 | tf_op jit(solution)/shard_map/ppermute | solution.py:179
  6.1 0.8 fusion.172
  6.9 1.9 %collective-permute-start = (bf16[7,7,128]{2,1,0:T(8,128)(2,1)S(1)}, bf16[7,7,128]{2,1,0:T(8,128)(2,1)S(1)}, u32[]{:S(2)}, u32[]{:S(2)}) collective-permute-start(bf16[7,7,128]{2,1,0:T(8,128)(2,1)S(1)} %get-tuple-element.30), channel_id=1, source_target_pairs={{0,17},{1,18},{2,19},{3,20},{4,21},{5,22},{6,23},{7,24},{8,25},{9,... | collective-permute-start | bytes 37640 | tf_op jit(solution)/shard_map/ppermute | solution.py:179
  8.8 1.9 %collective-permute-start.5 = (bf16[7,7,128]{2,1,0:T(8,128)(2,1)S(1)}, bf16[7,7,128]{2,1,0:T(8,128)(2,1)S(1)}, u32[]{:S(2)}, u32[]{:S(2)}) collective-permute-start(bf16[7,7,128]{2,1,0:T(8,128)(2,1)S(1)} %get-tuple-element.31), channel_id=1, source_target_pairs={{16,1},{17,2},{18,3},{19,4},{20,5},{21,6},{22,7},{23,8},{24,9},{25... | collective-permute-start | bytes 37640 | tf_op jit(solution)/shard_map/ppermute | solution.py:179
  10.7 9.1 %collective-permute-start.2 = (bf16[7,7,128]{2,1,0:T(8,128)(2,1)S(1)}, bf16[7,7,128]{2,1,0:T(8,128)(2,1)S(1)}, u32[]{:S(2)}, u32[]{:S(2)}) collective-permute-start(bf16[7,7,128]{2,1,0:T(8,128)(2,1)S(1)} %get-tuple-element.32), channel_id=1, source_target_pairs={{0,31},{1,16},{2,17},{3,18},{4,19},{5,20},{6,21},{7,22},{8,23},{9,... | collective-permute-start | bytes 37640 | tf_op jit(solution)/shard_map/ppermute | solution.py:179
  19.8 0.7 convert_element_type.103
  20.5 0.7 fusion.149
  21.3 0.9 bitcast_convert_fusion
  22.1 0.8 fusion.148
  22.9 0.9 bitcast_multiply_fusion
  23.8 0.8 pad_maximum_fusion.8
  24.6 4.8 %all-to-all-start = ((f32[1,16,256,10]{2,3,0,1:T(8,128)}), f32[1,16,256,10]{2,3,0,1:T(8,128)S(1)}, u32[]{:S(2)}, u32[]{:S(2)}) async-start(f32[1,16,256,10]{2,3,0,1:T(8,128)} %pad_maximum_fusion.8), calls=%async_computation | async-start | bytes 524288 | tf_op jit(solution)/shard_map/all_to_all | solution.py:127
  29.4 0.9 fusion.173
  30.3 1.0 slice_bitcast_fusion.7
  31.3 1.0 slice_bitcast_fusion.4
  32.2 1.0 slice_bitcast_fusion.1
  33.3 0.3 fusion.24
  33.6 0.3 fusion.27
  34.0 0.3 maximum_maximum_fusion
  34.3 2.7 %collective-permute-start.7 = (bf16[7,7,128]{2,1,0:T(8,128)(2,1)S(1)}, bf16[7,7,128]{2,1,0:T(8,128)(2,1)S(1)}, u32[]{:S(2)}, u32[]{:S(2)}) collective-permute-start(bf16[7,7,128]{2,1,0:T(8,128)(2,1)S(1)} %get-tuple-element.33), channel_id=1, source_target_pairs={{16,15},{17,0},{18,1},{19,2},{20,3},{21,4},{22,5},{23,6},{24,7},{2... | collective-permute-start | bytes 37640 | tf_op jit(solution)/shard_map/ppermute | solution.py:179
  37.0 9.0 %collective-permute-start.1 = (bf16[7,32,128]{2,1,0:T(8,128)(2,1)S(1)}, bf16[7,32,128]{2,1,0:T(8,128)(2,1)S(1)}, u32[]{:S(2)}, u32[]{:S(2)}) collective-permute-start(bf16[7,32,128]{2,1,0:T(8,128)(2,1)S(1)} %get-tuple-element.34), channel_id=1, source_target_pairs={{0,16},{1,17},{2,18},{3,19},{4,20},{5,21},{6,22},{7,23},{8,24},{9,... | collective-permute-start | bytes 172040 | tf_op jit(solution)/shard_map/ppermute | solution.py:179
  46.1 1.9 %collective-permute-start.6 = (bf16[7,32,128]{2,1,0:T(8,128)(2,1)S(1)}, bf16[7,32,128]{2,1,0:T(8,128)(2,1)S(1)}, u32[]{:S(2)}, u32[]{:S(2)}) collective-permute-start(bf16[7,32,128]{2,1,0:T(8,128)(2,1)S(1)} %get-tuple-element.35), channel_id=1, source_target_pairs={{16,0},{17,1},{18,2},{19,3},{20,4},{21,5},{22,6},{23,7},{24,8},{25... | collective-permute-start | bytes 172040 | tf_op jit(solution)/shard_map/ppermute | solution.py:179
  48.2 7.6 %collective-permute-done.6 = bf16[7,32,128]{2,1,0:T(8,128)(2,1)S(1)} collective-permute-done((bf16[7,32,128]{2,1,0:T(8,128)(2,1)S(1)}, bf16[7,32,128]{2,1,0:T(8,128)(2,1)S(1)}, u32[]{:S(2)}, u32[]{:S(2)}) %collective-permute-start.6) | collective-permute-done | bytes 57376 | tf_op jit(solution)/shard_map/ppermute | solution.py:179
  55.9 0.2 fusion.41
  56.1 0.2 convolution_add_fusion.8
  56.3 0.2 convolution_add_fusion.7
  56.7 0.2 convolution_add_fusion.5
  57.0 0.2 convolution_add_fusion.4
  57.4 0.2 convolution_add_fusion.2
  57.6 0.3 fusion.21
  57.9 0.3 reshape.174
  58.2 0.3 reduce_sum.31
  60.2 0.2 fusion.106
  62.6 4.7 %fusion.11 = f32[4096,256]{0,1:T(8,128)S(1)} fusion(f32[4096]{0:T(1024)S(1)} %bitcast.287, s32[4096]{0:T(1024)S(1)} %bitcast.307, f32[4096]{0:T(1024)S(1)} %bitcast.291, s32[4096]{0:T(1024)S(1)} %bitcast.311, f32[4096]{0:T(1024)S(1)} %bitcast.295, s32[4096]{0:T(1024)S(1)} %bitcast.315, f32[4096]{0:T(1024)S(1)} %bitcast.299, s32[4096]{0:T(1024)S(1)} %bitcast.303, ...), kind=kOutput, calls=%fused_computation.73 | convolution fusion | flops 550764544 | bytes 4456448 | tf_op jit(solution)/shard_map/dot_general | solution.py:140
  67.3 9.0 %fusion.7 = f32[4096]{0:T(1024)S(1)} fusion(bf16[256,128]{1,0:T(8,128)(2,1)S(1)} %get-tuple-element.21, f32[4096,256]{0,1:T(8,128)S(1)} %fusion.11, s32[4096]{0:T(1024)S(1)} %bitcast.279, f32[4096]{0:T(1024)S(1)} %bitcast.288, s32[4096]{0:T(1024)S(1)} %bitcast.308, f32[4096]{0:T(1024)S(1)} %bitcast.292, s32[4096]{0:T(1024)S(1)} %bitcast.312, ...), kind=kOutput, calls=%fused_computation.19 | convolution fusion | flops 285732864 | bytes 4423680 | tf_op jit(solution)/shard_map/dot_general | solution.py:141
  76.4 0.4 reduce-precision_convert_fusion.1
  76.8 5.7 %fusion.3 = f32[256,256]{1,0:T(8,128)S(1)} fusion(bf16[4096,128]{0,1:T(8,128)(2,1)S(1)} %get-tuple-element.43, bf16[4096,128]{0,1:T(8,128)(2,1)S(1)} %get-tuple-element.42, f32[4096]{0:T(1024)S(1)} %bitcast.289, s32[4096]{0:T(1024)S(1)} %bitcast.309, f32[4096]{0:T(1024)S(1)} %bitcast.293, s32[4096]{0:T(1024)S(1)} %bitcast.313, f32[4096]{0:T(1024)S(1)} %bitcast.297, ...), kind=kOutput, calls=%fused_computation.14 | convolution fusion | flops 554696704 | bytes 2490368 | tf_op jit(solution)/shard_map/dot_general | solution.py:149
  82.5 5.5 %convolution_add_fusion.25 = f32[256,128]{1,0:T(8,128)S(1)} fusion(f32[4096]{0:T(1024)S(1)} %bitcast.290, s32[4096]{0:T(1024)S(1)} %bitcast.310, f32[4096]{0:T(1024)S(1)} %bitcast.294, s32[4096]{0:T(1024)S(1)} %bitcast.314, f32[4096]{0:T(1024)S(1)} %bitcast.298, s32[4096]{0:T(1024)S(1)} %bitcast.318, f32[4096]{0:T(1024)S(1)} %bitcast.302, ...), kind=kOutput, calls=%fused_computation.46 | convolution fusion | flops 285278208 | bytes 557056 | tf_op jit(solution)/shard_map/dot_general | solution.py:152
  88.1 1.9 %collective-permute-start.8 = (bf16[5,5,128]{2,1,0:T(8,128)(2,1)S(1)}, bf16[5,5,128]{2,1,0:T(8,128)(2,1)S(1)}, u32[]{:S(2)}, u32[]{:S(2)}) collective-permute-start(bf16[5,5,128]{2,1,0:T(8,128)(2,1)S(1)} %get-tuple-element.22), channel_id=1, source_target_pairs={{0,17},{1,18},{2,19},{3,20},{4,21},{5,22},{6,23},{7,24},{8,25},{9,... | collective-permute-start | bytes 19208 | tf_op jit(solution)/shard_map/ppermute | solution.py:179
  90.0 6.7 %collective-permute-start.15 = (bf16[5,5,128]{2,1,0:T(8,128)(2,1)S(1)}, bf16[5,5,128]{2,1,0:T(8,128)(2,1)S(1)}, u32[]{:S(2)}, u32[]{:S(2)}) collective-permute-start(bf16[5,5,128]{2,1,0:T(8,128)(2,1)S(1)} %get-tuple-element.23), channel_id=1, source_target_pairs={{16,15},{17,0},{18,1},{19,2},{20,3},{21,4},{22,5},{23,6},{24,7},{2... | collective-permute-start | bytes 19208 | tf_op jit(solution)/shard_map/ppermute | solution.py:179
  96.7 1.9 %collective-permute-start.13 = (bf16[5,5,128]{2,1,0:T(8,128)(2,1)S(1)}, bf16[5,5,128]{2,1,0:T(8,128)(2,1)S(1)}, u32[]{:S(2)}, u32[]{:S(2)}) collective-permute-start(bf16[5,5,128]{2,1,0:T(8,128)(2,1)S(1)} %get-tuple-element.24), channel_id=1, source_target_pairs={{16,1},{17,2},{18,3},{19,4},{20,5},{21,6},{22,7},{23,8},{24,9},{25... | collective-permute-start | bytes 19208 | tf_op jit(solution)/shard_map/ppermute | solution.py:179
  98.6 0.6 sub.51
  99.2 3.5 %all-to-all-start.1 = ((f32[1,16,256]{2,0,1:T(1,128)}), f32[1,16,256]{2,0,1:T(1,128)S(1)}, u32[]{:S(2)}, u32[]{:S(2)}) async-start(f32[1,16,256]{2,0,1:T(1,128)} %sub.51), calls=%async_computation.1 | async-start | bytes 32768 | tf_op jit(solution)/shard_map/all_to_all | solution.py:155
  102.7 0.3 collective-permute-start.11
  103.0 3.6 %collective-permute-start.12 = (bf16[8,5,128]{2,1,0:T(8,128)(2,1)S(1)}, bf16[8,5,128]{2,1,0:T(8,128)(2,1)S(1)}, u32[]{:S(2)}, u32[]{:S(2)}) collective-permute-start(bf16[8,5,128]{2,1,0:T(8,128)(2,1)S(1)} %get-tuple-element.29), channel_id=1, source_target_pairs={{0,15},{1,0},{2,1},{3,2},{4,3},{5,4},{6,5},{7,6},{8,7},{9,8},{10,9... | collective-permute-start | bytes 30728 | tf_op jit(solution)/shard_map/ppermute | solution.py:179
  106.7 7.3 %collective-permute-start.10 = (bf16[5,5,128]{2,1,0:T(8,128)(2,1)S(1)}, bf16[5,5,128]{2,1,0:T(8,128)(2,1)S(1)}, u32[]{:S(2)}, u32[]{:S(2)}) collective-permute-start(bf16[5,5,128]{2,1,0:T(8,128)(2,1)S(1)} %get-tuple-element.25), channel_id=1, source_target_pairs={{0,31},{1,16},{2,17},{3,18},{4,19},{5,20},{6,21},{7,22},{8,23},{9,... | collective-permute-start | bytes 19208 | tf_op jit(solution)/shard_map/ppermute | solution.py:179
  114.0 3.0 %collective-permute-start.9 = (bf16[5,32,128]{2,1,0:T(8,128)(2,1)S(1)}, bf16[5,32,128]{2,1,0:T(8,128)(2,1)S(1)}, u32[]{:S(2)}, u32[]{:S(2)}) collective-permute-start(bf16[5,32,128]{2,1,0:T(8,128)(2,1)S(1)} %get-tuple-element.26), channel_id=1, source_target_pairs={{0,16},{1,17},{2,18},{3,19},{4,20},{5,21},{6,22},{7,23},{8,24},{9,... | collective-permute-start | bytes 122888 | tf_op jit(solution)/shard_map/ppermute | solution.py:179
  117.0 2.8 %collective-permute-start.14 = (bf16[5,32,128]{2,1,0:T(8,128)(2,1)S(1)}, bf16[5,32,128]{2,1,0:T(8,128)(2,1)S(1)}, u32[]{:S(2)}, u32[]{:S(2)}) collective-permute-start(bf16[5,32,128]{2,1,0:T(8,128)(2,1)S(1)} %get-tuple-element.27), channel_id=1, source_target_pairs={{16,0},{17,1},{18,2},{19,3},{20,4},{21,5},{22,6},{23,7},{24,8},{25... | collective-permute-start | bytes 122888 | tf_op jit(solution)/shard_map/ppermute | solution.py:179
  119.9 0.6 copy.59
  120.5 6.0 %collective-permute-done.14 = bf16[5,32,128]{2,1,0:T(8,128)(2,1)S(1)} collective-permute-done((bf16[5,32,128]{2,1,0:T(8,128)(2,1)S(1)}, bf16[5,32,128]{2,1,0:T(8,128)(2,1)S(1)}, u32[]{:S(2)}, u32[]{:S(2)}) %collective-permute-start.14) | collective-permute-done | bytes 40992 | tf_op jit(solution)/shard_map/ppermute | solution.py:179
  126.6 0.2 fusion.69
  126.9 0.2 convolution_add_fusion.16
  127.1 0.2 convolution_add_fusion.15
  127.4 0.2 convolution_add_fusion.14
  127.6 0.2 convolution_add_fusion.13
  127.9 0.2 convolution_add_fusion.12
  128.1 0.2 convolution_add_fusion.11
  128.4 0.2 convolution_add_fusion.10
  128.6 0.2 convolution_add_fusion.9
  128.9 0.2 reduce_sum.34
  129.1 0.3 fusion.10
  131.2 0.2 broadcast_select_fusion
  132.8 0.8 fusion.9
  (87 shorter events, 7.8 us)
Async XLA Ops:
  0.6 55.1 %copy-start = (bf16[8,32,128]{2,1,0:T(8,128)(2,1)S(1)}, bf16[8,32,128]{2,1,0:T(8,128)(2,1)}, u32[]{:S(2)}) copy-start(bf16[8,32,128]{2,1,0:T(8,128)(2,1)} %param.10) | copy-start | bytes 196612
  0.6 47.4 %copy-start.1 = (bf16[64,32]{0,1:T(8,128)(2,1)S(1)}, bf16[64,32]{0,1:T(8,128)(2,1)}, u32[]{:S(2)}) copy-start(bf16[64,32]{0,1:T(8,128)(2,1)} %param.14) | copy-start | bytes 12292
  1.4 46.7 %collective-permute-start.3 = (bf16[8,7,128]{2,1,0:T(8,128)(2,1)S(1)}, bf16[8,7,128]{2,1,0:T(8,128)(2,1)S(1)}, u32[]{:S(2)}, u32[]{:S(2)}) collective-permute-start(bf16[8,7,128]{2,1,0:T(8,128)(2,1)S(1)} %get-tuple-element.36), channel_id=1, source_target_pairs={{0,1},{1,2},{2,3},{3,4},{4,5},{5,6},{6,7},{7,8},{8,9},{9,10},{10,1... | collective-permute-start | bytes 43016 | tf_op jit(solution)/shard_map/ppermute | solution.py:179
  1.5 46.7 %collective-permute-start.4 = (bf16[8,7,128]{2,1,0:T(8,128)(2,1)S(1)}, bf16[8,7,128]{2,1,0:T(8,128)(2,1)S(1)}, u32[]{:S(2)}, u32[]{:S(2)}) collective-permute-start(bf16[8,7,128]{2,1,0:T(8,128)(2,1)S(1)} %get-tuple-element.37), channel_id=1, source_target_pairs={{0,15},{1,0},{2,1},{3,2},{4,3},{5,4},{6,5},{7,6},{8,7},{9,8},{10,9... | collective-permute-start | bytes 43016 | tf_op jit(solution)/shard_map/ppermute | solution.py:179
  6.9 27.4 %collective-permute-start = (bf16[7,7,128]{2,1,0:T(8,128)(2,1)S(1)}, bf16[7,7,128]{2,1,0:T(8,128)(2,1)S(1)}, u32[]{:S(2)}, u32[]{:S(2)}) collective-permute-start(bf16[7,7,128]{2,1,0:T(8,128)(2,1)S(1)} %get-tuple-element.30), channel_id=1, source_target_pairs={{0,17},{1,18},{2,19},{3,20},{4,21},{5,22},{6,23},{7,24},{8,25},{9,... | collective-permute-start | bytes 37640 | tf_op jit(solution)/shard_map/ppermute | solution.py:179
  8.8 28.2 %collective-permute-start.5 = (bf16[7,7,128]{2,1,0:T(8,128)(2,1)S(1)}, bf16[7,7,128]{2,1,0:T(8,128)(2,1)S(1)}, u32[]{:S(2)}, u32[]{:S(2)}) collective-permute-start(bf16[7,7,128]{2,1,0:T(8,128)(2,1)S(1)} %get-tuple-element.31), channel_id=1, source_target_pairs={{16,1},{17,2},{18,3},{19,4},{20,5},{21,6},{22,7},{23,8},{24,9},{25... | collective-permute-start | bytes 37640 | tf_op jit(solution)/shard_map/ppermute | solution.py:179
  10.7 35.4 %collective-permute-start.2 = (bf16[7,7,128]{2,1,0:T(8,128)(2,1)S(1)}, bf16[7,7,128]{2,1,0:T(8,128)(2,1)S(1)}, u32[]{:S(2)}, u32[]{:S(2)}) collective-permute-start(bf16[7,7,128]{2,1,0:T(8,128)(2,1)S(1)} %get-tuple-element.32), channel_id=1, source_target_pairs={{0,31},{1,16},{2,17},{3,18},{4,19},{5,20},{6,21},{7,22},{8,23},{9,... | collective-permute-start | bytes 37640 | tf_op jit(solution)/shard_map/ppermute | solution.py:179
  24.6 37.6 %all-to-all-start = ((f32[1,16,256,10]{2,3,0,1:T(8,128)}), f32[1,16,256,10]{2,3,0,1:T(8,128)S(1)}, u32[]{:S(2)}, u32[]{:S(2)}) async-start(f32[1,16,256,10]{2,3,0,1:T(8,128)} %pad_maximum_fusion.8), calls=%async_computation | async-start | bytes 524288 | tf_op jit(solution)/shard_map/all_to_all | solution.py:127
  34.3 13.8 %collective-permute-start.7 = (bf16[7,7,128]{2,1,0:T(8,128)(2,1)S(1)}, bf16[7,7,128]{2,1,0:T(8,128)(2,1)S(1)}, u32[]{:S(2)}, u32[]{:S(2)}) collective-permute-start(bf16[7,7,128]{2,1,0:T(8,128)(2,1)S(1)} %get-tuple-element.33), channel_id=1, source_target_pairs={{16,15},{17,0},{18,1},{19,2},{20,3},{21,4},{22,5},{23,6},{24,7},{2... | collective-permute-start | bytes 37640 | tf_op jit(solution)/shard_map/ppermute | solution.py:179
  37.0 11.1 %collective-permute-start.1 = (bf16[7,32,128]{2,1,0:T(8,128)(2,1)S(1)}, bf16[7,32,128]{2,1,0:T(8,128)(2,1)S(1)}, u32[]{:S(2)}, u32[]{:S(2)}) collective-permute-start(bf16[7,32,128]{2,1,0:T(8,128)(2,1)S(1)} %get-tuple-element.34), channel_id=1, source_target_pairs={{0,16},{1,17},{2,18},{3,19},{4,20},{5,21},{6,22},{7,23},{8,24},{9,... | collective-permute-start | bytes 172040 | tf_op jit(solution)/shard_map/ppermute | solution.py:179
  46.1 9.7 %collective-permute-start.6 = (bf16[7,32,128]{2,1,0:T(8,128)(2,1)S(1)}, bf16[7,32,128]{2,1,0:T(8,128)(2,1)S(1)}, u32[]{:S(2)}, u32[]{:S(2)}) collective-permute-start(bf16[7,32,128]{2,1,0:T(8,128)(2,1)S(1)} %get-tuple-element.35), channel_id=1, source_target_pairs={{16,0},{17,1},{18,2},{19,3},{20,4},{21,5},{22,6},{23,7},{24,8},{25... | collective-permute-start | bytes 172040 | tf_op jit(solution)/shard_map/ppermute | solution.py:179
  88.1 18.6 %collective-permute-start.8 = (bf16[5,5,128]{2,1,0:T(8,128)(2,1)S(1)}, bf16[5,5,128]{2,1,0:T(8,128)(2,1)S(1)}, u32[]{:S(2)}, u32[]{:S(2)}) collective-permute-start(bf16[5,5,128]{2,1,0:T(8,128)(2,1)S(1)} %get-tuple-element.22), channel_id=1, source_target_pairs={{0,17},{1,18},{2,19},{3,20},{4,21},{5,22},{6,23},{7,24},{8,25},{9,... | collective-permute-start | bytes 19208 | tf_op jit(solution)/shard_map/ppermute | solution.py:179
  90.0 24.0 %collective-permute-start.15 = (bf16[5,5,128]{2,1,0:T(8,128)(2,1)S(1)}, bf16[5,5,128]{2,1,0:T(8,128)(2,1)S(1)}, u32[]{:S(2)}, u32[]{:S(2)}) collective-permute-start(bf16[5,5,128]{2,1,0:T(8,128)(2,1)S(1)} %get-tuple-element.23), channel_id=1, source_target_pairs={{16,15},{17,0},{18,1},{19,2},{20,3},{21,4},{22,5},{23,6},{24,7},{2... | collective-permute-start | bytes 19208 | tf_op jit(solution)/shard_map/ppermute | solution.py:179
  96.7 20.4 %collective-permute-start.13 = (bf16[5,5,128]{2,1,0:T(8,128)(2,1)S(1)}, bf16[5,5,128]{2,1,0:T(8,128)(2,1)S(1)}, u32[]{:S(2)}, u32[]{:S(2)}) collective-permute-start(bf16[5,5,128]{2,1,0:T(8,128)(2,1)S(1)} %get-tuple-element.24), channel_id=1, source_target_pairs={{16,1},{17,2},{18,3},{19,4},{20,5},{21,6},{22,7},{23,8},{24,9},{25... | collective-permute-start | bytes 19208 | tf_op jit(solution)/shard_map/ppermute | solution.py:179
  99.2 20.6 %all-to-all-start.1 = ((f32[1,16,256]{2,0,1:T(1,128)}), f32[1,16,256]{2,0,1:T(1,128)S(1)}, u32[]{:S(2)}, u32[]{:S(2)}) async-start(f32[1,16,256]{2,0,1:T(1,128)} %sub.51), calls=%async_computation.1 | async-start | bytes 32768 | tf_op jit(solution)/shard_map/all_to_all | solution.py:155
  102.7 17.7 %collective-permute-start.11 = (bf16[8,5,128]{2,1,0:T(8,128)(2,1)S(1)}, bf16[8,5,128]{2,1,0:T(8,128)(2,1)S(1)}, u32[]{:S(2)}, u32[]{:S(2)}) collective-permute-start(bf16[8,5,128]{2,1,0:T(8,128)(2,1)S(1)} %get-tuple-element.28), channel_id=1, source_target_pairs={{0,1},{1,2},{2,3},{3,4},{4,5},{5,6},{6,7},{7,8},{8,9},{9,10},{10,1... | collective-permute-start | bytes 30728 | tf_op jit(solution)/shard_map/ppermute | solution.py:179
  103.0 17.5 %collective-permute-start.12 = (bf16[8,5,128]{2,1,0:T(8,128)(2,1)S(1)}, bf16[8,5,128]{2,1,0:T(8,128)(2,1)S(1)}, u32[]{:S(2)}, u32[]{:S(2)}) collective-permute-start(bf16[8,5,128]{2,1,0:T(8,128)(2,1)S(1)} %get-tuple-element.29), channel_id=1, source_target_pairs={{0,15},{1,0},{2,1},{3,2},{4,3},{5,4},{6,5},{7,6},{8,7},{9,8},{10,9... | collective-permute-start | bytes 30728 | tf_op jit(solution)/shard_map/ppermute | solution.py:179
  106.7 13.8 %collective-permute-start.10 = (bf16[5,5,128]{2,1,0:T(8,128)(2,1)S(1)}, bf16[5,5,128]{2,1,0:T(8,128)(2,1)S(1)}, u32[]{:S(2)}, u32[]{:S(2)}) collective-permute-start(bf16[5,5,128]{2,1,0:T(8,128)(2,1)S(1)} %get-tuple-element.25), channel_id=1, source_target_pairs={{0,31},{1,16},{2,17},{3,18},{4,19},{5,20},{6,21},{7,22},{8,23},{9,... | collective-permute-start | bytes 19208 | tf_op jit(solution)/shard_map/ppermute | solution.py:179
  114.0 6.5 %collective-permute-start.9 = (bf16[5,32,128]{2,1,0:T(8,128)(2,1)S(1)}, bf16[5,32,128]{2,1,0:T(8,128)(2,1)S(1)}, u32[]{:S(2)}, u32[]{:S(2)}) collective-permute-start(bf16[5,32,128]{2,1,0:T(8,128)(2,1)S(1)} %get-tuple-element.26), channel_id=1, source_target_pairs={{0,16},{1,17},{2,18},{3,19},{4,20},{5,21},{6,22},{7,23},{8,24},{9,... | collective-permute-start | bytes 122888 | tf_op jit(solution)/shard_map/ppermute | solution.py:179
  117.0 9.5 %collective-permute-start.14 = (bf16[5,32,128]{2,1,0:T(8,128)(2,1)S(1)}, bf16[5,32,128]{2,1,0:T(8,128)(2,1)S(1)}, u32[]{:S(2)}, u32[]{:S(2)}) collective-permute-start(bf16[5,32,128]{2,1,0:T(8,128)(2,1)S(1)} %get-tuple-element.27), channel_id=1, source_target_pairs={{16,0},{17,1},{18,2},{19,3},{20,4},{21,5},{22,6},{23,7},{24,8},{25... | collective-permute-start | bytes 122888 | tf_op jit(solution)/shard_map/ppermute | solution.py:179

commit v4 on v2

--- a/solution.py
+++ b/solution.py
@@ -1,6 +1,7 @@
 import jax
 import jax.numpy as jnp
 from jax import lax
+from jax.experimental import pallas as pl
 from jax.sharding import PartitionSpec as P
 
 C = 32
@@ -108,6 +109,47 @@
     return high.astype(jnp.bfloat16), (value - high).astype(jnp.bfloat16)
 
 
+def observe_kernel(got_ref, high_ref, low_ref, innov_ref, grad_ref):
+    fields, nslot = got_ref.shape[1], got_ref.shape[2]
+    feats, ncell = high_ref.shape
+    cell_ids = lax.broadcasted_iota(jnp.int32, (ncell, nslot), 0).astype(jnp.float32)
+    feat_ids = lax.broadcasted_iota(jnp.int32, (feats, nslot), 0).astype(jnp.float32)
+    high = high_ref[...]
+    low = low_ref[...]
+    both = jnp.concatenate([high, low], axis=0)
+    grad_ref[...] = jnp.zeros(grad_ref.shape, jnp.float32)
+    trans = (((1,), (1,)), ((), ()))
+
+    def body(owner, carry):
+        block = got_ref[owner]
+        table = jnp.zeros((ncell, nslot), jnp.float32)
+        for j in range(4):
+            table = table + jnp.where(
+                cell_ids == block[j : j + 1, :], block[5 + j : 6 + j, :], 0.0
+            )
+        t_hi = table.astype(jnp.bfloat16)
+        t_lo = (table - t_hi.astype(jnp.float32)).astype(jnp.bfloat16)
+        two = jnp.dot(both, t_hi, preferred_element_type=jnp.float32)
+        picked = two[:feats] + two[feats:] + jnp.dot(high, t_lo, preferred_element_type=jnp.float32)
+        pick = feat_ids == block[4:5, :]
+        innov = jnp.sum(jnp.where(pick, picked, 0.0), axis=0, keepdims=True) - block[9:10, :]
+        innov_ref[pl.ds(owner, 1), :] = innov
+        spread = jnp.where(pick, innov, 0.0)
+        s_hi = spread.astype(jnp.bfloat16)
+        s_lo = (spread - s_hi.astype(jnp.float32)).astype(jnp.bfloat16)
+        sums = lax.dot_general(
+            t_hi, jnp.concatenate([s_hi, s_lo], axis=0), trans, preferred_element_type=jnp.float32
+        )
+        grad_ref[...] += (
+            sums[:, :feats]
+            + sums[:, feats:]
+            + lax.dot_general(t_lo, s_hi, trans, preferred_element_type=jnp.float32)
+        )
+        return carry
+
+    lax.fori_loop(0, got_ref.shape[0], body, 0)
+
+
 def observe(output, obs_cells, obs_chan, obs_weights, obs_value, obs_count):
     rows, cols, feats = output.shape
     ncell = rows * cols
@@ -117,41 +159,24 @@
     values = obs_value * live
     packed = jnp.concatenate(
         [
-            obs_cells.astype(jnp.float32),
-            obs_chan[..., None].astype(jnp.float32),
-            weights,
-            values[..., None],
+            jnp.swapaxes(obs_cells, 2, 3).astype(jnp.float32),
+            obs_chan[:, :, None, :].astype(jnp.float32),
+            jnp.swapaxes(weights, 2, 3),
+            values[:, :, None, :],
         ],
-        axis=-1,
+        axis=2,
     )
     got = lax.all_to_all(packed, "lon", split_axis=1, concat_axis=1, tiled=True)
-    got = got.reshape(-1, packed.shape[-1])
-    cells = got[:, 0:4].astype(jnp.int32)
-    chan = got[:, 4:5].astype(jnp.int32)
-    wts = got[:, 5:9]
-    vals = got[:, 9]
-    count = got.shape[0]
-    cell_ids = lax.broadcasted_iota(jnp.int32, (count, ncell), 1)
-    table = jnp.zeros((count, ncell), jnp.float32)
-    for j in range(4):
-        table = table + jnp.where(cell_ids == cells[:, j : j + 1], wts[:, j : j + 1], 0.0)
-    t_hi, t_lo = split_bf16(table)
-    o_hi, o_lo = split_bf16(output.reshape(ncell, feats))
-    both = jnp.dot(t_hi, jnp.concatenate([o_hi, o_lo], axis=1), preferred_element_type=jnp.float32)
-    picked = both[:, :feats] + both[:, feats:] + jnp.dot(
-        t_lo, o_hi, preferred_element_type=jnp.float32
-    )
-    pick = lax.broadcasted_iota(jnp.int32, (count, feats), 1) == chan
-    innov = jnp.sum(jnp.where(pick, picked, 0.0), axis=1) - vals
-    spread = jnp.where(pick, innov[:, None], 0.0)
-    s_hi, s_lo = split_bf16(spread)
-    dims = (((0,), (0,)), ((), ()))
-    back = lax.dot_general(
-        t_hi, jnp.concatenate([s_hi, s_lo], axis=1), dims, preferred_element_type=jnp.float32
-    )
-    grad = back[:, :feats] + back[:, feats:] + lax.dot_general(
-        t_lo, s_hi, dims, preferred_element_type=jnp.float32
-    )
+    got = got.reshape(got.shape[1:])
+    owners, nslot = got.shape[0], got.shape[2]
+    o_hi, o_lo = split_bf16(output.reshape(ncell, feats).T)
+    innov, grad = pl.pallas_call(
+        observe_kernel,
+        out_shape=(
+            jax.ShapeDtypeStruct((owners, nslot), jnp.float32),
+            jax.ShapeDtypeStruct((ncell, feats), jnp.float32),
+        ),
+    )(got, o_hi, o_lo)
     innovation = lax.all_to_all(
         innov.reshape(obs_value.shape), "lon", split_axis=1, concat_axis=1, tiled=True
     )

time: 93.9 us -> 79.4 us (0.85)
  matrix products: 36.2 us -> 11.4 us
  Pallas kernels: 0 us -> 10.7 us
    dot_general x4 -> x0, matrix products: 24.8 us -> none  [the longest x1 8.99 us: observe(): jnp.dot(t_lo, o_hi, preferred_element_type=jnp.float32)]
    pallas_call x0 -> x1, Pallas kernels: none -> 10.7 us  [observe(): pl.pallas_call(observe_kernel, out_shape=(jax.ShapeDtypeStruct((owners, n...]
    squeeze x3, local copies, waits for them, and re-layouts: 2.93 us -> 0.05 us  [banded(): kernel[:, :, p - q + 1]]
    reshape x0 -> x3, local copies, waits for them, and re-layouts: none -> 2.15 us  [the longest x1 1.33 us: observe(): innov.reshape(obs_value.shape)]
where the time goes in v4:
time: 79.4 us; the launch traced here: 78.7 us
  starting transfers between devices  28.9 us (36%)
  waiting for transfers between devices  13.2 us (17%)
  matrix products  11.4 us (14%)
  Pallas kernels  10.7 us (13%)
  other arithmetic  7.88 us (10%)
  local copies, waits for them, and re-layouts  5.38 us (7%)
  between operations  1.29 us (2%)
    ppermute x4, waiting for transfers between devices, with_halo(): lax.ppermute(lax.slice_in_dim(block, 0, width, axis=dim), axis, backward)  13 us
    pallas_call x1, Pallas kernels, observe(): pl.pallas_call(observe_kernel, out_shape=(jax.ShapeDtypeStruct((owners, n...  10.7 us
    ppermute x4, starting transfers between devices, with_halo(): lax.ppermute(lax.slice_in_dim(block, 0, width, axis=dim), axis, backward)  9.31 us
    all_to_all x1, starting transfers between devices, observe(): got = lax.all_to_all(packed, 'lon', split_axis=1, concat_axis=1, tiled=True)  6.92 us
    ppermute x4, starting transfers between devices, with_halo(): lax.ppermute(lax.slice_in_dim(block, block.shape[dim] - width, None, axis...  6.35 us
    all_to_all x1, starting transfers between devices, observe(): lax.all_to_all(innov.reshape(obs_value.shape), 'lon', split_axis=1, conca...  6.31 us
    dot_general x27, matrix products, adjoint_valid(): jnp.einsum('ijg,fg->ijf', piece, matrices[row_off * 3 + col_off], preferr...  5.84 us
    dot_general x27, matrix products, conv_valid(): jnp.einsum('ijf,fg->ijg', piece, matrices[row_off * 3 + col_off], preferr...  4.99 us
  transfers between devices with their start and end apart: 10, of which 3 were waited for; matrix products, arithmetic and copies ran while one was open for 18% of the time, Pallas kernels for 0%

profile of v4, /device:TPU:14, one launch (start us, length us, event | category | flops | bytes accessed | tf_op | source)
XLA Modules:
  0.0 78.7 jit_solution(9585638584838166314)
XLA Ops:
  0.7 0.8 fusion.179
  1.5 1.7 %collective-permute-start.1 = (bf16[8,7,128]{2,1,0:T(8,128)(2,1)S(1)}, bf16[8,7,128]{2,1,0:T(8,128)(2,1)S(1)}, u32[]{:S(2)}, u32[]{:S(2)}) collective-permute-start(bf16[8,7,128]{2,1,0:T(8,128)(2,1)S(1)} %get-tuple-element.28), channel_id=1, source_target_pairs={{1,0},{2,1},{3,2},{4,3},{5,4},{6,5},{7,6},{8,7},{9,8},{10,9},{11,1... | collective-permute-start | bytes 43016 | tf_op jit(solution)/shard_map/ppermute | solution.py:22
  3.2 0.7 fusion.163
  3.9 0.9 %convert_element_type.66 = f32[1,16,256,4]{2,3,1,0:T(4,128)S(1)} convert(s32[1,16,256,4]{2,3,1,0:T(4,128)} %param.15) | non-fusion elementwise | flops 16384 | bytes 131072 | tf_op jit(solution)/shard_map/convert_element_type | solution.py:162
  4.8 0.8 convert_element_type.83
  5.6 0.9 %broadcast_multiply_fusion = f32[1,16,256,4]{2,3,1,0:T(4,128)S(1)} fusion(f32[1,16,256,4]{2,3,1,0:T(4,128)} %param.17, f32[16,256]{1,0:T(8,128)S(1)} %fusion.163), kind=kLoop, calls=%fused_computation.266 | loop fusion | flops 16384 | bytes 147456 | tf_op jit(solution)/shard_map/mul | solution.py:158
  6.7 0.8 %pad_maximum_fusion.10 = f32[1,16,10,256]{3,0,2,1:T(1,128)} fusion(f32[1,16,1,256]{3,0,2,1:T(1,128)S(1)} %get-tuple-element.35, f32[1,16,4,256]{3,0,2,1:T(1,128)S(1)} %get-tuple-element.33, f32[1,16,1,256]{3,0,2,1:T(1,128)S(1)} %get-tuple-element.36, f32[1,16,4,256]{3,0,2,1:T(1,128)S(1)} %get-tuple-element.34), kind=kLoop, calls=%fused_computation.148 | loop fusion | flops 122880 | bytes 327680 | tf_op jit(solution)/shard_map/concatenate | solution.py:160
  7.5 6.9 %all-to-all-start = ((f32[1,16,10,256]{3,0,2,1:T(1,128)}), f32[1,16,10,256]{3,0,2,1:T(1,128)S(1)}, u32[]{:S(2)}, u32[]{:S(2)}) async-start(f32[1,16,10,256]{3,0,2,1:T(1,128)} %pad_maximum_fusion.10), calls=%async_computation | async-start | bytes 327680 | tf_op jit(solution)/shard_map/all_to_all | solution.py:169
  14.6 0.3 fusion.27
  14.9 0.3 fusion.30
  15.3 0.3 maximum_maximum_fusion
  15.6 0.3 copy-done.6
  16.2 4.3 %collective-permute-start.2 = (bf16[7,46,128]{2,1,0:T(8,128)(2,1)S(1)}, bf16[7,46,128]{2,1,0:T(8,128)(2,1)S(1)}, u32[]{:S(2)}, u32[]{:S(2)}) collective-permute-start(bf16[7,46,128]{2,1,0:T(8,128)(2,1)S(1)} %get-tuple-element.23), channel_id=1, source_target_pairs={{0,16},{16,32},{32,48},{48,64},{64,80},{80,96},{96,112},{1,17},{17... | collective-permute-start | bytes 247304 | tf_op jit(solution)/shard_map/ppermute | solution.py:19
  20.5 1.9 %collective-permute-start.3 = (bf16[7,46,128]{2,1,0:T(8,128)(2,1)S(1)}, bf16[7,46,128]{2,1,0:T(8,128)(2,1)S(1)}, u32[]{:S(2)}, u32[]{:S(2)}) collective-permute-start(bf16[7,46,128]{2,1,0:T(8,128)(2,1)S(1)} %get-tuple-element.24), channel_id=1, source_target_pairs={{16,0},{32,16},{48,32},{64,48},{80,64},{96,80},{112,96},{17,1},{33... | collective-permute-start | bytes 247304 | tf_op jit(solution)/shard_map/ppermute | solution.py:22
  22.4 0.2 collective-permute-done.2
  22.6 7.9 %collective-permute-done.3 = bf16[7,46,128]{2,1,0:T(8,128)(2,1)S(1)} collective-permute-done((bf16[7,46,128]{2,1,0:T(8,128)(2,1)S(1)}, bf16[7,46,128]{2,1,0:T(8,128)(2,1)S(1)}, u32[]{:S(2)}, u32[]{:S(2)}) %collective-permute-start.3) | collective-permute-done | bytes 82464 | tf_op jit(solution)/shard_map/ppermute | solution.py:22
  30.5 0.2 fusion.37
  30.7 0.2 fusion.39
  30.9 0.2 fusion.41
  31.1 0.2 fusion.43
  31.4 0.2 fusion.45
  31.6 0.2 fusion.47
  31.8 0.2 fusion.49
  32.0 0.2 fusion.51
  32.2 0.4 fusion.24
  32.7 0.3 reshape.159
  32.9 0.3 reduce_sum.18
  33.9 0.2 convolution_add_fusion.7
  34.9 0.2 fusion.120
  36.7 0.2 multiply_add_fusion
  37.0 0.7 fusion.97
  37.6 0.7 copy.100
  38.4 10.7 %shard_map.113 = (f32[16,256]{1,0:T(8,128)}, f32[256,128]{1,0:T(8,128)}) custom-call(f32[16,10,256]{2,1,0:T(8,128)} %bitcast.256, bf16[128,256]{1,0:T(8,128)(2,1)} %get-tuple-element.20.high_ref, bf16[128,256]{1,0:T(8,128)(2,1)} %get-tuple-element.19.low_ref), custom_call_target="tpu_custom_call" | custom-call | tf_op jit(solution)/shard_map/pallas_call | solution.py:173
  49.1 1.0 %fusion.106 = bf16[8,32,128]{2,1,0:T(8,128)(2,1)S(1)} fusion(f32[8,32,128]{2,1,0:T(8,128)} %bitcast.258, f32[8,32,128]{2,1,0:T(8,128)S(1)} %get-tuple-element.32), kind=kLoop, calls=%fused_computation.166 | loop fusion | flops 622592 | bytes 327680 | tf_op jit(solution)/shard_map/convert_element_type | solution.py:238
  50.2 1.7 %collective-permute-start.5 = (bf16[8,5,128]{2,1,0:T(8,128)(2,1)S(1)}, bf16[8,5,128]{2,1,0:T(8,128)(2,1)S(1)}, u32[]{:S(2)}, u32[]{:S(2)}) collective-permute-start(bf16[8,5,128]{2,1,0:T(8,128)(2,1)S(1)} %get-tuple-element.26), channel_id=1, source_target_pairs={{1,0},{2,1},{3,2},{4,3},{5,4},{6,5},{7,6},{8,7},{9,8},{10,9},{11,1... | collective-permute-start | bytes 30728 | tf_op jit(solution)/shard_map/ppermute | solution.py:22
  51.9 1.3 %copy.82 = f32[1,16,256]{2,0,1:T(1,128)} copy(f32[1,16,256]{2,1,0:T(8,128)} %bitcast.260) | data formatting | bytes 32768 | tf_op jit(solution)/shard_map/reshape | solution.py:181
  53.2 6.3 %all-to-all-start.1 = ((f32[1,16,256]{2,0,1:T(1,128)}), f32[1,16,256]{2,0,1:T(1,128)S(1)}, u32[]{:S(2)}, u32[]{:S(2)}) async-start(f32[1,16,256]{2,0,1:T(1,128)} %copy.82), calls=%async_computation.1 | async-start | bytes 32768 | tf_op jit(solution)/shard_map/all_to_all | solution.py:180
  59.6 1.9 %collective-permute-start.6 = (bf16[5,42,128]{2,1,0:T(8,128)(2,1)S(1)}, bf16[5,42,128]{2,1,0:T(8,128)(2,1)S(1)}, u32[]{:S(2)}, u32[]{:S(2)}) collective-permute-start(bf16[5,42,128]{2,1,0:T(8,128)(2,1)S(1)} %get-tuple-element.21), channel_id=1, source_target_pairs={{0,16},{16,32},{32,48},{48,64},{64,80},{80,96},{96,112},{1,17},{17... | collective-permute-start | bytes 161288 | tf_op jit(solution)/shard_map/ppermute | solution.py:19
  61.6 3.9 %collective-permute-start.7 = (bf16[5,42,128]{2,1,0:T(8,128)(2,1)S(1)}, bf16[5,42,128]{2,1,0:T(8,128)(2,1)S(1)}, u32[]{:S(2)}, u32[]{:S(2)}) collective-permute-start(bf16[5,42,128]{2,1,0:T(8,128)(2,1)S(1)} %get-tuple-element.22), channel_id=1, source_target_pairs={{16,0},{32,16},{48,32},{64,48},{80,64},{96,80},{112,96},{17,1},{33... | collective-permute-start | bytes 161288 | tf_op jit(solution)/shard_map/ppermute | solution.py:22
  65.5 0.6 copy.83
  66.1 5.2 %collective-permute-done.7 = bf16[5,42,128]{2,1,0:T(8,128)(2,1)S(1)} collective-permute-done((bf16[5,42,128]{2,1,0:T(8,128)(2,1)S(1)}, bf16[5,42,128]{2,1,0:T(8,128)(2,1)S(1)}, u32[]{:S(2)}, u32[]{:S(2)}) %collective-permute-start.7) | collective-permute-done | bytes 53792 | tf_op jit(solution)/shard_map/ppermute | solution.py:22
  71.3 0.2 fusion.80
  71.6 0.2 fusion.82
  71.8 0.2 fusion.84
  72.1 0.2 fusion.86
  72.3 0.2 fusion.78
  72.6 0.2 fusion.76
  72.8 0.2 fusion.74
  73.0 0.2 fusion.72
  73.3 0.3 fusion.13
  73.6 0.2 reduce_sum.19
  73.8 0.3 fusion.16
  74.3 0.2 convolution_add_fusion.33
  74.5 0.2 convolution_add_fusion.32
  74.7 0.2 convolution_add_fusion.31
  74.8 0.2 convolution_add_fusion.30
  75.0 0.2 convolution_add_fusion.29
  75.2 0.2 convolution_add_fusion.28
  75.4 0.2 convolution_add_fusion.27
  75.5 0.2 convolution_add_fusion.26
  76.0 0.2 broadcast_select_fusion
  76.3 0.2 convolution_add_fusion.17
  77.5 0.4 copy-done.1
  77.9 0.8 %fusion.15 = f32[8,32,128]{2,1,0:T(8,128)} fusion(f32[8,32,128]{2,1,0:T(8,128)S(1)} %bitcast.259, f32[8,32,128]{2,1,0:T(8,128)S(1)} %convolution_add_fusion.11, bf16[10,34,128]{2,1,0:T(8,128)(2,1)S(1)} %broadcast_select_fusion, bf16[9,128,128]{2,1,0:T(8,128)(2,1)S(1)} %bitcast.236), kind=kOutput, calls=%fused_computation.27 | convolution fusion | flops 8454144 | bytes 491520 | tf_op jit(solution)/shard_map/ijg,fg->ijf/dot_general | solution.py:78
  (75 shorter events, 5.4 us)
Async XLA Ops:
  0.6 5.9 %copy-start.7 = (s32[1,16]{1,0:T(1,128)S(1)}, s32[1,16]{1,0:T(1,128)}, u32[]{:S(2)}) copy-start(s32[1,16]{1,0:T(1,128)} %param.19) | copy-start | bytes 196
  0.6 5.9 %copy-start.5 = (f32[1,16,256]{2,1,0:T(8,128)S(1)}, f32[1,16,256]{2,1,0:T(8,128)}, u32[]{:S(2)}) copy-start(f32[1,16,256]{2,1,0:T(8,128)} %param.18) | copy-start | bytes 49156
  1.4 14.6 %collective-permute-start = (bf16[8,7,128]{2,1,0:T(8,128)(2,1)S(1)}, bf16[8,7,128]{2,1,0:T(8,128)(2,1)S(1)}, u32[]{:S(2)}, u32[]{:S(2)}) collective-permute-start(bf16[8,7,128]{2,1,0:T(8,128)(2,1)S(1)} %get-tuple-element.27), channel_id=1, source_target_pairs={{0,1},{1,2},{2,3},{3,4},{4,5},{5,6},{6,7},{7,8},{8,9},{9,10},{10,1... | collective-permute-start | bytes 43016 | tf_op jit(solution)/shard_map/ppermute | solution.py:19
  1.5 14.6 %collective-permute-start.1 = (bf16[8,7,128]{2,1,0:T(8,128)(2,1)S(1)}, bf16[8,7,128]{2,1,0:T(8,128)(2,1)S(1)}, u32[]{:S(2)}, u32[]{:S(2)}) collective-permute-start(bf16[8,7,128]{2,1,0:T(8,128)(2,1)S(1)} %get-tuple-element.28), channel_id=1, source_target_pairs={{1,0},{2,1},{3,2},{4,3},{5,4},{6,5},{7,6},{8,7},{9,8},{10,9},{11,1... | collective-permute-start | bytes 43016 | tf_op jit(solution)/shard_map/ppermute | solution.py:22
  4.8 9.6 %copy-start.2 = (bf16[3,3,3,32,32]{4,3,2,1,0:T(8,128)(2,1)S(1)}, bf16[3,3,3,32,32]{4,3,2,1,0:T(8,128)(2,1)}, u32[]{:S(2)}) copy-start(bf16[3,3,3,32,32]{4,3,2,1,0:T(8,128)(2,1)} %param.11) | copy-start | bytes 165892
  6.6 7.9 %copy-start.3 = (bf16[3,3,3,32,64]{4,3,2,1,0:T(8,128)(2,1)S(1)}, bf16[3,3,3,32,64]{4,3,2,1,0:T(8,128)(2,1)}, u32[]{:S(2)}) copy-start(bf16[3,3,3,32,64]{4,3,2,1,0:T(8,128)(2,1)} %param.12) | copy-start | bytes 331780
  7.5 7.0 %copy-start.4 = (bf16[3,3,3,32,32]{4,3,2,1,0:T(8,128)(2,1)S(1)}, bf16[3,3,3,32,32]{4,3,2,1,0:T(8,128)(2,1)}, u32[]{:S(2)}) copy-start(bf16[3,3,3,32,32]{4,3,2,1,0:T(8,128)(2,1)} %param.13) | copy-start | bytes 165892
  7.5 30.1 %all-to-all-start = ((f32[1,16,10,256]{3,0,2,1:T(1,128)}), f32[1,16,10,256]{3,0,2,1:T(1,128)S(1)}, u32[]{:S(2)}, u32[]{:S(2)}) async-start(f32[1,16,10,256]{3,0,2,1:T(1,128)} %pad_maximum_fusion.10), calls=%async_computation | async-start | bytes 327680 | tf_op jit(solution)/shard_map/all_to_all | solution.py:169
  15.2 0.7 copy-start.6
  15.2 0.8 %copy-start = (bf16[8,32,128]{2,1,0:T(8,128)(2,1)S(1)}, bf16[8,32,128]{2,1,0:T(8,128)(2,1)}, u32[]{:S(2)}) copy-start(bf16[8,32,128]{2,1,0:T(8,128)(2,1)} %param.10) | copy-start | bytes 196612
  16.2 6.4 %collective-permute-start.2 = (bf16[7,46,128]{2,1,0:T(8,128)(2,1)S(1)}, bf16[7,46,128]{2,1,0:T(8,128)(2,1)S(1)}, u32[]{:S(2)}, u32[]{:S(2)}) collective-permute-start(bf16[7,46,128]{2,1,0:T(8,128)(2,1)S(1)} %get-tuple-element.23), channel_id=1, source_target_pairs={{0,16},{16,32},{32,48},{48,64},{64,80},{80,96},{96,112},{1,17},{17... | collective-permute-start | bytes 247304 | tf_op jit(solution)/shard_map/ppermute | solution.py:19
  20.5 10.0 %collective-permute-start.3 = (bf16[7,46,128]{2,1,0:T(8,128)(2,1)S(1)}, bf16[7,46,128]{2,1,0:T(8,128)(2,1)S(1)}, u32[]{:S(2)}, u32[]{:S(2)}) collective-permute-start(bf16[7,46,128]{2,1,0:T(8,128)(2,1)S(1)} %get-tuple-element.24), channel_id=1, source_target_pairs={{16,0},{32,16},{48,32},{64,48},{80,64},{96,80},{112,96},{17,1},{33... | collective-permute-start | bytes 247304 | tf_op jit(solution)/shard_map/ppermute | solution.py:22
  50.1 9.5 %collective-permute-start.4 = (bf16[8,5,128]{2,1,0:T(8,128)(2,1)S(1)}, bf16[8,5,128]{2,1,0:T(8,128)(2,1)S(1)}, u32[]{:S(2)}, u32[]{:S(2)}) collective-permute-start(bf16[8,5,128]{2,1,0:T(8,128)(2,1)S(1)} %get-tuple-element.25), channel_id=1, source_target_pairs={{0,1},{1,2},{2,3},{3,4},{4,5},{5,6},{6,7},{7,8},{8,9},{9,10},{10,1... | collective-permute-start | bytes 30728 | tf_op jit(solution)/shard_map/ppermute | solution.py:19
  50.2 9.4 %collective-permute-start.5 = (bf16[8,5,128]{2,1,0:T(8,128)(2,1)S(1)}, bf16[8,5,128]{2,1,0:T(8,128)(2,1)S(1)}, u32[]{:S(2)}, u32[]{:S(2)}) collective-permute-start(bf16[8,5,128]{2,1,0:T(8,128)(2,1)S(1)} %get-tuple-element.26), channel_id=1, source_target_pairs={{1,0},{2,1},{3,2},{4,3},{5,4},{6,5},{7,6},{8,7},{9,8},{10,9},{11,1... | collective-permute-start | bytes 30728 | tf_op jit(solution)/shard_map/ppermute | solution.py:22
  53.2 12.3 %all-to-all-start.1 = ((f32[1,16,256]{2,0,1:T(1,128)}), f32[1,16,256]{2,0,1:T(1,128)S(1)}, u32[]{:S(2)}, u32[]{:S(2)}) async-start(f32[1,16,256]{2,0,1:T(1,128)} %copy.82), calls=%async_computation.1 | async-start | bytes 32768 | tf_op jit(solution)/shard_map/all_to_all | solution.py:180
  59.6 6.5 %collective-permute-start.6 = (bf16[5,42,128]{2,1,0:T(8,128)(2,1)S(1)}, bf16[5,42,128]{2,1,0:T(8,128)(2,1)S(1)}, u32[]{:S(2)}, u32[]{:S(2)}) collective-permute-start(bf16[5,42,128]{2,1,0:T(8,128)(2,1)S(1)} %get-tuple-element.21), channel_id=1, source_target_pairs={{0,16},{16,32},{32,48},{48,64},{64,80},{80,96},{96,112},{1,17},{17... | collective-permute-start | bytes 161288 | tf_op jit(solution)/shard_map/ppermute | solution.py:19
  61.6 9.7 %collective-permute-start.7 = (bf16[5,42,128]{2,1,0:T(8,128)(2,1)S(1)}, bf16[5,42,128]{2,1,0:T(8,128)(2,1)S(1)}, u32[]{:S(2)}, u32[]{:S(2)}) collective-permute-start(bf16[5,42,128]{2,1,0:T(8,128)(2,1)S(1)} %get-tuple-element.22), channel_id=1, source_target_pairs={{16,0},{32,16},{48,32},{64,48},{80,64},{96,80},{112,96},{17,1},{33... | collective-permute-start | bytes 161288 | tf_op jit(solution)/shard_map/ppermute | solution.py:22
  77.0 0.9 %copy-start.1 = (f32[256,128]{1,0:T(8,128)S(1)}, f32[256,128]{1,0:T(8,128)}, u32[]{:S(2)}) copy-start(f32[256,128]{1,0:T(8,128)} %get-tuple-element.4) | copy-start | bytes 393220

commit v5 on v4

--- a/solution.py
+++ b/solution.py
@@ -1,7 +1,10 @@
 import jax
 import jax.numpy as jnp
 from jax import lax
+import functools
+
 from jax.experimental import pallas as pl
+from jax.experimental.pallas import tpu as pltpu
 from jax.sharding import PartitionSpec as P
 
 C = 32
@@ -183,9 +186,75 @@
     return grad.reshape(rows, cols, feats), innovation
 
 
+def halo_kernel(width, nlat, nlon, x_ref, o_ref, buf, send_sem, recv_sem):
+    rows, cols = x_ref.shape[0], x_ref.shape[1]
+    edge = (buf.shape[1] - cols) // 2
+    i = lax.axis_index("lat")
+    j = lax.axis_index("lon")
+    has = {-1: i > 0, 0: i >= 0, 1: i < nlat - 1}
+    dirs = [(a, b) for a in (-1, 0, 1) for b in (-1, 0, 1) if (a, b) != (0, 0)]
+    buf[...] = jnp.zeros(buf.shape, buf.dtype)
+    buf[width : width + rows, edge : edge + cols, :] = x_ref[...]
+    barrier = pltpu.get_barrier_semaphore()
+    for a, b in dirs:
+
+        @pl.when(has[a])
+        def _():
+            pl.semaphore_signal(
+                barrier,
+                inc=1,
+                device_id=((i + a) % nlat, (j + b) % nlon),
+                device_id_type=pl.DeviceIdType.MESH,
+            )
+
+    count = 2 + 3 * has[-1].astype(jnp.int32) + 3 * has[1].astype(jnp.int32)
+    pl.semaphore_wait(barrier, count)
+    src_rows = {1: pl.ds(rows - width, width), -1: pl.ds(0, width), 0: pl.ds(0, rows)}
+    dst_rows = {1: pl.ds(0, width), -1: pl.ds(width + rows, width), 0: pl.ds(width, rows)}
+    src_cols = {1: pl.ds(cols - edge, edge), -1: pl.ds(0, edge), 0: pl.ds(0, cols)}
+    dst_cols = {1: pl.ds(0, edge), -1: pl.ds(edge + cols, edge), 0: pl.ds(edge, cols)}
+    copies = []
+    for k, (a, b) in enumerate(dirs):
+        copy = pltpu.make_async_remote_copy(
+            src_ref=x_ref.at[src_rows[a], src_cols[b]],
+            dst_ref=buf.at[dst_rows[a], dst_cols[b]],
+            send_sem=send_sem.at[k],
+            recv_sem=recv_sem.at[k],
+            device_id=((i + a) % nlat, (j + b) % nlon),
+            device_id_type=pl.DeviceIdType.MESH,
+        )
+        copies.append((a, copy))
+        pl.when(has[a])(copy.start)
+    for a, copy in copies:
+        pl.when(has[a])(copy.wait_send)
+        pl.when(has[-a])(copy.wait_recv)
+    o_ref[...] = buf[...]
+
+
+EXCHANGE_IDS = {7: 0, 5: 1}
+
+
 def exchange(block, width):
-    wide = with_halo(block, (("lon", 1),), width, True)
-    return with_halo(wide, (("lat", 0),), width, False)
+    rows, cols, feats = block.shape
+    edge = 16
+    nlat = lax.axis_size("lat")
+    nlon = lax.axis_size("lon")
+    full = (rows + 2 * width, cols + 2 * edge, feats)
+    out = pl.pallas_call(
+        functools.partial(halo_kernel, width, nlat, nlon),
+        out_shape=jax.ShapeDtypeStruct(full, block.dtype),
+        in_specs=[pl.BlockSpec(memory_space=pltpu.VMEM)],
+        out_specs=pl.BlockSpec(memory_space=pltpu.VMEM),
+        scratch_shapes=[
+            pltpu.VMEM(full, block.dtype),
+            pltpu.SemaphoreType.DMA((8,)),
+            pltpu.SemaphoreType.DMA((8,)),
+        ],
+        compiler_params=pltpu.CompilerParams(
+            collective_id=EXCHANGE_IDS[width], has_side_effects=True
+        ),
+    )(block)
+    return out[:, edge - width : edge + cols + width]
 
 
 def inside(field, tile_rows, halo):

time: 79.4 us -> 79.9 us (level)
  the two profiles are of different devices: /device:TPU:14 before, /device:TPU:7 now
where the time goes in v5:
time: 79.9 us; the launch traced here: 79.2 us
  Pallas kernels  34.4 us (43%)
  matrix products  12.4 us (16%)
  starting transfers between devices  11.8 us (15%)
  other arithmetic  8.42 us (11%)
  local copies, waits for them, and re-layouts  5.96 us (7%)
  waiting for transfers between devices  5.02 us (6%)
  between operations  1.13 us (1%)
    pallas_call x2, Pallas kernels, exchange(): pl.pallas_call(functools.partial(halo_kernel, width, nlat, nlon), out_sha...  23.7 us
    pallas_call x1, Pallas kernels, observe(): pl.pallas_call(observe_kernel, out_shape=(jax.ShapeDtypeStruct((owners, n...  10.7 us
    all_to_all x1, starting transfers between devices, observe(): got = lax.all_to_all(packed, 'lon', split_axis=1, concat_axis=1, tiled=True)  7.01 us
    dot_general x27, matrix products, adjoint_valid(): jnp.einsum('ijg,fg->ijf', piece, matrices[row_off * 3 + col_off], preferr...  6.9 us
    all_to_all x1, waiting for transfers between devices, observe(): lax.all_to_all(innov.reshape(obs_value.shape), 'lon', split_axis=1, conca...  5.02 us
    dot_general x27, matrix products, conv_valid(): jnp.einsum('ijf,fg->ijg', piece, matrices[row_off * 3 + col_off], preferr...  4.95 us
    all_to_all x1, starting transfers between devices, observe(): lax.all_to_all(innov.reshape(obs_value.shape), 'lon', split_axis=1, conca...  4.82 us
    unnamed x24, local copies, waits for them, and re-layouts  3.59 us
  transfers between devices with their start and end apart: 2, of which 1 were waited for; matrix products, arithmetic and copies ran while one was open for 11% of the time, Pallas kernels for 15%

profile of v5, /device:TPU:7, one launch (start us, length us, event | category | flops | bytes accessed | tf_op | source)
XLA Modules:
  0.0 79.2 jit_solution(15336922532936001976)
XLA Ops:
  0.6 0.8 fusion.136
  1.4 0.9 %convert_element_type.66 = f32[1,16,256,4]{2,3,1,0:T(4,128)S(1)} convert(s32[1,16,256,4]{2,3,1,0:T(4,128)} %param.15) | non-fusion elementwise | flops 16384 | bytes 131072 | tf_op jit(solution)/shard_map/convert_element_type | solution.py:165
  2.3 0.8 convert_element_type.83
  3.1 0.9 %broadcast_multiply_fusion = f32[1,16,256,4]{2,3,1,0:T(4,128)S(1)} fusion(f32[1,16,256,4]{2,3,1,0:T(4,128)} %param.17, f32[16,256]{1,0:T(8,128)S(1)} %fusion.136), kind=kLoop, calls=%fused_computation.249 | loop fusion | flops 16384 | bytes 147456 | tf_op jit(solution)/shard_map/mul | solution.py:161
  4.2 0.8 %pad_maximum_fusion.8 = f32[1,16,10,256]{3,0,2,1:T(1,128)} fusion(f32[1,16,1,256]{3,0,2,1:T(1,128)S(1)} %get-tuple-element.27, f32[1,16,4,256]{3,0,2,1:T(1,128)S(1)} %get-tuple-element.25, f32[1,16,1,256]{3,0,2,1:T(1,128)S(1)} %get-tuple-element.28, f32[1,16,4,256]{3,0,2,1:T(1,128)S(1)} %get-tuple-element.26), kind=kLoop, calls=%fused_computation.123 | loop fusion | flops 122880 | bytes 327680 | tf_op jit(solution)/shard_map/concatenate | solution.py:163
  5.0 7.0 %all-to-all-start = ((f32[1,16,10,256]{3,0,2,1:T(1,128)}), f32[1,16,10,256]{3,0,2,1:T(1,128)S(1)}, u32[]{:S(2)}, u32[]{:S(2)}) async-start(f32[1,16,10,256]{3,0,2,1:T(1,128)} %pad_maximum_fusion.8), calls=%async_computation | async-start | bytes 327680 | tf_op jit(solution)/shard_map/all_to_all | solution.py:172
  12.0 12.1 %shard_map.113 = bf16[22,64,128]{2,1,0:T(8,128)(2,1)} custom-call(bf16[8,32,128]{2,1,0:T(8,128)(2,1)} %x_ref.1), custom_call_target="tpu_custom_call" | custom-call | tf_op jit(solution)/shard_map/pallas_call | solution.py:243
  24.2 0.3 fusion.14
  24.5 0.6 copy-done
  25.1 0.2 fusion.32
  25.3 0.2 convolution_add_fusion.7
  25.6 0.2 convolution_add_fusion.6
  25.8 0.2 convolution_add_fusion.5
  26.0 0.2 convolution_add_fusion.4
  26.2 0.2 convolution_add_fusion.3
  26.4 0.2 convolution_add_fusion.2
  26.7 0.2 convolution_add_fusion.1
  26.9 0.3 fusion.11
  27.2 0.3 reshape.159
  27.5 0.6 copy-done.5
  28.2 0.3 reduce_sum.18
  28.6 0.3 maximum_maximum_fusion
  29.1 0.2 convolution_add_fusion.23
  29.4 0.2 convolution_add_fusion.21
  29.6 0.2 convolution_add_fusion.20
  29.8 0.2 convolution_add_fusion.19
  30.5 0.4 copy-done.9
  30.9 0.2 fusion.93
  31.4 0.7 copy-done.6
  32.2 0.3 fusion.17
  33.8 0.4 copy-done.3
  34.2 0.2 multiply_add_fusion
  34.5 0.7 fusion.70
  35.2 0.7 copy.85
  35.9 10.7 %shard_map.114 = (f32[16,256]{1,0:T(8,128)}, f32[256,128]{1,0:T(8,128)}) custom-call(f32[16,10,256]{2,1,0:T(8,128)} %bitcast.258, bf16[128,256]{1,0:T(8,128)(2,1)} %get-tuple-element.20.high_ref, bf16[128,256]{1,0:T(8,128)(2,1)} %get-tuple-element.19.low_ref), custom_call_target="tpu_custom_call" | custom-call | tf_op jit(solution)/shard_map/pallas_call | solution.py:176
  46.6 1.6 %fusion.79.x_ref = bf16[8,32,128]{2,1,0:T(8,128)(2,1)} fusion(f32[8,32,128]{2,1,0:T(8,128)} %bitcast.260, f32[8,32,128]{2,1,0:T(8,128)S(1)} %get-tuple-element.24), kind=kLoop, calls=%fused_computation.151 | loop fusion | flops 622592 | bytes 327680 | tf_op jit(solution)/shard_map/convert_element_type | solution.py:307
  48.2 11.6 %shard_map.115 = bf16[18,64,128]{2,1,0:T(8,128)(2,1)} custom-call(bf16[8,32,128]{2,1,0:T(8,128)(2,1)} %fusion.79.x_ref), custom_call_target="tpu_custom_call" | custom-call | tf_op jit(solution)/shard_map/pallas_call | solution.py:243
  59.9 1.2 %fusion.60 = f32[16,40,128]{2,1,0:T(8,128)S(1)} fusion(bf16[18,64,128]{2,1,0:T(8,128)(2,1)} %shard_map.115, bf16[9,128,128]{2,1,0:T(8,128)(2,1)S(1)} %bitcast.248), kind=kOutput, calls=%fused_computation.132 | convolution fusion | flops 20971520 | bytes 524288 | tf_op jit(solution)/shard_map/ijg,fg->ijf/dot_general | solution.py:81
  61.1 0.2 convolution_add_fusion.15
  61.3 0.2 convolution_add_fusion.14
  61.6 0.2 convolution_add_fusion.13
  61.9 0.2 convolution_add_fusion.12
  62.1 0.2 convolution_add_fusion.11
  62.4 0.2 convolution_add_fusion.10
  62.6 0.2 convolution_add_fusion.9
  62.9 0.2 convolution_add_fusion.8
  63.1 0.2 reduce_sum.19
  63.4 0.3 fusion.3
  63.8 0.2 convolution_add_fusion.47
  64.0 0.2 convolution_add_fusion.46
  64.2 0.2 convolution_add_fusion.45
  64.4 0.2 convolution_add_fusion.44
  64.6 0.2 convolution_add_fusion.43
  64.7 0.2 convolution_add_fusion.42
  64.9 0.2 convolution_add_fusion.41
  65.1 0.2 convolution_add_fusion.40
  65.5 0.2 broadcast_select_fusion
  65.9 0.2 convolution_add_fusion.31
  67.1 0.2 copy-done.7
  67.3 0.6 copy.67
  67.9 4.8 %all-to-all-start.1 = ((f32[1,16,256]{2,0,1:T(1,128)}), f32[1,16,256]{2,0,1:T(1,128)S(1)}, u32[]{:S(2)}, u32[]{:S(2)}) async-start(f32[1,16,256]{2,0,1:T(1,128)} %copy.67), calls=%async_computation.1 | async-start | bytes 32768 | tf_op jit(solution)/shard_map/all_to_all | solution.py:183
  72.7 0.8 %fusion.2 = f32[8,32,128]{2,1,0:T(8,128)} fusion(f32[8,32,128]{2,1,0:T(8,128)S(1)} %bitcast.261, f32[8,32,128]{2,1,0:T(8,128)S(1)} %convolution_add_fusion.25, bf16[10,34,128]{2,1,0:T(8,128)(2,1)S(1)} %broadcast_select_fusion, bf16[9,128,128]{2,1,0:T(8,128)(2,1)S(1)} %bitcast.238), kind=kOutput, calls=%fused_computation.28 | convolution fusion | flops 8454144 | bytes 491520 | tf_op jit(solution)/shard_map/ijg,fg->ijf/dot_general | solution.py:81
  73.5 5.0 %all-to-all-done.1 = f32[1,16,256]{2,0,1:T(1,128)S(1)} async-done(((f32[1,16,256]{2,0,1:T(1,128)}), f32[1,16,256]{2,0,1:T(1,128)S(1)}, u32[]{:S(2)}, u32[]{:S(2)}) %all-to-all-start.1) | async-done | bytes 16416 | tf_op jit(solution)/shard_map/all_to_all | solution.py:183
  78.6 0.6 copy.68
  (59 shorter events, 4.5 us)
Async XLA Ops:
  0.6 3.4 %copy-start.10 = (s32[1,16]{1,0:T(1,128)S(1)}, s32[1,16]{1,0:T(1,128)}, u32[]{:S(2)}) copy-start(s32[1,16]{1,0:T(1,128)} %param.19) | copy-start | bytes 196
  0.6 3.4 %copy-start.8 = (f32[1,16,256]{2,1,0:T(8,128)S(1)}, f32[1,16,256]{2,1,0:T(8,128)}, u32[]{:S(2)}) copy-start(f32[1,16,256]{2,1,0:T(8,128)} %param.18) | copy-start | bytes 49156
  2.3 9.7 %copy-start.4 = (bf16[3,3,3,32,32]{4,3,2,1,0:T(8,128)(2,1)S(1)}, bf16[3,3,3,32,32]{4,3,2,1,0:T(8,128)(2,1)}, u32[]{:S(2)}) copy-start(bf16[3,3,3,32,32]{4,3,2,1,0:T(8,128)(2,1)} %param.11) | copy-start | bytes 165892
  5.0 30.2 %all-to-all-start = ((f32[1,16,10,256]{3,0,2,1:T(1,128)}), f32[1,16,10,256]{3,0,2,1:T(1,128)S(1)}, u32[]{:S(2)}, u32[]{:S(2)}) async-start(f32[1,16,10,256]{3,0,2,1:T(1,128)} %pad_maximum_fusion.8), calls=%async_computation | async-start | bytes 327680 | tf_op jit(solution)/shard_map/all_to_all | solution.py:172
  24.1 1.0 %copy-start = (bf16[22,64,128]{2,1,0:T(8,128)(2,1)S(1)}, bf16[22,64,128]{2,1,0:T(8,128)(2,1)}, u32[]{:S(2)}) copy-start(bf16[22,64,128]{2,1,0:T(8,128)(2,1)} %shard_map.113) | copy-start | bytes 1081348
  27.2 0.9 %copy-start.5 = (bf16[3,3,3,32,64]{4,3,2,1,0:T(8,128)(2,1)S(1)}, bf16[3,3,3,32,64]{4,3,2,1,0:T(8,128)(2,1)}, u32[]{:S(2)}) copy-start(bf16[3,3,3,32,64]{4,3,2,1,0:T(8,128)(2,1)} %param.12) | copy-start | bytes 331780
  30.1 0.7 copy-start.9
  31.2 0.9 %copy-start.6 = (bf16[3,3,3,32,32]{4,3,2,1,0:T(8,128)(2,1)S(1)}, bf16[3,3,3,32,32]{4,3,2,1,0:T(8,128)(2,1)}, u32[]{:S(2)}) copy-start(bf16[3,3,3,32,32]{4,3,2,1,0:T(8,128)(2,1)} %param.13) | copy-start | bytes 165892
  33.3 0.8 %copy-start.3 = (bf16[8,32,128]{2,1,0:T(8,128)(2,1)S(1)}, bf16[8,32,128]{2,1,0:T(8,128)(2,1)}, u32[]{:S(2)}) copy-start(bf16[8,32,128]{2,1,0:T(8,128)(2,1)} %x_ref.1) | copy-start | bytes 196612
  59.9 1.2 %copy-start.1 = (bf16[18,64,128]{2,1,0:T(8,128)(2,1)S(1)}, bf16[18,64,128]{2,1,0:T(8,128)(2,1)}, u32[]{:S(2)}) copy-start(bf16[18,64,128]{2,1,0:T(8,128)(2,1)} %shard_map.115) | copy-start | bytes 884740
  66.6 0.7 copy-start.7
  66.6 6.1 %copy-start.2 = (f32[256,128]{1,0:T(8,128)S(1)}, f32[256,128]{1,0:T(8,128)}, u32[]{:S(2)}) copy-start(f32[256,128]{1,0:T(8,128)} %get-tuple-element.4) | copy-start | bytes 393220
  67.9 10.7 %all-to-all-start.1 = ((f32[1,16,256]{2,0,1:T(1,128)}), f32[1,16,256]{2,0,1:T(1,128)S(1)}, u32[]{:S(2)}, u32[]{:S(2)}) async-start(f32[1,16,256]{2,0,1:T(1,128)} %copy.67), calls=%async_computation.1 | async-start | bytes 32768 | tf_op jit(solution)/shard_map/all_to_all | solution.py:183

commit v6 on v5

--- a/solution.py
+++ b/solution.py
@@ -153,9 +153,7 @@
     lax.fori_loop(0, got_ref.shape[0], body, 0)
 
 
-def observe(output, obs_cells, obs_chan, obs_weights, obs_value, obs_count):
-    rows, cols, feats = output.shape
-    ncell = rows * cols
+def pack(obs_cells, obs_chan, obs_weights, obs_value, obs_count):
     slots = lax.broadcasted_iota(jnp.int32, obs_chan.shape, 2)
     live = (slots < obs_count[:, :, None]).astype(jnp.float32)
     weights = obs_weights * live[..., None]
@@ -169,8 +167,12 @@
         ],
         axis=2,
     )
-    got = lax.all_to_all(packed, "lon", split_axis=1, concat_axis=1, tiled=True)
-    got = got.reshape(got.shape[1:])
+    return packed.reshape(packed.shape[1:])
+
+
+def observe(output, got):
+    rows, cols, feats = output.shape
+    ncell = rows * cols
     owners, nslot = got.shape[0], got.shape[2]
     o_hi, o_lo = split_bf16(output.reshape(ncell, feats).T)
     innov, grad = pl.pallas_call(
@@ -180,34 +182,39 @@
             jax.ShapeDtypeStruct((ncell, feats), jnp.float32),
         ),
     )(got, o_hi, o_lo)
-    innovation = lax.all_to_all(
-        innov.reshape(obs_value.shape), "lon", split_axis=1, concat_axis=1, tiled=True
-    )
-    return grad.reshape(rows, cols, feats), innovation
-
-
-def halo_kernel(width, nlat, nlon, x_ref, o_ref, buf, send_sem, recv_sem):
+    return grad.reshape(rows, cols, feats), innov
+
+
+def halo_kernel(
+    width, nlat, nlon, x_ref, p_ref, o_ref, q_ref, buf, inbox, send_sem, recv_sem, p_send, p_recv
+):
     rows, cols = x_ref.shape[0], x_ref.shape[1]
     edge = (buf.shape[1] - cols) // 2
     i = lax.axis_index("lat")
     j = lax.axis_index("lon")
     has = {-1: i > 0, 0: i >= 0, 1: i < nlat - 1}
+    mesh = pl.DeviceIdType.MESH
     dirs = [(a, b) for a in (-1, 0, 1) for b in (-1, 0, 1) if (a, b) != (0, 0)]
     buf[...] = jnp.zeros(buf.shape, buf.dtype)
     buf[width : width + rows, edge : edge + cols, :] = x_ref[...]
+    inbox[pl.ds(j, 1)] = p_ref[pl.ds(j, 1)]
     barrier = pltpu.get_barrier_semaphore()
-    for a, b in dirs:
-
-        @pl.when(has[a])
+    for a in (-1, 1):
+        for b in (-1, 0, 1):
+
+            @pl.when(has[a])
+            def _():
+                pl.semaphore_signal(
+                    barrier, inc=1, device_id=((i + a) % nlat, (j + b) % nlon), device_id_type=mesh
+                )
+
+    for t in range(nlon):
+
+        @pl.when(t != j)
         def _():
-            pl.semaphore_signal(
-                barrier,
-                inc=1,
-                device_id=((i + a) % nlat, (j + b) % nlon),
-                device_id_type=pl.DeviceIdType.MESH,
-            )
-
-    count = 2 + 3 * has[-1].astype(jnp.int32) + 3 * has[1].astype(jnp.int32)
+            pl.semaphore_signal(barrier, inc=1, device_id=(i, t), device_id_type=mesh)
+
+    count = (nlon - 1) + 3 * has[-1].astype(jnp.int32) + 3 * has[1].astype(jnp.int32)
     pl.semaphore_wait(barrier, count)
     src_rows = {1: pl.ds(rows - width, width), -1: pl.ds(0, width), 0: pl.ds(0, rows)}
     dst_rows = {1: pl.ds(0, width), -1: pl.ds(width + rows, width), 0: pl.ds(width, rows)}
@@ -221,40 +228,71 @@
             send_sem=send_sem.at[k],
             recv_sem=recv_sem.at[k],
             device_id=((i + a) % nlat, (j + b) % nlon),
-            device_id_type=pl.DeviceIdType.MESH,
+            device_id_type=mesh,
         )
         copies.append((a, copy))
         pl.when(has[a])(copy.start)
+    sends = []
+    for t in range(nlon):
+        copy = pltpu.make_async_remote_copy(
+            src_ref=p_ref.at[pl.ds(t, 1)],
+            dst_ref=inbox.at[pl.ds(j, 1)],
+            send_sem=p_send.at[t],
+            recv_sem=p_recv.at[j],
+            device_id=(i, t),
+            device_id_type=mesh,
+        )
+        sends.append(copy)
+        pl.when(t != j)(copy.start)
     for a, copy in copies:
         pl.when(has[a])(copy.wait_send)
         pl.when(has[-a])(copy.wait_recv)
+    for t in range(nlon):
+        arrival = pltpu.make_async_remote_copy(
+            src_ref=p_ref.at[pl.ds(t, 1)],
+            dst_ref=inbox.at[pl.ds(t, 1)],
+            send_sem=p_send.at[t],
+            recv_sem=p_recv.at[t],
+            device_id=(i, t),
+            device_id_type=mesh,
+        )
+        pl.when(t != j)(sends[t].wait_send)
+        pl.when(t != j)(arrival.wait_recv)
     o_ref[...] = buf[...]
+    q_ref[...] = inbox[...]
 
 
 EXCHANGE_IDS = {7: 0, 5: 1}
 
 
-def exchange(block, width):
+def exchange(block, width, payload):
     rows, cols, feats = block.shape
     edge = 16
     nlat = lax.axis_size("lat")
     nlon = lax.axis_size("lon")
     full = (rows + 2 * width, cols + 2 * edge, feats)
-    out = pl.pallas_call(
+    vmem = pl.BlockSpec(memory_space=pltpu.VMEM)
+    out, got = pl.pallas_call(
         functools.partial(halo_kernel, width, nlat, nlon),
-        out_shape=jax.ShapeDtypeStruct(full, block.dtype),
-        in_specs=[pl.BlockSpec(memory_space=pltpu.VMEM)],
-        out_specs=pl.BlockSpec(memory_space=pltpu.VMEM),
+        out_shape=(
+            jax.ShapeDtypeStruct(full, block.dtype),
+            jax.ShapeDtypeStruct(payload.shape, payload.dtype),
+        ),
+        in_specs=[vmem, vmem],
+        out_specs=(vmem, vmem),
         scratch_shapes=[
             pltpu.VMEM(full, block.dtype),
+            pltpu.VMEM(payload.shape, payload.dtype),
             pltpu.SemaphoreType.DMA((8,)),
             pltpu.SemaphoreType.DMA((8,)),
+            pltpu.SemaphoreType.DMA((nlon,)),
+            pltpu.SemaphoreType.DMA((nlon,)),
         ],
         compiler_params=pltpu.CompilerParams(
             collective_id=EXCHANGE_IDS[width], has_side_effects=True
         ),
-    )(block)
-    return out[:, edge - width : edge + cols + width]
+    )(block, payload)
+    return out[:, edge - width : edge + cols + width], got
 
 
 def inside(field, tile_rows, halo):
@@ -287,7 +325,8 @@
     mat_mid = banded(kernel_mid, LEV)
     mat_out = banded(kernel_out, LEV)
     lift_full = block_diagonal(lift, LEV)
-    padded = exchange(state, 7)
+    packed = pack(obs_cells, obs_chan, obs_weights, obs_value, obs_count)
+    padded, got = exchange(state, 7, packed)
     pre_first = conv_valid(padded, mat_in, rows + 12, cols + 12)
     act_first = jax.nn.gelu(pre_first, approximate=True).astype(jnp.bfloat16)
     pooled = (block_sum(act_first.astype(jnp.float32)) * 0.25).astype(jnp.bfloat16)
@@ -301,11 +340,10 @@
     slope_first = gelu_slope(trim(pre_first, 5))
     slope_mid = gelu_slope(pre_mid)
     output = state.astype(jnp.float32) + jax.nn.gelu(pre_last, approximate=True)
-    grad_out, innovation = observe(
-        output, obs_cells, obs_chan, obs_weights, obs_value, obs_count
-    )
+    grad_out, innov = observe(output, got)
     grad_pre_last = (grad_out * gelu_slope(pre_last)).astype(jnp.bfloat16)
-    grads = exchange(grad_pre_last, 5)
+    grads, innovation = exchange(grad_pre_last, 5, innov.reshape(innov.shape[0], 1, innov.shape[1]))
+    innovation = innovation.reshape(obs_value.shape)
     grad_merged = adjoint_valid(grads, mat_out, rows + 8, cols + 8)
     grad_coarse = block_sum(grad_merged).astype(jnp.bfloat16)
     back_mid = jnp.einsum("ijf,gf->ijg", grad_coarse, lift_full, preferred_element_type=jnp.float32)

time: 79.9 us -> 66.8 us (0.84)
  the two profiles are of different devices: /device:TPU:7 before, /device:TPU:6 now
where the time goes in v6:
time: 66.8 us; the launch traced here: 66.2 us
  Pallas kernels  37.9 us (57%)
  matrix products  12.4 us (19%)
  other arithmetic  9.01 us (13%)
  local copies, waits for them, and re-layouts  5.81 us (9%)
  between operations  1.11 us (2%)
    pallas_call x2, Pallas kernels, exchange(): pl.pallas_call(functools.partial(halo_kernel, width, nlat, nlon), out_sha...  27.2 us
    pallas_call x1, Pallas kernels, observe(): pl.pallas_call(observe_kernel, out_shape=(jax.ShapeDtypeStruct((owners, n...  10.7 us
    dot_general x27, matrix products, adjoint_valid(): jnp.einsum('ijg,fg->ijf', piece, matrices[row_off * 3 + col_off], preferr...  6.89 us
    dot_general x27, matrix products, conv_valid(): jnp.einsum('ijf,fg->ijg', piece, matrices[row_off * 3 + col_off], preferr...  4.93 us
    unnamed x20, local copies, waits for them, and re-layouts  3.6 us
    convert_element_type x1, other arithmetic, shards(): grad_pre_last = (grad_out * gelu_slope(pre_last)).astype(jnp.bfloat16)  1.62 us

profile of v6, /device:TPU:6, one launch (start us, length us, event | category | flops | bytes accessed | tf_op | source)
XLA Modules:
  0.0 66.2 jit_solution(18116058966308174219)
XLA Ops:
  0.6 0.8 %convert_element_type.83 = f32[1,16,256]{2,1,0:T(8,128)S(1)} convert(s32[1,16,256]{2,1,0:T(8,128)} %param.16) | non-fusion elementwise | flops 4096 | bytes 32768 | tf_op jit(solution)/shard_map/convert_element_type | solution.py:164
  1.4 0.8 %fusion.134 = (f32[1,16,1,256]{3,2,1,0:T(1,128)S(1)}, f32[1,16,1,256]{3,2,1,0:T(1,128)S(1)}) fusion(f32[1,16,256]{2,1,0:T(8,128)} %param.18, s32[16]{0:T(128)} %bitcast.258, f32[1,16,256]{2,1,0:T(8,128)S(1)} %convert_element_type.83), kind=kLoop, calls=%fused_computation.247 | loop fusion | flops 8192 | bytes 65600 | tf_op jit(solution)/shard_map/broadcast_in_dim | solution.py:166
  2.2 0.7 %fusion.135 = f32[16,256]{1,0:T(8,128)S(1)} fusion(s32[16]{0:T(128)} %bitcast.259), kind=kLoop, calls=%fused_computation.250 | loop fusion | flops 8192 | bytes 16448 | tf_op jit(solution)/shard_map/convert_element_type | solution.py:158
  2.9 0.9 %multiply_bitcast_fusion = f32[1,16,4,256]{3,2,1,0:T(4,128)S(1)} fusion(f32[1,16,256,4]{2,3,1,0:T(4,128)} %param.17, f32[16,256]{1,0:T(8,128)S(1)} %fusion.135), kind=kLoop, calls=%fused_computation.212 | loop fusion | flops 16384 | bytes 147456 | tf_op jit(solution)/shard_map/transpose | solution.py:165
  3.8 0.9 %convert_bitcast_fusion = f32[1,16,4,256]{3,2,1,0:T(4,128)S(1)} fusion(s32[1,16,256,4]{2,3,1,0:T(4,128)} %param.15), kind=kLoop, calls=%fused_computation.213 | loop fusion | flops 16384 | bytes 131072 | tf_op jit(solution)/shard_map/convert_element_type | solution.py:163
  4.7 0.8 %maximum_bitcast_fusion.p_ref = f32[16,10,256]{2,1,0:T(8,128)} fusion(f32[1,16,1,256]{3,2,1,0:T(1,128)S(1)} %get-tuple-element.31, f32[1,16,4,256]{3,2,1,0:T(4,128)S(1)} %multiply_bitcast_fusion, f32[1,16,1,256]{3,2,1,0:T(1,128)S(1)} %get-tuple-element.32, f32[1,16,4,256]{3,2,1,0:T(4,128)S(1)} %convert_bitcast_fusion), kind=kLoop, calls=%fused_computation.86 | loop fusion | flops 122880 | bytes 327680 | tf_op jit(solution)/shard_map/reshape | solution.py:170
  5.4 15.4 %shard_map.113 = (bf16[22,64,128]{2,1,0:T(8,128)(2,1)}, f32[16,10,256]{2,1,0:T(8,128)}) custom-call(bf16[8,32,128]{2,1,0:T(8,128)(2,1)} %x_ref.1, f32[16,10,256]{2,1,0:T(8,128)} %maximum_bitcast_fusion.p_ref), custom_call_target="tpu_custom_call" | custom-call | tf_op jit(solution)/shard_map/pallas_call | solution.py:275
  20.9 0.3 maximum_maximum_fusion
  21.2 0.6 copy-done.5
  21.8 0.3 fusion.13
  22.2 0.6 copy-done
  22.8 0.2 fusion.31
  23.0 0.2 convolution_add_fusion.7
  23.2 0.2 convolution_add_fusion.6
  23.4 0.2 convolution_add_fusion.5
  23.7 0.2 convolution_add_fusion.4
  23.9 0.2 convolution_add_fusion.3
  24.1 0.2 convolution_add_fusion.2
  24.3 0.2 convolution_add_fusion.1
  24.5 0.3 fusion.10
  24.9 0.3 reshape.163
  25.1 0.3 reduce_sum.18
  25.7 0.2 convolution_add_fusion.23
  25.9 0.2 convolution_add_fusion.22
  26.1 0.2 convolution_add_fusion.21
  26.3 0.2 convolution_add_fusion.20
  26.4 0.2 convolution_add_fusion.19
  26.6 0.2 convolution_add_fusion.18
  26.9 0.2 convolution_add_fusion.16
  27.1 0.4 copy-done.8
  27.6 0.2 fusion.92
  28.2 0.6 copy-done.6
  28.8 0.3 fusion.16
  30.3 0.4 copy-done.3
  30.7 0.2 multiply_add_fusion
  31.0 0.7 %fusion.69 = (bf16[128,256]{1,0:T(8,128)(2,1)}, bf16[128,256]{1,0:T(8,128)(2,1)}) fusion(f32[256,128]{0,1:T(8,128)S(1)} %copy.26), kind=kLoop, calls=%fused_computation.140 | loop fusion | flops 131072 | bytes 262144 | tf_op jit(solution)/shard_map/convert_element_type | solution.py:112
  31.7 10.7 %shard_map.114 = (f32[16,256]{1,0:T(8,128)}, f32[256,128]{1,0:T(8,128)}) custom-call(f32[16,10,256]{2,1,0:T(8,128)} %get-tuple-element.8.got_ref, bf16[128,256]{1,0:T(8,128)(2,1)} %get-tuple-element.26.high_ref, bf16[128,256]{1,0:T(8,128)(2,1)} %get-tuple-element.25.low_ref), custom_call_target="tpu_custom_call" | custom-call | tf_op jit(solution)/shard_map/pallas_call | solution.py:178
  42.4 1.6 %fusion.78.x_ref = bf16[8,32,128]{2,1,0:T(8,128)(2,1)} fusion(f32[8,32,128]{2,1,0:T(8,128)} %bitcast.255, f32[8,32,128]{2,1,0:T(8,128)S(1)} %get-tuple-element.30), kind=kLoop, calls=%fused_computation.149 | loop fusion | flops 622592 | bytes 327680 | tf_op jit(solution)/shard_map/convert_element_type | solution.py:344
  44.0 1.3 %reshape.158.p_ref = f32[16,1,256]{2,1,0:T(1,128)} reshape(f32[16,256]{1,0:T(8,128)} %get-tuple-element.11) | data formatting | bytes 32768 | tf_op jit(solution)/shard_map/reshape | solution.py:345
  45.3 11.8 %shard_map.115 = (bf16[18,64,128]{2,1,0:T(8,128)(2,1)}, f32[16,1,256]{2,1,0:T(1,128)}) custom-call(bf16[8,32,128]{2,1,0:T(8,128)(2,1)} %fusion.78.x_ref, f32[16,1,256]{2,1,0:T(1,128)} %reshape.158.p_ref), custom_call_target="tpu_custom_call" | custom-call | tf_op jit(solution)/shard_map/pallas_call | solution.py:275
  57.2 1.2 %fusion.59 = f32[16,40,128]{2,1,0:T(8,128)S(1)} fusion(bf16[18,64,128]{2,1,0:T(8,128)(2,1)} %get-tuple-element.12, bf16[9,128,128]{2,1,0:T(8,128)(2,1)S(1)} %bitcast.244), kind=kOutput, calls=%fused_computation.130 | convolution fusion | flops 20971520 | bytes 524288 | tf_op jit(solution)/shard_map/ijg,fg->ijf/dot_general | solution.py:81
  58.4 0.2 convolution_add_fusion.15
  58.6 0.2 convolution_add_fusion.14
  58.9 0.2 convolution_add_fusion.13
  59.1 0.2 convolution_add_fusion.12
  59.4 0.2 convolution_add_fusion.11
  59.7 0.2 convolution_add_fusion.10
  59.9 0.2 convolution_add_fusion.9
  60.2 0.2 convolution_add_fusion.8
  60.4 0.2 reduce_sum.19
  60.7 0.3 fusion.2
  61.1 0.2 convolution_add_fusion.47
  61.3 0.2 convolution_add_fusion.46
  61.5 0.2 convolution_add_fusion.45
  61.7 0.2 convolution_add_fusion.44
  61.9 0.2 convolution_add_fusion.43
  62.0 0.2 convolution_add_fusion.42
  62.2 0.2 convolution_add_fusion.41
  62.4 0.2 convolution_add_fusion.40
  62.8 0.2 broadcast_select_fusion
  63.2 0.2 convolution_add_fusion.31
  64.4 0.4 copy-done.2
  64.8 0.8 %fusion.1 = f32[8,32,128]{2,1,0:T(8,128)} fusion(f32[8,32,128]{2,1,0:T(8,128)S(1)} %bitcast.256, f32[8,32,128]{2,1,0:T(8,128)S(1)} %convolution_add_fusion.25, bf16[10,34,128]{2,1,0:T(8,128)(2,1)S(1)} %broadcast_select_fusion, bf16[9,128,128]{2,1,0:T(8,128)(2,1)S(1)} %bitcast.234), kind=kOutput, calls=%fused_computation.27 | convolution fusion | flops 8454144 | bytes 491520 | tf_op jit(solution)/shard_map/ijg,fg->ijf/dot_general | solution.py:81
  65.6 0.6 copy.27
  (49 shorter events, 3.7 us)
Async XLA Ops:
  0.6 20.2 %copy-start.4 = (bf16[3,3,3,32,64]{4,3,2,1,0:T(8,128)(2,1)S(1)}, bf16[3,3,3,32,64]{4,3,2,1,0:T(8,128)(2,1)}, u32[]{:S(2)}) copy-start(bf16[3,3,3,32,64]{4,3,2,1,0:T(8,128)(2,1)} %param.12) | copy-start | bytes 331780
  20.9 0.9 %copy-start.5 = (bf16[3,3,3,32,32]{4,3,2,1,0:T(8,128)(2,1)S(1)}, bf16[3,3,3,32,32]{4,3,2,1,0:T(8,128)(2,1)}, u32[]{:S(2)}) copy-start(bf16[3,3,3,32,32]{4,3,2,1,0:T(8,128)(2,1)} %param.11) | copy-start | bytes 165892
  21.8 1.0 %copy-start = (bf16[22,64,128]{2,1,0:T(8,128)(2,1)S(1)}, bf16[22,64,128]{2,1,0:T(8,128)(2,1)}, u32[]{:S(2)}) copy-start(bf16[22,64,128]{2,1,0:T(8,128)(2,1)} %get-tuple-element.9) | copy-start | bytes 1081348
  26.8 0.7 %copy-start.8 = (bf16[64,32]{0,1:T(8,128)(2,1)S(1)}, bf16[64,32]{0,1:T(8,128)(2,1)}, u32[]{:S(2)}) copy-start(bf16[64,32]{0,1:T(8,128)(2,1)} %param.14) | copy-start | bytes 12292
  27.8 0.9 %copy-start.6 = (bf16[3,3,3,32,32]{4,3,2,1,0:T(8,128)(2,1)S(1)}, bf16[3,3,3,32,32]{4,3,2,1,0:T(8,128)(2,1)}, u32[]{:S(2)}) copy-start(bf16[3,3,3,32,32]{4,3,2,1,0:T(8,128)(2,1)} %param.13) | copy-start | bytes 165892
  29.9 0.8 %copy-start.3 = (bf16[8,32,128]{2,1,0:T(8,128)(2,1)S(1)}, bf16[8,32,128]{2,1,0:T(8,128)(2,1)}, u32[]{:S(2)}) copy-start(bf16[8,32,128]{2,1,0:T(8,128)(2,1)} %x_ref.1) | copy-start | bytes 196612
  57.1 1.2 %copy-start.1 = (bf16[18,64,128]{2,1,0:T(8,128)(2,1)S(1)}, bf16[18,64,128]{2,1,0:T(8,128)(2,1)}, u32[]{:S(2)}) copy-start(bf16[18,64,128]{2,1,0:T(8,128)(2,1)} %get-tuple-element.12) | copy-start | bytes 884740
  63.8 0.9 %copy-start.2 = (f32[256,128]{1,0:T(8,128)S(1)}, f32[256,128]{1,0:T(8,128)}, u32[]{:S(2)}) copy-start(f32[256,128]{1,0:T(8,128)} %get-tuple-element.10) | copy-start | bytes 393220
  64.0 1.6 %copy-start.7 = (f32[16,1,256]{2,1,0:T(1,128)S(1)}, f32[16,1,256]{2,1,0:T(1,128)}, u32[]{:S(2)}) copy-start(f32[16,1,256]{2,1,0:T(1,128)} %get-tuple-element.13) | copy-start | bytes 49156

commit v7 on v6

--- a/solution.py
+++ b/solution.py
@@ -60,31 +60,30 @@
 
 
 def conv_valid(padded, matrices, rows, cols):
-    total = jnp.zeros((rows, cols, matrices.shape[2]), jnp.float32)
-    for row_off in range(3):
-        for col_off in range(3):
-            piece = padded[row_off : row_off + rows, col_off : col_off + cols]
-            total = total + jnp.einsum(
-                "ijf,fg->ijg",
-                piece,
-                matrices[row_off * 3 + col_off],
-                preferred_element_type=jnp.float32,
-            )
-    return total
+    taps = matrices.reshape(3, 3, matrices.shape[1], matrices.shape[2])
+    out = lax.conv_general_dilated(
+        padded[None],
+        taps,
+        (1, 1),
+        "VALID",
+        dimension_numbers=("NHWC", "HWIO", "NHWC"),
+        preferred_element_type=jnp.float32,
+    )
+    return out[0]
 
 
 def adjoint_valid(padded, matrices, rows, cols):
-    total = jnp.zeros((rows, cols, matrices.shape[1]), jnp.float32)
-    for row_off in range(3):
-        for col_off in range(3):
-            piece = padded[2 - row_off : 2 - row_off + rows, 2 - col_off : 2 - col_off + cols]
-            total = total + jnp.einsum(
-                "ijg,fg->ijf",
-                piece,
-                matrices[row_off * 3 + col_off],
-                preferred_element_type=jnp.float32,
-            )
-    return total
+    taps = matrices.reshape(3, 3, matrices.shape[1], matrices.shape[2])
+    taps = jnp.swapaxes(taps[::-1, ::-1], 2, 3)
+    out = lax.conv_general_dilated(
+        padded[None],
+        taps,
+        (1, 1),
+        "VALID",
+        dimension_numbers=("NHWC", "HWIO", "NHWC"),
+        preferred_element_type=jnp.float32,
+    )
+    return out[0]
 
 
 def convolve(field, matrices):
@@ -136,7 +135,7 @@
         picked = two[:feats] + two[feats:] + jnp.dot(high, t_lo, preferred_element_type=jnp.float32)
         pick = feat_ids == block[4:5, :]
         innov = jnp.sum(jnp.where(pick, picked, 0.0), axis=0, keepdims=True) - block[9:10, :]
-        innov_ref[pl.ds(owner, 1), :] = innov
+        innov_ref[owner] = innov
         spread = jnp.where(pick, innov, 0.0)
         s_hi = spread.astype(jnp.bfloat16)
         s_lo = (spread - s_hi.astype(jnp.float32)).astype(jnp.bfloat16)
@@ -178,7 +177,7 @@
     innov, grad = pl.pallas_call(
         observe_kernel,
         out_shape=(
-            jax.ShapeDtypeStruct((owners, nslot), jnp.float32),
+            jax.ShapeDtypeStruct((owners, 1, nslot), jnp.float32),
             jax.ShapeDtypeStruct((ncell, feats), jnp.float32),
         ),
     )(got, o_hi, o_lo)
@@ -342,7 +341,7 @@
     output = state.astype(jnp.float32) + jax.nn.gelu(pre_last, approximate=True)
     grad_out, innov = observe(output, got)
     grad_pre_last = (grad_out * gelu_slope(pre_last)).astype(jnp.bfloat16)
-    grads, innovation = exchange(grad_pre_last, 5, innov.reshape(innov.shape[0], 1, innov.shape[1]))
+    grads, innovation = exchange(grad_pre_last, 5, innov)
     innovation = innovation.reshape(obs_value.shape)
     grad_merged = adjoint_valid(grads, mat_out, rows + 8, cols + 8)
     grad_coarse = block_sum(grad_merged).astype(jnp.bfloat16)

time: 66.8 us -> 59.2 us (0.89)
  matrix products: 12.4 us -> 5.02 us
  other arithmetic: 9.01 us -> 6.63 us
  local copies, waits for them, and re-layouts: 5.81 us -> 7.95 us
    dot_general x54 -> x0, matrix products: 11.8 us -> none  [the longest x27 6.89 us: adjoint_valid(): jnp.einsum('ijg,fg->ijf', piece, matrices[row_off * 3 + col_off], preferr...]
    conv_general_dilated x0 -> x6, matrix products: none -> 4.52 us  [the longest x3 3.19 us: conv_valid(): lax.conv_general_dilated(padded[None], taps, (1, 1), 'VALID', dimension_n...]
    broadcast_in_dim x0 -> x5, local copies, waits for them, and re-layouts: none -> 2.11 us  [the longest x4 1.07 us: adjoint_valid(): padded[None]]
    reshape x2 -> x0, local copies, waits for them, and re-layouts: 1.59 us -> none  [the longest x1 1.32 us: shards(): innov.reshape(innov.shape[0], 1, innov.shape[1])]
    squeeze x3, local copies, waits for them, and re-layouts: 0.05 us -> 1.04 us  [banded(): kernel[:, :, p - q + 1]]
    convert_element_type x1, other arithmetic: 0.85 us -> 0.01 us  [pack(): jnp.swapaxes(obs_cells, 2, 3).astype(jnp.float32)]
    transpose x1, other arithmetic: 0.86 us -> 0.02 us  [pack(): jnp.swapaxes(weights, 2, 3)]
    add x0 -> x3, other arithmetic: none -> 0.82 us  [the longest x1 0.69 us: shards(): gradient = grad_out + adjoint_valid(grad_first, mat_in, rows, cols)]
where the time goes in v7:
time: 59.2 us; the launch traced here: 58.7 us
  Pallas kernels  37.9 us (64%)
  local copies, waits for them, and re-layouts  7.95 us (13%)
  other arithmetic  6.63 us (11%)
  matrix products  5.02 us (8%)
  between operations  1.2 us (2%)
    pallas_call x2, Pallas kernels, exchange(): pl.pallas_call(functools.partial(halo_kernel, width, nlat, nlon), out_sha...  27.2 us
    pallas_call x1, Pallas kernels, observe(): pl.pallas_call(observe_kernel, out_shape=(jax.ShapeDtypeStruct((owners, 1...  10.7 us
    unnamed x31, local copies, waits for them, and re-layouts  3.57 us
    conv_general_dilated x3, matrix products, conv_valid(): lax.conv_general_dilated(padded[None], taps, (1, 1), 'VALID', dimension_n...  3.19 us
    convert_element_type x1, other arithmetic, shards(): grad_pre_last = (grad_out * gelu_slope(pre_last)).astype(jnp.bfloat16)  1.62 us
    conv_general_dilated x3, matrix products, adjoint_valid(): lax.conv_general_dilated(padded[None], taps, (1, 1), 'VALID', dimension_n...  1.33 us

profile of v7, /device:TPU:6, one launch (start us, length us, event | category | flops | bytes accessed | tf_op | source)
XLA Modules:
  0.0 58.7 jit_solution(12258566811771176032)
XLA Ops:
  0.6 0.0 copy-start.10
  0.6 0.0 copy-start.6
  0.7 0.0 copy-start.8
  0.7 0.0 copy-start.4
  0.7 1.0 %slice_bitcast_fusion.10 = (bf16[3,3,32,32]{3,2,1,0:T(8,128)(2,1)S(1)}, bf16[3,3,32,32]{3,2,1,0:T(8,128)(2,1)S(1)}, bf16[3,3,32,32]{3,2,1,0:T(8,128)(2,1)S(1)}) fusion(bf16[3,3,3,32,32]{4,3,2,1,0:T(8,128)(2,1)} %param.11), kind=kLoop, calls=%fused_computation.149 | loop fusion | bytes 110592 | tf_op jit(solution)/shard_map/squeeze | solution.py:34
  1.7 0.0 copy-start.5
  1.7 0.3 fusion.19
  2.1 0.0 copy-done.6
  2.1 0.0 copy-done.10
  2.1 0.0 copy-done.8
  2.1 0.1 fusion.112
  2.2 0.1 fusion.113
  2.3 0.0 copy-done.4
  2.3 0.2 copy-done.5
  2.5 0.8 %maximum_bitcast_fusion.p_ref = f32[16,10,256]{2,1,0:T(8,128)} fusion(f32[1,16,1,256]{3,2,1,0:T(1,128)S(1)} %get-tuple-element.33, f32[1,16,4,256]{3,2,1,0:T(4,128)S(1)} %multiply_bitcast_fusion, f32[1,16,1,256]{3,2,1,0:T(1,128)S(1)} %get-tuple-element.34, f32[1,16,4,256]{3,2,1,0:T(4,128)S(1)} %convert_bitcast_fusion), kind=kLoop, calls=%fused_computation.58 | loop fusion | flops 122880 | bytes 327680 | tf_op jit(solution)/shard_map/reshape | solution.py:169
  3.3 15.4 %shard_map.113 = (bf16[22,64,128]{2,1,0:T(8,128)(2,1)}, f32[16,10,256]{2,1,0:T(8,128)}) custom-call(bf16[8,32,128]{2,1,0:T(8,128)(2,1)} %x_ref.1, f32[16,10,256]{2,1,0:T(8,128)} %maximum_bitcast_fusion.p_ref), custom_call_target="tpu_custom_call" | custom-call | tf_op jit(solution)/shard_map/pallas_call | solution.py:274
  18.7 1.0 %slice_bitcast_fusion = bf16[1,22,46,128]{3,2,1,0:T(8,128)(2,1)S(1)} fusion(bf16[22,64,128]{2,1,0:T(8,128)(2,1)} %get-tuple-element.9), kind=kLoop, calls=%fused_computation.57 | loop fusion | bytes 518144 | tf_op jit(solution)/shard_map/broadcast_in_dim | solution.py:65
  19.8 1.8 %fusion.4 = f32[1,20,44,128]{3,0,2,1:T(1,128)S(1)} fusion(bf16[3,3,128,128]{3,2,1,0:T(8,128)(2,1)S(1)} %fusion.19, bf16[1,22,46,128]{3,2,1,0:T(8,128)(2,1)S(1)} %slice_bitcast_fusion), kind=kOutput, calls=%fused_computation.12 | convolution fusion | flops 259522560 | bytes 1004544 | tf_op jit(solution)/shard_map/conv_general_dilated | solution.py:64
  21.6 0.0 copy-start.2
  21.6 0.8 %convert_reduce_fusion = f32[10,22,128]{2,1,0:T(8,128)S(1)} fusion(f32[10,2,22,2,128]{4,3,2,1,0:T(2,128)S(1)} %bitcast.119), kind=kLoop, calls=%fused_computation.24 | loop fusion | flops 1210880 | bytes 563200 | tf_op jit(solution)/shard_map/reduce_sum | solution.py:106
  22.5 0.1 fusion.106
  22.6 0.3 maximum_maximum_fusion
  23.0 0.0 copy-start.9
  23.0 0.7 %fusion.95 = f32[1,8,20,256]{3,0,2,1:T(1,128)S(1)} fusion(bf16[3,3,128,256]{3,2,1,0:T(8,128)(2,1)S(1)} %maximum_maximum_fusion, bf16[1,10,22,128]{3,2,1,0:T(8,128)(2,1)S(1)} %fusion.106), kind=kOutput, calls=%fused_computation.134 | convolution fusion | flops 94371840 | bytes 809984 | tf_op jit(solution)/shard_map/conv_general_dilated | solution.py:64
  23.7 0.1 fusion.74
  23.8 0.1 copy.91
  23.9 0.2 fusion.98
  24.1 0.1 broadcast_in_dim.77
  24.2 0.2 reshape.147
  24.4 0.1 fusion.7
  24.5 0.0 copy-start.3
  24.5 0.1 select_bitcast_fusion.1
  24.6 0.8 %copy-done.3 = bf16[3,3,3,32,32]{4,3,2,1,0:T(8,128)(2,1)S(1)} copy-done((bf16[3,3,3,32,32]{4,3,2,1,0:T(8,128)(2,1)S(1)}, bf16[3,3,3,32,32]{4,3,2,1,0:T(8,128)(2,1)}, u32[]{:S(2)}) %copy-start.3) | copy-done | bytes 55320
  25.4 0.3 fusion.22
  25.8 0.0 copy-start.1
  25.8 0.7 %fusion.52 = f32[1,8,32,128]{3,0,2,1:T(1,128)S(1)} fusion(bf16[3,3,128,128]{3,2,1,0:T(8,128)(2,1)S(1)} %fusion.22, bf16[1,10,34,128]{3,2,1,0:T(8,128)(2,1)S(1)} %select_bitcast_fusion.1), kind=kOutput, calls=%fused_computation.86 | convolution fusion | flops 75497472 | bytes 513024 | tf_op jit(solution)/shard_map/conv_general_dilated | solution.py:64
  26.5 0.1 copy-done.1
  26.6 0.1 multiply_add_fusion
  26.7 0.1 copy.100
  26.8 0.7 %fusion.82 = (bf16[128,256]{1,0:T(8,128)(2,1)}, bf16[128,256]{1,0:T(8,128)(2,1)}) fusion(f32[256,128]{0,1:T(8,128)S(1)} %copy.100), kind=kLoop, calls=%fused_computation.115 | loop fusion | flops 131072 | bytes 262144 | tf_op jit(solution)/shard_map/convert_element_type | solution.py:111
  27.4 10.7 %shard_map.114 = (f32[16,1,256]{2,1,0:T(1,128)}, f32[256,128]{1,0:T(8,128)}) custom-call(f32[16,10,256]{2,1,0:T(8,128)} %get-tuple-element.8.got_ref, bf16[128,256]{1,0:T(8,128)(2,1)} %get-tuple-element.32.high_ref, bf16[128,256]{1,0:T(8,128)(2,1)} %get-tuple-element.31.low_ref), custom_call_target="tpu_custom_call" | custom-call | tf_op jit(solution)/shard_map/pallas_call | solution.py:177
  38.1 1.6 %fusion.91.x_ref = bf16[8,32,128]{2,1,0:T(8,128)(2,1)} fusion(f32[8,32,128]{2,1,0:T(8,128)} %bitcast.127, f32[8,32,128]{2,1,0:T(8,128)S(1)} %bitcast.130), kind=kLoop, calls=%fused_computation.124 | loop fusion | flops 622592 | bytes 327680 | tf_op jit(solution)/shard_map/convert_element_type | solution.py:343
  39.8 11.8 %shard_map.115 = (bf16[18,64,128]{2,1,0:T(8,128)(2,1)}, f32[16,1,256]{2,1,0:T(1,128)}) custom-call(bf16[8,32,128]{2,1,0:T(8,128)(2,1)} %fusion.91.x_ref, f32[16,1,256]{2,1,0:T(1,128)} %get-tuple-element.11.p_ref), custom_call_target="tpu_custom_call" | custom-call | tf_op jit(solution)/shard_map/pallas_call | solution.py:274
  51.6 1.0 %slice_bitcast_fusion.1 = bf16[18,1,42,128]{3,2,0,1:T(8,128)(2,1)S(1)} fusion(bf16[18,64,128]{2,1,0:T(8,128)(2,1)} %get-tuple-element.12), kind=kLoop, calls=%fused_computation.61 | loop fusion | bytes 387072 | tf_op jit(solution)/shard_map/broadcast_in_dim | solution.py:79
  52.6 0.0 copy-start.12
  52.6 0.1 reshape.154
  52.8 0.5 copy-done.12
  53.3 0.6 %convolution_select_fusion = f32[16,8,6,128]{3,1,2,0:T(8,128)S(1)} fusion(bf16[3,3,128,128]{3,2,1,0:T(8,128)(2,1)S(1)} %fusion.22, bf16[18,1,7,2,128]{4,2,3,0,1:T(8,128)(2,1)S(1)} %slice.99, bf16[18,1,8,6,128]{4,2,3,0,1:T(8,128)(2,1)S(1)} %copy.102, pred[8,6]{0,1:T(8,128)(4,1)S(1)} %copy-done.12), kind=kOutput, calls=%fused_computation | convolution fusion | flops 227475456 | bytes 973872 | tf_op jit(solution)/shard_map/conv_general_dilated | solution.py:78
  53.9 0.1 copy.103
  54.1 0.1 copy.154
  54.2 0.2 reduce_sum.19
  54.5 0.0 copy-start.13
  54.5 0.3 fusion.2
  54.9 0.3 copy-done.13
  55.2 0.3 convolution_select_fusion.2
  55.6 0.1 broadcast_in_dim.84
  55.7 0.2 reshape.150
  55.8 0.0 copy-start.11
  55.8 0.2 select_bitcast_fusion
  56.2 0.3 copy-done.11
  56.5 0.4 convolution_select_fusion.1
  57.0 0.5 copy-done
  57.4 0.7 %fusion.92 = f32[8,32,128]{2,1,0:T(8,128)} fusion(f32[8,32,128]{2,1,0:T(8,128)S(1)} %bitcast.128, f32[8,1,32,128]{3,0,2,1:T(8,128)S(1)} %slice.107), kind=kLoop, calls=%fused_computation.128 | loop fusion | flops 32768 | bytes 393216 | tf_op jit(solution)/shard_map/add | solution.py:355
  58.1 0.6 %copy.113 = f32[1,16,256]{2,1,0:T(8,128)} copy(f32[1,16,256]{2,0,1:T(1,128)S(1)} %bitcast.133) | data formatting | bytes 32768
  (36 shorter events, 0.6 us)
Async XLA Ops:
  0.6 1.5 %copy-start.10 = (s32[1,16]{1,0:T(1,128)S(1)}, s32[1,16]{1,0:T(1,128)}, u32[]{:S(2)}) copy-start(s32[1,16]{1,0:T(1,128)} %param.19) | copy-start | bytes 196
  0.6 1.4 %copy-start.6 = (s32[1,16,256]{2,1,0:T(8,128)S(1)}, s32[1,16,256]{2,1,0:T(8,128)}, u32[]{:S(2)}) copy-start(s32[1,16,256]{2,1,0:T(8,128)} %param.16) | copy-start | bytes 49156
  0.7 1.5 %copy-start.8 = (f32[1,16,256]{2,1,0:T(8,128)S(1)}, f32[1,16,256]{2,1,0:T(8,128)}, u32[]{:S(2)}) copy-start(f32[1,16,256]{2,1,0:T(8,128)} %param.18) | copy-start | bytes 49156
  0.7 1.6 %copy-start.4 = (f32[1,16,256,4]{2,3,1,0:T(4,128)S(1)}, f32[1,16,256,4]{2,3,1,0:T(4,128)}, u32[]{:S(2)}) copy-start(f32[1,16,256,4]{2,3,1,0:T(4,128)} %param.17) | copy-start | bytes 196612
  1.7 0.8 %copy-start.5 = (s32[1,16,256,4]{2,3,1,0:T(4,128)S(1)}, s32[1,16,256,4]{2,3,1,0:T(4,128)}, u32[]{:S(2)}) copy-start(s32[1,16,256,4]{2,3,1,0:T(4,128)} %param.15) | copy-start | bytes 196612
  21.6 1.0 %copy-start.2 = (bf16[3,3,3,32,64]{4,3,2,1,0:T(8,128)(2,1)S(1)}, bf16[3,3,3,32,64]{4,3,2,1,0:T(8,128)(2,1)}, u32[]{:S(2)}) copy-start(bf16[3,3,3,32,64]{4,3,2,1,0:T(8,128)(2,1)} %param.12) | copy-start | bytes 331780
  23.0 0.8 %copy-start.9 = (bf16[64,32]{0,1:T(8,128)(2,1)S(1)}, bf16[64,32]{0,1:T(8,128)(2,1)}, u32[]{:S(2)}) copy-start(bf16[64,32]{0,1:T(8,128)(2,1)} %param.14) | copy-start | bytes 12292
  24.5 0.9 %copy-start.3 = (bf16[3,3,3,32,32]{4,3,2,1,0:T(8,128)(2,1)S(1)}, bf16[3,3,3,32,32]{4,3,2,1,0:T(8,128)(2,1)}, u32[]{:S(2)}) copy-start(bf16[3,3,3,32,32]{4,3,2,1,0:T(8,128)(2,1)} %param.13) | copy-start | bytes 165892
  25.8 0.8 %copy-start.1 = (bf16[8,32,128]{2,1,0:T(8,128)(2,1)S(1)}, bf16[8,32,128]{2,1,0:T(8,128)(2,1)}, u32[]{:S(2)}) copy-start(bf16[8,32,128]{2,1,0:T(8,128)(2,1)} %x_ref.1) | copy-start | bytes 196612
  52.6 0.7 %copy-start.12 = (pred[8,6]{0,1:T(8,128)(4,1)S(1)}, pred[8,6]{0,1:T(8,128)(4,1)}, u32[]{:S(2)}) copy-start(pred[8,6]{0,1:T(8,128)(4,1)} %constant.46) | copy-start | bytes 148
  54.5 0.7 %copy-start.13 = (pred[8,3]{0,1:T(4,128)(4,1)S(1)}, pred[8,3]{0,1:T(4,128)(4,1)}, u32[]{:S(2)}) copy-start(pred[8,3]{0,1:T(4,128)(4,1)} %constant.94) | copy-start | bytes 76
  55.8 0.7 %copy-start.11 = (pred[8,5]{0,1:T(8,128)(4,1)S(1)}, pred[8,5]{0,1:T(8,128)(4,1)}, u32[]{:S(2)}) copy-start(pred[8,5]{0,1:T(8,128)(4,1)} %constant.45) | copy-start | bytes 124
  56.5 0.9 %copy-start = (f32[256,128]{1,0:T(8,128)S(1)}, f32[256,128]{1,0:T(8,128)}, u32[]{:S(2)}) copy-start(f32[256,128]{1,0:T(8,128)} %get-tuple-element.10) | copy-start | bytes 393220
  56.9 1.2 %copy-start.7 = (f32[16,1,256]{2,1,0:T(1,128)S(1)}, f32[16,1,256]{2,1,0:T(1,128)}, u32[]{:S(2)}) copy-start(f32[16,1,256]{2,1,0:T(1,128)} %get-tuple-element.13) | copy-start | bytes 49156

commit v8 on v7

--- a/solution.py
+++ b/solution.py
@@ -184,9 +184,31 @@
     return grad.reshape(rows, cols, feats), innov
 
 
-def halo_kernel(
-    width, nlat, nlon, x_ref, p_ref, o_ref, q_ref, buf, inbox, send_sem, recv_sem, p_send, p_recv
-):
+def greet(nlat, nlon):
+    i = lax.axis_index("lat")
+    j = lax.axis_index("lon")
+    has = {-1: i > 0, 0: i >= 0, 1: i < nlat - 1}
+    mesh = pl.DeviceIdType.MESH
+    barrier = pltpu.get_barrier_semaphore()
+    for a in (-1, 1):
+        for b in (-1, 0, 1):
+
+            @pl.when(has[a])
+            def _():
+                pl.semaphore_signal(
+                    barrier, inc=1, device_id=((i + a) % nlat, (j + b) % nlon), device_id_type=mesh
+                )
+
+    for t in range(nlon):
+
+        @pl.when(t != j)
+        def _():
+            pl.semaphore_signal(barrier, inc=1, device_id=(i, t), device_id_type=mesh)
+
+    return (nlon - 1) + 3 * has[-1].astype(jnp.int32) + 3 * has[1].astype(jnp.int32)
+
+
+def trade(width, nlat, nlon, count, x_ref, p_ref, buf, inbox, send_sem, recv_sem, p_send, p_recv):
     rows, cols = x_ref.shape[0], x_ref.shape[1]
     edge = (buf.shape[1] - cols) // 2
     i = lax.axis_index("lat")
@@ -194,27 +216,7 @@
     has = {-1: i > 0, 0: i >= 0, 1: i < nlat - 1}
     mesh = pl.DeviceIdType.MESH
     dirs = [(a, b) for a in (-1, 0, 1) for b in (-1, 0, 1) if (a, b) != (0, 0)]
-    buf[...] = jnp.zeros(buf.shape, buf.dtype)
-    buf[width : width + rows, edge : edge + cols, :] = x_ref[...]
-    inbox[pl.ds(j, 1)] = p_ref[pl.ds(j, 1)]
-    barrier = pltpu.get_barrier_semaphore()
-    for a in (-1, 1):
-        for b in (-1, 0, 1):
-
-            @pl.when(has[a])
-            def _():
-                pl.semaphore_signal(
-                    barrier, inc=1, device_id=((i + a) % nlat, (j + b) % nlon), device_id_type=mesh
-                )
-
-    for t in range(nlon):
-
-        @pl.when(t != j)
-        def _():
-            pl.semaphore_signal(barrier, inc=1, device_id=(i, t), device_id_type=mesh)
-
-    count = (nlon - 1) + 3 * has[-1].astype(jnp.int32) + 3 * has[1].astype(jnp.int32)
-    pl.semaphore_wait(barrier, count)
+    pl.semaphore_wait(pltpu.get_barrier_semaphore(), count)
     src_rows = {1: pl.ds(rows - width, width), -1: pl.ds(0, width), 0: pl.ds(0, rows)}
     dst_rows = {1: pl.ds(0, width), -1: pl.ds(width + rows, width), 0: pl.ds(width, rows)}
     src_cols = {1: pl.ds(cols - edge, edge), -1: pl.ds(0, edge), 0: pl.ds(0, cols)}
@@ -257,11 +259,47 @@
         )
         pl.when(t != j)(sends[t].wait_send)
         pl.when(t != j)(arrival.wait_recv)
+
+
+def halo_kernel(width, nlat, nlon, x_ref, p_ref, o_ref, q_ref, buf, inbox, *sems):
+    rows, cols = x_ref.shape[0], x_ref.shape[1]
+    edge = (buf.shape[1] - cols) // 2
+    j = lax.axis_index("lon")
+    buf[...] = jnp.zeros(buf.shape, buf.dtype)
+    buf[width : width + rows, edge : edge + cols, :] = x_ref[...]
+    inbox[pl.ds(j, 1)] = p_ref[pl.ds(j, 1)]
+    count = greet(nlat, nlon)
+    trade(width, nlat, nlon, count, x_ref, p_ref, buf, inbox, *sems)
     o_ref[...] = buf[...]
     q_ref[...] = inbox[...]
 
 
-EXCHANGE_IDS = {7: 0, 5: 1}
+def back_kernel(
+    width, nlat, nlon, got_ref, high_ref, low_ref, slope_ref,
+    grad_ref, o_ref, q_ref, buf, inbox, innov_ref, x_src, *sems
+):
+    rows, cols = x_src.shape[0], x_src.shape[1]
+    edge = (buf.shape[1] - cols) // 2
+    j = lax.axis_index("lon")
+    buf[...] = jnp.zeros(buf.shape, buf.dtype)
+    count = greet(nlat, nlon)
+    observe_kernel(got_ref, high_ref, low_ref, innov_ref, grad_ref)
+    grads = (grad_ref[...] * slope_ref[...]).astype(x_src.dtype).reshape(x_src.shape)
+    x_src[...] = grads
+    trade(width, nlat, nlon, count, x_src, innov_ref, buf, inbox, *sems)
+    buf[width : width + rows, edge : edge + cols, :] = x_src[...]
+    inbox[pl.ds(j, 1)] = innov_ref[pl.ds(j, 1)]
+    o_ref[...] = buf[...]
+    q_ref[...] = inbox[...]
+
+
+def sem_scratch(nlon):
+    return [
+        pltpu.SemaphoreType.DMA((8,)),
+        pltpu.SemaphoreType.DMA((8,)),
+        pltpu.SemaphoreType.DMA((nlon,)),
+        pltpu.SemaphoreType.DMA((nlon,)),
+    ]
 
 
 def exchange(block, width, payload):
@@ -282,16 +320,44 @@
         scratch_shapes=[
             pltpu.VMEM(full, block.dtype),
             pltpu.VMEM(payload.shape, payload.dtype),
-            pltpu.SemaphoreType.DMA((8,)),
-            pltpu.SemaphoreType.DMA((8,)),
-            pltpu.SemaphoreType.DMA((nlon,)),
-            pltpu.SemaphoreType.DMA((nlon,)),
-        ],
-        compiler_params=pltpu.CompilerParams(
-            collective_id=EXCHANGE_IDS[width], has_side_effects=True
-        ),
+        ]
+        + sem_scratch(nlon),
+        compiler_params=pltpu.CompilerParams(collective_id=0, has_side_effects=True),
     )(block, payload)
     return out[:, edge - width : edge + cols + width], got
+
+
+def observe_and_exchange(output, got, slope, width):
+    rows, cols, feats = output.shape
+    ncell = rows * cols
+    edge = 16
+    nlat = lax.axis_size("lat")
+    nlon = lax.axis_size("lon")
+    owners, nslot = got.shape[0], got.shape[2]
+    o_hi, o_lo = split_bf16(output.reshape(ncell, feats).T)
+    full = (rows + 2 * width, cols + 2 * edge, feats)
+    vmem = pl.BlockSpec(memory_space=pltpu.VMEM)
+    innov_shape = (owners, 1, nslot)
+    grad, out, innovation = pl.pallas_call(
+        functools.partial(back_kernel, width, nlat, nlon),
+        out_shape=(
+            jax.ShapeDtypeStruct((ncell, feats), jnp.float32),
+            jax.ShapeDtypeStruct(full, jnp.bfloat16),
+            jax.ShapeDtypeStruct(innov_shape, jnp.float32),
+        ),
+        in_specs=[vmem] * 4,
+        out_specs=(vmem, vmem, vmem),
+        scratch_shapes=[
+            pltpu.VMEM(full, jnp.bfloat16),
+            pltpu.VMEM(innov_shape, jnp.float32),
+            pltpu.VMEM(innov_shape, jnp.float32),
+            pltpu.VMEM((rows, cols, feats), jnp.bfloat16),
+        ]
+        + sem_scratch(nlon),
+        compiler_params=pltpu.CompilerParams(collective_id=1, has_side_effects=True),
+    )(got, o_hi, o_lo, slope.reshape(ncell, feats))
+    grads = out[:, edge - width : edge + cols + width]
+    return grad.reshape(rows, cols, feats), grads, innovation
 
 
 def inside(field, tile_rows, halo):
@@ -339,9 +405,7 @@
     slope_first = gelu_slope(trim(pre_first, 5))
     slope_mid = gelu_slope(pre_mid)
     output = state.astype(jnp.float32) + jax.nn.gelu(pre_last, approximate=True)
-    grad_out, innov = observe(output, got)
-    grad_pre_last = (grad_out * gelu_slope(pre_last)).astype(jnp.bfloat16)
-    grads, innovation = exchange(grad_pre_last, 5, innov)
+    grad_out, grads, innovation = observe_and_exchange(output, got, gelu_slope(pre_last), 5)
     innovation = innovation.reshape(obs_value.shape)
     grad_merged = adjoint_valid(grads, mat_out, rows + 8, cols + 8)
     grad_coarse = block_sum(grad_merged).astype(jnp.bfloat16)

time: 59.2 us -> 55.4 us (0.936)
  the two profiles are of different devices: /device:TPU:6 before, /device:TPU:1 now
where the time goes in v8:
time: 55.4 us; the launch traced here: 54.9 us
  Pallas kernels  34.9 us (63%)
  local copies, waits for them, and re-layouts  8.65 us (16%)
  other arithmetic  5.16 us (9%)
  matrix products  5.02 us (9%)
  between operations  1.19 us (2%)
    pallas_call x1, Pallas kernels, observe_and_exchange(): pl.pallas_call(functools.partial(back_kernel, width, nlat, nlon), out_sha...  20.8 us
    pallas_call x1, Pallas kernels, exchange(): pl.pallas_call(functools.partial(halo_kernel, width, nlat, nlon), out_sha...  14.1 us
    unnamed x32, local copies, waits for them, and re-layouts  4.27 us
    conv_general_dilated x3, matrix products, conv_valid(): lax.conv_general_dilated(padded[None], taps, (1, 1), 'VALID', dimension_n...  3.19 us
    conv_general_dilated x3, matrix products, adjoint_valid(): lax.conv_general_dilated(padded[None], taps, (1, 1), 'VALID', dimension_n...  1.33 us

profile of v8, /device:TPU:1, one launch (start us, length us, event | category | flops | bytes accessed | tf_op | source)
XLA Modules:
  0.0 54.9 jit_solution(17639063886353132127)
XLA Ops:
  0.6 0.0 copy-start.10
  0.6 0.0 copy-start.6
  0.7 0.0 copy-start.8
  0.7 0.0 copy-start.4
  0.7 1.0 %slice_bitcast_fusion.11 = (bf16[3,3,32,32]{3,2,1,0:T(8,128)(2,1)S(1)}, bf16[3,3,32,32]{3,2,1,0:T(8,128)(2,1)S(1)}, bf16[3,3,32,32]{3,2,1,0:T(8,128)(2,1)S(1)}) fusion(bf16[3,3,3,32,32]{4,3,2,1,0:T(8,128)(2,1)} %param.11), kind=kLoop, calls=%fused_computation.154 | loop fusion | bytes 110592 | tf_op jit(solution)/shard_map/squeeze | solution.py:34
  1.7 0.0 copy-start.5
  1.7 0.3 fusion.19
  2.1 0.0 copy-done.6
  2.1 0.0 copy-done.10
  2.1 0.0 copy-done.8
  2.1 0.1 fusion.118
  2.2 0.1 fusion.119
  2.3 0.2 copy-done.5
  2.5 0.8 %maximum_bitcast_fusion.p_ref = f32[16,10,256]{2,1,0:T(8,128)} fusion(f32[1,16,1,256]{3,2,1,0:T(1,128)S(1)} %get-tuple-element.31, f32[1,16,4,256]{3,2,1,0:T(4,128)S(1)} %multiply_bitcast_fusion, f32[1,16,1,256]{3,2,1,0:T(1,128)S(1)} %get-tuple-element.32, f32[1,16,4,256]{3,2,1,0:T(4,128)S(1)} %convert_bitcast_fusion), kind=kLoop, calls=%fused_computation.58 | loop fusion | flops 122880 | bytes 327680 | tf_op jit(solution)/shard_map/reshape | solution.py:169
  3.3 14.1 %shard_map.113 = (bf16[22,64,128]{2,1,0:T(8,128)(2,1)}, f32[16,10,256]{2,1,0:T(8,128)}) custom-call(bf16[8,32,128]{2,1,0:T(8,128)(2,1)} %x_ref.1, f32[16,10,256]{2,1,0:T(8,128)} %maximum_bitcast_fusion.p_ref), custom_call_target="tpu_custom_call" | custom-call | tf_op jit(solution)/shard_map/pallas_call | solution.py:312
  17.4 1.0 %slice_bitcast_fusion = bf16[1,22,46,128]{3,2,1,0:T(8,128)(2,1)S(1)} fusion(bf16[22,64,128]{2,1,0:T(8,128)(2,1)} %get-tuple-element.8), kind=kLoop, calls=%fused_computation.57 | loop fusion | bytes 518144 | tf_op jit(solution)/shard_map/broadcast_in_dim | solution.py:65
  18.5 1.8 %fusion.4 = f32[1,20,44,128]{3,0,2,1:T(1,128)S(1)} fusion(bf16[3,3,128,128]{3,2,1,0:T(8,128)(2,1)S(1)} %fusion.19, bf16[1,22,46,128]{3,2,1,0:T(8,128)(2,1)S(1)} %slice_bitcast_fusion), kind=kOutput, calls=%fused_computation.12 | convolution fusion | flops 259522560 | bytes 1004544 | tf_op jit(solution)/shard_map/conv_general_dilated | solution.py:64
  20.3 0.0 copy-start.1
  20.3 0.8 %convert_reduce_fusion = f32[10,22,128]{2,1,0:T(8,128)S(1)} fusion(f32[10,2,22,2,128]{4,3,2,1,0:T(2,128)S(1)} %bitcast.120), kind=kLoop, calls=%fused_computation.24 | loop fusion | flops 1210880 | bytes 563200 | tf_op jit(solution)/shard_map/reduce_sum | solution.py:106
  21.2 0.1 fusion.112
  21.3 0.3 maximum_maximum_fusion
  21.6 0.0 copy-start.9
  21.6 0.7 %fusion.101 = f32[1,8,20,256]{3,0,2,1:T(1,128)S(1)} fusion(bf16[3,3,128,256]{3,2,1,0:T(8,128)(2,1)S(1)} %maximum_maximum_fusion, bf16[1,10,22,128]{3,2,1,0:T(8,128)(2,1)S(1)} %fusion.112), kind=kOutput, calls=%fused_computation.139 | convolution fusion | flops 94371840 | bytes 809984 | tf_op jit(solution)/shard_map/conv_general_dilated | solution.py:64
  22.4 0.1 fusion.74
  22.5 0.1 copy.91
  22.6 0.2 fusion.104
  22.8 0.1 broadcast_in_dim.77
  22.9 0.2 reshape.149
  23.1 0.1 fusion.7
  23.2 0.0 copy-start.2
  23.2 0.1 select_bitcast_fusion.1
  23.3 0.8 %copy-done.2 = bf16[3,3,3,32,32]{4,3,2,1,0:T(8,128)(2,1)S(1)} copy-done((bf16[3,3,3,32,32]{4,3,2,1,0:T(8,128)(2,1)S(1)}, bf16[3,3,3,32,32]{4,3,2,1,0:T(8,128)(2,1)}, u32[]{:S(2)}) %copy-start.2) | copy-done | bytes 55320
  24.1 0.3 fusion.22
  24.5 0.0 copy-start
  24.5 0.7 %fusion.52 = f32[1,8,32,128]{3,0,2,1:T(1,128)S(1)} fusion(bf16[3,3,128,128]{3,2,1,0:T(8,128)(2,1)S(1)} %fusion.22, bf16[1,10,34,128]{3,2,1,0:T(8,128)(2,1)S(1)} %select_bitcast_fusion.1), kind=kOutput, calls=%fused_computation.87 | convolution fusion | flops 75497472 | bytes 513024 | tf_op jit(solution)/shard_map/conv_general_dilated | solution.py:64
  25.1 0.1 copy-done
  25.3 0.1 fusion.90
  25.3 0.1 copy.100
  25.5 0.7 %fusion.82 = (bf16[128,256]{1,0:T(8,128)(2,1)}, bf16[128,256]{1,0:T(8,128)(2,1)}) fusion(f32[256,128]{0,1:T(8,128)S(1)} %copy.100), kind=kLoop, calls=%fused_computation.116 | loop fusion | flops 131072 | bytes 262144 | tf_op jit(solution)/shard_map/convert_element_type | solution.py:111
  26.1 0.7 %fusion.97.slope_ref = f32[256,128]{1,0:T(8,128)} fusion(f32[256,128]{1,0:T(8,128)S(1)} %bitcast.129), kind=kLoop, calls=%fused_computation.131 | loop fusion | flops 557056 | bytes 262144 | tf_op jit(solution)/shard_map/add | solution.py:52
  26.9 20.8 %shard_map.114 = (f32[256,128]{1,0:T(8,128)}, bf16[18,64,128]{2,1,0:T(8,128)(2,1)}, f32[16,1,256]{2,1,0:T(1,128)}) custom-call(f32[16,10,256]{2,1,0:T(8,128)} %get-tuple-element.7.got_ref, bf16[128,256]{1,0:T(8,128)(2,1)} %get-tuple-element.30.high_ref, bf16[128,256]{1,0:T(8,128)(2,1)} %get-tuple-element.29.low_ref, f32[256,128]{1,0:T(8,128)} %fusion.97.slope_ref), custom_call_target="tpu_custom_call" | custom-call | tf_op jit(solution)/shard_map/pallas_call | solution.py:341
  47.7 1.0 %slice_bitcast_fusion.1 = bf16[18,1,42,128]{3,2,0,1:T(8,128)(2,1)S(1)} fusion(bf16[18,64,128]{2,1,0:T(8,128)(2,1)} %get-tuple-element.10), kind=kLoop, calls=%fused_computation.61 | loop fusion | bytes 387072 | tf_op jit(solution)/shard_map/broadcast_in_dim | solution.py:79
  48.7 0.0 copy-start.12
  48.7 0.1 reshape.156
  48.9 0.5 copy-done.12
  49.4 0.6 %convolution_select_fusion = f32[16,8,6,128]{3,1,2,0:T(8,128)S(1)} fusion(bf16[3,3,128,128]{3,2,1,0:T(8,128)(2,1)S(1)} %fusion.22, bf16[18,1,7,2,128]{4,2,3,0,1:T(8,128)(2,1)S(1)} %slice.99, bf16[18,1,8,6,128]{4,2,3,0,1:T(8,128)(2,1)S(1)} %copy.102, pred[8,6]{0,1:T(8,128)(4,1)S(1)} %copy-done.12), kind=kOutput, calls=%fused_computation | convolution fusion | flops 227475456 | bytes 973872 | tf_op jit(solution)/shard_map/conv_general_dilated | solution.py:78
  50.0 0.1 copy.103
  50.2 0.1 copy.152
  50.3 0.2 reduce_sum.19
  50.6 0.0 copy-start.13
  50.6 0.3 fusion.2
  51.0 0.3 copy-done.13
  51.3 0.3 convolution_select_fusion.2
  51.7 0.1 broadcast_in_dim.84
  51.8 0.2 reshape.152
  51.9 0.0 copy-start.11
  51.9 0.2 select_bitcast_fusion
  52.3 0.3 copy-done.11
  52.6 0.4 convolution_select_fusion.1
  53.0 0.0 copy-start.7
  53.0 0.5 copy-done.3
  53.5 0.1 fusion.98
  53.6 0.7 %copy.113 = f32[8,32,128]{2,1,0:T(8,128)} copy(f32[8,32,128]{2,0,1:T(8,128)S(1)} %fusion.98) | data formatting | bytes 262144
  54.3 0.6 %copy.114 = f32[1,16,256]{2,1,0:T(8,128)} copy(f32[1,16,256]{2,0,1:T(1,128)S(1)} %bitcast.133) | data formatting | bytes 32768
  (35 shorter events, 0.6 us)
Async XLA Ops:
  0.6 1.5 %copy-start.10 = (s32[1,16]{1,0:T(1,128)S(1)}, s32[1,16]{1,0:T(1,128)}, u32[]{:S(2)}) copy-start(s32[1,16]{1,0:T(1,128)} %param.19) | copy-start | bytes 196
  0.6 1.4 %copy-start.6 = (s32[1,16,256]{2,1,0:T(8,128)S(1)}, s32[1,16,256]{2,1,0:T(8,128)}, u32[]{:S(2)}) copy-start(s32[1,16,256]{2,1,0:T(8,128)} %param.16) | copy-start | bytes 49156
  0.7 1.5 %copy-start.8 = (f32[1,16,256]{2,1,0:T(8,128)S(1)}, f32[1,16,256]{2,1,0:T(8,128)}, u32[]{:S(2)}) copy-start(f32[1,16,256]{2,1,0:T(8,128)} %param.18) | copy-start | bytes 49156
  0.7 1.6 %copy-start.4 = (f32[1,16,256,4]{2,3,1,0:T(4,128)S(1)}, f32[1,16,256,4]{2,3,1,0:T(4,128)}, u32[]{:S(2)}) copy-start(f32[1,16,256,4]{2,3,1,0:T(4,128)} %param.17) | copy-start | bytes 196612
  1.7 0.8 %copy-start.5 = (s32[1,16,256,4]{2,3,1,0:T(4,128)S(1)}, s32[1,16,256,4]{2,3,1,0:T(4,128)}, u32[]{:S(2)}) copy-start(s32[1,16,256,4]{2,3,1,0:T(4,128)} %param.15) | copy-start | bytes 196612
  20.3 1.0 %copy-start.1 = (bf16[3,3,3,32,64]{4,3,2,1,0:T(8,128)(2,1)S(1)}, bf16[3,3,3,32,64]{4,3,2,1,0:T(8,128)(2,1)}, u32[]{:S(2)}) copy-start(bf16[3,3,3,32,64]{4,3,2,1,0:T(8,128)(2,1)} %param.12) | copy-start | bytes 331780
  21.6 0.8 %copy-start.9 = (bf16[64,32]{0,1:T(8,128)(2,1)S(1)}, bf16[64,32]{0,1:T(8,128)(2,1)}, u32[]{:S(2)}) copy-start(bf16[64,32]{0,1:T(8,128)(2,1)} %param.14) | copy-start | bytes 12292
  23.2 0.9 %copy-start.2 = (bf16[3,3,3,32,32]{4,3,2,1,0:T(8,128)(2,1)S(1)}, bf16[3,3,3,32,32]{4,3,2,1,0:T(8,128)(2,1)}, u32[]{:S(2)}) copy-start(bf16[3,3,3,32,32]{4,3,2,1,0:T(8,128)(2,1)} %param.13) | copy-start | bytes 165892
  24.5 0.8 %copy-start = (bf16[8,32,128]{2,1,0:T(8,128)(2,1)S(1)}, bf16[8,32,128]{2,1,0:T(8,128)(2,1)}, u32[]{:S(2)}) copy-start(bf16[8,32,128]{2,1,0:T(8,128)(2,1)} %x_ref.1) | copy-start | bytes 196612
  48.7 0.7 %copy-start.12 = (pred[8,6]{0,1:T(8,128)(4,1)S(1)}, pred[8,6]{0,1:T(8,128)(4,1)}, u32[]{:S(2)}) copy-start(pred[8,6]{0,1:T(8,128)(4,1)} %constant.46) | copy-start | bytes 148
  50.6 0.7 %copy-start.13 = (pred[8,3]{0,1:T(4,128)(4,1)S(1)}, pred[8,3]{0,1:T(4,128)(4,1)}, u32[]{:S(2)}) copy-start(pred[8,3]{0,1:T(4,128)(4,1)} %constant.94) | copy-start | bytes 76
  51.9 0.7 %copy-start.11 = (pred[8,5]{0,1:T(8,128)(4,1)S(1)}, pred[8,5]{0,1:T(8,128)(4,1)}, u32[]{:S(2)}) copy-start(pred[8,5]{0,1:T(8,128)(4,1)} %constant.45) | copy-start | bytes 124
  52.6 0.9 %copy-start.3 = (f32[256,128]{1,0:T(8,128)S(1)}, f32[256,128]{1,0:T(8,128)}, u32[]{:S(2)}) copy-start(f32[256,128]{1,0:T(8,128)} %get-tuple-element.9) | copy-start | bytes 393220
  53.0 1.3 %copy-start.7 = (f32[16,1,256]{2,1,0:T(1,128)S(1)}, f32[16,1,256]{2,1,0:T(1,128)}, u32[]{:S(2)}) copy-start(f32[16,1,256]{2,1,0:T(1,128)} %get-tuple-element.11) | copy-start | bytes 49156

commit v9 on v8

--- a/solution.py
+++ b/solution.py
@@ -261,7 +261,25 @@
         pl.when(t != j)(arrival.wait_recv)
 
 
-def halo_kernel(width, nlat, nlon, x_ref, p_ref, o_ref, q_ref, buf, inbox, *sems):
+def band_into(k_ref, t_ref):
+    levels = t_ref.shape[2] // k_ref.shape[3]
+    cin, cout = k_ref.shape[3], k_ref.shape[4]
+    t_ref[...] = jnp.zeros(t_ref.shape, t_ref.dtype)
+    for a in range(3):
+        for b in range(3):
+            for p in range(levels):
+                for q in range(levels):
+                    tap = p - q + 1
+                    if 0 <= tap < 3:
+                        t_ref[a, b, p * cin : (p + 1) * cin, q * cout : (q + 1) * cout] = k_ref[
+                            a, b, tap
+                        ]
+
+
+def halo_kernel(
+    width, nlat, nlon, x_ref, p_ref, kin_ref, kmid_ref, kout_ref,
+    o_ref, q_ref, tin_ref, tmid_ref, tout_ref, buf, inbox, *sems
+):
     rows, cols = x_ref.shape[0], x_ref.shape[1]
     edge = (buf.shape[1] - cols) // 2
     j = lax.axis_index("lon")
@@ -269,6 +287,9 @@
     buf[width : width + rows, edge : edge + cols, :] = x_ref[...]
     inbox[pl.ds(j, 1)] = p_ref[pl.ds(j, 1)]
     count = greet(nlat, nlon)
+    band_into(kin_ref, tin_ref)
+    band_into(kmid_ref, tmid_ref)
+    band_into(kout_ref, tout_ref)
     trade(width, nlat, nlon, count, x_ref, p_ref, buf, inbox, *sems)
     o_ref[...] = buf[...]
     q_ref[...] = inbox[...]
@@ -302,29 +323,33 @@
     ]
 
 
-def exchange(block, width, payload):
+def exchange(block, width, payload, kernels):
     rows, cols, feats = block.shape
     edge = 16
     nlat = lax.axis_size("lat")
     nlon = lax.axis_size("lon")
     full = (rows + 2 * width, cols + 2 * edge, feats)
     vmem = pl.BlockSpec(memory_space=pltpu.VMEM)
-    out, got = pl.pallas_call(
+    taps = [
+        jax.ShapeDtypeStruct((3, 3, LEV * k.shape[3], LEV * k.shape[4]), k.dtype) for k in kernels
+    ]
+    out, got, *mats = pl.pallas_call(
         functools.partial(halo_kernel, width, nlat, nlon),
         out_shape=(
             jax.ShapeDtypeStruct(full, block.dtype),
             jax.ShapeDtypeStruct(payload.shape, payload.dtype),
+            *taps,
         ),
-        in_specs=[vmem, vmem],
-        out_specs=(vmem, vmem),
+        in_specs=[vmem] * 5,
+        out_specs=(vmem,) * 5,
         scratch_shapes=[
             pltpu.VMEM(full, block.dtype),
             pltpu.VMEM(payload.shape, payload.dtype),
         ]
         + sem_scratch(nlon),
         compiler_params=pltpu.CompilerParams(collective_id=0, has_side_effects=True),
-    )(block, payload)
-    return out[:, edge - width : edge + cols + width], got
+    )(block, payload, *kernels)
+    return out[:, edge - width : edge + cols + width], got, mats
 
 
 def observe_and_exchange(output, got, slope, width):
@@ -386,12 +411,10 @@
 ):
     rows, cols = (state.shape[0], state.shape[1])
     crows = rows // 2
-    mat_in = banded(kernel_in, LEV)
-    mat_mid = banded(kernel_mid, LEV)
-    mat_out = banded(kernel_out, LEV)
     lift_full = block_diagonal(lift, LEV)
     packed = pack(obs_cells, obs_chan, obs_weights, obs_value, obs_count)
-    padded, got = exchange(state, 7, packed)
+    padded, got, mats = exchange(state, 7, packed, (kernel_in, kernel_mid, kernel_out))
+    mat_in, mat_mid, mat_out = [m.reshape(9, m.shape[2], m.shape[3]) for m in mats]
     pre_first = conv_valid(padded, mat_in, rows + 12, cols + 12)
     act_first = jax.nn.gelu(pre_first, approximate=True).astype(jnp.bfloat16)
     pooled = (block_sum(act_first.astype(jnp.float32)) * 0.25).astype(jnp.bfloat16)

time: 55.4 us -> 57.9 us (1.045)
  local copies, waits for them, and re-layouts: 8.65 us -> 11.5 us
  other arithmetic: 5.16 us -> 4.2 us
  Pallas kernels: 34.9 us -> 35.5 us
    unnamed x32, local copies, waits for them, and re-layouts: 4.27 us -> 8.17 us
    squeeze x3 -> x0, local copies, waits for them, and re-layouts: 1.04 us -> none  [banded(): kernel[:, :, p - q + 1]]
    concatenate x3 -> x0, other arithmetic: 0.99 us -> none  [banded(): full = jnp.concatenate(rows, axis=-2)]
    pallas_call x1, Pallas kernels: 14.1 us -> 14.7 us  [exchange(): pl.pallas_call(functools.partial(halo_kernel, width, nlat, nlon), out_sha...]
where the time goes in v9:
time: 57.9 us; the launch traced here: 57.3 us
  Pallas kernels  35.5 us (61%)
  local copies, waits for them, and re-layouts  11.5 us (20%)
  matrix products  5 us (9%)
  other arithmetic  4.2 us (7%)
  between operations  1.1 us (2%)
    pallas_call x1, Pallas kernels, observe_and_exchange(): pl.pallas_call(functools.partial(back_kernel, width, nlat, nlon), out_sha...  20.8 us
    pallas_call x1, Pallas kernels, exchange(): pl.pallas_call(functools.partial(halo_kernel, width, nlat, nlon), out_sha...  14.7 us
    unnamed x32, local copies, waits for them, and re-layouts  8.17 us
    conv_general_dilated x3, matrix products, conv_valid(): lax.conv_general_dilated(padded[None], taps, (1, 1), 'VALID', dimension_n...  3.17 us
    conv_general_dilated x3, matrix products, adjoint_valid(): lax.conv_general_dilated(padded[None], taps, (1, 1), 'VALID', dimension_n...  1.33 us

profile of v9, /device:TPU:1, one launch (start us, length us, event | category | flops | bytes accessed | tf_op | source)
XLA Modules:
  0.0 57.3 jit_solution(6088836411706690505)
XLA Ops:
  0.6 0.0 copy-start.6
  0.6 0.0 copy-start.4
  0.7 0.6 %copy-done.6 = bf16[64,32]{0,1:T(8,128)(2,1)S(1)} copy-done((bf16[64,32]{0,1:T(8,128)(2,1)S(1)}, bf16[64,32]{0,1:T(8,128)(2,1)}, u32[]{:S(2)}) %copy-start.6) | copy-done | bytes 4120
  1.3 0.0 copy-start.7
  1.3 0.0 copy-start.5
  1.3 0.1 copy.67
  1.4 0.0 copy-done.4
  1.4 0.0 copy-start.2
  1.5 0.5 copy-done.7
  2.0 0.1 fusion.107
  2.1 0.0 copy-done.5
  2.1 0.1 fusion.106
  2.2 0.1 copy-done.2
  2.3 0.0 copy-start.3
  2.3 0.8 %copy-done.3 = s32[1,16,256,4]{2,3,1,0:T(4,128)S(1)} copy-done((s32[1,16,256,4]{2,3,1,0:T(4,128)S(1)}, s32[1,16,256,4]{2,3,1,0:T(4,128)}, u32[]{:S(2)}) %copy-start.3) | copy-done | bytes 65560
  3.1 0.8 %maximum_bitcast_fusion.p_ref = f32[16,10,256]{2,1,0:T(8,128)} fusion(f32[1,16,1,256]{3,2,1,0:T(1,128)S(1)} %get-tuple-element.28, f32[1,16,4,256]{3,2,1,0:T(4,128)S(1)} %multiply_bitcast_fusion, f32[1,16,1,256]{3,2,1,0:T(1,128)S(1)} %get-tuple-element.29, f32[1,16,4,256]{3,2,1,0:T(4,128)S(1)} %convert_bitcast_fusion), kind=kLoop, calls=%fused_computation.37 | loop fusion | flops 122880 | bytes 327680 | tf_op jit(solution)/shard_map/reshape | solution.py:169
  3.9 14.7 %shard_map.113 = (bf16[22,64,128]{2,1,0:T(8,128)(2,1)}, f32[16,10,256]{2,1,0:T(8,128)}, bf16[3,3,128,128]{3,2,1,0:T(8,128)(2,1)}, bf16[3,3,128,256]{3,2,1,0:T(8,128)(2,1)}, bf16[3,3,128,128]{3,2,1,0:T(8,128)(2,1)}) custom-call(bf16[8,32,128]{2,1,0:T(8,128)(2,1)} %x_ref.1, f32[16,10,256]{2,1,0:T(8,128)} %maximum_bitcast_fusion.p_ref, ...), custom_call_target="tpu_custom_call" | custom-call | tf_op jit(solution)/shard_map/pallas_call | solution.py:336
  18.6 0.0 copy-start.9
  18.6 1.1 %slice_bitcast_fusion = bf16[1,22,46,128]{3,2,1,0:T(8,128)(2,1)S(1)} fusion(bf16[22,64,128]{2,1,0:T(8,128)(2,1)} %get-tuple-element.11), kind=kLoop, calls=%fused_computation.36 | loop fusion | bytes 518144 | tf_op jit(solution)/shard_map/broadcast_in_dim | solution.py:65
  19.7 0.0 copy-done.9
  19.7 1.8 %fusion.4 = f32[1,20,44,128]{3,0,2,1:T(1,128)S(1)} fusion(bf16[3,3,128,128]{3,2,1,0:T(8,128)(2,1)S(1)} %copy-done.9, bf16[1,22,46,128]{3,2,1,0:T(8,128)(2,1)S(1)} %slice_bitcast_fusion), kind=kOutput, calls=%fused_computation.11 | convolution fusion | flops 259522560 | bytes 1004544 | tf_op jit(solution)/shard_map/conv_general_dilated | solution.py:64
  21.6 0.0 copy-start.8
  21.6 0.8 %convert_reduce_fusion = f32[10,22,128]{2,1,0:T(8,128)S(1)} fusion(f32[10,2,22,2,128]{4,3,2,1,0:T(2,128)S(1)} %bitcast.84), kind=kLoop, calls=%fused_computation.23 | loop fusion | flops 1210880 | bytes 563200 | tf_op jit(solution)/shard_map/reduce_sum | solution.py:106
  22.4 0.1 fusion.100
  22.5 0.1 copy-done.8
  22.6 0.7 %fusion.89 = f32[1,8,20,256]{3,0,2,1:T(1,128)S(1)} fusion(bf16[3,3,128,256]{3,2,1,0:T(8,128)(2,1)S(1)} %copy-done.8, bf16[1,10,22,128]{3,2,1,0:T(8,128)(2,1)S(1)} %fusion.100), kind=kOutput, calls=%fused_computation.118 | convolution fusion | flops 94371840 | bytes 809984 | tf_op jit(solution)/shard_map/conv_general_dilated | solution.py:64
  23.4 0.1 fusion.62
  23.4 0.2 fusion.92
  23.7 0.1 broadcast_in_dim.77
  23.7 0.2 reshape.149
  23.9 0.1 fusion.7
  24.0 0.0 copy-start.10
  24.0 0.1 select_bitcast_fusion.1
  24.2 0.8 %copy-done.10 = bf16[3,3,128,128]{3,2,1,0:T(8,128)(2,1)S(1)} copy-done((bf16[3,3,128,128]{3,2,1,0:T(8,128)(2,1)S(1)}, bf16[3,3,128,128]{3,2,1,0:T(8,128)(2,1)}, u32[]{:S(2)}) %copy-start.10) | copy-done | bytes 294936
  25.0 0.7 %fusion.40 = f32[1,8,32,128]{3,0,2,1:T(1,128)S(1)} fusion(bf16[3,3,128,128]{3,2,1,0:T(8,128)(2,1)S(1)} %copy-done.10, bf16[1,10,34,128]{3,2,1,0:T(8,128)(2,1)S(1)} %select_bitcast_fusion.1), kind=kOutput, calls=%fused_computation.66 | convolution fusion | flops 75497472 | bytes 513024 | tf_op jit(solution)/shard_map/conv_general_dilated | solution.py:64
  25.7 0.2 copy-done
  25.8 0.1 fusion.78
  25.9 0.1 copy.73
  26.0 0.7 %fusion.70 = (bf16[128,256]{1,0:T(8,128)(2,1)}, bf16[128,256]{1,0:T(8,128)(2,1)}) fusion(f32[256,128]{0,1:T(8,128)S(1)} %copy.73), kind=kLoop, calls=%fused_computation.95 | loop fusion | flops 131072 | bytes 262144 | tf_op jit(solution)/shard_map/convert_element_type | solution.py:111
  26.7 0.7 %fusion.85.slope_ref = f32[256,128]{1,0:T(8,128)} fusion(f32[256,128]{1,0:T(8,128)S(1)} %bitcast.93), kind=kLoop, calls=%fused_computation.110 | loop fusion | flops 557056 | bytes 262144 | tf_op jit(solution)/shard_map/add | solution.py:52
  27.4 20.8 %shard_map.114 = (f32[256,128]{1,0:T(8,128)}, bf16[18,64,128]{2,1,0:T(8,128)(2,1)}, f32[16,1,256]{2,1,0:T(1,128)}) custom-call(f32[16,10,256]{2,1,0:T(8,128)} %get-tuple-element.10.got_ref, bf16[128,256]{1,0:T(8,128)(2,1)} %get-tuple-element.27.high_ref, bf16[128,256]{1,0:T(8,128)(2,1)} %get-tuple-element.26.low_ref, f32[256,128]{1,0:T(8,128)} %fusion.85.slope_ref), custom_call_target="tpu_custom_call" | custom-call | tf_op jit(solution)/shard_map/pallas_call | solution.py:366
  48.3 1.3 %copy.87 = f32[1,16,256]{2,1,0:T(8,128)} copy(f32[1,16,256]{2,0,1:T(1,128)} %bitcast.97) | data formatting | bytes 32768
  49.6 1.0 %slice_bitcast_fusion.1 = bf16[18,1,42,128]{3,2,0,1:T(8,128)(2,1)S(1)} fusion(bf16[18,64,128]{2,1,0:T(8,128)(2,1)} %get-tuple-element.16), kind=kLoop, calls=%fused_computation.40 | loop fusion | bytes 387072 | tf_op jit(solution)/shard_map/broadcast_in_dim | solution.py:79
  50.6 0.1 reshape.156
  50.8 0.0 copy-start.12
  50.8 0.6 %copy-done.12 = pred[8,6]{0,1:T(8,128)(4,1)S(1)} copy-done((pred[8,6]{0,1:T(8,128)(4,1)S(1)}, pred[8,6]{0,1:T(8,128)(4,1)}, u32[]{:S(2)}) %copy-start.12) | copy-done | bytes 72
  51.4 0.6 %convolution_select_fusion = f32[16,8,6,128]{3,1,2,0:T(8,128)S(1)} fusion(bf16[3,3,128,128]{3,2,1,0:T(8,128)(2,1)S(1)} %copy-done.10, bf16[18,1,7,2,128]{4,2,3,0,1:T(8,128)(2,1)S(1)} %slice.42, bf16[18,1,8,6,128]{4,2,3,0,1:T(8,128)(2,1)S(1)} %copy.75, pred[8,6]{0,1:T(8,128)(4,1)S(1)} %copy-done.12), kind=kOutput, calls=%fused_computation | convolution fusion | flops 227475456 | bytes 973872 | tf_op jit(solution)/shard_map/conv_general_dilated | solution.py:78
  52.1 0.1 copy.76
  52.2 0.1 copy.116
  52.4 0.2 reduce_sum.19
  52.6 0.3 fusion.2
  52.9 0.0 copy-start.13
  53.0 0.6 %copy-done.13 = pred[8,3]{0,1:T(4,128)(4,1)S(1)} copy-done((pred[8,3]{0,1:T(4,128)(4,1)S(1)}, pred[8,3]{0,1:T(4,128)(4,1)}, u32[]{:S(2)}) %copy-start.13) | copy-done | bytes 48
  53.6 0.3 convolution_select_fusion.2
  54.0 0.1 broadcast_in_dim.84
  54.1 0.2 reshape.152
  54.3 0.2 select_bitcast_fusion
  54.6 0.0 copy-start.11
  54.6 0.6 %copy-done.11 = pred[8,5]{0,1:T(8,128)(4,1)S(1)} copy-done((pred[8,5]{0,1:T(8,128)(4,1)S(1)}, pred[8,5]{0,1:T(8,128)(4,1)}, u32[]{:S(2)}) %copy-start.11) | copy-done | bytes 64
  55.3 0.4 convolution_select_fusion.1
  55.6 0.0 copy-start.1
  55.7 0.9 %copy-done.1 = f32[256,128]{1,0:T(8,128)S(1)} copy-done((f32[256,128]{1,0:T(8,128)S(1)}, f32[256,128]{1,0:T(8,128)}, u32[]{:S(2)}) %copy-start.1) | copy-done | bytes 131096
  56.5 0.1 fusion.86
  56.6 0.7 %copy.86 = f32[8,32,128]{2,1,0:T(8,128)} copy(f32[8,32,128]{2,0,1:T(8,128)S(1)} %fusion.86) | data formatting | bytes 262144
  (26 shorter events, 0.5 us)
Async XLA Ops:
  0.6 0.7 %copy-start.6 = (bf16[64,32]{0,1:T(8,128)(2,1)S(1)}, bf16[64,32]{0,1:T(8,128)(2,1)}, u32[]{:S(2)}) copy-start(bf16[64,32]{0,1:T(8,128)(2,1)} %param.14) | copy-start | bytes 12292
  0.6 0.8 %copy-start.4 = (s32[1,16,256]{2,1,0:T(8,128)S(1)}, s32[1,16,256]{2,1,0:T(8,128)}, u32[]{:S(2)}) copy-start(s32[1,16,256]{2,1,0:T(8,128)} %param.16) | copy-start | bytes 49156
  1.3 0.7 %copy-start.7 = (s32[1,16]{1,0:T(1,128)S(1)}, s32[1,16]{1,0:T(1,128)}, u32[]{:S(2)}) copy-start(s32[1,16]{1,0:T(1,128)} %param.19) | copy-start | bytes 196
  1.3 0.7 %copy-start.5 = (f32[1,16,256]{2,1,0:T(8,128)S(1)}, f32[1,16,256]{2,1,0:T(8,128)}, u32[]{:S(2)}) copy-start(f32[1,16,256]{2,1,0:T(8,128)} %param.18) | copy-start | bytes 49156
  1.4 0.8 %copy-start.2 = (f32[1,16,256,4]{2,3,1,0:T(4,128)S(1)}, f32[1,16,256,4]{2,3,1,0:T(4,128)}, u32[]{:S(2)}) copy-start(f32[1,16,256,4]{2,3,1,0:T(4,128)} %param.17) | copy-start | bytes 196612
  2.3 0.8 %copy-start.3 = (s32[1,16,256,4]{2,3,1,0:T(4,128)S(1)}, s32[1,16,256,4]{2,3,1,0:T(4,128)}, u32[]{:S(2)}) copy-start(s32[1,16,256,4]{2,3,1,0:T(4,128)} %param.15) | copy-start | bytes 196612
  18.6 1.1 %copy-start.9 = (bf16[3,3,128,128]{3,2,1,0:T(8,128)(2,1)S(1)}, bf16[3,3,128,128]{3,2,1,0:T(8,128)(2,1)}, u32[]{:S(2)}) copy-start(bf16[3,3,128,128]{3,2,1,0:T(8,128)(2,1)} %get-tuple-element.12) | copy-start | bytes 884740
  21.6 1.1 %copy-start.8 = (bf16[3,3,128,256]{3,2,1,0:T(8,128)(2,1)S(1)}, bf16[3,3,128,256]{3,2,1,0:T(8,128)(2,1)}, u32[]{:S(2)}) copy-start(bf16[3,3,128,256]{3,2,1,0:T(8,128)(2,1)} %get-tuple-element.13) | copy-start | bytes 1769476
  24.0 1.0 %copy-start.10 = (bf16[3,3,128,128]{3,2,1,0:T(8,128)(2,1)S(1)}, bf16[3,3,128,128]{3,2,1,0:T(8,128)(2,1)}, u32[]{:S(2)}) copy-start(bf16[3,3,128,128]{3,2,1,0:T(8,128)(2,1)} %get-tuple-element.14) | copy-start | bytes 884740
  25.0 0.8 %copy-start = (bf16[8,32,128]{2,1,0:T(8,128)(2,1)S(1)}, bf16[8,32,128]{2,1,0:T(8,128)(2,1)}, u32[]{:S(2)}) copy-start(bf16[8,32,128]{2,1,0:T(8,128)(2,1)} %x_ref.1) | copy-start | bytes 196612
  50.8 0.7 %copy-start.12 = (pred[8,6]{0,1:T(8,128)(4,1)S(1)}, pred[8,6]{0,1:T(8,128)(4,1)}, u32[]{:S(2)}) copy-start(pred[8,6]{0,1:T(8,128)(4,1)} %constant.90) | copy-start | bytes 148
  52.9 0.7 %copy-start.13 = (pred[8,3]{0,1:T(4,128)(4,1)S(1)}, pred[8,3]{0,1:T(4,128)(4,1)}, u32[]{:S(2)}) copy-start(pred[8,3]{0,1:T(4,128)(4,1)} %constant.91) | copy-start | bytes 76
  54.6 0.7 %copy-start.11 = (pred[8,5]{0,1:T(8,128)(4,1)S(1)}, pred[8,5]{0,1:T(8,128)(4,1)}, u32[]{:S(2)}) copy-start(pred[8,5]{0,1:T(8,128)(4,1)} %constant.89) | copy-start | bytes 124
  55.6 0.9 %copy-start.1 = (f32[256,128]{1,0:T(8,128)S(1)}, f32[256,128]{1,0:T(8,128)}, u32[]{:S(2)}) copy-start(f32[256,128]{1,0:T(8,128)} %get-tuple-element.15) | copy-start | bytes 393220

commit v10 on v8

--- a/solution.py
+++ b/solution.py
@@ -284,7 +284,7 @@
     buf[...] = jnp.zeros(buf.shape, buf.dtype)
     count = greet(nlat, nlon)
     observe_kernel(got_ref, high_ref, low_ref, innov_ref, grad_ref)
-    grads = (grad_ref[...] * slope_ref[...]).astype(x_src.dtype).reshape(x_src.shape)
+    grads = (grad_ref[...] * gelu_slope(slope_ref[...])).astype(x_src.dtype).reshape(x_src.shape)
     x_src[...] = grads
     trade(width, nlat, nlon, count, x_src, innov_ref, buf, inbox, *sems)
     buf[width : width + rows, edge : edge + cols, :] = x_src[...]
@@ -405,7 +405,7 @@
     slope_first = gelu_slope(trim(pre_first, 5))
     slope_mid = gelu_slope(pre_mid)
     output = state.astype(jnp.float32) + jax.nn.gelu(pre_last, approximate=True)
-    grad_out, grads, innovation = observe_and_exchange(output, got, gelu_slope(pre_last), 5)
+    grad_out, grads, innovation = observe_and_exchange(output, got, pre_last, 5)
     innovation = innovation.reshape(obs_value.shape)
     grad_merged = adjoint_valid(grads, mat_out, rows + 8, cols + 8)
     grad_coarse = block_sum(grad_merged).astype(jnp.bfloat16)

time: 55.4 us -> 54.7 us (0.987)
  other arithmetic: 5.16 us -> 4.43 us
    add x1 -> x0, other arithmetic: 0.74 us -> none  [gelu_slope(): 0.5 * (1.0 + tval)]
    unnamed x32 -> x34, local copies, waits for them, and re-layouts: 4.27 us -> 4.26 us
where the time goes in v10:
time: 54.7 us; the launch traced here: 54.2 us
  Pallas kernels  34.9 us (64%)
  local copies, waits for them, and re-layouts  8.64 us (16%)
  matrix products  5.02 us (9%)
  other arithmetic  4.43 us (8%)
  between operations  1.2 us (2%)
    pallas_call x1, Pallas kernels, observe_and_exchange(): pl.pallas_call(functools.partial(back_kernel, width, nlat, nlon), out_sha...  20.9 us
    pallas_call x1, Pallas kernels, exchange(): pl.pallas_call(functools.partial(halo_kernel, width, nlat, nlon), out_sha...  14.1 us
    unnamed x34, local copies, waits for them, and re-layouts  4.26 us
    conv_general_dilated x3, matrix products, conv_valid(): lax.conv_general_dilated(padded[None], taps, (1, 1), 'VALID', dimension_n...  3.19 us
    conv_general_dilated x3, matrix products, adjoint_valid(): lax.conv_general_dilated(padded[None], taps, (1, 1), 'VALID', dimension_n...  1.33 us

profile of v10, /device:TPU:1, one launch (start us, length us, event | category | flops | bytes accessed | tf_op | source)
XLA Modules:
  0.0 54.2 jit_solution(17871130900606330435)
XLA Ops:
  0.6 0.0 copy-start.11
  0.6 0.0 copy-start.7
  0.7 0.0 copy-start.9
  0.7 0.0 copy-start.5
  0.7 1.0 %slice_bitcast_fusion.11 = (bf16[3,3,32,32]{3,2,1,0:T(8,128)(2,1)S(1)}, bf16[3,3,32,32]{3,2,1,0:T(8,128)(2,1)S(1)}, bf16[3,3,32,32]{3,2,1,0:T(8,128)(2,1)S(1)}) fusion(bf16[3,3,3,32,32]{4,3,2,1,0:T(8,128)(2,1)} %param.11), kind=kLoop, calls=%fused_computation.145 | loop fusion | bytes 110592 | tf_op jit(solution)/shard_map/squeeze | solution.py:34
  1.7 0.0 copy-start.6
  1.7 0.3 fusion.19
  2.1 0.0 copy-done.7
  2.1 0.0 copy-done.11
  2.1 0.1 fusion.111
  2.2 0.1 fusion.112
  2.3 0.2 copy-done.6
  2.5 0.8 %maximum_bitcast_fusion.p_ref = f32[16,10,256]{2,1,0:T(8,128)} fusion(f32[1,16,1,256]{3,2,1,0:T(1,128)S(1)} %get-tuple-element.31, f32[1,16,4,256]{3,2,1,0:T(4,128)S(1)} %multiply_bitcast_fusion, f32[1,16,1,256]{3,2,1,0:T(1,128)S(1)} %get-tuple-element.32, f32[1,16,4,256]{3,2,1,0:T(4,128)S(1)} %convert_bitcast_fusion), kind=kLoop, calls=%fused_computation.58 | loop fusion | flops 122880 | bytes 327680 | tf_op jit(solution)/shard_map/reshape | solution.py:169
  3.3 14.1 %shard_map.113 = (bf16[22,64,128]{2,1,0:T(8,128)(2,1)}, f32[16,10,256]{2,1,0:T(8,128)}) custom-call(bf16[8,32,128]{2,1,0:T(8,128)(2,1)} %x_ref.1, f32[16,10,256]{2,1,0:T(8,128)} %maximum_bitcast_fusion.p_ref), custom_call_target="tpu_custom_call" | custom-call | tf_op jit(solution)/shard_map/pallas_call | solution.py:312
  17.4 1.0 %slice_bitcast_fusion = bf16[1,22,46,128]{3,2,1,0:T(8,128)(2,1)S(1)} fusion(bf16[22,64,128]{2,1,0:T(8,128)(2,1)} %get-tuple-element.8), kind=kLoop, calls=%fused_computation.57 | loop fusion | bytes 518144 | tf_op jit(solution)/shard_map/broadcast_in_dim | solution.py:65
  18.4 1.8 %fusion.4 = f32[1,20,44,128]{3,0,2,1:T(1,128)S(1)} fusion(bf16[3,3,128,128]{3,2,1,0:T(8,128)(2,1)S(1)} %fusion.19, bf16[1,22,46,128]{3,2,1,0:T(8,128)(2,1)S(1)} %slice_bitcast_fusion), kind=kOutput, calls=%fused_computation.12 | convolution fusion | flops 259522560 | bytes 1004544 | tf_op jit(solution)/shard_map/conv_general_dilated | solution.py:64
  20.3 0.0 copy-start.2
  20.3 0.8 %convert_reduce_fusion = f32[10,22,128]{2,1,0:T(8,128)S(1)} fusion(f32[10,2,22,2,128]{4,3,2,1,0:T(2,128)S(1)} %bitcast.120), kind=kLoop, calls=%fused_computation.24 | loop fusion | flops 1210880 | bytes 563200 | tf_op jit(solution)/shard_map/reduce_sum | solution.py:106
  21.2 0.1 fusion.105
  21.3 0.3 maximum_maximum_fusion
  21.6 0.0 copy-start.10
  21.6 0.7 %fusion.94 = f32[1,8,20,256]{3,0,2,1:T(1,128)S(1)} fusion(bf16[3,3,128,256]{3,2,1,0:T(8,128)(2,1)S(1)} %maximum_maximum_fusion, bf16[1,10,22,128]{3,2,1,0:T(8,128)(2,1)S(1)} %fusion.105), kind=kOutput, calls=%fused_computation.130 | convolution fusion | flops 94371840 | bytes 809984 | tf_op jit(solution)/shard_map/conv_general_dilated | solution.py:64
  22.4 0.1 fusion.74
  22.4 0.0 copy-done.10
  22.4 0.1 copy.91
  22.6 0.2 fusion.97
  22.8 0.1 broadcast_in_dim.77
  22.9 0.2 reshape.147
  23.1 0.1 fusion.7
  23.2 0.0 copy-start.3
  23.2 0.1 select_bitcast_fusion.1
  23.3 0.8 %copy-done.3 = bf16[3,3,3,32,32]{4,3,2,1,0:T(8,128)(2,1)S(1)} copy-done((bf16[3,3,3,32,32]{4,3,2,1,0:T(8,128)(2,1)S(1)}, bf16[3,3,3,32,32]{4,3,2,1,0:T(8,128)(2,1)}, u32[]{:S(2)}) %copy-start.3) | copy-done | bytes 55320
  24.1 0.3 fusion.22
  24.4 0.0 copy-start.1
  24.5 0.7 %fusion.52 = f32[1,8,32,128]{3,0,2,1:T(1,128)S(1)} fusion(bf16[3,3,128,128]{3,2,1,0:T(8,128)(2,1)S(1)} %fusion.22, bf16[1,10,34,128]{3,2,1,0:T(8,128)(2,1)S(1)} %select_bitcast_fusion.1), kind=kOutput, calls=%fused_computation.85 | convolution fusion | flops 75497472 | bytes 513024 | tf_op jit(solution)/shard_map/conv_general_dilated | solution.py:64
  25.1 0.0 copy-start
  25.1 0.1 copy-done.1
  25.3 0.1 fusion.90
  25.3 0.1 copy.100
  25.4 0.7 %fusion.82 = (bf16[128,256]{1,0:T(8,128)(2,1)}, bf16[128,256]{1,0:T(8,128)(2,1)}) fusion(f32[256,128]{0,1:T(8,128)S(1)} %copy.100), kind=kLoop, calls=%fused_computation.114 | loop fusion | flops 131072 | bytes 262144 | tf_op jit(solution)/shard_map/convert_element_type | solution.py:111
  26.1 20.9 %shard_map.114 = (f32[256,128]{1,0:T(8,128)}, bf16[18,64,128]{2,1,0:T(8,128)(2,1)}, f32[16,1,256]{2,1,0:T(1,128)}) custom-call(f32[16,10,256]{2,1,0:T(8,128)} %get-tuple-element.7.got_ref, bf16[128,256]{1,0:T(8,128)(2,1)} %get-tuple-element.30.high_ref, bf16[128,256]{1,0:T(8,128)(2,1)} %get-tuple-element.29.low_ref, f32[256,128]{1,0:T(8,128)} %bitcast.130), custom_call_target="tpu_custom_call" | custom-call | tf_op jit(solution)/shard_map/pallas_call | solution.py:341
  47.0 1.0 %slice_bitcast_fusion.1 = bf16[18,1,42,128]{3,2,0,1:T(8,128)(2,1)S(1)} fusion(bf16[18,64,128]{2,1,0:T(8,128)(2,1)} %get-tuple-element.10), kind=kLoop, calls=%fused_computation.61 | loop fusion | bytes 387072 | tf_op jit(solution)/shard_map/broadcast_in_dim | solution.py:79
  48.1 0.0 copy-start.13
  48.1 0.1 reshape.154
  48.2 0.5 copy-done.13
  48.8 0.6 %convolution_select_fusion = f32[16,8,6,128]{3,1,2,0:T(8,128)S(1)} fusion(bf16[3,3,128,128]{3,2,1,0:T(8,128)(2,1)S(1)} %fusion.22, bf16[18,1,7,2,128]{4,2,3,0,1:T(8,128)(2,1)S(1)} %slice.99, bf16[18,1,8,6,128]{4,2,3,0,1:T(8,128)(2,1)S(1)} %copy.102, pred[8,6]{0,1:T(8,128)(4,1)S(1)} %copy-done.13), kind=kOutput, calls=%fused_computation | convolution fusion | flops 227475456 | bytes 973872 | tf_op jit(solution)/shard_map/conv_general_dilated | solution.py:78
  49.4 0.1 copy.103
  49.6 0.1 copy.152
  49.7 0.2 reduce_sum.19
  49.9 0.0 copy-start.14
  50.0 0.3 fusion.2
  50.3 0.3 copy-done.14
  50.6 0.3 convolution_select_fusion.2
  51.0 0.1 broadcast_in_dim.84
  51.1 0.2 reshape.150
  51.3 0.0 copy-start.12
  51.3 0.2 select_bitcast_fusion
  51.6 0.3 copy-done.12
  52.0 0.4 convolution_select_fusion.1
  52.4 0.5 copy-done.4
  52.9 0.1 fusion.91
  52.9 0.7 %copy.113 = f32[8,32,128]{2,1,0:T(8,128)} copy(f32[8,32,128]{2,0,1:T(8,128)S(1)} %fusion.91) | data formatting | bytes 262144
  53.6 0.0 copy-done.8
  53.6 0.6 %copy.114 = f32[1,16,256]{2,1,0:T(8,128)} copy(f32[1,16,256]{2,0,1:T(1,128)S(1)} %bitcast.133) | data formatting | bytes 32768
  (36 shorter events, 0.6 us)
Async XLA Ops:
  0.6 1.5 %copy-start.11 = (s32[1,16]{1,0:T(1,128)S(1)}, s32[1,16]{1,0:T(1,128)}, u32[]{:S(2)}) copy-start(s32[1,16]{1,0:T(1,128)} %param.19) | copy-start | bytes 196
  0.6 1.4 %copy-start.7 = (s32[1,16,256]{2,1,0:T(8,128)S(1)}, s32[1,16,256]{2,1,0:T(8,128)}, u32[]{:S(2)}) copy-start(s32[1,16,256]{2,1,0:T(8,128)} %param.16) | copy-start | bytes 49156
  0.7 1.5 %copy-start.9 = (f32[1,16,256]{2,1,0:T(8,128)S(1)}, f32[1,16,256]{2,1,0:T(8,128)}, u32[]{:S(2)}) copy-start(f32[1,16,256]{2,1,0:T(8,128)} %param.18) | copy-start | bytes 49156
  0.7 1.6 %copy-start.5 = (f32[1,16,256,4]{2,3,1,0:T(4,128)S(1)}, f32[1,16,256,4]{2,3,1,0:T(4,128)}, u32[]{:S(2)}) copy-start(f32[1,16,256,4]{2,3,1,0:T(4,128)} %param.17) | copy-start | bytes 196612
  1.7 0.8 %copy-start.6 = (s32[1,16,256,4]{2,3,1,0:T(4,128)S(1)}, s32[1,16,256,4]{2,3,1,0:T(4,128)}, u32[]{:S(2)}) copy-start(s32[1,16,256,4]{2,3,1,0:T(4,128)} %param.15) | copy-start | bytes 196612
  20.3 1.0 %copy-start.2 = (bf16[3,3,3,32,64]{4,3,2,1,0:T(8,128)(2,1)S(1)}, bf16[3,3,3,32,64]{4,3,2,1,0:T(8,128)(2,1)}, u32[]{:S(2)}) copy-start(bf16[3,3,3,32,64]{4,3,2,1,0:T(8,128)(2,1)} %param.12) | copy-start | bytes 331780
  21.6 0.8 %copy-start.10 = (bf16[64,32]{0,1:T(8,128)(2,1)S(1)}, bf16[64,32]{0,1:T(8,128)(2,1)}, u32[]{:S(2)}) copy-start(bf16[64,32]{0,1:T(8,128)(2,1)} %param.14) | copy-start | bytes 12292
  23.2 0.9 %copy-start.3 = (bf16[3,3,3,32,32]{4,3,2,1,0:T(8,128)(2,1)S(1)}, bf16[3,3,3,32,32]{4,3,2,1,0:T(8,128)(2,1)}, u32[]{:S(2)}) copy-start(bf16[3,3,3,32,32]{4,3,2,1,0:T(8,128)(2,1)} %param.13) | copy-start | bytes 165892
  24.4 0.8 %copy-start.1 = (bf16[8,32,128]{2,1,0:T(8,128)(2,1)S(1)}, bf16[8,32,128]{2,1,0:T(8,128)(2,1)}, u32[]{:S(2)}) copy-start(bf16[8,32,128]{2,1,0:T(8,128)(2,1)} %x_ref.1) | copy-start | bytes 196612
  25.1 1.0 %copy-start = (f32[1,8,32,128]{3,0,2,1:T(1,128)}, f32[1,8,32,128]{3,0,2,1:T(1,128)S(1)}, u32[]{:S(2)}) copy-start(f32[1,8,32,128]{3,0,2,1:T(1,128)S(1)} %fusion.52) | copy-start | bytes 393220
  48.1 0.7 %copy-start.13 = (pred[8,6]{0,1:T(8,128)(4,1)S(1)}, pred[8,6]{0,1:T(8,128)(4,1)}, u32[]{:S(2)}) copy-start(pred[8,6]{0,1:T(8,128)(4,1)} %constant.92) | copy-start | bytes 148
  49.9 0.7 %copy-start.14 = (pred[8,3]{0,1:T(4,128)(4,1)S(1)}, pred[8,3]{0,1:T(4,128)(4,1)}, u32[]{:S(2)}) copy-start(pred[8,3]{0,1:T(4,128)(4,1)} %constant.93) | copy-start | bytes 76
  51.3 0.7 %copy-start.12 = (pred[8,5]{0,1:T(8,128)(4,1)S(1)}, pred[8,5]{0,1:T(8,128)(4,1)}, u32[]{:S(2)}) copy-start(pred[8,5]{0,1:T(8,128)(4,1)} %constant.45) | copy-start | bytes 124
  52.0 0.9 %copy-start.4 = (f32[256,128]{1,0:T(8,128)S(1)}, f32[256,128]{1,0:T(8,128)}, u32[]{:S(2)}) copy-start(f32[256,128]{1,0:T(8,128)} %get-tuple-element.9) | copy-start | bytes 393220
  52.3 1.3 %copy-start.8 = (f32[16,1,256]{2,1,0:T(1,128)S(1)}, f32[16,1,256]{2,1,0:T(1,128)}, u32[]{:S(2)}) copy-start(f32[16,1,256]{2,1,0:T(1,128)} %get-tuple-element.11) | copy-start | bytes 49156

commit v11 on v10

--- a/solution.py
+++ b/solution.py
@@ -111,13 +111,14 @@
     return high.astype(jnp.bfloat16), (value - high).astype(jnp.bfloat16)
 
 
-def observe_kernel(got_ref, high_ref, low_ref, innov_ref, grad_ref):
+def observe_kernel(got_ref, high_ref, innov_ref, grad_ref):
     fields, nslot = got_ref.shape[1], got_ref.shape[2]
-    feats, ncell = high_ref.shape
+    ncell, feats = high_ref.shape
     cell_ids = lax.broadcasted_iota(jnp.int32, (ncell, nslot), 0).astype(jnp.float32)
     feat_ids = lax.broadcasted_iota(jnp.int32, (feats, nslot), 0).astype(jnp.float32)
-    high = high_ref[...]
-    low = low_ref[...]
+    value = high_ref[...].T
+    high = value.astype(jnp.bfloat16)
+    low = (value - high.astype(jnp.float32)).astype(jnp.bfloat16)
     both = jnp.concatenate([high, low], axis=0)
     grad_ref[...] = jnp.zeros(grad_ref.shape, jnp.float32)
     trans = (((1,), (1,)), ((), ()))
@@ -275,7 +276,7 @@
 
 
 def back_kernel(
-    width, nlat, nlon, got_ref, high_ref, low_ref, slope_ref,
+    width, nlat, nlon, got_ref, high_ref, slope_ref,
     grad_ref, o_ref, q_ref, buf, inbox, innov_ref, x_src, *sems
 ):
     rows, cols = x_src.shape[0], x_src.shape[1]
@@ -283,7 +284,7 @@
     j = lax.axis_index("lon")
     buf[...] = jnp.zeros(buf.shape, buf.dtype)
     count = greet(nlat, nlon)
-    observe_kernel(got_ref, high_ref, low_ref, innov_ref, grad_ref)
+    observe_kernel(got_ref, high_ref, innov_ref, grad_ref)
     grads = (grad_ref[...] * gelu_slope(slope_ref[...])).astype(x_src.dtype).reshape(x_src.shape)
     x_src[...] = grads
     trade(width, nlat, nlon, count, x_src, innov_ref, buf, inbox, *sems)
@@ -334,7 +335,6 @@
     nlat = lax.axis_size("lat")
     nlon = lax.axis_size("lon")
     owners, nslot = got.shape[0], got.shape[2]
-    o_hi, o_lo = split_bf16(output.reshape(ncell, feats).T)
     full = (rows + 2 * width, cols + 2 * edge, feats)
     vmem = pl.BlockSpec(memory_space=pltpu.VMEM)
     innov_shape = (owners, 1, nslot)
@@ -345,7 +345,7 @@
             jax.ShapeDtypeStruct(full, jnp.bfloat16),
             jax.ShapeDtypeStruct(innov_shape, jnp.float32),
         ),
-        in_specs=[vmem] * 4,
+        in_specs=[vmem] * 3,
         out_specs=(vmem, vmem, vmem),
         scratch_shapes=[
             pltpu.VMEM(full, jnp.bfloat16),
@@ -355,7 +355,7 @@
         ]
         + sem_scratch(nlon),
         compiler_params=pltpu.CompilerParams(collective_id=1, has_side_effects=True),
-    )(got, o_hi, o_lo, slope.reshape(ncell, feats))
+    )(got, output.reshape(ncell, feats), slope.reshape(ncell, feats))
     grads = out[:, edge - width : edge + cols + width]
     return grad.reshape(rows, cols, feats), grads, innovation
 

time: 54.7 us -> 54.7 us (level)
    convert_element_type x1 -> x0, other arithmetic: 0.68 us -> none  [split_bf16(): return (high.astype(jnp.bfloat16), (value - high).astype(jnp.bfloat16))]
    add x1, other arithmetic: 0.06 us -> 0.71 us  [shards(): output = state.astype(jnp.float32) + jax.nn.gelu(pre_last, approximate=True)]
where the time goes in v11:
time: 54.7 us; the launch traced here: 54.2 us
  Pallas kernels  35 us (64%)
  local copies, waits for them, and re-layouts  8.55 us (16%)
  matrix products  5.03 us (9%)
  other arithmetic  4.41 us (8%)
  between operations  1.19 us (2%)
    pallas_call x1, Pallas kernels, observe_and_exchange(): pl.pallas_call(functools.partial(back_kernel, width, nlat, nlon), out_sha...  21 us
    pallas_call x1, Pallas kernels, exchange(): pl.pallas_call(functools.partial(halo_kernel, width, nlat, nlon), out_sha...  14.1 us
    unnamed x34, local copies, waits for them, and re-layouts  4.27 us
    conv_general_dilated x3, matrix products, conv_valid(): lax.conv_general_dilated(padded[None], taps, (1, 1), 'VALID', dimension_n...  3.19 us
    conv_general_dilated x3, matrix products, adjoint_valid(): lax.conv_general_dilated(padded[None], taps, (1, 1), 'VALID', dimension_n...  1.33 us

profile of v11, /device:TPU:1, one launch (start us, length us, event | category | flops | bytes accessed | tf_op | source)
XLA Modules:
  0.0 54.2 jit_solution(8209077781254519780)
XLA Ops:
  0.6 0.0 copy-start.11
  0.6 0.0 copy-start.7
  0.7 0.0 copy-start.9
  0.7 0.0 copy-start.5
  0.7 1.0 %slice_bitcast_fusion.11 = (bf16[3,3,32,32]{3,2,1,0:T(8,128)(2,1)S(1)}, bf16[3,3,32,32]{3,2,1,0:T(8,128)(2,1)S(1)}, bf16[3,3,32,32]{3,2,1,0:T(8,128)(2,1)S(1)}) fusion(bf16[3,3,3,32,32]{4,3,2,1,0:T(8,128)(2,1)} %param.11), kind=kLoop, calls=%fused_computation.142 | loop fusion | bytes 110592 | tf_op jit(solution)/shard_map/squeeze | solution.py:34
  1.7 0.0 copy-start.6
  1.7 0.3 fusion.19
  2.1 0.0 copy-done.7
  2.1 0.0 copy-done.11
  2.1 0.0 copy-done.9
  2.1 0.1 fusion.110
  2.2 0.1 fusion.111
  2.3 0.0 copy-done.5
  2.3 0.2 copy-done.6
  2.5 0.8 %maximum_bitcast_fusion.p_ref = f32[16,10,256]{2,1,0:T(8,128)} fusion(f32[1,16,1,256]{3,2,1,0:T(1,128)S(1)} %get-tuple-element.29, f32[1,16,4,256]{3,2,1,0:T(4,128)S(1)} %multiply_bitcast_fusion, f32[1,16,1,256]{3,2,1,0:T(1,128)S(1)} %get-tuple-element.30, f32[1,16,4,256]{3,2,1,0:T(4,128)S(1)} %convert_bitcast_fusion), kind=kLoop, calls=%fused_computation.58 | loop fusion | flops 122880 | bytes 327680 | tf_op jit(solution)/shard_map/reshape | solution.py:170
  3.3 14.1 %shard_map.113 = (bf16[22,64,128]{2,1,0:T(8,128)(2,1)}, f32[16,10,256]{2,1,0:T(8,128)}) custom-call(bf16[8,32,128]{2,1,0:T(8,128)(2,1)} %x_ref.1, f32[16,10,256]{2,1,0:T(8,128)} %maximum_bitcast_fusion.p_ref), custom_call_target="tpu_custom_call" | custom-call | tf_op jit(solution)/shard_map/pallas_call | solution.py:313
  17.4 1.0 %slice_bitcast_fusion = bf16[1,22,46,128]{3,2,1,0:T(8,128)(2,1)S(1)} fusion(bf16[22,64,128]{2,1,0:T(8,128)(2,1)} %get-tuple-element.8), kind=kLoop, calls=%fused_computation.57 | loop fusion | bytes 518144 | tf_op jit(solution)/shard_map/broadcast_in_dim | solution.py:65
  18.5 1.8 %fusion.4 = f32[1,20,44,128]{3,0,2,1:T(1,128)S(1)} fusion(bf16[3,3,128,128]{3,2,1,0:T(8,128)(2,1)S(1)} %fusion.19, bf16[1,22,46,128]{3,2,1,0:T(8,128)(2,1)S(1)} %slice_bitcast_fusion), kind=kOutput, calls=%fused_computation.12 | convolution fusion | flops 259522560 | bytes 1004544 | tf_op jit(solution)/shard_map/conv_general_dilated | solution.py:64
  20.3 0.0 copy-start.2
  20.3 0.8 %convert_reduce_fusion = f32[10,22,128]{2,1,0:T(8,128)S(1)} fusion(f32[10,2,22,2,128]{4,3,2,1,0:T(2,128)S(1)} %bitcast.117), kind=kLoop, calls=%fused_computation.24 | loop fusion | flops 1210880 | bytes 563200 | tf_op jit(solution)/shard_map/reduce_sum | solution.py:106
  21.2 0.1 fusion.104
  21.3 0.3 maximum_maximum_fusion
  21.6 0.0 copy-start.10
  21.6 0.7 %fusion.93 = f32[1,8,20,256]{3,0,2,1:T(1,128)S(1)} fusion(bf16[3,3,128,256]{3,2,1,0:T(8,128)(2,1)S(1)} %maximum_maximum_fusion, bf16[1,10,22,128]{3,2,1,0:T(8,128)(2,1)S(1)} %fusion.104), kind=kOutput, calls=%fused_computation.127 | convolution fusion | flops 94371840 | bytes 809984 | tf_op jit(solution)/shard_map/conv_general_dilated | solution.py:64
  22.4 0.1 fusion.74
  22.5 0.1 copy.89
  22.6 0.2 fusion.96
  22.8 0.1 broadcast_in_dim.77
  22.9 0.2 reshape.147
  23.1 0.1 fusion.7
  23.2 0.0 copy-start.3
  23.2 0.1 select_bitcast_fusion.1
  23.3 0.8 %copy-done.3 = bf16[3,3,3,32,32]{4,3,2,1,0:T(8,128)(2,1)S(1)} copy-done((bf16[3,3,3,32,32]{4,3,2,1,0:T(8,128)(2,1)S(1)}, bf16[3,3,3,32,32]{4,3,2,1,0:T(8,128)(2,1)}, u32[]{:S(2)}) %copy-start.3) | copy-done | bytes 55320
  24.1 0.3 fusion.22
  24.5 0.0 copy-start.1
  24.5 0.7 %fusion.52 = f32[1,8,32,128]{3,0,2,1:T(1,128)S(1)} fusion(bf16[3,3,128,128]{3,2,1,0:T(8,128)(2,1)S(1)} %fusion.22, bf16[1,10,34,128]{3,2,1,0:T(8,128)(2,1)S(1)} %select_bitcast_fusion.1), kind=kOutput, calls=%fused_computation.83 | convolution fusion | flops 75497472 | bytes 513024 | tf_op jit(solution)/shard_map/conv_general_dilated | solution.py:64
  25.2 0.1 copy-done.1
  25.3 0.7 %fusion.89 = f32[8,32,128]{2,1,0:T(8,128)} fusion(f32[8,32,128]{2,1,0:T(8,128)S(1)} %bitcast.125, bf16[8,32,128]{2,1,0:T(8,128)(2,1)S(1)} %copy-done.1), kind=kLoop, calls=%fused_computation.119 | loop fusion | flops 327680 | bytes 327680 | tf_op jit(solution)/shard_map/add | solution.py:407
  26.0 0.0 copy-done
  26.0 21.0 %shard_map.114 = (f32[256,128]{1,0:T(8,128)}, bf16[18,64,128]{2,1,0:T(8,128)(2,1)}, f32[16,1,256]{2,1,0:T(1,128)}) custom-call(f32[16,10,256]{2,1,0:T(8,128)} %get-tuple-element.7.got_ref, f32[256,128]{1,0:T(8,128)} %bitcast.127, f32[256,128]{1,0:T(8,128)} %bitcast.126), custom_call_target="tpu_custom_call" | custom-call | tf_op jit(solution)/shard_map/pallas_call | solution.py:341
  47.0 1.0 %slice_bitcast_fusion.1 = bf16[18,1,42,128]{3,2,0,1:T(8,128)(2,1)S(1)} fusion(bf16[18,64,128]{2,1,0:T(8,128)(2,1)} %get-tuple-element.10), kind=kLoop, calls=%fused_computation.61 | loop fusion | bytes 387072 | tf_op jit(solution)/shard_map/broadcast_in_dim | solution.py:79
  48.0 0.0 copy-start.13
  48.0 0.1 reshape.154
  48.2 0.5 copy-done.13
  48.7 0.6 %convolution_select_fusion = f32[16,8,6,128]{3,1,2,0:T(8,128)S(1)} fusion(bf16[3,3,128,128]{3,2,1,0:T(8,128)(2,1)S(1)} %fusion.22, bf16[18,1,7,2,128]{4,2,3,0,1:T(8,128)(2,1)S(1)} %slice.99, bf16[18,1,8,6,128]{4,2,3,0,1:T(8,128)(2,1)S(1)} %copy.99, pred[8,6]{0,1:T(8,128)(4,1)S(1)} %copy-done.13), kind=kOutput, calls=%fused_computation | convolution fusion | flops 227475456 | bytes 973872 | tf_op jit(solution)/shard_map/conv_general_dilated | solution.py:78
  49.3 0.1 copy.100
  49.5 0.1 copy.149
  49.6 0.2 reduce_sum.19
  49.9 0.0 copy-start.14
  49.9 0.3 fusion.2
  50.3 0.3 copy-done.14
  50.6 0.3 convolution_select_fusion.2
  51.0 0.1 broadcast_in_dim.84
  51.1 0.2 reshape.150
  51.2 0.0 copy-start.12
  51.2 0.2 select_bitcast_fusion
  51.6 0.3 copy-done.12
  51.9 0.4 convolution_select_fusion.1
  52.3 0.0 copy-start.8
  52.3 0.5 copy-done.4
  52.8 0.1 fusion.90
  52.9 0.7 %copy.110 = f32[8,32,128]{2,1,0:T(8,128)} copy(f32[8,32,128]{2,0,1:T(8,128)S(1)} %fusion.90) | data formatting | bytes 262144
  53.6 0.0 copy-done.8
  53.6 0.6 %copy.111 = f32[1,16,256]{2,1,0:T(8,128)} copy(f32[1,16,256]{2,0,1:T(1,128)S(1)} %bitcast.130) | data formatting | bytes 32768
  (34 shorter events, 0.6 us)
Async XLA Ops:
  0.6 1.5 %copy-start.11 = (s32[1,16]{1,0:T(1,128)S(1)}, s32[1,16]{1,0:T(1,128)}, u32[]{:S(2)}) copy-start(s32[1,16]{1,0:T(1,128)} %param.19) | copy-start | bytes 196
  0.6 1.4 %copy-start.7 = (s32[1,16,256]{2,1,0:T(8,128)S(1)}, s32[1,16,256]{2,1,0:T(8,128)}, u32[]{:S(2)}) copy-start(s32[1,16,256]{2,1,0:T(8,128)} %param.16) | copy-start | bytes 49156
  0.7 1.5 %copy-start.9 = (f32[1,16,256]{2,1,0:T(8,128)S(1)}, f32[1,16,256]{2,1,0:T(8,128)}, u32[]{:S(2)}) copy-start(f32[1,16,256]{2,1,0:T(8,128)} %param.18) | copy-start | bytes 49156
  0.7 1.6 %copy-start.5 = (f32[1,16,256,4]{2,3,1,0:T(4,128)S(1)}, f32[1,16,256,4]{2,3,1,0:T(4,128)}, u32[]{:S(2)}) copy-start(f32[1,16,256,4]{2,3,1,0:T(4,128)} %param.17) | copy-start | bytes 196612
  1.7 0.8 %copy-start.6 = (s32[1,16,256,4]{2,3,1,0:T(4,128)S(1)}, s32[1,16,256,4]{2,3,1,0:T(4,128)}, u32[]{:S(2)}) copy-start(s32[1,16,256,4]{2,3,1,0:T(4,128)} %param.15) | copy-start | bytes 196612
  20.3 1.0 %copy-start.2 = (bf16[3,3,3,32,64]{4,3,2,1,0:T(8,128)(2,1)S(1)}, bf16[3,3,3,32,64]{4,3,2,1,0:T(8,128)(2,1)}, u32[]{:S(2)}) copy-start(bf16[3,3,3,32,64]{4,3,2,1,0:T(8,128)(2,1)} %param.12) | copy-start | bytes 331780
  21.6 0.8 %copy-start.10 = (bf16[64,32]{0,1:T(8,128)(2,1)S(1)}, bf16[64,32]{0,1:T(8,128)(2,1)}, u32[]{:S(2)}) copy-start(bf16[64,32]{0,1:T(8,128)(2,1)} %param.14) | copy-start | bytes 12292
  23.2 0.9 %copy-start.3 = (bf16[3,3,3,32,32]{4,3,2,1,0:T(8,128)(2,1)S(1)}, bf16[3,3,3,32,32]{4,3,2,1,0:T(8,128)(2,1)}, u32[]{:S(2)}) copy-start(bf16[3,3,3,32,32]{4,3,2,1,0:T(8,128)(2,1)} %param.13) | copy-start | bytes 165892
  24.5 0.8 %copy-start.1 = (bf16[8,32,128]{2,1,0:T(8,128)(2,1)S(1)}, bf16[8,32,128]{2,1,0:T(8,128)(2,1)}, u32[]{:S(2)}) copy-start(bf16[8,32,128]{2,1,0:T(8,128)(2,1)} %x_ref.1) | copy-start | bytes 196612
  25.1 0.9 %copy-start = (f32[1,8,32,128]{3,0,2,1:T(1,128)}, f32[1,8,32,128]{3,0,2,1:T(1,128)S(1)}, u32[]{:S(2)}) copy-start(f32[1,8,32,128]{3,0,2,1:T(1,128)S(1)} %fusion.52) | copy-start | bytes 393220
  48.0 0.7 %copy-start.13 = (pred[8,6]{0,1:T(8,128)(4,1)S(1)}, pred[8,6]{0,1:T(8,128)(4,1)}, u32[]{:S(2)}) copy-start(pred[8,6]{0,1:T(8,128)(4,1)} %constant.92) | copy-start | bytes 148
  49.9 0.7 %copy-start.14 = (pred[8,3]{0,1:T(4,128)(4,1)S(1)}, pred[8,3]{0,1:T(4,128)(4,1)}, u32[]{:S(2)}) copy-start(pred[8,3]{0,1:T(4,128)(4,1)} %constant.93) | copy-start | bytes 76
  51.2 0.7 %copy-start.12 = (pred[8,5]{0,1:T(8,128)(4,1)S(1)}, pred[8,5]{0,1:T(8,128)(4,1)}, u32[]{:S(2)}) copy-start(pred[8,5]{0,1:T(8,128)(4,1)} %constant.45) | copy-start | bytes 124
  51.9 0.9 %copy-start.4 = (f32[256,128]{1,0:T(8,128)S(1)}, f32[256,128]{1,0:T(8,128)}, u32[]{:S(2)}) copy-start(f32[256,128]{1,0:T(8,128)} %get-tuple-element.9) | copy-start | bytes 393220
  52.3 1.3 %copy-start.8 = (f32[16,1,256]{2,1,0:T(1,128)S(1)}, f32[16,1,256]{2,1,0:T(1,128)}, u32[]{:S(2)}) copy-start(f32[16,1,256]{2,1,0:T(1,128)} %get-tuple-element.11) | copy-start | bytes 49156

commit v12 on v11

--- a/solution.py
+++ b/solution.py
@@ -150,7 +150,7 @@
         )
         return carry
 
-    lax.fori_loop(0, got_ref.shape[0], body, 0)
+    lax.fori_loop(0, got_ref.shape[0], body, 0, unroll=4)
 
 
 def pack(obs_cells, obs_chan, obs_weights, obs_value, obs_count):

time: 54.7 us -> 50.7 us (0.927)
  Pallas kernels: 35 us -> 31.1 us
    pallas_call x1, Pallas kernels: 21 us -> 17 us  [observe_and_exchange(): pl.pallas_call(functools.partial(back_kernel, width, nlat, nlon), out_sha...]
where the time goes in v12:
time: 50.7 us; the launch traced here: 50.3 us
  Pallas kernels  31.1 us (61%)
  local copies, waits for them, and re-layouts  8.55 us (17%)
  matrix products  5.02 us (10%)
  other arithmetic  4.41 us (9%)
  between operations  1.19 us (2%)
    pallas_call x1, Pallas kernels, observe_and_exchange(): pl.pallas_call(functools.partial(back_kernel, width, nlat, nlon), out_sha...  17 us
    pallas_call x1, Pallas kernels, exchange(): pl.pallas_call(functools.partial(halo_kernel, width, nlat, nlon), out_sha...  14.1 us
    unnamed x34, local copies, waits for them, and re-layouts  4.27 us
    conv_general_dilated x3, matrix products, conv_valid(): lax.conv_general_dilated(padded[None], taps, (1, 1), 'VALID', dimension_n...  3.19 us
    conv_general_dilated x3, matrix products, adjoint_valid(): lax.conv_general_dilated(padded[None], taps, (1, 1), 'VALID', dimension_n...  1.33 us
    reduce_sum x2, other arithmetic, block_sum(): return fine.reshape(rows // 2, 2, cols // 2, 2, feats).sum(axis=(1, 3))  1.08 us
    broadcast_in_dim x4, local copies, waits for them, and re-layouts, adjoint_valid(): padded[None]  1.07 us
    broadcast_in_dim x1, local copies, waits for them, and re-layouts, conv_valid(): padded[None]  1.05 us

profile of v12, /device:TPU:1, one launch (start us, length us, event | category | flops | bytes accessed | tf_op | source)
XLA Modules:
  0.0 50.3 jit_solution(12555228745956622918)
XLA Ops:
  0.6 0.0 copy-start.11
  0.6 0.0 copy-start.7
  0.7 0.0 copy-start.9
  0.7 0.0 copy-start.5
  0.7 1.0 %slice_bitcast_fusion.11 = (bf16[3,3,32,32]{3,2,1,0:T(8,128)(2,1)S(1)}, bf16[3,3,32,32]{3,2,1,0:T(8,128)(2,1)S(1)}, bf16[3,3,32,32]{3,2,1,0:T(8,128)(2,1)S(1)}) fusion(bf16[3,3,3,32,32]{4,3,2,1,0:T(8,128)(2,1)} %param.11), kind=kLoop, calls=%fused_computation.142 | loop fusion | bytes 110592 | tf_op jit(solution)/shard_map/squeeze | solution.py:34
  1.7 0.0 copy-start.6
  1.7 0.3 fusion.19
  2.1 0.0 copy-done.7
  2.1 0.0 copy-done.11
  2.1 0.0 copy-done.9
  2.1 0.1 fusion.110
  2.2 0.1 fusion.111
  2.3 0.0 copy-done.5
  2.3 0.2 copy-done.6
  2.5 0.8 %maximum_bitcast_fusion.p_ref = f32[16,10,256]{2,1,0:T(8,128)} fusion(f32[1,16,1,256]{3,2,1,0:T(1,128)S(1)} %get-tuple-element.29, f32[1,16,4,256]{3,2,1,0:T(4,128)S(1)} %multiply_bitcast_fusion, f32[1,16,1,256]{3,2,1,0:T(1,128)S(1)} %get-tuple-element.30, f32[1,16,4,256]{3,2,1,0:T(4,128)S(1)} %convert_bitcast_fusion), kind=kLoop, calls=%fused_computation.58 | loop fusion | flops 122880 | bytes 327680 | tf_op jit(solution)/shard_map/reshape | solution.py:170
  3.3 14.1 %shard_map.113 = (bf16[22,64,128]{2,1,0:T(8,128)(2,1)}, f32[16,10,256]{2,1,0:T(8,128)}) custom-call(bf16[8,32,128]{2,1,0:T(8,128)(2,1)} %x_ref.1, f32[16,10,256]{2,1,0:T(8,128)} %maximum_bitcast_fusion.p_ref), custom_call_target="tpu_custom_call" | custom-call | tf_op jit(solution)/shard_map/pallas_call | solution.py:313
  17.4 1.0 %slice_bitcast_fusion = bf16[1,22,46,128]{3,2,1,0:T(8,128)(2,1)S(1)} fusion(bf16[22,64,128]{2,1,0:T(8,128)(2,1)} %get-tuple-element.8), kind=kLoop, calls=%fused_computation.57 | loop fusion | bytes 518144 | tf_op jit(solution)/shard_map/broadcast_in_dim | solution.py:65
  18.5 1.8 %fusion.4 = f32[1,20,44,128]{3,0,2,1:T(1,128)S(1)} fusion(bf16[3,3,128,128]{3,2,1,0:T(8,128)(2,1)S(1)} %fusion.19, bf16[1,22,46,128]{3,2,1,0:T(8,128)(2,1)S(1)} %slice_bitcast_fusion), kind=kOutput, calls=%fused_computation.12 | convolution fusion | flops 259522560 | bytes 1004544 | tf_op jit(solution)/shard_map/conv_general_dilated | solution.py:64
  20.3 0.0 copy-start.2
  20.3 0.8 %convert_reduce_fusion = f32[10,22,128]{2,1,0:T(8,128)S(1)} fusion(f32[10,2,22,2,128]{4,3,2,1,0:T(2,128)S(1)} %bitcast.117), kind=kLoop, calls=%fused_computation.24 | loop fusion | flops 1210880 | bytes 563200 | tf_op jit(solution)/shard_map/reduce_sum | solution.py:106
  21.2 0.1 fusion.104
  21.3 0.0 copy-done.2
  21.3 0.3 maximum_maximum_fusion
  21.6 0.0 copy-start.10
  21.6 0.7 %fusion.93 = f32[1,8,20,256]{3,0,2,1:T(1,128)S(1)} fusion(bf16[3,3,128,256]{3,2,1,0:T(8,128)(2,1)S(1)} %maximum_maximum_fusion, bf16[1,10,22,128]{3,2,1,0:T(8,128)(2,1)S(1)} %fusion.104), kind=kOutput, calls=%fused_computation.127 | convolution fusion | flops 94371840 | bytes 809984 | tf_op jit(solution)/shard_map/conv_general_dilated | solution.py:64
  22.4 0.1 fusion.74
  22.5 0.1 copy.89
  22.6 0.2 fusion.96
  22.8 0.1 broadcast_in_dim.77
  22.9 0.2 reshape.147
  23.1 0.1 fusion.7
  23.2 0.0 copy-start.3
  23.2 0.1 select_bitcast_fusion.1
  23.3 0.8 %copy-done.3 = bf16[3,3,3,32,32]{4,3,2,1,0:T(8,128)(2,1)S(1)} copy-done((bf16[3,3,3,32,32]{4,3,2,1,0:T(8,128)(2,1)S(1)}, bf16[3,3,3,32,32]{4,3,2,1,0:T(8,128)(2,1)}, u32[]{:S(2)}) %copy-start.3) | copy-done | bytes 55320
  24.1 0.3 fusion.22
  24.5 0.0 copy-start.1
  24.5 0.7 %fusion.52 = f32[1,8,32,128]{3,0,2,1:T(1,128)S(1)} fusion(bf16[3,3,128,128]{3,2,1,0:T(8,128)(2,1)S(1)} %fusion.22, bf16[1,10,34,128]{3,2,1,0:T(8,128)(2,1)S(1)} %select_bitcast_fusion.1), kind=kOutput, calls=%fused_computation.83 | convolution fusion | flops 75497472 | bytes 513024 | tf_op jit(solution)/shard_map/conv_general_dilated | solution.py:64
  25.2 0.1 copy-done.1
  25.3 0.7 %fusion.89 = f32[8,32,128]{2,1,0:T(8,128)} fusion(f32[8,32,128]{2,1,0:T(8,128)S(1)} %bitcast.125, bf16[8,32,128]{2,1,0:T(8,128)(2,1)S(1)} %copy-done.1), kind=kLoop, calls=%fused_computation.119 | loop fusion | flops 327680 | bytes 327680 | tf_op jit(solution)/shard_map/add | solution.py:407
  26.0 0.0 copy-done
  26.0 17.0 %shard_map.114 = (f32[256,128]{1,0:T(8,128)}, bf16[18,64,128]{2,1,0:T(8,128)(2,1)}, f32[16,1,256]{2,1,0:T(1,128)}) custom-call(f32[16,10,256]{2,1,0:T(8,128)} %get-tuple-element.7.got_ref, f32[256,128]{1,0:T(8,128)} %bitcast.127, f32[256,128]{1,0:T(8,128)} %bitcast.126), custom_call_target="tpu_custom_call" | custom-call | tf_op jit(solution)/shard_map/pallas_call | solution.py:341
  43.1 1.0 %slice_bitcast_fusion.1 = bf16[18,1,42,128]{3,2,0,1:T(8,128)(2,1)S(1)} fusion(bf16[18,64,128]{2,1,0:T(8,128)(2,1)} %get-tuple-element.10), kind=kLoop, calls=%fused_computation.61 | loop fusion | bytes 387072 | tf_op jit(solution)/shard_map/broadcast_in_dim | solution.py:79
  44.1 0.0 copy-start.13
  44.1 0.1 reshape.154
  44.3 0.5 %copy-done.13 = pred[8,6]{0,1:T(8,128)(4,1)S(1)} copy-done((pred[8,6]{0,1:T(8,128)(4,1)S(1)}, pred[8,6]{0,1:T(8,128)(4,1)}, u32[]{:S(2)}) %copy-start.13) | copy-done | bytes 72
  44.8 0.6 %convolution_select_fusion = f32[16,8,6,128]{3,1,2,0:T(8,128)S(1)} fusion(bf16[3,3,128,128]{3,2,1,0:T(8,128)(2,1)S(1)} %fusion.22, bf16[18,1,7,2,128]{4,2,3,0,1:T(8,128)(2,1)S(1)} %slice.99, bf16[18,1,8,6,128]{4,2,3,0,1:T(8,128)(2,1)S(1)} %copy.99, pred[8,6]{0,1:T(8,128)(4,1)S(1)} %copy-done.13), kind=kOutput, calls=%fused_computation | convolution fusion | flops 227475456 | bytes 973872 | tf_op jit(solution)/shard_map/conv_general_dilated | solution.py:78
  45.4 0.1 copy.100
  45.6 0.1 copy.149
  45.7 0.2 reduce_sum.19
  46.0 0.0 copy-start.14
  46.0 0.3 fusion.2
  46.4 0.3 copy-done.14
  46.6 0.3 convolution_select_fusion.2
  47.1 0.1 broadcast_in_dim.84
  47.2 0.2 reshape.150
  47.3 0.0 copy-start.12
  47.3 0.2 select_bitcast_fusion
  47.7 0.3 copy-done.12
  48.0 0.4 convolution_select_fusion.1
  48.4 0.0 copy-start.8
  48.4 0.5 copy-done.4
  48.9 0.1 fusion.90
  49.0 0.7 %copy.110 = f32[8,32,128]{2,1,0:T(8,128)} copy(f32[8,32,128]{2,0,1:T(8,128)S(1)} %fusion.90) | data formatting | bytes 262144
  49.7 0.6 %copy.111 = f32[1,16,256]{2,1,0:T(8,128)} copy(f32[1,16,256]{2,0,1:T(1,128)S(1)} %bitcast.130) | data formatting | bytes 32768
  (34 shorter events, 0.6 us)
Async XLA Ops:
  0.6 1.5 %copy-start.11 = (s32[1,16]{1,0:T(1,128)S(1)}, s32[1,16]{1,0:T(1,128)}, u32[]{:S(2)}) copy-start(s32[1,16]{1,0:T(1,128)} %param.19) | copy-start | bytes 196
  0.6 1.4 %copy-start.7 = (s32[1,16,256]{2,1,0:T(8,128)S(1)}, s32[1,16,256]{2,1,0:T(8,128)}, u32[]{:S(2)}) copy-start(s32[1,16,256]{2,1,0:T(8,128)} %param.16) | copy-start | bytes 49156
  0.7 1.5 %copy-start.9 = (f32[1,16,256]{2,1,0:T(8,128)S(1)}, f32[1,16,256]{2,1,0:T(8,128)}, u32[]{:S(2)}) copy-start(f32[1,16,256]{2,1,0:T(8,128)} %param.18) | copy-start | bytes 49156
  0.7 1.6 %copy-start.5 = (f32[1,16,256,4]{2,3,1,0:T(4,128)S(1)}, f32[1,16,256,4]{2,3,1,0:T(4,128)}, u32[]{:S(2)}) copy-start(f32[1,16,256,4]{2,3,1,0:T(4,128)} %param.17) | copy-start | bytes 196612
  1.7 0.8 %copy-start.6 = (s32[1,16,256,4]{2,3,1,0:T(4,128)S(1)}, s32[1,16,256,4]{2,3,1,0:T(4,128)}, u32[]{:S(2)}) copy-start(s32[1,16,256,4]{2,3,1,0:T(4,128)} %param.15) | copy-start | bytes 196612
  20.3 1.0 %copy-start.2 = (bf16[3,3,3,32,64]{4,3,2,1,0:T(8,128)(2,1)S(1)}, bf16[3,3,3,32,64]{4,3,2,1,0:T(8,128)(2,1)}, u32[]{:S(2)}) copy-start(bf16[3,3,3,32,64]{4,3,2,1,0:T(8,128)(2,1)} %param.12) | copy-start | bytes 331780
  21.6 0.8 %copy-start.10 = (bf16[64,32]{0,1:T(8,128)(2,1)S(1)}, bf16[64,32]{0,1:T(8,128)(2,1)}, u32[]{:S(2)}) copy-start(bf16[64,32]{0,1:T(8,128)(2,1)} %param.14) | copy-start | bytes 12292
  23.2 0.9 %copy-start.3 = (bf16[3,3,3,32,32]{4,3,2,1,0:T(8,128)(2,1)S(1)}, bf16[3,3,3,32,32]{4,3,2,1,0:T(8,128)(2,1)}, u32[]{:S(2)}) copy-start(bf16[3,3,3,32,32]{4,3,2,1,0:T(8,128)(2,1)} %param.13) | copy-start | bytes 165892
  24.5 0.8 %copy-start.1 = (bf16[8,32,128]{2,1,0:T(8,128)(2,1)S(1)}, bf16[8,32,128]{2,1,0:T(8,128)(2,1)}, u32[]{:S(2)}) copy-start(bf16[8,32,128]{2,1,0:T(8,128)(2,1)} %x_ref.1) | copy-start | bytes 196612
  25.1 0.9 %copy-start = (f32[1,8,32,128]{3,0,2,1:T(1,128)}, f32[1,8,32,128]{3,0,2,1:T(1,128)S(1)}, u32[]{:S(2)}) copy-start(f32[1,8,32,128]{3,0,2,1:T(1,128)S(1)} %fusion.52) | copy-start | bytes 393220
  44.1 0.7 %copy-start.13 = (pred[8,6]{0,1:T(8,128)(4,1)S(1)}, pred[8,6]{0,1:T(8,128)(4,1)}, u32[]{:S(2)}) copy-start(pred[8,6]{0,1:T(8,128)(4,1)} %constant.92) | copy-start | bytes 148
  46.0 0.7 %copy-start.14 = (pred[8,3]{0,1:T(4,128)(4,1)S(1)}, pred[8,3]{0,1:T(4,128)(4,1)}, u32[]{:S(2)}) copy-start(pred[8,3]{0,1:T(4,128)(4,1)} %constant.93) | copy-start | bytes 76
  47.3 0.7 %copy-start.12 = (pred[8,5]{0,1:T(8,128)(4,1)S(1)}, pred[8,5]{0,1:T(8,128)(4,1)}, u32[]{:S(2)}) copy-start(pred[8,5]{0,1:T(8,128)(4,1)} %constant.45) | copy-start | bytes 124
  48.0 0.9 %copy-start.4 = (f32[256,128]{1,0:T(8,128)S(1)}, f32[256,128]{1,0:T(8,128)}, u32[]{:S(2)}) copy-start(f32[256,128]{1,0:T(8,128)} %get-tuple-element.9) | copy-start | bytes 393220
  48.4 1.3 %copy-start.8 = (f32[16,1,256]{2,1,0:T(1,128)S(1)}, f32[16,1,256]{2,1,0:T(1,128)}, u32[]{:S(2)}) copy-start(f32[16,1,256]{2,1,0:T(1,128)} %get-tuple-element.11) | copy-start | bytes 49156

commit v13 on v12

--- a/solution.py
+++ b/solution.py
@@ -150,7 +150,7 @@
         )
         return carry
 
-    lax.fori_loop(0, got_ref.shape[0], body, 0, unroll=4)
+    lax.fori_loop(0, got_ref.shape[0], body, 0, unroll=16)
 
 
 def pack(obs_cells, obs_chan, obs_weights, obs_value, obs_count):

time: 50.7 us -> 49.4 us (0.974)
  Pallas kernels: 31.1 us -> 29.8 us
    pallas_call x1, Pallas kernels: 17 us -> 15.7 us  [observe_and_exchange(): pl.pallas_call(functools.partial(back_kernel, width, nlat, nlon), out_sha...]
where the time goes in v13:
time: 49.4 us; the launch traced here: 48.9 us
  Pallas kernels  29.8 us (60%)
  local copies, waits for them, and re-layouts  8.54 us (17%)
  matrix products  5.02 us (10%)
  other arithmetic  4.41 us (9%)
  between operations  1.2 us (2%)
    pallas_call x1, Pallas kernels, observe_and_exchange(): pl.pallas_call(functools.partial(back_kernel, width, nlat, nlon), out_sha...  15.7 us
    pallas_call x1, Pallas kernels, exchange(): pl.pallas_call(functools.partial(halo_kernel, width, nlat, nlon), out_sha...  14.1 us
    unnamed x34, local copies, waits for them, and re-layouts  4.27 us
    conv_general_dilated x3, matrix products, conv_valid(): lax.conv_general_dilated(padded[None], taps, (1, 1), 'VALID', dimension_n...  3.19 us
    conv_general_dilated x3, matrix products, adjoint_valid(): lax.conv_general_dilated(padded[None], taps, (1, 1), 'VALID', dimension_n...  1.33 us
    reduce_sum x2, other arithmetic, block_sum(): return fine.reshape(rows // 2, 2, cols // 2, 2, feats).sum(axis=(1, 3))  1.08 us
    broadcast_in_dim x4, local copies, waits for them, and re-layouts, adjoint_valid(): padded[None]  1.07 us
    broadcast_in_dim x1, local copies, waits for them, and re-layouts, conv_valid(): padded[None]  1.05 us

profile of v13, /device:TPU:1, one launch (start us, length us, event | category | flops | bytes accessed | tf_op | source)
XLA Modules:
  0.0 48.9 jit_solution(15547679945229403969)
XLA Ops:
  0.6 0.0 copy-start.11
  0.6 0.0 copy-start.7
  0.7 0.0 copy-start.9
  0.7 0.0 copy-start.5
  0.7 1.0 %slice_bitcast_fusion.11 = (bf16[3,3,32,32]{3,2,1,0:T(8,128)(2,1)S(1)}, bf16[3,3,32,32]{3,2,1,0:T(8,128)(2,1)S(1)}, bf16[3,3,32,32]{3,2,1,0:T(8,128)(2,1)S(1)}) fusion(bf16[3,3,3,32,32]{4,3,2,1,0:T(8,128)(2,1)} %param.11), kind=kLoop, calls=%fused_computation.142 | loop fusion | bytes 110592 | tf_op jit(solution)/shard_map/squeeze | solution.py:34
  1.7 0.0 copy-start.6
  1.7 0.3 fusion.19
  2.1 0.0 copy-done.7
  2.1 0.0 copy-done.11
  2.1 0.0 copy-done.9
  2.1 0.1 fusion.110
  2.2 0.1 fusion.111
  2.3 0.0 copy-done.5
  2.3 0.2 copy-done.6
  2.5 0.8 %maximum_bitcast_fusion.p_ref = f32[16,10,256]{2,1,0:T(8,128)} fusion(f32[1,16,1,256]{3,2,1,0:T(1,128)S(1)} %get-tuple-element.29, f32[1,16,4,256]{3,2,1,0:T(4,128)S(1)} %multiply_bitcast_fusion, f32[1,16,1,256]{3,2,1,0:T(1,128)S(1)} %get-tuple-element.30, f32[1,16,4,256]{3,2,1,0:T(4,128)S(1)} %convert_bitcast_fusion), kind=kLoop, calls=%fused_computation.58 | loop fusion | flops 122880 | bytes 327680 | tf_op jit(solution)/shard_map/reshape | solution.py:170
  3.3 14.1 %shard_map.113 = (bf16[22,64,128]{2,1,0:T(8,128)(2,1)}, f32[16,10,256]{2,1,0:T(8,128)}) custom-call(bf16[8,32,128]{2,1,0:T(8,128)(2,1)} %x_ref.1, f32[16,10,256]{2,1,0:T(8,128)} %maximum_bitcast_fusion.p_ref), custom_call_target="tpu_custom_call" | custom-call | tf_op jit(solution)/shard_map/pallas_call | solution.py:313
  17.4 1.0 %slice_bitcast_fusion = bf16[1,22,46,128]{3,2,1,0:T(8,128)(2,1)S(1)} fusion(bf16[22,64,128]{2,1,0:T(8,128)(2,1)} %get-tuple-element.8), kind=kLoop, calls=%fused_computation.57 | loop fusion | bytes 518144 | tf_op jit(solution)/shard_map/broadcast_in_dim | solution.py:65
  18.5 1.8 %fusion.4 = f32[1,20,44,128]{3,0,2,1:T(1,128)S(1)} fusion(bf16[3,3,128,128]{3,2,1,0:T(8,128)(2,1)S(1)} %fusion.19, bf16[1,22,46,128]{3,2,1,0:T(8,128)(2,1)S(1)} %slice_bitcast_fusion), kind=kOutput, calls=%fused_computation.12 | convolution fusion | flops 259522560 | bytes 1004544 | tf_op jit(solution)/shard_map/conv_general_dilated | solution.py:64
  20.3 0.0 copy-start.2
  20.3 0.8 %convert_reduce_fusion = f32[10,22,128]{2,1,0:T(8,128)S(1)} fusion(f32[10,2,22,2,128]{4,3,2,1,0:T(2,128)S(1)} %bitcast.117), kind=kLoop, calls=%fused_computation.24 | loop fusion | flops 1210880 | bytes 563200 | tf_op jit(solution)/shard_map/reduce_sum | solution.py:106
  21.2 0.1 fusion.104
  21.3 0.0 copy-done.2
  21.3 0.3 maximum_maximum_fusion
  21.6 0.0 copy-start.10
  21.6 0.7 %fusion.93 = f32[1,8,20,256]{3,0,2,1:T(1,128)S(1)} fusion(bf16[3,3,128,256]{3,2,1,0:T(8,128)(2,1)S(1)} %maximum_maximum_fusion, bf16[1,10,22,128]{3,2,1,0:T(8,128)(2,1)S(1)} %fusion.104), kind=kOutput, calls=%fused_computation.127 | convolution fusion | flops 94371840 | bytes 809984 | tf_op jit(solution)/shard_map/conv_general_dilated | solution.py:64
  22.4 0.1 fusion.74
  22.4 0.0 copy-done.10
  22.5 0.1 copy.89
  22.6 0.2 fusion.96
  22.8 0.1 broadcast_in_dim.77
  22.9 0.2 reshape.147
  23.1 0.1 fusion.7
  23.2 0.0 copy-start.3
  23.2 0.1 select_bitcast_fusion.1
  23.3 0.8 %copy-done.3 = bf16[3,3,3,32,32]{4,3,2,1,0:T(8,128)(2,1)S(1)} copy-done((bf16[3,3,3,32,32]{4,3,2,1,0:T(8,128)(2,1)S(1)}, bf16[3,3,3,32,32]{4,3,2,1,0:T(8,128)(2,1)}, u32[]{:S(2)}) %copy-start.3) | copy-done | bytes 55320
  24.1 0.3 fusion.22
  24.4 0.0 copy-start.1
  24.5 0.7 %fusion.52 = f32[1,8,32,128]{3,0,2,1:T(1,128)S(1)} fusion(bf16[3,3,128,128]{3,2,1,0:T(8,128)(2,1)S(1)} %fusion.22, bf16[1,10,34,128]{3,2,1,0:T(8,128)(2,1)S(1)} %select_bitcast_fusion.1), kind=kOutput, calls=%fused_computation.83 | convolution fusion | flops 75497472 | bytes 513024 | tf_op jit(solution)/shard_map/conv_general_dilated | solution.py:64
  25.1 0.0 copy-start
  25.2 0.1 copy-done.1
  25.3 0.7 %fusion.89 = f32[8,32,128]{2,1,0:T(8,128)} fusion(f32[8,32,128]{2,1,0:T(8,128)S(1)} %bitcast.125, bf16[8,32,128]{2,1,0:T(8,128)(2,1)S(1)} %copy-done.1), kind=kLoop, calls=%fused_computation.119 | loop fusion | flops 327680 | bytes 327680 | tf_op jit(solution)/shard_map/add | solution.py:407
  26.0 15.7 %shard_map.114 = (f32[256,128]{1,0:T(8,128)}, bf16[18,64,128]{2,1,0:T(8,128)(2,1)}, f32[16,1,256]{2,1,0:T(1,128)}) custom-call(f32[16,10,256]{2,1,0:T(8,128)} %get-tuple-element.7.got_ref, f32[256,128]{1,0:T(8,128)} %bitcast.127, f32[256,128]{1,0:T(8,128)} %bitcast.126), custom_call_target="tpu_custom_call" | custom-call | tf_op jit(solution)/shard_map/pallas_call | solution.py:341
  41.7 1.0 %slice_bitcast_fusion.1 = bf16[18,1,42,128]{3,2,0,1:T(8,128)(2,1)S(1)} fusion(bf16[18,64,128]{2,1,0:T(8,128)(2,1)} %get-tuple-element.10), kind=kLoop, calls=%fused_computation.61 | loop fusion | bytes 387072 | tf_op jit(solution)/shard_map/broadcast_in_dim | solution.py:79
  42.8 0.0 copy-start.13
  42.8 0.1 reshape.154
  42.9 0.5 %copy-done.13 = pred[8,6]{0,1:T(8,128)(4,1)S(1)} copy-done((pred[8,6]{0,1:T(8,128)(4,1)S(1)}, pred[8,6]{0,1:T(8,128)(4,1)}, u32[]{:S(2)}) %copy-start.13) | copy-done | bytes 72
  43.4 0.6 %convolution_select_fusion = f32[16,8,6,128]{3,1,2,0:T(8,128)S(1)} fusion(bf16[3,3,128,128]{3,2,1,0:T(8,128)(2,1)S(1)} %fusion.22, bf16[18,1,7,2,128]{4,2,3,0,1:T(8,128)(2,1)S(1)} %slice.99, bf16[18,1,8,6,128]{4,2,3,0,1:T(8,128)(2,1)S(1)} %copy.99, pred[8,6]{0,1:T(8,128)(4,1)S(1)} %copy-done.13), kind=kOutput, calls=%fused_computation | convolution fusion | flops 227475456 | bytes 973872 | tf_op jit(solution)/shard_map/conv_general_dilated | solution.py:78
  44.1 0.1 copy.100
  44.2 0.1 copy.149
  44.4 0.2 reduce_sum.19
  44.6 0.0 copy-start.14
  44.6 0.3 fusion.2
  45.0 0.3 copy-done.14
  45.3 0.3 convolution_select_fusion.2
  45.7 0.1 broadcast_in_dim.84
  45.8 0.2 reshape.150
  46.0 0.0 copy-start.12
  46.0 0.2 select_bitcast_fusion
  46.3 0.3 copy-done.12
  46.6 0.4 convolution_select_fusion.1
  47.1 0.5 copy-done.4
  47.5 0.1 fusion.90
  47.6 0.7 %copy.110 = f32[8,32,128]{2,1,0:T(8,128)} copy(f32[8,32,128]{2,0,1:T(8,128)S(1)} %fusion.90) | data formatting | bytes 262144
  48.3 0.6 %copy.111 = f32[1,16,256]{2,1,0:T(8,128)} copy(f32[1,16,256]{2,0,1:T(1,128)S(1)} %bitcast.130) | data formatting | bytes 32768
  (34 shorter events, 0.6 us)
Async XLA Ops:
  0.6 1.5 %copy-start.11 = (s32[1,16]{1,0:T(1,128)S(1)}, s32[1,16]{1,0:T(1,128)}, u32[]{:S(2)}) copy-start(s32[1,16]{1,0:T(1,128)} %param.19) | copy-start | bytes 196
  0.6 1.4 %copy-start.7 = (s32[1,16,256]{2,1,0:T(8,128)S(1)}, s32[1,16,256]{2,1,0:T(8,128)}, u32[]{:S(2)}) copy-start(s32[1,16,256]{2,1,0:T(8,128)} %param.16) | copy-start | bytes 49156
  0.7 1.5 %copy-start.9 = (f32[1,16,256]{2,1,0:T(8,128)S(1)}, f32[1,16,256]{2,1,0:T(8,128)}, u32[]{:S(2)}) copy-start(f32[1,16,256]{2,1,0:T(8,128)} %param.18) | copy-start | bytes 49156
  0.7 1.6 %copy-start.5 = (f32[1,16,256,4]{2,3,1,0:T(4,128)S(1)}, f32[1,16,256,4]{2,3,1,0:T(4,128)}, u32[]{:S(2)}) copy-start(f32[1,16,256,4]{2,3,1,0:T(4,128)} %param.17) | copy-start | bytes 196612
  1.7 0.8 %copy-start.6 = (s32[1,16,256,4]{2,3,1,0:T(4,128)S(1)}, s32[1,16,256,4]{2,3,1,0:T(4,128)}, u32[]{:S(2)}) copy-start(s32[1,16,256,4]{2,3,1,0:T(4,128)} %param.15) | copy-start | bytes 196612
  20.3 1.0 %copy-start.2 = (bf16[3,3,3,32,64]{4,3,2,1,0:T(8,128)(2,1)S(1)}, bf16[3,3,3,32,64]{4,3,2,1,0:T(8,128)(2,1)}, u32[]{:S(2)}) copy-start(bf16[3,3,3,32,64]{4,3,2,1,0:T(8,128)(2,1)} %param.12) | copy-start | bytes 331780
  21.6 0.8 %copy-start.10 = (bf16[64,32]{0,1:T(8,128)(2,1)S(1)}, bf16[64,32]{0,1:T(8,128)(2,1)}, u32[]{:S(2)}) copy-start(bf16[64,32]{0,1:T(8,128)(2,1)} %param.14) | copy-start | bytes 12292
  23.2 0.9 %copy-start.3 = (bf16[3,3,3,32,32]{4,3,2,1,0:T(8,128)(2,1)S(1)}, bf16[3,3,3,32,32]{4,3,2,1,0:T(8,128)(2,1)}, u32[]{:S(2)}) copy-start(bf16[3,3,3,32,32]{4,3,2,1,0:T(8,128)(2,1)} %param.13) | copy-start | bytes 165892
  24.4 0.8 %copy-start.1 = (bf16[8,32,128]{2,1,0:T(8,128)(2,1)S(1)}, bf16[8,32,128]{2,1,0:T(8,128)(2,1)}, u32[]{:S(2)}) copy-start(bf16[8,32,128]{2,1,0:T(8,128)(2,1)} %x_ref.1) | copy-start | bytes 196612
  25.1 0.9 %copy-start = (f32[1,8,32,128]{3,0,2,1:T(1,128)}, f32[1,8,32,128]{3,0,2,1:T(1,128)S(1)}, u32[]{:S(2)}) copy-start(f32[1,8,32,128]{3,0,2,1:T(1,128)S(1)} %fusion.52) | copy-start | bytes 393220
  42.8 0.7 %copy-start.13 = (pred[8,6]{0,1:T(8,128)(4,1)S(1)}, pred[8,6]{0,1:T(8,128)(4,1)}, u32[]{:S(2)}) copy-start(pred[8,6]{0,1:T(8,128)(4,1)} %constant.92) | copy-start | bytes 148
  44.6 0.7 %copy-start.14 = (pred[8,3]{0,1:T(4,128)(4,1)S(1)}, pred[8,3]{0,1:T(4,128)(4,1)}, u32[]{:S(2)}) copy-start(pred[8,3]{0,1:T(4,128)(4,1)} %constant.93) | copy-start | bytes 76
  46.0 0.7 %copy-start.12 = (pred[8,5]{0,1:T(8,128)(4,1)S(1)}, pred[8,5]{0,1:T(8,128)(4,1)}, u32[]{:S(2)}) copy-start(pred[8,5]{0,1:T(8,128)(4,1)} %constant.45) | copy-start | bytes 124
  46.6 0.9 %copy-start.4 = (f32[256,128]{1,0:T(8,128)S(1)}, f32[256,128]{1,0:T(8,128)}, u32[]{:S(2)}) copy-start(f32[256,128]{1,0:T(8,128)} %get-tuple-element.9) | copy-start | bytes 393220
  47.0 1.3 %copy-start.8 = (f32[16,1,256]{2,1,0:T(1,128)S(1)}, f32[16,1,256]{2,1,0:T(1,128)}, u32[]{:S(2)}) copy-start(f32[16,1,256]{2,1,0:T(1,128)} %get-tuple-element.11) | copy-start | bytes 49156

commit v14 on v13

--- a/solution.py
+++ b/solution.py
@@ -271,7 +271,7 @@
     inbox[pl.ds(j, 1)] = p_ref[pl.ds(j, 1)]
     count = greet(nlat, nlon)
     trade(width, nlat, nlon, count, x_ref, p_ref, buf, inbox, *sems)
-    o_ref[...] = buf[...]
+    o_ref[...] = buf[:, edge - width : edge + cols + width, :]
     q_ref[...] = inbox[...]
 
 
@@ -290,7 +290,7 @@
     trade(width, nlat, nlon, count, x_src, innov_ref, buf, inbox, *sems)
     buf[width : width + rows, edge : edge + cols, :] = x_src[...]
     inbox[pl.ds(j, 1)] = innov_ref[pl.ds(j, 1)]
-    o_ref[...] = buf[...]
+    o_ref[...] = buf[:, edge - width : edge + cols + width, :]
     q_ref[...] = inbox[...]
 
 
@@ -313,7 +313,7 @@
     out, got = pl.pallas_call(
         functools.partial(halo_kernel, width, nlat, nlon),
         out_shape=(
-            jax.ShapeDtypeStruct(full, block.dtype),
+            jax.ShapeDtypeStruct((rows + 2 * width, cols + 2 * width, feats), block.dtype),
             jax.ShapeDtypeStruct(payload.shape, payload.dtype),
         ),
         in_specs=[vmem, vmem],
@@ -325,7 +325,7 @@
         + sem_scratch(nlon),
         compiler_params=pltpu.CompilerParams(collective_id=0, has_side_effects=True),
     )(block, payload)
-    return out[:, edge - width : edge + cols + width], got
+    return out, got
 
 
 def observe_and_exchange(output, got, slope, width):
@@ -342,7 +342,7 @@
         functools.partial(back_kernel, width, nlat, nlon),
         out_shape=(
             jax.ShapeDtypeStruct((ncell, feats), jnp.float32),
-            jax.ShapeDtypeStruct(full, jnp.bfloat16),
+            jax.ShapeDtypeStruct((rows + 2 * width, cols + 2 * width, feats), jnp.bfloat16),
             jax.ShapeDtypeStruct(innov_shape, jnp.float32),
         ),
         in_specs=[vmem] * 3,
@@ -356,7 +356,7 @@
         + sem_scratch(nlon),
         compiler_params=pltpu.CompilerParams(collective_id=1, has_side_effects=True),
     )(got, output.reshape(ncell, feats), slope.reshape(ncell, feats))
-    grads = out[:, edge - width : edge + cols + width]
+    grads = out
     return grad.reshape(rows, cols, feats), grads, innovation
 
 

time: 49.4 us -> 49.2 us (level)
  local copies, waits for them, and re-layouts: 8.54 us -> 7.42 us
  matrix products: 5.02 us -> 5.97 us
    broadcast_in_dim x1 -> x0, local copies, waits for them, and re-layouts: 1.05 us -> none  [conv_valid(): padded[None]]
    conv_general_dilated x3, matrix products: 3.19 us -> 4.13 us  [conv_valid(): lax.conv_general_dilated(padded[None], taps, (1, 1), 'VALID', dimension_n...]
    broadcast_in_dim x4 -> x3, local copies, waits for them, and re-layouts: 1.07 us -> 0.99 us  [adjoint_valid(): padded[None]]
where the time goes in v14:
time: 49.2 us; the launch traced here: 48.8 us
  Pallas kernels  29.8 us (61%)
  local copies, waits for them, and re-layouts  7.42 us (15%)
  matrix products  5.97 us (12%)
  other arithmetic  4.41 us (9%)
  between operations  1.18 us (2%)
    pallas_call x1, Pallas kernels, observe_and_exchange(): pl.pallas_call(functools.partial(back_kernel, width, nlat, nlon), out_sha...  15.7 us
    pallas_call x1, Pallas kernels, exchange(): pl.pallas_call(functools.partial(halo_kernel, width, nlat, nlon), out_sha...  14.1 us
    unnamed x34, local copies, waits for them, and re-layouts  4.27 us
    conv_general_dilated x3, matrix products, conv_valid(): lax.conv_general_dilated(padded[None], taps, (1, 1), 'VALID', dimension_n...  4.13 us
    conv_general_dilated x3, matrix products, adjoint_valid(): lax.conv_general_dilated(padded[None], taps, (1, 1), 'VALID', dimension_n...  1.33 us
    reduce_sum x2, other arithmetic, block_sum(): return fine.reshape(rows // 2, 2, cols // 2, 2, feats).sum(axis=(1, 3))  1.08 us
    squeeze x3, local copies, waits for them, and re-layouts, banded(): kernel[:, :, p - q + 1]  1.04 us
    broadcast_in_dim x3, local copies, waits for them, and re-layouts, adjoint_valid(): padded[None]  0.99 us

profile of v14, /device:TPU:1, one launch (start us, length us, event | category | flops | bytes accessed | tf_op | source)
XLA Modules:
  0.0 48.8 jit_solution(1022002329863765413)
XLA Ops:
  0.6 0.0 copy-start.11
  0.6 0.0 copy-start.7
  0.7 0.0 copy-start.9
  0.7 0.0 copy-start.5
  0.7 1.0 %slice_bitcast_fusion.9 = (bf16[3,3,32,32]{3,2,1,0:T(8,128)(2,1)S(1)}, bf16[3,3,32,32]{3,2,1,0:T(8,128)(2,1)S(1)}, bf16[3,3,32,32]{3,2,1,0:T(8,128)(2,1)S(1)}) fusion(bf16[3,3,3,32,32]{4,3,2,1,0:T(8,128)(2,1)} %param.11), kind=kLoop, calls=%fused_computation.140 | loop fusion | bytes 110592 | tf_op jit(solution)/shard_map/squeeze | solution.py:34
  1.7 0.0 copy-start.6
  1.7 0.3 fusion.19
  2.1 0.0 copy-done.7
  2.1 0.0 copy-done.11
  2.1 0.0 copy-done.9
  2.1 0.1 fusion.110
  2.2 0.1 fusion.111
  2.3 0.0 copy-done.5
  2.3 0.2 copy-done.6
  2.5 0.8 %maximum_bitcast_fusion.p_ref = f32[16,10,256]{2,1,0:T(8,128)} fusion(f32[1,16,1,256]{3,2,1,0:T(1,128)S(1)} %get-tuple-element.29, f32[1,16,4,256]{3,2,1,0:T(4,128)S(1)} %multiply_bitcast_fusion, f32[1,16,1,256]{3,2,1,0:T(1,128)S(1)} %get-tuple-element.30, f32[1,16,4,256]{3,2,1,0:T(4,128)S(1)} %convert_bitcast_fusion), kind=kLoop, calls=%fused_computation.57 | loop fusion | flops 122880 | bytes 327680 | tf_op jit(solution)/shard_map/reshape | solution.py:170
  3.3 14.1 %shard_map.113 = (bf16[22,46,128]{2,1,0:T(8,128)(2,1)}, f32[16,10,256]{2,1,0:T(8,128)}) custom-call(bf16[8,32,128]{2,1,0:T(8,128)(2,1)} %x_ref.1, f32[16,10,256]{2,1,0:T(8,128)} %maximum_bitcast_fusion.p_ref), custom_call_target="tpu_custom_call" | custom-call | tf_op jit(solution)/shard_map/pallas_call | solution.py:313
  17.4 2.8 %fusion.4 = f32[1,20,44,128]{3,0,2,1:T(1,128)S(1)} fusion(bf16[3,3,128,128]{3,2,1,0:T(8,128)(2,1)S(1)} %fusion.19, bf16[1,22,46,128]{3,2,1,0:T(8,128)(2,1)} %bitcast.132), kind=kOutput, calls=%fused_computation.12 | convolution fusion | flops 259522560 | bytes 1004544 | tf_op jit(solution)/shard_map/conv_general_dilated | solution.py:64
  20.2 0.0 copy-start.2
  20.2 0.8 %convert_reduce_fusion = f32[10,22,128]{2,1,0:T(8,128)S(1)} fusion(f32[10,2,22,2,128]{4,3,2,1,0:T(2,128)S(1)} %bitcast.115), kind=kLoop, calls=%fused_computation.24 | loop fusion | flops 1210880 | bytes 563200 | tf_op jit(solution)/shard_map/reduce_sum | solution.py:106
  21.1 0.1 fusion.104
  21.2 0.0 copy-done.2
  21.2 0.3 maximum_maximum_fusion
  21.5 0.0 copy-start.10
  21.5 0.7 %fusion.93 = f32[1,8,20,256]{3,0,2,1:T(1,128)S(1)} fusion(bf16[3,3,128,256]{3,2,1,0:T(8,128)(2,1)S(1)} %maximum_maximum_fusion, bf16[1,10,22,128]{3,2,1,0:T(8,128)(2,1)S(1)} %fusion.104), kind=kOutput, calls=%fused_computation.125 | convolution fusion | flops 94371840 | bytes 809984 | tf_op jit(solution)/shard_map/conv_general_dilated | solution.py:64
  22.3 0.1 fusion.74
  22.3 0.0 copy-done.10
  22.4 0.1 copy.89
  22.5 0.2 fusion.96
  22.7 0.1 broadcast_in_dim.77
  22.8 0.2 reshape.147
  23.0 0.1 fusion.7
  23.1 0.0 copy-start.3
  23.1 0.1 select_bitcast_fusion.1
  23.2 0.8 %copy-done.3 = bf16[3,3,3,32,32]{4,3,2,1,0:T(8,128)(2,1)S(1)} copy-done((bf16[3,3,3,32,32]{4,3,2,1,0:T(8,128)(2,1)S(1)}, bf16[3,3,3,32,32]{4,3,2,1,0:T(8,128)(2,1)}, u32[]{:S(2)}) %copy-start.3) | copy-done | bytes 55320
  24.0 0.3 fusion.22
  24.4 0.0 copy-start.1
  24.4 0.7 %fusion.52 = f32[1,8,32,128]{3,0,2,1:T(1,128)S(1)} fusion(bf16[3,3,128,128]{3,2,1,0:T(8,128)(2,1)S(1)} %fusion.22, bf16[1,10,34,128]{3,2,1,0:T(8,128)(2,1)S(1)} %select_bitcast_fusion.1), kind=kOutput, calls=%fused_computation.81 | convolution fusion | flops 75497472 | bytes 513024 | tf_op jit(solution)/shard_map/conv_general_dilated | solution.py:64
  25.0 0.0 copy-start
  25.1 0.1 copy-done.1
  25.2 0.7 %fusion.89 = f32[8,32,128]{2,1,0:T(8,128)} fusion(f32[8,32,128]{2,1,0:T(8,128)S(1)} %bitcast.123, bf16[8,32,128]{2,1,0:T(8,128)(2,1)S(1)} %copy-done.1), kind=kLoop, calls=%fused_computation.117 | loop fusion | flops 327680 | bytes 327680 | tf_op jit(solution)/shard_map/add | solution.py:407
  25.9 15.7 %shard_map.114 = (f32[256,128]{1,0:T(8,128)}, bf16[18,42,128]{2,1,0:T(8,128)(2,1)}, f32[16,1,256]{2,1,0:T(1,128)}) custom-call(f32[16,10,256]{2,1,0:T(8,128)} %get-tuple-element.7.got_ref, f32[256,128]{1,0:T(8,128)} %bitcast.125, f32[256,128]{1,0:T(8,128)} %bitcast.124), custom_call_target="tpu_custom_call" | custom-call | tf_op jit(solution)/shard_map/pallas_call | solution.py:341
  41.7 1.0 %pad.2 = bf16[18,1,48,128]{3,2,0,1:T(8,128)(2,1)S(1)} pad(bf16[18,1,42,128]{3,2,0,1:T(8,128)(2,1)} %bitcast.127, bf16[]{:T(256)} %constant.25.clone.1), padding=0_0x0_0x0_6x0_0 | pad | bytes 414722 | tf_op jit(solution)/shard_map/broadcast_in_dim | solution.py:79
  42.6 0.0 copy-start.13
  42.6 0.1 reshape.154
  42.8 0.5 %copy-done.13 = pred[8,6]{0,1:T(8,128)(4,1)S(1)} copy-done((pred[8,6]{0,1:T(8,128)(4,1)S(1)}, pred[8,6]{0,1:T(8,128)(4,1)}, u32[]{:S(2)}) %copy-start.13) | copy-done | bytes 72
  43.3 0.6 %convolution_select_fusion = f32[16,8,6,128]{3,1,2,0:T(8,128)S(1)} fusion(bf16[3,3,128,128]{3,2,1,0:T(8,128)(2,1)S(1)} %fusion.22, bf16[18,1,7,2,128]{4,2,3,0,1:T(8,128)(2,1)S(1)} %slice.91, bf16[18,1,8,6,128]{4,2,3,0,1:T(8,128)(2,1)S(1)} %copy.99, pred[8,6]{0,1:T(8,128)(4,1)S(1)} %copy-done.13), kind=kOutput, calls=%fused_computation | convolution fusion | flops 227475456 | bytes 973872 | tf_op jit(solution)/shard_map/conv_general_dilated | solution.py:78
  43.9 0.1 copy.100
  44.1 0.1 copy.149
  44.2 0.2 reduce_sum.19
  44.5 0.0 copy-start.14
  44.5 0.3 fusion.2
  44.9 0.3 copy-done.14
  45.2 0.3 convolution_select_fusion.2
  45.6 0.1 broadcast_in_dim.84
  45.7 0.2 reshape.150
  45.8 0.0 copy-start.12
  45.8 0.2 select_bitcast_fusion
  46.2 0.3 copy-done.12
  46.5 0.4 convolution_select_fusion.1
  46.9 0.0 copy-start.8
  46.9 0.5 copy-done.4
  47.4 0.1 fusion.90
  47.5 0.7 %copy.110 = f32[8,32,128]{2,1,0:T(8,128)} copy(f32[8,32,128]{2,0,1:T(8,128)S(1)} %fusion.90) | data formatting | bytes 262144
  48.2 0.6 %copy.111 = f32[1,16,256]{2,1,0:T(8,128)} copy(f32[1,16,256]{2,0,1:T(1,128)S(1)} %bitcast.129) | data formatting | bytes 32768
  (32 shorter events, 0.5 us)
Async XLA Ops:
  0.6 1.5 %copy-start.11 = (s32[1,16]{1,0:T(1,128)S(1)}, s32[1,16]{1,0:T(1,128)}, u32[]{:S(2)}) copy-start(s32[1,16]{1,0:T(1,128)} %param.19) | copy-start | bytes 196
  0.6 1.4 %copy-start.7 = (s32[1,16,256]{2,1,0:T(8,128)S(1)}, s32[1,16,256]{2,1,0:T(8,128)}, u32[]{:S(2)}) copy-start(s32[1,16,256]{2,1,0:T(8,128)} %param.16) | copy-start | bytes 49156
  0.7 1.5 %copy-start.9 = (f32[1,16,256]{2,1,0:T(8,128)S(1)}, f32[1,16,256]{2,1,0:T(8,128)}, u32[]{:S(2)}) copy-start(f32[1,16,256]{2,1,0:T(8,128)} %param.18) | copy-start | bytes 49156
  0.7 1.6 %copy-start.5 = (f32[1,16,256,4]{2,3,1,0:T(4,128)S(1)}, f32[1,16,256,4]{2,3,1,0:T(4,128)}, u32[]{:S(2)}) copy-start(f32[1,16,256,4]{2,3,1,0:T(4,128)} %param.17) | copy-start | bytes 196612
  1.7 0.8 %copy-start.6 = (s32[1,16,256,4]{2,3,1,0:T(4,128)S(1)}, s32[1,16,256,4]{2,3,1,0:T(4,128)}, u32[]{:S(2)}) copy-start(s32[1,16,256,4]{2,3,1,0:T(4,128)} %param.15) | copy-start | bytes 196612
  20.2 1.0 %copy-start.2 = (bf16[3,3,3,32,64]{4,3,2,1,0:T(8,128)(2,1)S(1)}, bf16[3,3,3,32,64]{4,3,2,1,0:T(8,128)(2,1)}, u32[]{:S(2)}) copy-start(bf16[3,3,3,32,64]{4,3,2,1,0:T(8,128)(2,1)} %param.12) | copy-start | bytes 331780
  21.5 0.8 %copy-start.10 = (bf16[64,32]{0,1:T(8,128)(2,1)S(1)}, bf16[64,32]{0,1:T(8,128)(2,1)}, u32[]{:S(2)}) copy-start(bf16[64,32]{0,1:T(8,128)(2,1)} %param.14) | copy-start | bytes 12292
  23.1 0.9 %copy-start.3 = (bf16[3,3,3,32,32]{4,3,2,1,0:T(8,128)(2,1)S(1)}, bf16[3,3,3,32,32]{4,3,2,1,0:T(8,128)(2,1)}, u32[]{:S(2)}) copy-start(bf16[3,3,3,32,32]{4,3,2,1,0:T(8,128)(2,1)} %param.13) | copy-start | bytes 165892
  24.4 0.8 %copy-start.1 = (bf16[8,32,128]{2,1,0:T(8,128)(2,1)S(1)}, bf16[8,32,128]{2,1,0:T(8,128)(2,1)}, u32[]{:S(2)}) copy-start(bf16[8,32,128]{2,1,0:T(8,128)(2,1)} %x_ref.1) | copy-start | bytes 196612
  25.0 0.9 %copy-start = (f32[1,8,32,128]{3,0,2,1:T(1,128)}, f32[1,8,32,128]{3,0,2,1:T(1,128)S(1)}, u32[]{:S(2)}) copy-start(f32[1,8,32,128]{3,0,2,1:T(1,128)S(1)} %fusion.52) | copy-start | bytes 393220
  42.6 0.7 %copy-start.13 = (pred[8,6]{0,1:T(8,128)(4,1)S(1)}, pred[8,6]{0,1:T(8,128)(4,1)}, u32[]{:S(2)}) copy-start(pred[8,6]{0,1:T(8,128)(4,1)} %constant.92) | copy-start | bytes 148
  44.5 0.7 %copy-start.14 = (pred[8,3]{0,1:T(4,128)(4,1)S(1)}, pred[8,3]{0,1:T(4,128)(4,1)}, u32[]{:S(2)}) copy-start(pred[8,3]{0,1:T(4,128)(4,1)} %constant.93) | copy-start | bytes 76
  45.8 0.7 %copy-start.12 = (pred[8,5]{0,1:T(8,128)(4,1)S(1)}, pred[8,5]{0,1:T(8,128)(4,1)}, u32[]{:S(2)}) copy-start(pred[8,5]{0,1:T(8,128)(4,1)} %constant.45) | copy-start | bytes 124
  46.5 0.9 %copy-start.4 = (f32[256,128]{1,0:T(8,128)S(1)}, f32[256,128]{1,0:T(8,128)}, u32[]{:S(2)}) copy-start(f32[256,128]{1,0:T(8,128)} %get-tuple-element.9) | copy-start | bytes 393220
  46.9 1.3 %copy-start.8 = (f32[16,1,256]{2,1,0:T(1,128)S(1)}, f32[16,1,256]{2,1,0:T(1,128)}, u32[]{:S(2)}) copy-start(f32[16,1,256]{2,1,0:T(1,128)} %get-tuple-element.11) | copy-start | bytes 49156

commit v15 on v14

--- a/solution.py
+++ b/solution.py
@@ -28,13 +28,15 @@
 
 
 def banded(kernel, levels):
-    zero = jnp.zeros(kernel.shape[:2] + kernel.shape[3:], kernel.dtype)
-    rows = []
-    for p in range(levels):
-        blocks = [kernel[:, :, p - q + 1] if 0 <= p - q + 1 < 3 else zero for q in range(levels)]
-        rows.append(jnp.concatenate(blocks, axis=-1))
-    full = jnp.concatenate(rows, axis=-2)
-    return full.reshape(9, full.shape[2], full.shape[3])
+    lin = jnp.arange(levels, dtype=jnp.int32)
+    taps = jnp.arange(3, dtype=jnp.int32)
+    select = (lin[:, None, None] - lin[None, :, None] + 1 == taps[None, None, :]).astype(
+        kernel.dtype
+    )
+    full = jnp.einsum("pqt,abtcg->abpcqg", select, kernel, preferred_element_type=jnp.float32)
+    cin = kernel.shape[3]
+    cout = kernel.shape[4]
+    return full.reshape(9, levels * cin, levels * cout).astype(kernel.dtype)
 
 
 def block_diagonal(matrix, levels):

time: 49.2 us -> 55.2 us (1.12)
  other arithmetic: 4.41 us -> 7.22 us
  local copies, waits for them, and re-layouts: 7.42 us -> 9.66 us
  matrix products: 5.97 us -> 6.71 us
    convert_element_type x0 -> x6, local copies, waits for them, and re-layouts: none -> 3.38 us  [banded(): return full.reshape(9, levels * cin, levels * cout).astype(kernel.dtype)]
    dot_general x0 -> x3, matrix products: none -> 1.69 us  [banded(): jnp.einsum('pqt,abtcg->abpcqg', select, kernel, preferred_element_type=jn...]
    squeeze x3 -> x0, local copies, waits for them, and re-layouts: 1.04 us -> none  [banded(): kernel[:, :, p - q + 1]]
    concatenate x3 -> x0, other arithmetic: 0.99 us -> none  [banded(): full = jnp.concatenate(rows, axis=-2)]
    conv_general_dilated x3, matrix products: 4.13 us -> 3.19 us  [conv_valid(): lax.conv_general_dilated(padded[None], taps, (1, 1), 'VALID', dimension_n...]
    transpose x1, other arithmetic: 0.02 us -> 0.86 us  [pack(): jnp.swapaxes(weights, 2, 3)]
    convert_element_type x1, other arithmetic: 0.01 us -> 0.85 us  [pack(): jnp.swapaxes(obs_cells, 2, 3).astype(jnp.float32)]
    convert_element_type x1, other arithmetic: 0.01 us -> 0.73 us  [pack(): obs_chan[:, :, None, :].astype(jnp.float32)]
where the time goes in v15:
time: 55.2 us; the launch traced here: 54.6 us
  Pallas kernels  29.8 us (54%)
  local copies, waits for them, and re-layouts  9.66 us (18%)
  other arithmetic  7.22 us (13%)
  matrix products  6.71 us (12%)
  between operations  1.15 us (2%)
    pallas_call x1, Pallas kernels, observe_and_exchange(): pl.pallas_call(functools.partial(back_kernel, width, nlat, nlon), out_sha...  15.7 us
    pallas_call x1, Pallas kernels, exchange(): pl.pallas_call(functools.partial(halo_kernel, width, nlat, nlon), out_sha...  14.1 us
    unnamed x24, local copies, waits for them, and re-layouts  4.2 us
    convert_element_type x6, local copies, waits for them, and re-layouts, banded(): return full.reshape(9, levels * cin, levels * cout).astype(kernel.dtype)  3.38 us
    conv_general_dilated x3, matrix products, conv_valid(): lax.conv_general_dilated(padded[None], taps, (1, 1), 'VALID', dimension_n...  3.19 us
    dot_general x3, matrix products, banded(): jnp.einsum('pqt,abtcg->abpcqg', select, kernel, preferred_element_type=jn...  1.69 us
    conv_general_dilated x3, matrix products, adjoint_valid(): lax.conv_general_dilated(padded[None], taps, (1, 1), 'VALID', dimension_n...  1.33 us

profile of v15, /device:TPU:1, one launch (start us, length us, event | category | flops | bytes accessed | tf_op | source)
XLA Modules:
  0.0 54.6 jit_solution(6520915240578401573)
XLA Ops:
  0.6 0.0 copy-start.1
  0.7 0.8 %copy.78 = bf16[64,32]{1,0:T(8,128)(2,1)S(1)} copy(bf16[64,32]{0,1:T(8,128)(2,1)} %param.14) | data formatting | bytes 8192 | tf_op args[4]
  1.5 0.7 %convert_element_type.140 = f32[1,16,256]{2,1,0:T(8,128)S(1)} convert(s32[1,16,256]{2,1,0:T(8,128)} %param.16) | non-fusion elementwise | flops 4096 | bytes 32768 | tf_op jit(solution)/shard_map/convert_element_type | solution.py:166
  2.3 0.7 %fusion.108 = f32[16,256]{1,0:T(8,128)S(1)} fusion(s32[16]{0:T(128)} %bitcast.116), kind=kLoop, calls=%fused_computation.140 | loop fusion | flops 8192 | bytes 16448 | tf_op jit(solution)/shard_map/convert_element_type | solution.py:160
  3.0 0.8 %fusion.107 = (f32[1,16,1,256]{3,2,1,0:T(1,128)S(1)}, f32[1,16,1,256]{3,2,1,0:T(1,128)S(1)}) fusion(f32[1,16,256]{2,1,0:T(8,128)} %param.18, s32[16]{0:T(128)} %bitcast.117, f32[1,16,256]{2,1,0:T(8,128)S(1)} %convert_element_type.140), kind=kLoop, calls=%fused_computation.137 | loop fusion | flops 8192 | bytes 65600 | tf_op jit(solution)/shard_map/broadcast_in_dim | solution.py:168
  3.8 0.9 %multiply_bitcast_fusion = f32[1,16,4,256]{3,2,1,0:T(4,128)S(1)} fusion(f32[1,16,256,4]{2,3,1,0:T(4,128)} %param.17, f32[16,256]{1,0:T(8,128)S(1)} %fusion.108), kind=kLoop, calls=%fused_computation.129 | loop fusion | flops 16384 | bytes 147456 | tf_op jit(solution)/shard_map/transpose | solution.py:167
  4.7 0.9 %convert_bitcast_fusion = f32[1,16,4,256]{3,2,1,0:T(4,128)S(1)} fusion(s32[1,16,256,4]{2,3,1,0:T(4,128)} %param.15), kind=kLoop, calls=%fused_computation.130 | loop fusion | flops 16384 | bytes 131072 | tf_op jit(solution)/shard_map/convert_element_type | solution.py:165
  5.5 0.8 %maximum_bitcast_fusion.p_ref = f32[16,10,256]{2,1,0:T(8,128)} fusion(f32[1,16,1,256]{3,2,1,0:T(1,128)S(1)} %get-tuple-element.20, f32[1,16,4,256]{3,2,1,0:T(4,128)S(1)} %multiply_bitcast_fusion, f32[1,16,1,256]{3,2,1,0:T(1,128)S(1)} %get-tuple-element.21, f32[1,16,4,256]{3,2,1,0:T(4,128)S(1)} %convert_bitcast_fusion), kind=kLoop, calls=%fused_computation.48 | loop fusion | flops 122880 | bytes 327680 | tf_op jit(solution)/shard_map/reshape | solution.py:172
  6.3 14.1 %shard_map.113 = (bf16[22,46,128]{2,1,0:T(8,128)(2,1)}, f32[16,10,256]{2,1,0:T(8,128)}) custom-call(bf16[8,32,128]{2,1,0:T(8,128)(2,1)} %x_ref.1, f32[16,10,256]{2,1,0:T(8,128)} %maximum_bitcast_fusion.p_ref), custom_call_target="tpu_custom_call" | custom-call | tf_op jit(solution)/shard_map/pallas_call | solution.py:315
  20.4 0.0 copy-done.1
  20.4 0.6 %fusion.1 = bf16[3,3,4,32,4,64]{5,4,3,1,0,2:T(4,128)(2,1)S(1)} fusion(bf16[3,3,3,32,64]{4,3,2,1,0:T(8,128)(2,1)S(1)} %copy-done.1, s32[4,4]{1,0:T(4,128)S(1)} %subtract_add_fusion), kind=kOutput, calls=%fused_computation.4 | convolution fusion | flops 2064432 | bytes 700480 | tf_op jit(solution)/shard_map/pqt,abtcg->abpcqg/dot_general | solution.py:36
  21.0 0.5 copy.75
  21.5 0.0 copy-start.2
  21.5 0.7 %convert_element_type.131 = bf16[3,3,128,256]{3,2,1,0:T(8,128)(2,1)S(1)} reshape(bf16[3,3,4,32,4,64]{5,4,3,2,1,0:T(4,128)(2,1)S(1)} %copy.75) | data formatting | bytes 1179648 | tf_op jit(solution)/shard_map/convert_element_type | solution.py:39
  22.2 0.2 copy-done.2
  22.4 0.6 %fusion.2 = bf16[3,3,4,32,4,32]{5,4,3,1,0,2:T(4,128)(2,1)S(1)} fusion(bf16[3,3,3,32,32]{4,3,2,1,0:T(8,128)(2,1)S(1)} %copy-done.2, s32[4,4]{1,0:T(4,128)S(1)} %subtract_add_fusion), kind=kOutput, calls=%fused_computation.5 | convolution fusion | flops 1032240 | bytes 350272 | tf_op jit(solution)/shard_map/pqt,abtcg->abpcqg/dot_general | solution.py:36
  23.0 0.5 copy.84
  23.5 0.0 copy-start.3
  23.5 0.6 %convert_element_type.136 = bf16[3,3,128,128]{3,2,1,0:T(8,128)(2,1)S(1)} reshape(bf16[3,3,4,32,4,32]{5,4,3,2,1,0:T(4,128)(2,1)S(1)} %copy.84) | data formatting | bytes 589824 | tf_op jit(solution)/shard_map/convert_element_type | solution.py:39
  24.1 0.3 copy-done.3
  24.4 0.6 %fusion = bf16[3,3,4,32,4,32]{5,4,3,1,0,2:T(4,128)(2,1)S(1)} fusion(bf16[3,3,3,32,32]{4,3,2,1,0:T(8,128)(2,1)S(1)} %copy-done.3, s32[4,4]{1,0:T(4,128)S(1)} %subtract_add_fusion), kind=kOutput, calls=%fused_computation.3 | convolution fusion | flops 1032240 | bytes 350272 | tf_op jit(solution)/shard_map/pqt,abtcg->abpcqg/dot_general | solution.py:36
  25.0 0.5 copy.72
  25.5 0.0 copy-start.6
  25.5 0.6 %convert_element_type.122 = bf16[3,3,128,128]{3,2,1,0:T(8,128)(2,1)S(1)} reshape(bf16[3,3,4,32,4,32]{5,4,3,2,1,0:T(4,128)(2,1)S(1)} %copy.72) | data formatting | bytes 589824 | tf_op jit(solution)/shard_map/convert_element_type | solution.py:39
  26.1 0.4 copy-done.6
  26.5 1.8 %fusion.7 = f32[1,20,44,128]{3,0,2,1:T(1,128)S(1)} fusion(bf16[3,3,128,128]{3,2,1,0:T(8,128)(2,1)S(1)} %convert_element_type.122, bf16[1,22,46,128]{3,2,1,0:T(8,128)(2,1)S(1)} %bitcast.118), kind=kOutput, calls=%fused_computation.17 | convolution fusion | flops 259522560 | bytes 1004544 | tf_op jit(solution)/shard_map/conv_general_dilated | solution.py:66
  28.3 0.8 %convert_reduce_fusion = f32[10,22,128]{2,1,0:T(8,128)S(1)} fusion(f32[10,2,22,2,128]{4,3,2,1,0:T(2,128)S(1)} %bitcast.101), kind=kLoop, calls=%fused_computation.29 | loop fusion | flops 1210880 | bytes 563200 | tf_op jit(solution)/shard_map/reduce_sum | solution.py:108
  29.2 0.1 fusion.101
  29.3 0.7 %fusion.90 = f32[1,8,20,256]{3,0,2,1:T(1,128)S(1)} fusion(bf16[3,3,128,256]{3,2,1,0:T(8,128)(2,1)S(1)} %convert_element_type.131, bf16[1,10,22,128]{3,2,1,0:T(8,128)(2,1)S(1)} %fusion.101), kind=kOutput, calls=%fused_computation.116 | convolution fusion | flops 94371840 | bytes 809984 | tf_op jit(solution)/shard_map/conv_general_dilated | solution.py:66
  30.0 0.1 fusion.71
  30.1 0.2 fusion.93
  30.3 0.1 broadcast_in_dim.86
  30.4 0.2 reshape.179
  30.5 0.1 fusion.10
  30.6 0.0 copy-start.4
  30.7 0.1 select_bitcast_fusion.1
  30.8 0.7 %fusion.49 = f32[1,8,32,128]{3,0,2,1:T(1,128)S(1)} fusion(bf16[3,3,128,128]{3,2,1,0:T(8,128)(2,1)S(1)} %convert_element_type.136, bf16[1,10,34,128]{3,2,1,0:T(8,128)(2,1)S(1)} %select_bitcast_fusion.1), kind=kOutput, calls=%fused_computation.72 | convolution fusion | flops 75497472 | bytes 513024 | tf_op jit(solution)/shard_map/conv_general_dilated | solution.py:66
  31.5 0.0 copy-start
  31.5 0.0 copy-done.4
  31.5 0.0 copy-start.8
  31.5 0.7 %fusion.86 = f32[8,32,128]{2,1,0:T(8,128)} fusion(f32[8,32,128]{2,1,0:T(8,128)S(1)} %bitcast.109, bf16[8,32,128]{2,1,0:T(8,128)(2,1)S(1)} %copy-done.4), kind=kLoop, calls=%fused_computation.108 | loop fusion | flops 327680 | bytes 327680 | tf_op jit(solution)/shard_map/add | solution.py:409
  32.2 0.0 copy-done
  32.2 15.7 %shard_map.114 = (f32[256,128]{1,0:T(8,128)}, bf16[18,42,128]{2,1,0:T(8,128)(2,1)}, f32[16,1,256]{2,1,0:T(1,128)}) custom-call(f32[16,10,256]{2,1,0:T(8,128)} %get-tuple-element.7.got_ref, f32[256,128]{1,0:T(8,128)} %bitcast.111, f32[256,128]{1,0:T(8,128)} %bitcast.110), custom_call_target="tpu_custom_call" | custom-call | tf_op jit(solution)/shard_map/pallas_call | solution.py:343
  48.0 1.0 %pad.2 = bf16[18,1,48,128]{3,2,0,1:T(8,128)(2,1)S(1)} pad(bf16[18,1,42,128]{3,2,0,1:T(8,128)(2,1)} %bitcast.113, bf16[]{:T(256)} %constant.35.clone.1), padding=0_0x0_0x0_6x0_0 | pad | bytes 414722 | tf_op jit(solution)/shard_map/broadcast_in_dim | solution.py:81
  48.9 1.3 %copy.99 = f32[1,16,256]{2,1,0:T(8,128)} copy(f32[1,16,256]{2,0,1:T(1,128)} %bitcast.115) | data formatting | bytes 32768
  50.3 0.1 reshape.186
  50.4 0.0 copy-done.8
  50.4 0.6 %convolution_select_fusion = f32[16,8,6,128]{3,1,2,0:T(8,128)S(1)} fusion(bf16[3,3,128,128]{3,2,1,0:T(8,128)(2,1)S(1)} %convert_element_type.136, bf16[18,1,7,2,128]{4,2,3,0,1:T(8,128)(2,1)S(1)} %slice.34, bf16[18,1,8,6,128]{4,2,3,0,1:T(8,128)(2,1)S(1)} %copy.87, pred[8,6]{0,1:T(8,128)(4,1)S(1)} %copy-done.8), kind=kOutput, calls=%fused_computation.6 | convolution fusion | flops 227475456 | bytes 973872 | tf_op jit(solution)/shard_map/conv_general_dilated | solution.py:80
  51.1 0.1 copy.88
  51.2 0.1 copy.141
  51.3 0.0 copy-start.9
  51.4 0.2 reduce_sum.19
  51.6 0.3 fusion.5
  52.0 0.0 copy-done.9
  52.0 0.3 convolution_select_fusion.2
  52.4 0.0 copy-start.7
  52.5 0.1 broadcast_in_dim.93
  52.5 0.2 reshape.182
  52.7 0.2 select_bitcast_fusion
  53.0 0.1 copy-done.7
  53.1 0.4 convolution_select_fusion.1
  53.5 0.3 copy-done.5
  53.8 0.1 fusion.87
  53.9 0.7 %copy.98 = f32[8,32,128]{2,1,0:T(8,128)} copy(f32[8,32,128]{2,0,1:T(8,128)S(1)} %fusion.87) | data formatting | bytes 262144
  (23 shorter events, 0.4 us)
Async XLA Ops:
  0.6 19.8 %copy-start.1 = (bf16[3,3,3,32,64]{4,3,2,1,0:T(8,128)(2,1)S(1)}, bf16[3,3,3,32,64]{4,3,2,1,0:T(8,128)(2,1)}, u32[]{:S(2)}) copy-start(bf16[3,3,3,32,64]{4,3,2,1,0:T(8,128)(2,1)} %param.12) | copy-start | bytes 331780
  21.5 0.9 %copy-start.2 = (bf16[3,3,3,32,32]{4,3,2,1,0:T(8,128)(2,1)S(1)}, bf16[3,3,3,32,32]{4,3,2,1,0:T(8,128)(2,1)}, u32[]{:S(2)}) copy-start(bf16[3,3,3,32,32]{4,3,2,1,0:T(8,128)(2,1)} %param.13) | copy-start | bytes 165892
  23.5 0.9 %copy-start.3 = (bf16[3,3,3,32,32]{4,3,2,1,0:T(8,128)(2,1)S(1)}, bf16[3,3,3,32,32]{4,3,2,1,0:T(8,128)(2,1)}, u32[]{:S(2)}) copy-start(bf16[3,3,3,32,32]{4,3,2,1,0:T(8,128)(2,1)} %param.11) | copy-start | bytes 165892
  25.5 1.0 %copy-start.6 = (bf16[22,46,128]{2,1,0:T(8,128)(2,1)S(1)}, bf16[22,46,128]{2,1,0:T(8,128)(2,1)}, u32[]{:S(2)}) copy-start(bf16[22,46,128]{2,1,0:T(8,128)(2,1)} %get-tuple-element.8) | copy-start | bytes 777220
  30.6 0.9 %copy-start.4 = (bf16[8,32,128]{2,1,0:T(8,128)(2,1)S(1)}, bf16[8,32,128]{2,1,0:T(8,128)(2,1)}, u32[]{:S(2)}) copy-start(bf16[8,32,128]{2,1,0:T(8,128)(2,1)} %x_ref.1) | copy-start | bytes 196612
  31.5 0.7 %copy-start = (f32[1,8,32,128]{3,0,2,1:T(1,128)}, f32[1,8,32,128]{3,0,2,1:T(1,128)S(1)}, u32[]{:S(2)}) copy-start(f32[1,8,32,128]{3,0,2,1:T(1,128)S(1)} %fusion.49) | copy-start | bytes 393220
  31.5 18.9 %copy-start.8 = (pred[8,6]{0,1:T(8,128)(4,1)S(1)}, pred[8,6]{0,1:T(8,128)(4,1)}, u32[]{:S(2)}) copy-start(pred[8,6]{0,1:T(8,128)(4,1)} %constant.91) | copy-start | bytes 148
  51.3 0.7 %copy-start.9 = (pred[8,3]{0,1:T(4,128)(4,1)S(1)}, pred[8,3]{0,1:T(4,128)(4,1)}, u32[]{:S(2)}) copy-start(pred[8,3]{0,1:T(4,128)(4,1)} %constant.92) | copy-start | bytes 76
  52.4 0.7 %copy-start.7 = (pred[8,5]{0,1:T(8,128)(4,1)S(1)}, pred[8,5]{0,1:T(8,128)(4,1)}, u32[]{:S(2)}) copy-start(pred[8,5]{0,1:T(8,128)(4,1)} %constant.90) | copy-start | bytes 124
  52.9 0.9 %copy-start.5 = (f32[256,128]{1,0:T(8,128)S(1)}, f32[256,128]{1,0:T(8,128)}, u32[]{:S(2)}) copy-start(f32[256,128]{1,0:T(8,128)} %get-tuple-element.9) | copy-start | bytes 393220

commit v16 on v14

--- a/solution.py
+++ b/solution.py
@@ -222,6 +222,18 @@
     dst_rows = {1: pl.ds(0, width), -1: pl.ds(width + rows, width), 0: pl.ds(width, rows)}
     src_cols = {1: pl.ds(cols - edge, edge), -1: pl.ds(0, edge), 0: pl.ds(0, cols)}
     dst_cols = {1: pl.ds(0, edge), -1: pl.ds(edge + cols, edge), 0: pl.ds(edge, cols)}
+    sends = []
+    for t in range(nlon):
+        copy = pltpu.make_async_remote_copy(
+            src_ref=p_ref.at[pl.ds(t, 1)],
+            dst_ref=inbox.at[pl.ds(j, 1)],
+            send_sem=p_send.at[t],
+            recv_sem=p_recv.at[j],
+            device_id=(i, t),
+            device_id_type=mesh,
+        )
+        sends.append(copy)
+        pl.when(t != j)(copy.start)
     copies = []
     for k, (a, b) in enumerate(dirs):
         copy = pltpu.make_async_remote_copy(
@@ -234,18 +246,6 @@
         )
         copies.append((a, copy))
         pl.when(has[a])(copy.start)
-    sends = []
-    for t in range(nlon):
-        copy = pltpu.make_async_remote_copy(
-            src_ref=p_ref.at[pl.ds(t, 1)],
-            dst_ref=inbox.at[pl.ds(j, 1)],
-            send_sem=p_send.at[t],
-            recv_sem=p_recv.at[j],
-            device_id=(i, t),
-            device_id_type=mesh,
-        )
-        sends.append(copy)
-        pl.when(t != j)(copy.start)
     for a, copy in copies:
         pl.when(has[a])(copy.wait_send)
         pl.when(has[-a])(copy.wait_recv)

time: 49.2 us -> 48 us (0.976)
  the two profiles are of different devices: /device:TPU:1 before, /device:TPU:0 now
where the time goes in v16:
time: 48 us; the launch traced here: 47.5 us
  Pallas kernels  28.5 us (59%)
  local copies, waits for them, and re-layouts  7.42 us (15%)
  matrix products  5.97 us (12%)
  other arithmetic  4.41 us (9%)
  between operations  1.18 us (2%)
    pallas_call x1, Pallas kernels, exchange(): pl.pallas_call(functools.partial(halo_kernel, width, nlat, nlon), out_sha...  15.4 us
    pallas_call x1, Pallas kernels, observe_and_exchange(): pl.pallas_call(functools.partial(back_kernel, width, nlat, nlon), out_sha...  13.1 us
    unnamed x34, local copies, waits for them, and re-layouts  4.26 us
    conv_general_dilated x3, matrix products, conv_valid(): lax.conv_general_dilated(padded[None], taps, (1, 1), 'VALID', dimension_n...  4.13 us
    conv_general_dilated x3, matrix products, adjoint_valid(): lax.conv_general_dilated(padded[None], taps, (1, 1), 'VALID', dimension_n...  1.33 us
    reduce_sum x2, other arithmetic, block_sum(): return fine.reshape(rows // 2, 2, cols // 2, 2, feats).sum(axis=(1, 3))  1.08 us
    squeeze x3, local copies, waits for them, and re-layouts, banded(): kernel[:, :, p - q + 1]  1.04 us
    broadcast_in_dim x3, local copies, waits for them, and re-layouts, adjoint_valid(): padded[None]  0.99 us

profile of v16, /device:TPU:0, one launch (start us, length us, event | category | flops | bytes accessed | tf_op | source)
XLA Modules:
  0.0 47.5 jit_solution(14467056385815725835)
XLA Ops:
  0.6 0.0 copy-start.11
  0.6 0.0 copy-start.7
  0.7 0.0 copy-start.9
  0.7 0.0 copy-start.5
  0.7 1.0 %slice_bitcast_fusion.9 = (bf16[3,3,32,32]{3,2,1,0:T(8,128)(2,1)S(1)}, bf16[3,3,32,32]{3,2,1,0:T(8,128)(2,1)S(1)}, bf16[3,3,32,32]{3,2,1,0:T(8,128)(2,1)S(1)}) fusion(bf16[3,3,3,32,32]{4,3,2,1,0:T(8,128)(2,1)} %param.11), kind=kLoop, calls=%fused_computation.140 | loop fusion | bytes 110592 | tf_op jit(solution)/shard_map/squeeze | solution.py:34
  1.7 0.0 copy-start.6
  1.7 0.3 fusion.19
  2.1 0.0 copy-done.7
  2.1 0.0 copy-done.11
  2.1 0.0 copy-done.9
  2.1 0.1 fusion.110
  2.2 0.1 fusion.111
  2.3 0.0 copy-done.5
  2.3 0.2 copy-done.6
  2.5 0.8 %maximum_bitcast_fusion.p_ref = f32[16,10,256]{2,1,0:T(8,128)} fusion(f32[1,16,1,256]{3,2,1,0:T(1,128)S(1)} %get-tuple-element.29, f32[1,16,4,256]{3,2,1,0:T(4,128)S(1)} %multiply_bitcast_fusion, f32[1,16,1,256]{3,2,1,0:T(1,128)S(1)} %get-tuple-element.30, f32[1,16,4,256]{3,2,1,0:T(4,128)S(1)} %convert_bitcast_fusion), kind=kLoop, calls=%fused_computation.57 | loop fusion | flops 122880 | bytes 327680 | tf_op jit(solution)/shard_map/reshape | solution.py:170
  3.3 15.4 %shard_map.113 = (bf16[22,46,128]{2,1,0:T(8,128)(2,1)}, f32[16,10,256]{2,1,0:T(8,128)}) custom-call(bf16[8,32,128]{2,1,0:T(8,128)(2,1)} %x_ref.1, f32[16,10,256]{2,1,0:T(8,128)} %maximum_bitcast_fusion.p_ref), custom_call_target="tpu_custom_call" | custom-call | tf_op jit(solution)/shard_map/pallas_call | solution.py:313
  18.8 2.8 %fusion.4 = f32[1,20,44,128]{3,0,2,1:T(1,128)S(1)} fusion(bf16[3,3,128,128]{3,2,1,0:T(8,128)(2,1)S(1)} %fusion.19, bf16[1,22,46,128]{3,2,1,0:T(8,128)(2,1)} %bitcast.132), kind=kOutput, calls=%fused_computation.12 | convolution fusion | flops 259522560 | bytes 1004544 | tf_op jit(solution)/shard_map/conv_general_dilated | solution.py:64
  21.6 0.0 copy-start.2
  21.6 0.8 %convert_reduce_fusion = f32[10,22,128]{2,1,0:T(8,128)S(1)} fusion(f32[10,2,22,2,128]{4,3,2,1,0:T(2,128)S(1)} %bitcast.115), kind=kLoop, calls=%fused_computation.24 | loop fusion | flops 1210880 | bytes 563200 | tf_op jit(solution)/shard_map/reduce_sum | solution.py:106
  22.4 0.1 fusion.104
  22.5 0.0 copy-done.2
  22.6 0.3 maximum_maximum_fusion
  22.9 0.0 copy-start.10
  22.9 0.7 %fusion.93 = f32[1,8,20,256]{3,0,2,1:T(1,128)S(1)} fusion(bf16[3,3,128,256]{3,2,1,0:T(8,128)(2,1)S(1)} %maximum_maximum_fusion, bf16[1,10,22,128]{3,2,1,0:T(8,128)(2,1)S(1)} %fusion.104), kind=kOutput, calls=%fused_computation.125 | convolution fusion | flops 94371840 | bytes 809984 | tf_op jit(solution)/shard_map/conv_general_dilated | solution.py:64
  23.6 0.1 fusion.74
  23.7 0.0 copy-done.10
  23.7 0.1 copy.89
  23.8 0.2 fusion.96
  24.1 0.1 broadcast_in_dim.77
  24.1 0.2 reshape.147
  24.3 0.1 fusion.7
  24.4 0.0 copy-start.3
  24.5 0.1 select_bitcast_fusion.1
  24.6 0.8 %copy-done.3 = bf16[3,3,3,32,32]{4,3,2,1,0:T(8,128)(2,1)S(1)} copy-done((bf16[3,3,3,32,32]{4,3,2,1,0:T(8,128)(2,1)S(1)}, bf16[3,3,3,32,32]{4,3,2,1,0:T(8,128)(2,1)}, u32[]{:S(2)}) %copy-start.3) | copy-done | bytes 55320
  25.4 0.3 fusion.22
  25.7 0.0 copy-start.1
  25.7 0.7 %fusion.52 = f32[1,8,32,128]{3,0,2,1:T(1,128)S(1)} fusion(bf16[3,3,128,128]{3,2,1,0:T(8,128)(2,1)S(1)} %fusion.22, bf16[1,10,34,128]{3,2,1,0:T(8,128)(2,1)S(1)} %select_bitcast_fusion.1), kind=kOutput, calls=%fused_computation.81 | convolution fusion | flops 75497472 | bytes 513024 | tf_op jit(solution)/shard_map/conv_general_dilated | solution.py:64
  26.4 0.0 copy-start
  26.4 0.1 copy-done.1
  26.6 0.7 %fusion.89 = f32[8,32,128]{2,1,0:T(8,128)} fusion(f32[8,32,128]{2,1,0:T(8,128)S(1)} %bitcast.123, bf16[8,32,128]{2,1,0:T(8,128)(2,1)S(1)} %copy-done.1), kind=kLoop, calls=%fused_computation.117 | loop fusion | flops 327680 | bytes 327680 | tf_op jit(solution)/shard_map/add | solution.py:407
  27.3 13.1 %shard_map.114 = (f32[256,128]{1,0:T(8,128)}, bf16[18,42,128]{2,1,0:T(8,128)(2,1)}, f32[16,1,256]{2,1,0:T(1,128)}) custom-call(f32[16,10,256]{2,1,0:T(8,128)} %get-tuple-element.7.got_ref, f32[256,128]{1,0:T(8,128)} %bitcast.125, f32[256,128]{1,0:T(8,128)} %bitcast.124), custom_call_target="tpu_custom_call" | custom-call | tf_op jit(solution)/shard_map/pallas_call | solution.py:341
  40.4 1.0 %pad.2 = bf16[18,1,48,128]{3,2,0,1:T(8,128)(2,1)S(1)} pad(bf16[18,1,42,128]{3,2,0,1:T(8,128)(2,1)} %bitcast.127, bf16[]{:T(256)} %constant.25.clone.1), padding=0_0x0_0x0_6x0_0 | pad | bytes 414722 | tf_op jit(solution)/shard_map/broadcast_in_dim | solution.py:79
  41.4 0.0 copy-start.13
  41.4 0.1 reshape.154
  41.5 0.5 %copy-done.13 = pred[8,6]{0,1:T(8,128)(4,1)S(1)} copy-done((pred[8,6]{0,1:T(8,128)(4,1)S(1)}, pred[8,6]{0,1:T(8,128)(4,1)}, u32[]{:S(2)}) %copy-start.13) | copy-done | bytes 72
  42.0 0.6 %convolution_select_fusion = f32[16,8,6,128]{3,1,2,0:T(8,128)S(1)} fusion(bf16[3,3,128,128]{3,2,1,0:T(8,128)(2,1)S(1)} %fusion.22, bf16[18,1,7,2,128]{4,2,3,0,1:T(8,128)(2,1)S(1)} %slice.91, bf16[18,1,8,6,128]{4,2,3,0,1:T(8,128)(2,1)S(1)} %copy.99, pred[8,6]{0,1:T(8,128)(4,1)S(1)} %copy-done.13), kind=kOutput, calls=%fused_computation | convolution fusion | flops 227475456 | bytes 973872 | tf_op jit(solution)/shard_map/conv_general_dilated | solution.py:78
  42.7 0.1 copy.100
  42.8 0.1 copy.149
  43.0 0.2 reduce_sum.19
  43.2 0.0 copy-start.14
  43.2 0.3 fusion.2
  43.6 0.3 copy-done.14
  43.9 0.3 convolution_select_fusion.2
  44.3 0.1 broadcast_in_dim.84
  44.4 0.2 reshape.150
  44.6 0.0 copy-start.12
  44.6 0.2 select_bitcast_fusion
  44.9 0.3 copy-done.12
  45.2 0.4 convolution_select_fusion.1
  45.7 0.5 %copy-done.4 = f32[256,128]{1,0:T(8,128)S(1)} copy-done((f32[256,128]{1,0:T(8,128)S(1)}, f32[256,128]{1,0:T(8,128)}, u32[]{:S(2)}) %copy-start.4) | copy-done | bytes 131096
  46.1 0.1 fusion.90
  46.2 0.7 %copy.110 = f32[8,32,128]{2,1,0:T(8,128)} copy(f32[8,32,128]{2,0,1:T(8,128)S(1)} %fusion.90) | data formatting | bytes 262144
  46.9 0.0 copy-done.8
  46.9 0.6 %copy.111 = f32[1,16,256]{2,1,0:T(8,128)} copy(f32[1,16,256]{2,0,1:T(1,128)S(1)} %bitcast.129) | data formatting | bytes 32768
  (32 shorter events, 0.5 us)
Async XLA Ops:
  0.6 1.5 %copy-start.11 = (s32[1,16]{1,0:T(1,128)S(1)}, s32[1,16]{1,0:T(1,128)}, u32[]{:S(2)}) copy-start(s32[1,16]{1,0:T(1,128)} %param.19) | copy-start | bytes 196
  0.6 1.4 %copy-start.7 = (s32[1,16,256]{2,1,0:T(8,128)S(1)}, s32[1,16,256]{2,1,0:T(8,128)}, u32[]{:S(2)}) copy-start(s32[1,16,256]{2,1,0:T(8,128)} %param.16) | copy-start | bytes 49156
  0.7 1.5 %copy-start.9 = (f32[1,16,256]{2,1,0:T(8,128)S(1)}, f32[1,16,256]{2,1,0:T(8,128)}, u32[]{:S(2)}) copy-start(f32[1,16,256]{2,1,0:T(8,128)} %param.18) | copy-start | bytes 49156
  0.7 1.6 %copy-start.5 = (f32[1,16,256,4]{2,3,1,0:T(4,128)S(1)}, f32[1,16,256,4]{2,3,1,0:T(4,128)}, u32[]{:S(2)}) copy-start(f32[1,16,256,4]{2,3,1,0:T(4,128)} %param.17) | copy-start | bytes 196612
  1.7 0.8 %copy-start.6 = (s32[1,16,256,4]{2,3,1,0:T(4,128)S(1)}, s32[1,16,256,4]{2,3,1,0:T(4,128)}, u32[]{:S(2)}) copy-start(s32[1,16,256,4]{2,3,1,0:T(4,128)} %param.15) | copy-start | bytes 196612
  21.6 1.0 %copy-start.2 = (bf16[3,3,3,32,64]{4,3,2,1,0:T(8,128)(2,1)S(1)}, bf16[3,3,3,32,64]{4,3,2,1,0:T(8,128)(2,1)}, u32[]{:S(2)}) copy-start(bf16[3,3,3,32,64]{4,3,2,1,0:T(8,128)(2,1)} %param.12) | copy-start | bytes 331780
  22.9 0.8 %copy-start.10 = (bf16[64,32]{0,1:T(8,128)(2,1)S(1)}, bf16[64,32]{0,1:T(8,128)(2,1)}, u32[]{:S(2)}) copy-start(bf16[64,32]{0,1:T(8,128)(2,1)} %param.14) | copy-start | bytes 12292
  24.4 0.9 %copy-start.3 = (bf16[3,3,3,32,32]{4,3,2,1,0:T(8,128)(2,1)S(1)}, bf16[3,3,3,32,32]{4,3,2,1,0:T(8,128)(2,1)}, u32[]{:S(2)}) copy-start(bf16[3,3,3,32,32]{4,3,2,1,0:T(8,128)(2,1)} %param.13) | copy-start | bytes 165892
  25.7 0.8 %copy-start.1 = (bf16[8,32,128]{2,1,0:T(8,128)(2,1)S(1)}, bf16[8,32,128]{2,1,0:T(8,128)(2,1)}, u32[]{:S(2)}) copy-start(bf16[8,32,128]{2,1,0:T(8,128)(2,1)} %x_ref.1) | copy-start | bytes 196612
  26.4 0.9 %copy-start = (f32[1,8,32,128]{3,0,2,1:T(1,128)}, f32[1,8,32,128]{3,0,2,1:T(1,128)S(1)}, u32[]{:S(2)}) copy-start(f32[1,8,32,128]{3,0,2,1:T(1,128)S(1)} %fusion.52) | copy-start | bytes 393220
  41.4 0.7 %copy-start.13 = (pred[8,6]{0,1:T(8,128)(4,1)S(1)}, pred[8,6]{0,1:T(8,128)(4,1)}, u32[]{:S(2)}) copy-start(pred[8,6]{0,1:T(8,128)(4,1)} %constant.92) | copy-start | bytes 148
  43.2 0.7 %copy-start.14 = (pred[8,3]{0,1:T(4,128)(4,1)S(1)}, pred[8,3]{0,1:T(4,128)(4,1)}, u32[]{:S(2)}) copy-start(pred[8,3]{0,1:T(4,128)(4,1)} %constant.93) | copy-start | bytes 76
  44.6 0.7 %copy-start.12 = (pred[8,5]{0,1:T(8,128)(4,1)S(1)}, pred[8,5]{0,1:T(8,128)(4,1)}, u32[]{:S(2)}) copy-start(pred[8,5]{0,1:T(8,128)(4,1)} %constant.45) | copy-start | bytes 124
  45.2 0.9 %copy-start.4 = (f32[256,128]{1,0:T(8,128)S(1)}, f32[256,128]{1,0:T(8,128)}, u32[]{:S(2)}) copy-start(f32[256,128]{1,0:T(8,128)} %get-tuple-element.9) | copy-start | bytes 393220
  45.6 1.3 %copy-start.8 = (f32[16,1,256]{2,1,0:T(1,128)S(1)}, f32[16,1,256]{2,1,0:T(1,128)}, u32[]{:S(2)}) copy-start(f32[16,1,256]{2,1,0:T(1,128)} %get-tuple-element.11) | copy-start | bytes 49156

commit v17 on v16

--- a/solution.py
+++ b/solution.py
@@ -216,7 +216,7 @@
     j = lax.axis_index("lon")
     has = {-1: i > 0, 0: i >= 0, 1: i < nlat - 1}
     mesh = pl.DeviceIdType.MESH
-    dirs = [(a, b) for a in (-1, 0, 1) for b in (-1, 0, 1) if (a, b) != (0, 0)]
+    dirs = [(a, b) for a in (-1, 1) for b in (-1, 1)] + [(-1, 0), (1, 0), (0, -1), (0, 1)]
     pl.semaphore_wait(pltpu.get_barrier_semaphore(), count)
     src_rows = {1: pl.ds(rows - width, width), -1: pl.ds(0, width), 0: pl.ds(0, rows)}
     dst_rows = {1: pl.ds(0, width), -1: pl.ds(width + rows, width), 0: pl.ds(width, rows)}

time: 48 us -> 48.2 us (level)
    pallas_call x1, Pallas kernels: 13.1 us -> 13.7 us  [observe_and_exchange(): pl.pallas_call(functools.partial(back_kernel, width, nlat, nlon), out_sha...]
where the time goes in v17:
time: 48.2 us; the launch traced here: 47.7 us
  Pallas kernels  28.7 us (60%)
  local copies, waits for them, and re-layouts  7.42 us (15%)
  matrix products  5.97 us (12%)
  other arithmetic  4.41 us (9%)
  between operations  1.18 us (2%)
    pallas_call x1, Pallas kernels, exchange(): pl.pallas_call(functools.partial(halo_kernel, width, nlat, nlon), out_sha...  15 us
    pallas_call x1, Pallas kernels, observe_and_exchange(): pl.pallas_call(functools.partial(back_kernel, width, nlat, nlon), out_sha...  13.7 us
    unnamed x34, local copies, waits for them, and re-layouts  4.26 us
    conv_general_dilated x3, matrix products, conv_valid(): lax.conv_general_dilated(padded[None], taps, (1, 1), 'VALID', dimension_n...  4.13 us
    conv_general_dilated x3, matrix products, adjoint_valid(): lax.conv_general_dilated(padded[None], taps, (1, 1), 'VALID', dimension_n...  1.33 us
    reduce_sum x2, other arithmetic, block_sum(): return fine.reshape(rows // 2, 2, cols // 2, 2, feats).sum(axis=(1, 3))  1.08 us
    squeeze x3, local copies, waits for them, and re-layouts, banded(): kernel[:, :, p - q + 1]  1.04 us
    broadcast_in_dim x3, local copies, waits for them, and re-layouts, adjoint_valid(): padded[None]  0.99 us

profile of v17, /device:TPU:0, one launch (start us, length us, event | category | flops | bytes accessed | tf_op | source)
XLA Modules:
  0.0 47.7 jit_solution(2335883555689889120)
XLA Ops:
  0.6 0.0 copy-start.11
  0.6 0.0 copy-start.7
  0.7 0.0 copy-start.9
  0.7 0.0 copy-start.5
  0.7 1.0 %slice_bitcast_fusion.9 = (bf16[3,3,32,32]{3,2,1,0:T(8,128)(2,1)S(1)}, bf16[3,3,32,32]{3,2,1,0:T(8,128)(2,1)S(1)}, bf16[3,3,32,32]{3,2,1,0:T(8,128)(2,1)S(1)}) fusion(bf16[3,3,3,32,32]{4,3,2,1,0:T(8,128)(2,1)} %param.11), kind=kLoop, calls=%fused_computation.140 | loop fusion | bytes 110592 | tf_op jit(solution)/shard_map/squeeze | solution.py:34
  1.7 0.0 copy-start.6
  1.7 0.3 fusion.19
  2.1 0.0 copy-done.7
  2.1 0.0 copy-done.11
  2.1 0.0 copy-done.9
  2.1 0.1 fusion.110
  2.2 0.1 fusion.111
  2.3 0.0 copy-done.5
  2.3 0.2 copy-done.6
  2.5 0.8 %maximum_bitcast_fusion.p_ref = f32[16,10,256]{2,1,0:T(8,128)} fusion(f32[1,16,1,256]{3,2,1,0:T(1,128)S(1)} %get-tuple-element.29, f32[1,16,4,256]{3,2,1,0:T(4,128)S(1)} %multiply_bitcast_fusion, f32[1,16,1,256]{3,2,1,0:T(1,128)S(1)} %get-tuple-element.30, f32[1,16,4,256]{3,2,1,0:T(4,128)S(1)} %convert_bitcast_fusion), kind=kLoop, calls=%fused_computation.57 | loop fusion | flops 122880 | bytes 327680 | tf_op jit(solution)/shard_map/reshape | solution.py:170
  3.3 15.0 %shard_map.113 = (bf16[22,46,128]{2,1,0:T(8,128)(2,1)}, f32[16,10,256]{2,1,0:T(8,128)}) custom-call(bf16[8,32,128]{2,1,0:T(8,128)(2,1)} %x_ref.1, f32[16,10,256]{2,1,0:T(8,128)} %maximum_bitcast_fusion.p_ref), custom_call_target="tpu_custom_call" | custom-call | tf_op jit(solution)/shard_map/pallas_call | solution.py:313
  18.4 2.8 %fusion.4 = f32[1,20,44,128]{3,0,2,1:T(1,128)S(1)} fusion(bf16[3,3,128,128]{3,2,1,0:T(8,128)(2,1)S(1)} %fusion.19, bf16[1,22,46,128]{3,2,1,0:T(8,128)(2,1)} %bitcast.132), kind=kOutput, calls=%fused_computation.12 | convolution fusion | flops 259522560 | bytes 1004544 | tf_op jit(solution)/shard_map/conv_general_dilated | solution.py:64
  21.2 0.0 copy-start.2
  21.2 0.8 %convert_reduce_fusion = f32[10,22,128]{2,1,0:T(8,128)S(1)} fusion(f32[10,2,22,2,128]{4,3,2,1,0:T(2,128)S(1)} %bitcast.115), kind=kLoop, calls=%fused_computation.24 | loop fusion | flops 1210880 | bytes 563200 | tf_op jit(solution)/shard_map/reduce_sum | solution.py:106
  22.0 0.1 fusion.104
  22.1 0.0 copy-done.2
  22.2 0.3 maximum_maximum_fusion
  22.5 0.0 copy-start.10
  22.5 0.7 %fusion.93 = f32[1,8,20,256]{3,0,2,1:T(1,128)S(1)} fusion(bf16[3,3,128,256]{3,2,1,0:T(8,128)(2,1)S(1)} %maximum_maximum_fusion, bf16[1,10,22,128]{3,2,1,0:T(8,128)(2,1)S(1)} %fusion.104), kind=kOutput, calls=%fused_computation.125 | convolution fusion | flops 94371840 | bytes 809984 | tf_op jit(solution)/shard_map/conv_general_dilated | solution.py:64
  23.2 0.1 fusion.74
  23.3 0.0 copy-done.10
  23.3 0.1 copy.89
  23.4 0.2 fusion.96
  23.7 0.1 broadcast_in_dim.77
  23.7 0.2 reshape.147
  23.9 0.1 fusion.7
  24.0 0.0 copy-start.3
  24.1 0.1 select_bitcast_fusion.1
  24.2 0.8 %copy-done.3 = bf16[3,3,3,32,32]{4,3,2,1,0:T(8,128)(2,1)S(1)} copy-done((bf16[3,3,3,32,32]{4,3,2,1,0:T(8,128)(2,1)S(1)}, bf16[3,3,3,32,32]{4,3,2,1,0:T(8,128)(2,1)}, u32[]{:S(2)}) %copy-start.3) | copy-done | bytes 55320
  25.0 0.3 fusion.22
  25.3 0.0 copy-start.1
  25.3 0.7 %fusion.52 = f32[1,8,32,128]{3,0,2,1:T(1,128)S(1)} fusion(bf16[3,3,128,128]{3,2,1,0:T(8,128)(2,1)S(1)} %fusion.22, bf16[1,10,34,128]{3,2,1,0:T(8,128)(2,1)S(1)} %select_bitcast_fusion.1), kind=kOutput, calls=%fused_computation.81 | convolution fusion | flops 75497472 | bytes 513024 | tf_op jit(solution)/shard_map/conv_general_dilated | solution.py:64
  26.0 0.0 copy-start
  26.0 0.1 copy-done.1
  26.2 0.7 %fusion.89 = f32[8,32,128]{2,1,0:T(8,128)} fusion(f32[8,32,128]{2,1,0:T(8,128)S(1)} %bitcast.123, bf16[8,32,128]{2,1,0:T(8,128)(2,1)S(1)} %copy-done.1), kind=kLoop, calls=%fused_computation.117 | loop fusion | flops 327680 | bytes 327680 | tf_op jit(solution)/shard_map/add | solution.py:407
  26.9 13.7 %shard_map.114 = (f32[256,128]{1,0:T(8,128)}, bf16[18,42,128]{2,1,0:T(8,128)(2,1)}, f32[16,1,256]{2,1,0:T(1,128)}) custom-call(f32[16,10,256]{2,1,0:T(8,128)} %get-tuple-element.7.got_ref, f32[256,128]{1,0:T(8,128)} %bitcast.125, f32[256,128]{1,0:T(8,128)} %bitcast.124), custom_call_target="tpu_custom_call" | custom-call | tf_op jit(solution)/shard_map/pallas_call | solution.py:341
  40.6 1.0 %pad.2 = bf16[18,1,48,128]{3,2,0,1:T(8,128)(2,1)S(1)} pad(bf16[18,1,42,128]{3,2,0,1:T(8,128)(2,1)} %bitcast.127, bf16[]{:T(256)} %constant.25.clone.1), padding=0_0x0_0x0_6x0_0 | pad | bytes 414722 | tf_op jit(solution)/shard_map/broadcast_in_dim | solution.py:79
  41.6 0.0 copy-start.13
  41.6 0.1 reshape.154
  41.7 0.5 %copy-done.13 = pred[8,6]{0,1:T(8,128)(4,1)S(1)} copy-done((pred[8,6]{0,1:T(8,128)(4,1)S(1)}, pred[8,6]{0,1:T(8,128)(4,1)}, u32[]{:S(2)}) %copy-start.13) | copy-done | bytes 72
  42.2 0.6 %convolution_select_fusion = f32[16,8,6,128]{3,1,2,0:T(8,128)S(1)} fusion(bf16[3,3,128,128]{3,2,1,0:T(8,128)(2,1)S(1)} %fusion.22, bf16[18,1,7,2,128]{4,2,3,0,1:T(8,128)(2,1)S(1)} %slice.91, bf16[18,1,8,6,128]{4,2,3,0,1:T(8,128)(2,1)S(1)} %copy.99, pred[8,6]{0,1:T(8,128)(4,1)S(1)} %copy-done.13), kind=kOutput, calls=%fused_computation | convolution fusion | flops 227475456 | bytes 973872 | tf_op jit(solution)/shard_map/conv_general_dilated | solution.py:78
  42.9 0.1 copy.100
  43.0 0.1 copy.149
  43.2 0.2 reduce_sum.19
  43.4 0.0 copy-start.14
  43.4 0.3 fusion.2
  43.8 0.3 copy-done.14
  44.1 0.3 convolution_select_fusion.2
  44.5 0.1 broadcast_in_dim.84
  44.6 0.2 reshape.150
  44.8 0.0 copy-start.12
  44.8 0.2 select_bitcast_fusion
  45.1 0.3 copy-done.12
  45.4 0.4 convolution_select_fusion.1
  45.8 0.0 copy-start.8
  45.9 0.5 %copy-done.4 = f32[256,128]{1,0:T(8,128)S(1)} copy-done((f32[256,128]{1,0:T(8,128)S(1)}, f32[256,128]{1,0:T(8,128)}, u32[]{:S(2)}) %copy-start.4) | copy-done | bytes 131096
  46.3 0.1 fusion.90
  46.4 0.7 %copy.110 = f32[8,32,128]{2,1,0:T(8,128)} copy(f32[8,32,128]{2,0,1:T(8,128)S(1)} %fusion.90) | data formatting | bytes 262144
  47.1 0.6 %copy.111 = f32[1,16,256]{2,1,0:T(8,128)} copy(f32[1,16,256]{2,0,1:T(1,128)S(1)} %bitcast.129) | data formatting | bytes 32768
  (32 shorter events, 0.5 us)
Async XLA Ops:
  0.6 1.5 %copy-start.11 = (s32[1,16]{1,0:T(1,128)S(1)}, s32[1,16]{1,0:T(1,128)}, u32[]{:S(2)}) copy-start(s32[1,16]{1,0:T(1,128)} %param.19) | copy-start | bytes 196
  0.6 1.4 %copy-start.7 = (s32[1,16,256]{2,1,0:T(8,128)S(1)}, s32[1,16,256]{2,1,0:T(8,128)}, u32[]{:S(2)}) copy-start(s32[1,16,256]{2,1,0:T(8,128)} %param.16) | copy-start | bytes 49156
  0.7 1.5 %copy-start.9 = (f32[1,16,256]{2,1,0:T(8,128)S(1)}, f32[1,16,256]{2,1,0:T(8,128)}, u32[]{:S(2)}) copy-start(f32[1,16,256]{2,1,0:T(8,128)} %param.18) | copy-start | bytes 49156
  0.7 1.6 %copy-start.5 = (f32[1,16,256,4]{2,3,1,0:T(4,128)S(1)}, f32[1,16,256,4]{2,3,1,0:T(4,128)}, u32[]{:S(2)}) copy-start(f32[1,16,256,4]{2,3,1,0:T(4,128)} %param.17) | copy-start | bytes 196612
  1.7 0.8 %copy-start.6 = (s32[1,16,256,4]{2,3,1,0:T(4,128)S(1)}, s32[1,16,256,4]{2,3,1,0:T(4,128)}, u32[]{:S(2)}) copy-start(s32[1,16,256,4]{2,3,1,0:T(4,128)} %param.15) | copy-start | bytes 196612
  21.2 1.0 %copy-start.2 = (bf16[3,3,3,32,64]{4,3,2,1,0:T(8,128)(2,1)S(1)}, bf16[3,3,3,32,64]{4,3,2,1,0:T(8,128)(2,1)}, u32[]{:S(2)}) copy-start(bf16[3,3,3,32,64]{4,3,2,1,0:T(8,128)(2,1)} %param.12) | copy-start | bytes 331780
  22.5 0.8 %copy-start.10 = (bf16[64,32]{0,1:T(8,128)(2,1)S(1)}, bf16[64,32]{0,1:T(8,128)(2,1)}, u32[]{:S(2)}) copy-start(bf16[64,32]{0,1:T(8,128)(2,1)} %param.14) | copy-start | bytes 12292
  24.0 0.9 %copy-start.3 = (bf16[3,3,3,32,32]{4,3,2,1,0:T(8,128)(2,1)S(1)}, bf16[3,3,3,32,32]{4,3,2,1,0:T(8,128)(2,1)}, u32[]{:S(2)}) copy-start(bf16[3,3,3,32,32]{4,3,2,1,0:T(8,128)(2,1)} %param.13) | copy-start | bytes 165892
  25.3 0.8 %copy-start.1 = (bf16[8,32,128]{2,1,0:T(8,128)(2,1)S(1)}, bf16[8,32,128]{2,1,0:T(8,128)(2,1)}, u32[]{:S(2)}) copy-start(bf16[8,32,128]{2,1,0:T(8,128)(2,1)} %x_ref.1) | copy-start | bytes 196612
  26.0 0.9 %copy-start = (f32[1,8,32,128]{3,0,2,1:T(1,128)}, f32[1,8,32,128]{3,0,2,1:T(1,128)S(1)}, u32[]{:S(2)}) copy-start(f32[1,8,32,128]{3,0,2,1:T(1,128)S(1)} %fusion.52) | copy-start | bytes 393220
  41.6 0.7 %copy-start.13 = (pred[8,6]{0,1:T(8,128)(4,1)S(1)}, pred[8,6]{0,1:T(8,128)(4,1)}, u32[]{:S(2)}) copy-start(pred[8,6]{0,1:T(8,128)(4,1)} %constant.92) | copy-start | bytes 148
  43.4 0.7 %copy-start.14 = (pred[8,3]{0,1:T(4,128)(4,1)S(1)}, pred[8,3]{0,1:T(4,128)(4,1)}, u32[]{:S(2)}) copy-start(pred[8,3]{0,1:T(4,128)(4,1)} %constant.93) | copy-start | bytes 76
  44.8 0.7 %copy-start.12 = (pred[8,5]{0,1:T(8,128)(4,1)S(1)}, pred[8,5]{0,1:T(8,128)(4,1)}, u32[]{:S(2)}) copy-start(pred[8,5]{0,1:T(8,128)(4,1)} %constant.45) | copy-start | bytes 124
  45.4 0.9 %copy-start.4 = (f32[256,128]{1,0:T(8,128)S(1)}, f32[256,128]{1,0:T(8,128)}, u32[]{:S(2)}) copy-start(f32[256,128]{1,0:T(8,128)} %get-tuple-element.9) | copy-start | bytes 393220
  45.8 1.3 %copy-start.8 = (f32[16,1,256]{2,1,0:T(1,128)S(1)}, f32[16,1,256]{2,1,0:T(1,128)}, u32[]{:S(2)}) copy-start(f32[16,1,256]{2,1,0:T(1,128)} %get-tuple-element.11) | copy-start | bytes 49156

commit v18 on v17

--- a/solution.py
+++ b/solution.py
@@ -222,18 +222,28 @@
     dst_rows = {1: pl.ds(0, width), -1: pl.ds(width + rows, width), 0: pl.ds(width, rows)}
     src_cols = {1: pl.ds(cols - edge, edge), -1: pl.ds(0, edge), 0: pl.ds(0, cols)}
     dst_cols = {1: pl.ds(0, edge), -1: pl.ds(edge + cols, edge), 0: pl.ds(edge, cols)}
-    sends = []
-    for t in range(nlon):
-        copy = pltpu.make_async_remote_copy(
+    order = sorted(range(1, nlon), key=lambda d: -min(d, nlon - d))
+    for d in order:
+        t = (j + d) % nlon
+        pltpu.make_async_remote_copy(
             src_ref=p_ref.at[pl.ds(t, 1)],
             dst_ref=inbox.at[pl.ds(j, 1)],
             send_sem=p_send.at[t],
             recv_sem=p_recv.at[j],
             device_id=(i, t),
             device_id_type=mesh,
-        )
-        sends.append(copy)
-        pl.when(t != j)(copy.start)
+        ).start()
+    sends = [
+        pltpu.make_async_remote_copy(
+            src_ref=p_ref.at[pl.ds(t, 1)],
+            dst_ref=inbox.at[pl.ds(j, 1)],
+            send_sem=p_send.at[t],
+            recv_sem=p_recv.at[j],
+            device_id=(i, t),
+            device_id_type=mesh,
+        )
+        for t in range(nlon)
+    ]
     copies = []
     for k, (a, b) in enumerate(dirs):
         copy = pltpu.make_async_remote_copy(

time: 48.2 us -> 47.8 us (level)
  no operation moved by 1% of the time
where the time goes in v18:
time: 47.8 us; the launch traced here: 47.4 us
  Pallas kernels  28.4 us (59%)
  local copies, waits for them, and re-layouts  7.42 us (16%)
  matrix products  5.97 us (12%)
  other arithmetic  4.41 us (9%)
  between operations  1.18 us (2%)
    pallas_call x1, Pallas kernels, exchange(): pl.pallas_call(functools.partial(halo_kernel, width, nlat, nlon), out_sha...  15 us
    pallas_call x1, Pallas kernels, observe_and_exchange(): pl.pallas_call(functools.partial(back_kernel, width, nlat, nlon), out_sha...  13.4 us
    unnamed x34, local copies, waits for them, and re-layouts  4.26 us
    conv_general_dilated x3, matrix products, conv_valid(): lax.conv_general_dilated(padded[None], taps, (1, 1), 'VALID', dimension_n...  4.13 us
    conv_general_dilated x3, matrix products, adjoint_valid(): lax.conv_general_dilated(padded[None], taps, (1, 1), 'VALID', dimension_n...  1.33 us
    reduce_sum x2, other arithmetic, block_sum(): return fine.reshape(rows // 2, 2, cols // 2, 2, feats).sum(axis=(1, 3))  1.08 us
    squeeze x3, local copies, waits for them, and re-layouts, banded(): kernel[:, :, p - q + 1]  1.04 us
    broadcast_in_dim x3, local copies, waits for them, and re-layouts, adjoint_valid(): padded[None]  0.99 us

profile of v18, /device:TPU:0, one launch (start us, length us, event | category | flops | bytes accessed | tf_op | source)
XLA Modules:
  0.0 47.4 jit_solution(3367205566252172161)
XLA Ops:
  0.6 0.0 copy-start.11
  0.6 0.0 copy-start.7
  0.7 0.0 copy-start.9
  0.7 0.0 copy-start.5
  0.7 1.0 %slice_bitcast_fusion.9 = (bf16[3,3,32,32]{3,2,1,0:T(8,128)(2,1)S(1)}, bf16[3,3,32,32]{3,2,1,0:T(8,128)(2,1)S(1)}, bf16[3,3,32,32]{3,2,1,0:T(8,128)(2,1)S(1)}) fusion(bf16[3,3,3,32,32]{4,3,2,1,0:T(8,128)(2,1)} %param.11), kind=kLoop, calls=%fused_computation.140 | loop fusion | bytes 110592 | tf_op jit(solution)/shard_map/squeeze | solution.py:34
  1.7 0.0 copy-start.6
  1.7 0.3 fusion.19
  2.1 0.0 copy-done.7
  2.1 0.0 copy-done.11
  2.1 0.0 copy-done.9
  2.1 0.1 fusion.110
  2.2 0.1 fusion.111
  2.3 0.0 copy-done.5
  2.3 0.2 copy-done.6
  2.5 0.8 %maximum_bitcast_fusion.p_ref = f32[16,10,256]{2,1,0:T(8,128)} fusion(f32[1,16,1,256]{3,2,1,0:T(1,128)S(1)} %get-tuple-element.29, f32[1,16,4,256]{3,2,1,0:T(4,128)S(1)} %multiply_bitcast_fusion, f32[1,16,1,256]{3,2,1,0:T(1,128)S(1)} %get-tuple-element.30, f32[1,16,4,256]{3,2,1,0:T(4,128)S(1)} %convert_bitcast_fusion), kind=kLoop, calls=%fused_computation.57 | loop fusion | flops 122880 | bytes 327680 | tf_op jit(solution)/shard_map/reshape | solution.py:170
  3.3 15.0 %shard_map.113 = (bf16[22,46,128]{2,1,0:T(8,128)(2,1)}, f32[16,10,256]{2,1,0:T(8,128)}) custom-call(bf16[8,32,128]{2,1,0:T(8,128)(2,1)} %x_ref.1, f32[16,10,256]{2,1,0:T(8,128)} %maximum_bitcast_fusion.p_ref), custom_call_target="tpu_custom_call" | custom-call | tf_op jit(solution)/shard_map/pallas_call | solution.py:323
  18.4 2.8 %fusion.4 = f32[1,20,44,128]{3,0,2,1:T(1,128)S(1)} fusion(bf16[3,3,128,128]{3,2,1,0:T(8,128)(2,1)S(1)} %fusion.19, bf16[1,22,46,128]{3,2,1,0:T(8,128)(2,1)} %bitcast.132), kind=kOutput, calls=%fused_computation.12 | convolution fusion | flops 259522560 | bytes 1004544 | tf_op jit(solution)/shard_map/conv_general_dilated | solution.py:64
  21.2 0.0 copy-start.2
  21.2 0.8 %convert_reduce_fusion = f32[10,22,128]{2,1,0:T(8,128)S(1)} fusion(f32[10,2,22,2,128]{4,3,2,1,0:T(2,128)S(1)} %bitcast.115), kind=kLoop, calls=%fused_computation.24 | loop fusion | flops 1210880 | bytes 563200 | tf_op jit(solution)/shard_map/reduce_sum | solution.py:106
  22.0 0.1 fusion.104
  22.1 0.0 copy-done.2
  22.2 0.3 maximum_maximum_fusion
  22.5 0.0 copy-start.10
  22.5 0.7 %fusion.93 = f32[1,8,20,256]{3,0,2,1:T(1,128)S(1)} fusion(bf16[3,3,128,256]{3,2,1,0:T(8,128)(2,1)S(1)} %maximum_maximum_fusion, bf16[1,10,22,128]{3,2,1,0:T(8,128)(2,1)S(1)} %fusion.104), kind=kOutput, calls=%fused_computation.125 | convolution fusion | flops 94371840 | bytes 809984 | tf_op jit(solution)/shard_map/conv_general_dilated | solution.py:64
  23.2 0.1 fusion.74
  23.3 0.0 copy-done.10
  23.3 0.1 copy.89
  23.4 0.2 fusion.96
  23.7 0.1 broadcast_in_dim.77
  23.7 0.2 reshape.147
  23.9 0.1 fusion.7
  24.0 0.0 copy-start.3
  24.1 0.1 select_bitcast_fusion.1
  24.2 0.8 %copy-done.3 = bf16[3,3,3,32,32]{4,3,2,1,0:T(8,128)(2,1)S(1)} copy-done((bf16[3,3,3,32,32]{4,3,2,1,0:T(8,128)(2,1)S(1)}, bf16[3,3,3,32,32]{4,3,2,1,0:T(8,128)(2,1)}, u32[]{:S(2)}) %copy-start.3) | copy-done | bytes 55320
  25.0 0.3 fusion.22
  25.3 0.0 copy-start.1
  25.3 0.7 %fusion.52 = f32[1,8,32,128]{3,0,2,1:T(1,128)S(1)} fusion(bf16[3,3,128,128]{3,2,1,0:T(8,128)(2,1)S(1)} %fusion.22, bf16[1,10,34,128]{3,2,1,0:T(8,128)(2,1)S(1)} %select_bitcast_fusion.1), kind=kOutput, calls=%fused_computation.81 | convolution fusion | flops 75497472 | bytes 513024 | tf_op jit(solution)/shard_map/conv_general_dilated | solution.py:64
  26.0 0.1 copy-done.1
  26.2 0.7 %fusion.89 = f32[8,32,128]{2,1,0:T(8,128)} fusion(f32[8,32,128]{2,1,0:T(8,128)S(1)} %bitcast.123, bf16[8,32,128]{2,1,0:T(8,128)(2,1)S(1)} %copy-done.1), kind=kLoop, calls=%fused_computation.117 | loop fusion | flops 327680 | bytes 327680 | tf_op jit(solution)/shard_map/add | solution.py:417
  26.9 0.0 copy-done
  26.9 13.4 %shard_map.114 = (f32[256,128]{1,0:T(8,128)}, bf16[18,42,128]{2,1,0:T(8,128)(2,1)}, f32[16,1,256]{2,1,0:T(1,128)}) custom-call(f32[16,10,256]{2,1,0:T(8,128)} %get-tuple-element.7.got_ref, f32[256,128]{1,0:T(8,128)} %bitcast.125, f32[256,128]{1,0:T(8,128)} %bitcast.124), custom_call_target="tpu_custom_call" | custom-call | tf_op jit(solution)/shard_map/pallas_call | solution.py:351
  40.2 1.0 %pad.2 = bf16[18,1,48,128]{3,2,0,1:T(8,128)(2,1)S(1)} pad(bf16[18,1,42,128]{3,2,0,1:T(8,128)(2,1)} %bitcast.127, bf16[]{:T(256)} %constant.25.clone.1), padding=0_0x0_0x0_6x0_0 | pad | bytes 414722 | tf_op jit(solution)/shard_map/broadcast_in_dim | solution.py:79
  41.2 0.0 copy-start.13
  41.2 0.1 reshape.154
  41.4 0.5 %copy-done.13 = pred[8,6]{0,1:T(8,128)(4,1)S(1)} copy-done((pred[8,6]{0,1:T(8,128)(4,1)S(1)}, pred[8,6]{0,1:T(8,128)(4,1)}, u32[]{:S(2)}) %copy-start.13) | copy-done | bytes 72
  41.9 0.6 %convolution_select_fusion = f32[16,8,6,128]{3,1,2,0:T(8,128)S(1)} fusion(bf16[3,3,128,128]{3,2,1,0:T(8,128)(2,1)S(1)} %fusion.22, bf16[18,1,7,2,128]{4,2,3,0,1:T(8,128)(2,1)S(1)} %slice.91, bf16[18,1,8,6,128]{4,2,3,0,1:T(8,128)(2,1)S(1)} %copy.99, pred[8,6]{0,1:T(8,128)(4,1)S(1)} %copy-done.13), kind=kOutput, calls=%fused_computation | convolution fusion | flops 227475456 | bytes 973872 | tf_op jit(solution)/shard_map/conv_general_dilated | solution.py:78
  42.5 0.1 copy.100
  42.7 0.1 copy.149
  42.8 0.2 reduce_sum.19
  43.1 0.0 copy-start.14
  43.1 0.3 fusion.2
  43.5 0.3 copy-done.14
  43.7 0.3 convolution_select_fusion.2
  44.2 0.1 broadcast_in_dim.84
  44.3 0.2 reshape.150
  44.4 0.0 copy-start.12
  44.4 0.2 select_bitcast_fusion
  44.8 0.3 copy-done.12
  45.1 0.4 convolution_select_fusion.1
  45.5 0.5 %copy-done.4 = f32[256,128]{1,0:T(8,128)S(1)} copy-done((f32[256,128]{1,0:T(8,128)S(1)}, f32[256,128]{1,0:T(8,128)}, u32[]{:S(2)}) %copy-start.4) | copy-done | bytes 131096
  46.0 0.1 fusion.90
  46.1 0.7 %copy.110 = f32[8,32,128]{2,1,0:T(8,128)} copy(f32[8,32,128]{2,0,1:T(8,128)S(1)} %fusion.90) | data formatting | bytes 262144
  46.8 0.0 copy-done.8
  46.8 0.6 %copy.111 = f32[1,16,256]{2,1,0:T(8,128)} copy(f32[1,16,256]{2,0,1:T(1,128)S(1)} %bitcast.129) | data formatting | bytes 32768
  (32 shorter events, 0.5 us)
Async XLA Ops:
  0.6 1.5 %copy-start.11 = (s32[1,16]{1,0:T(1,128)S(1)}, s32[1,16]{1,0:T(1,128)}, u32[]{:S(2)}) copy-start(s32[1,16]{1,0:T(1,128)} %param.19) | copy-start | bytes 196
  0.6 1.4 %copy-start.7 = (s32[1,16,256]{2,1,0:T(8,128)S(1)}, s32[1,16,256]{2,1,0:T(8,128)}, u32[]{:S(2)}) copy-start(s32[1,16,256]{2,1,0:T(8,128)} %param.16) | copy-start | bytes 49156
  0.7 1.5 %copy-start.9 = (f32[1,16,256]{2,1,0:T(8,128)S(1)}, f32[1,16,256]{2,1,0:T(8,128)}, u32[]{:S(2)}) copy-start(f32[1,16,256]{2,1,0:T(8,128)} %param.18) | copy-start | bytes 49156
  0.7 1.6 %copy-start.5 = (f32[1,16,256,4]{2,3,1,0:T(4,128)S(1)}, f32[1,16,256,4]{2,3,1,0:T(4,128)}, u32[]{:S(2)}) copy-start(f32[1,16,256,4]{2,3,1,0:T(4,128)} %param.17) | copy-start | bytes 196612
  1.7 0.8 %copy-start.6 = (s32[1,16,256,4]{2,3,1,0:T(4,128)S(1)}, s32[1,16,256,4]{2,3,1,0:T(4,128)}, u32[]{:S(2)}) copy-start(s32[1,16,256,4]{2,3,1,0:T(4,128)} %param.15) | copy-start | bytes 196612
  21.2 1.0 %copy-start.2 = (bf16[3,3,3,32,64]{4,3,2,1,0:T(8,128)(2,1)S(1)}, bf16[3,3,3,32,64]{4,3,2,1,0:T(8,128)(2,1)}, u32[]{:S(2)}) copy-start(bf16[3,3,3,32,64]{4,3,2,1,0:T(8,128)(2,1)} %param.12) | copy-start | bytes 331780
  22.5 0.8 %copy-start.10 = (bf16[64,32]{0,1:T(8,128)(2,1)S(1)}, bf16[64,32]{0,1:T(8,128)(2,1)}, u32[]{:S(2)}) copy-start(bf16[64,32]{0,1:T(8,128)(2,1)} %param.14) | copy-start | bytes 12292
  24.0 0.9 %copy-start.3 = (bf16[3,3,3,32,32]{4,3,2,1,0:T(8,128)(2,1)S(1)}, bf16[3,3,3,32,32]{4,3,2,1,0:T(8,128)(2,1)}, u32[]{:S(2)}) copy-start(bf16[3,3,3,32,32]{4,3,2,1,0:T(8,128)(2,1)} %param.13) | copy-start | bytes 165892
  25.3 0.8 %copy-start.1 = (bf16[8,32,128]{2,1,0:T(8,128)(2,1)S(1)}, bf16[8,32,128]{2,1,0:T(8,128)(2,1)}, u32[]{:S(2)}) copy-start(bf16[8,32,128]{2,1,0:T(8,128)(2,1)} %x_ref.1) | copy-start | bytes 196612
  26.0 0.9 %copy-start = (f32[1,8,32,128]{3,0,2,1:T(1,128)}, f32[1,8,32,128]{3,0,2,1:T(1,128)S(1)}, u32[]{:S(2)}) copy-start(f32[1,8,32,128]{3,0,2,1:T(1,128)S(1)} %fusion.52) | copy-start | bytes 393220
  41.2 0.7 %copy-start.13 = (pred[8,6]{0,1:T(8,128)(4,1)S(1)}, pred[8,6]{0,1:T(8,128)(4,1)}, u32[]{:S(2)}) copy-start(pred[8,6]{0,1:T(8,128)(4,1)} %constant.92) | copy-start | bytes 148
  43.1 0.7 %copy-start.14 = (pred[8,3]{0,1:T(4,128)(4,1)S(1)}, pred[8,3]{0,1:T(4,128)(4,1)}, u32[]{:S(2)}) copy-start(pred[8,3]{0,1:T(4,128)(4,1)} %constant.93) | copy-start | bytes 76
  44.4 0.7 %copy-start.12 = (pred[8,5]{0,1:T(8,128)(4,1)S(1)}, pred[8,5]{0,1:T(8,128)(4,1)}, u32[]{:S(2)}) copy-start(pred[8,5]{0,1:T(8,128)(4,1)} %constant.45) | copy-start | bytes 124
  45.1 0.9 %copy-start.4 = (f32[256,128]{1,0:T(8,128)S(1)}, f32[256,128]{1,0:T(8,128)}, u32[]{:S(2)}) copy-start(f32[256,128]{1,0:T(8,128)} %get-tuple-element.9) | copy-start | bytes 393220
  45.5 1.3 %copy-start.8 = (f32[16,1,256]{2,1,0:T(1,128)S(1)}, f32[16,1,256]{2,1,0:T(1,128)}, u32[]{:S(2)}) copy-start(f32[16,1,256]{2,1,0:T(1,128)} %get-tuple-element.11) | copy-start | bytes 49156
